TPU v7x, 256 devices: a whole 4x4x8 slice. The times are simulated.
256 devices in a mesh: gx: 16 (over z_lo, x, core), gy: 4 (over y), tx: 4 (over z_hi).
Axes of the slice: x: 4, y: 4, z: 8 (z_hi: 4, z_lo: 2; z = z_hi * 2 + z_lo), core: 2. Of those that a mesh axis runs over, the one named last changes fastest.
Arguments:
- src_cell: int32 [8], P('tx'), may hold values from 0 to 524287
- basis: bfloat16 [16, 2, 3, 8, 128, 512], P('tx', None, None, None, 'gx', 'gy'), as said below
- images: bfloat16 [16, 2, 3, 8, 128, 512], P('tx', None, None, None, 'gx', 'gy'), as said below
- induction: bfloat16 [3, 8, 128, 512], P(None, 'tx', 'gx', 'gy'), may hold values from 0.25 to 4
Outputs:
- solution: float32 [8, 2, 3, 8, 128, 512], P('tx', None, None, None, 'gx', 'gy')
- residual: float32 [8, 2, 3, 8, 128, 512], P('tx', None, None, None, 'gx', 'gy')
Inputs may be any that keep to these rules, and one draw needn't show every extreme that they name: `basis`: entries of order one. `images`: entries of order one.
All inputs are finite; a program needn't handle non-finite values.
Results may differ from a plain program's by a relative error of at most 0.0003.
Values may be sent and summed in bfloat16 or wider, within the bound.
No kernel may reach another device: no remote copies, remote signals or barrier semaphores. Data moves between devices by JAX's collectives and lax.ppermute only.
A program may use at most 64 MiB of HBM per device.

v0:
```python
import jax
import jax.numpy as jnp
from jax import lax
from jax.sharding import PartitionSpec as P

CYCLES = 2
ARNOLDI = 2


eps = 1e-06


def with_halo(x, sides, width):
    for axis, dim in sides:
        size, length = (lax.axis_size(axis), x.shape[dim])
        up = [(i, (i + 1) % size) for i in range(size - 1)]
        down = [(j, i) for i, j in up]
        last = lax.slice_in_dim(x, length - width, length, axis=dim)
        initial = lax.slice_in_dim(x, 0, width, axis=dim)
        before = lax.ppermute(last, axis, up)
        after = lax.ppermute(initial, axis, down)
        x = jnp.concatenate([before, x, after], axis=dim)
    return x


def differ(field, axis, forward):
    axis = field.ndim + axis
    count = field.shape[axis]
    delta = lax.slice_in_dim(field, 1, count, axis=axis) - lax.slice_in_dim(
        field, 0, count - 1, axis=axis
    )
    zero = jnp.zeros_like(lax.slice_in_dim(field, 0, 1, axis=axis))
    if forward:
        return jnp.concatenate([delta, zero], axis=axis)
    return jnp.concatenate([zero, delta], axis=axis)


def curl_curl(padded):
    e_x = padded[..., 0, :, :, :]
    e_y = padded[..., 1, :, :, :]
    e_z = padded[..., 2, :, :, :]
    b_x = differ(e_z, -1, True) - differ(e_y, -3, True)
    b_y = differ(e_x, -3, True) - differ(e_z, -2, True)
    b_z = differ(e_y, -2, True) - differ(e_x, -1, True)
    c_x = differ(b_z, -1, False) - differ(b_y, -3, False)
    c_y = differ(b_x, -3, False) - differ(b_z, -2, False)
    c_z = differ(b_y, -2, False) - differ(b_x, -1, False)
    whole = jnp.stack([c_x, c_y, c_z], axis=-4)
    return whole[..., 1:-1, 1:-1, 1:-1]


def apply_operator(field, induct):
    framed = with_halo(field, (("gx", 4), ("gy", 5)), 1)
    padded = jnp.pad(framed, [(0, 0), (0, 0), (0, 0), (1, 1), (0, 0), (0, 0)])
    curled = curl_curl(padded)
    real_part = curled[:, 0] - induct[None] * field[:, 1]
    imag_part = curled[:, 1] + induct[None] * field[:, 0]
    return jnp.stack([real_part, imag_part], axis=1)


def source_field(cells, z_pos, x_pos, y_pos, size_x, size_y, induct):
    plane = size_x * size_y
    src_z = cells // plane
    rest = cells % plane
    src_x = rest // size_y
    src_y = rest % size_y
    d_z = (z_pos[None, :] - src_z[:, None]).astype(jnp.float32)
    d_x = (x_pos[None, :] - src_x[:, None]).astype(jnp.float32)
    d_y = (y_pos[None, :] - src_y[:, None]).astype(jnp.float32)
    dist = jnp.sqrt(
        d_z[:, :, None, None] ** 2 + d_x[:, None, :, None] ** 2 + d_y[:, None, None, :] ** 2
    )
    primary = jnp.exp(-dist / ((size_x + size_y) / 8.0))
    weights = jnp.array([1.0, 0.5, 0.25], dtype=jnp.float32)
    real_part = (induct - 1.0)[None] * weights[None, :, None, None, None] * primary[:, None]
    return jnp.stack([real_part, 0.5 * real_part], axis=1)


def inner_basis(vectors, field):
    return jnp.einsum(
        "kpczxy,spczxy->ks",
        vectors,
        field,
        precision=lax.Precision.HIGHEST,
        preferred_element_type=jnp.float32,
    )


def combine(coeffs, vectors):
    return jnp.einsum(
        "ks,kpczxy->spczxy",
        coeffs,
        vectors,
        precision=lax.Precision.HIGHEST,
        preferred_element_type=jnp.float32,
    )


def per_source(left, right):
    return jnp.sum(left * right, axis=(1, 2, 3, 4, 5))


def expand(values):
    return values[:, None, None, None, None, None]


def small_solve(matrix, rhs):
    factor = jnp.linalg.cholesky(matrix)
    return jax.scipy.linalg.cho_solve((factor, True), rhs)


def on_device(src_cell, basis, images, induction):
    all_basis, all_images, gathered = (
        lax.all_gather(basis, "tx", axis=0, tiled=True),
        lax.all_gather(images, "tx", axis=0, tiled=True),
        lax.all_gather(induction, "tx", axis=1, tiled=True),
    )
    induct = gathered.astype(jnp.float32)
    depth = basis.shape[3]
    width_x = basis.shape[4]
    width_y = basis.shape[5]
    size_x = width_x * lax.axis_size("gx")
    size_y = width_y * lax.axis_size("gy")
    z_pos = jnp.arange(depth, dtype=jnp.int32)
    x_pos = lax.axis_index("gx") * width_x + jnp.arange(width_x, dtype=jnp.int32)
    y_pos = lax.axis_index("gy") * width_y + jnp.arange(width_y, dtype=jnp.int32)
    rhs = source_field(src_cell, z_pos, x_pos, y_pos, size_x, size_y, induct)
    gram_part = jnp.einsum(
        "kpczxy,lpczxy->kl", all_images, all_images, preferred_element_type=jnp.float32
    )
    gram, start_inner = lax.psum((gram_part, inner_basis(all_images, rhs)), ("gx", "gy"))
    factor = jnp.linalg.cholesky(gram)
    h_zero = jax.scipy.linalg.cho_solve((factor, True), start_inner)
    residual = rhs - combine(h_zero, all_images)
    solution = combine(h_zero, all_basis)
    for cycle in range(CYCLES):
        beta = jnp.sqrt(lax.psum(per_source(residual, residual), ("gx", "gy")) + eps)
        krylov = [residual / expand(beta)]
        h_cols = []
        g_cols = []
        for step in range(ARNOLDI):
            work = apply_operator(krylov[step], induct)
            g_raw = lax.psum(inner_basis(all_images, work), ("gx", "gy"))
            g_now = jax.scipy.linalg.cho_solve((factor, True), g_raw)
            work = work - combine(g_now, all_images)
            h_now = lax.psum(jnp.stack([per_source(vec, work) for vec in krylov]), ("gx", "gy"))
            for index in range(step + 1):
                work = work - expand(h_now[index]) * krylov[index]
            h_next = jnp.sqrt(lax.psum(per_source(work, work), ("gx", "gy")) + eps)
            krylov.append(work / expand(h_next))
            pad_rows = jnp.zeros((ARNOLDI - step - 1, h_next.shape[0]), dtype=jnp.float32)
            h_cols.append(jnp.concatenate([h_now, h_next[None], pad_rows], axis=0))
            g_cols.append(g_now)
        hess = jnp.stack(h_cols, axis=1)
        g_all = jnp.stack(g_cols, axis=1)
        normal = jnp.einsum("ijs,iks->sjk", hess, hess, precision=lax.Precision.HIGHEST)
        target = beta[:, None] * jnp.transpose(hess[0])
        y_coef = jax.vmap(small_solve)(normal, target)
        update = expand(y_coef[:, 0]) * krylov[0]
        step = 1
        update = update + expand(y_coef[:, step]) * krylov[step]
        u_coef = jnp.einsum("kjs,sj->ks", g_all, y_coef, precision=lax.Precision.HIGHEST)
        solution = solution + update - combine(u_coef, all_basis)
        first = jnp.zeros((ARNOLDI + 1, beta.shape[0]), dtype=jnp.float32).at[0].set(beta)
        t_coef = first - jnp.einsum("ijs,sj->is", hess, y_coef, precision=lax.Precision.HIGHEST)
        residual = expand(t_coef[0]) * krylov[0]
        for index in range(1, ARNOLDI + 1):
            residual = residual + expand(t_coef[index]) * krylov[index]
    return (solution, residual)


def solution(mesh):
    in_specs = (
        P("tx"),
        P("tx", None, None, None, "gx", "gy"),
        P("tx", None, None, None, "gx", "gy"),
        P(None, "tx", "gx", "gy"),
    )
    out_specs = (P("tx", None, None, None, "gx", "gy"), P("tx", None, None, None, "gx", "gy"))
    return jax.shard_map(
        on_device, mesh=mesh, in_specs=in_specs, out_specs=out_specs, check_vma=False
    )
```

profile of v0, /device:TPU:1, one launch (start us, length us, event | category | flops | bytes accessed | tf_op | source)
XLA Modules:
  0.0 2355.7 jit_solution(5453150176349590648)
XLA Ops:
  7.9 15.6 all_gather.10
  25.5 31.1 %all-gather.3.cloned.1.call-done = bf16[16,2,3,8,8,128]{5,4,3,2,1,0:T(8,128)(2,1)} async-done(((bf16[4,2,3,8,8,128]{5,4,3,2,1,0:T(8,128)(2,1)}), bf16[16,2,3,8,8,128]{5,4,3,2,1,0:T(8,128)(2,1)}) %all-gather.3.cloned.1.call-update) | async-done | bytes 1572880 | tf_op jit(solution)/shard_map/all_gather | solution.py:115
  56.6 5.4 convolution_bitcast_fusion
  62.0 3.7 convolution_bitcast_fusion.8
  65.7 139.0 %all-reduce.54 = (f32[16,2]{0,1:T(2,128)S(1)}, f32[16,16]{0,1:T(8,128)S(1)}) all-reduce(f32[16,2]{0,1:T(2,128)S(1)} %convolution_bitcast_fusion.8, f32[16,16]{0,1:T(8,128)S(1)} %convolution_bitcast_fusion), channel_id=1, replica_groups=mesh['gx'=16,'gy'=4,'tx'=4] {'gx','gy'}, use_global_device_ids=true, to_apply=%region_3.4 | all-reduce | flops 288 | bytes 2304 | tf_op jit(solution)/shard_map/psum | solution.py:131
  209.0 3.3 multiply_reduce_fusion.11
  212.3 138.4 %psum.114 = f32[2]{0:T(128)S(1)} all-reduce(f32[2]{0:T(128)S(1)} %get-tuple-element.119), channel_id=1, replica_groups=mesh['gx'=16,'gy'=4,'tx'=4] {'gx','gy'}, use_global_device_ids=true, to_apply=%region_5.7 | all-reduce | flops 2 | bytes 16 | tf_op jit(solution)/shard_map/psum | solution.py:137
  352.9 8.1 collective-permute-start.1
  362.7 3.9 collective-permute-start.2
  368.1 8.7 collective-permute-done.2
  376.8 3.9 collective-permute-done.3
  380.8 2.4 select_maximum_fusion.12
  390.8 3.7 convolution_bitcast_fusion.7
  394.4 134.2 %psum.115 = f32[16,2]{0,1:T(2,128)S(1)} all-reduce(f32[16,2]{0,1:T(2,128)S(1)} %convolution_bitcast_fusion.7), channel_id=1, replica_groups=mesh['gx'=16,'gy'=4,'tx'=4] {'gx','gy'}, use_global_device_ids=true, to_apply=%region_6.8 | all-reduce | flops 32 | bytes 256 | tf_op jit(solution)/shard_map/psum | solution.py:143
  528.9 3.3 multiply_reduce_fusion.10
  532.2 140.0 %psum.116 = f32[1,2]{1,0:T(1,128)S(1)} all-reduce(f32[1,2]{1,0:T(1,128)S(1)} %bitcast.337), channel_id=1, replica_groups=mesh['gx'=16,'gy'=4,'tx'=4] {'gx','gy'}, use_global_device_ids=true, to_apply=%region_8.10 | all-reduce | flops 2 | bytes 16 | tf_op jit(solution)/shard_map/psum | solution.py:146
  672.8 139.2 %psum.117 = f32[2]{0:T(128)S(1)} all-reduce(f32[2]{0:T(128)S(1)} %get-tuple-element.49), channel_id=1, replica_groups=mesh['gx'=16,'gy'=4,'tx'=4] {'gx','gy'}, use_global_device_ids=true, to_apply=%region_10.12 | all-reduce | flops 2 | bytes 16 | tf_op jit(solution)/shard_map/psum | solution.py:149
  814.2 8.1 collective-permute-start.5
  823.9 3.2 collective-permute-start.6
  828.5 8.8 collective-permute-done.6
  837.3 3.8 collective-permute-done.7
  841.2 2.4 select_maximum_fusion.8
  851.2 3.6 convolution_bitcast_fusion.6
  854.8 133.8 %psum.118 = f32[16,2]{0,1:T(2,128)S(1)} all-reduce(f32[16,2]{0,1:T(2,128)S(1)} %convolution_bitcast_fusion.6), channel_id=1, replica_groups=mesh['gx'=16,'gy'=4,'tx'=4] {'gx','gy'}, use_global_device_ids=true, to_apply=%region_11.13 | all-reduce | flops 32 | bytes 256 | tf_op jit(solution)/shard_map/psum | solution.py:143
  988.9 3.4 multiply_reduce_fusion.8
  992.4 140.4 %psum.119 = f32[2,2]{1,0:T(2,128)S(1)} all-reduce(f32[2,2]{1,0:T(2,128)S(1)} %pad_maximum_fusion.26), channel_id=1, replica_groups=mesh['gx'=16,'gy'=4,'tx'=4] {'gx','gy'}, use_global_device_ids=true, to_apply=%region_14.16 | all-reduce | flops 4 | bytes 32 | tf_op jit(solution)/shard_map/psum | solution.py:146
  1133.6 138.7 %psum.120 = f32[2]{0:T(128)S(1)} all-reduce(f32[2]{0:T(128)S(1)} %get-tuple-element.47), channel_id=1, replica_groups=mesh['gx'=16,'gy'=4,'tx'=4] {'gx','gy'}, use_global_device_ids=true, to_apply=%region_16.18 | all-reduce | flops 2 | bytes 16 | tf_op jit(solution)/shard_map/psum | solution.py:149
  1275.3 140.4 %psum.121 = f32[2]{0:T(128)S(1)} all-reduce(f32[2]{0:T(128)S(1)} %get-tuple-element.45), channel_id=1, replica_groups=mesh['gx'=16,'gy'=4,'tx'=4] {'gx','gy'}, use_global_device_ids=true, to_apply=%region_20.24 | all-reduce | flops 2 | bytes 16 | tf_op jit(solution)/shard_map/psum | solution.py:137
  1418.0 8.1 collective-permute-start.9
  1426.1 3.7 convolution_add_fusion
  1434.1 9.3 collective-permute-done.10
  1443.4 4.1 collective-permute-done.11
  1457.6 3.7 convolution_bitcast_fusion.5
  1461.3 132.4 %psum.122 = f32[16,2]{0,1:T(2,128)S(1)} all-reduce(f32[16,2]{0,1:T(2,128)S(1)} %convolution_bitcast_fusion.5), channel_id=1, replica_groups=mesh['gx'=16,'gy'=4,'tx'=4] {'gx','gy'}, use_global_device_ids=true, to_apply=%region_21.25 | all-reduce | flops 32 | bytes 256 | tf_op jit(solution)/shard_map/psum | solution.py:143
  1593.9 3.3 multiply_reduce_fusion.4
  1597.2 140.7 %psum.123 = f32[1,2]{1,0:T(1,128)S(1)} all-reduce(f32[1,2]{1,0:T(1,128)S(1)} %bitcast.338), channel_id=1, replica_groups=mesh['gx'=16,'gy'=4,'tx'=4] {'gx','gy'}, use_global_device_ids=true, to_apply=%region_23.27 | all-reduce | flops 2 | bytes 16 | tf_op jit(solution)/shard_map/psum | solution.py:146
  1738.6 138.5 %psum.124 = f32[2]{0:T(128)S(1)} all-reduce(f32[2]{0:T(128)S(1)} %get-tuple-element.43), channel_id=1, replica_groups=mesh['gx'=16,'gy'=4,'tx'=4] {'gx','gy'}, use_global_device_ids=true, to_apply=%region_25.29 | all-reduce | flops 2 | bytes 16 | tf_op jit(solution)/shard_map/psum | solution.py:149
  1879.2 8.1 collective-permute-start.13
  1889.0 3.9 collective-permute-start.14
  1894.3 8.8 collective-permute-done.14
  1903.1 3.8 collective-permute-done.15
  1906.9 2.4 select_maximum_fusion
  1916.9 3.7 convolution_bitcast_fusion.4
  1920.6 133.7 %psum.125 = f32[16,2]{0,1:T(2,128)S(1)} all-reduce(f32[16,2]{0,1:T(2,128)S(1)} %convolution_bitcast_fusion.4), channel_id=1, replica_groups=mesh['gx'=16,'gy'=4,'tx'=4] {'gx','gy'}, use_global_device_ids=true, to_apply=%region_26.30 | all-reduce | flops 32 | bytes 256 | tf_op jit(solution)/shard_map/psum | solution.py:143
  2054.6 3.4 multiply_reduce_fusion.2
  2058.0 140.4 %psum.126 = f32[2,2]{1,0:T(2,128)S(1)} all-reduce(f32[2,2]{1,0:T(2,128)S(1)} %pad_maximum_fusion.27), channel_id=1, replica_groups=mesh['gx'=16,'gy'=4,'tx'=4] {'gx','gy'}, use_global_device_ids=true, to_apply=%region_29.33 | all-reduce | flops 4 | bytes 32 | tf_op jit(solution)/shard_map/psum | solution.py:146
  2199.8 138.7 %psum.127 = f32[2]{0:T(128)S(1)} all-reduce(f32[2]{0:T(128)S(1)} %get-tuple-element.41), channel_id=1, replica_groups=mesh['gx'=16,'gy'=4,'tx'=4] {'gx','gy'}, use_global_device_ids=true, to_apply=%region_31.35 | all-reduce | flops 2 | bytes 16 | tf_op jit(solution)/shard_map/psum | solution.py:149
  2343.3 2.7 fusion
  (225 shorter events, 76.2 us)
Async XLA Ops:
  7.2 49.4 %all-gather.3.cloned.1.call-start = ((), (), s32[]{:S(2)}) async-start(), calls=%async_computation | async-start | bytes 1966080 | tf_op jit(solution)/shard_map/all_gather | solution.py:115
  7.9 1418.2 %all-gather.5.cloned.1.call-start = ((), (), s32[]{:S(2)}) async-start(), calls=%async_computation.1 | async-start | bytes 1966080 | tf_op jit(solution)/shard_map/all_gather | solution.py:114
  56.6 5.4 copy-start.1
  351.0 10.1 collective-permute-start
  352.9 9.0 collective-permute-start.1
  362.7 14.2 collective-permute-start.2
  366.6 14.1 collective-permute-start.3
  389.4 1.4 copy-start.2
  812.2 10.1 collective-permute-start.4
  814.2 8.9 collective-permute-start.5
  823.9 13.4 collective-permute-start.6
  827.1 14.0 collective-permute-start.7
  849.8 1.4 copy-start.3
  1416.0 13.8 collective-permute-start.8
  1418.0 11.9 collective-permute-start.9
  1430.6 12.8 collective-permute-start.10
  1432.6 15.0 collective-permute-start.11
  1456.2 1.4 copy-start.4
  1877.3 10.1 collective-permute-start.12
  1879.2 8.9 collective-permute-start.13
  1889.0 14.1 collective-permute-start.14
  1892.9 14.0 collective-permute-start.15
  1915.5 1.4 copy-start.5
  2339.3 4.0 copy-start
Sparse Core Ops, SparseCore 0:
  9.8 46.7 all-gather.2
  361.2 44.0 all-gather.4
where the time goes:
time: 2380 us; the launch traced here: 2360 us
  blocking collectives  2080 us (87%)
  waiting for transfers between devices  85.5 us (4%)
  starting transfers between devices  58.6 us (2%)
  matrix products  50.6 us (2%)
  other arithmetic  50.3 us (2%)
    psum x4, blocking collectives, on_device(): lax.psum(jnp.stack([per_source(vec, work) for vec in krylov]), ('gx', 'gy'))  562 us
    psum x4, blocking collectives, on_device(): h_next = jnp.sqrt(lax.psum(per_source(work, work), ('gx', 'gy')) + eps)  555 us
    psum x4, blocking collectives, on_device(): g_raw = lax.psum(inner_basis(all_images, work), ('gx', 'gy'))  534 us
    psum x2, blocking collectives, on_device(): lax.psum(per_source(residual, residual), ('gx', 'gy')) + eps  279 us
    psum x1, blocking collectives, on_device(): lax.psum((gram_part, inner_basis(all_images, rhs)), ('gx', 'gy'))  139 us
  transfers between devices with their start and end apart: 18, of which 12 were waited for; matrix products, arithmetic and copies ran while one was open for 2% of the time, Pallas kernels for 0%

commit v1 on v0

v1 whole, which is shorter than its diff:
```python
import functools

import jax
import jax.numpy as jnp
from jax import lax
from jax.experimental import pallas as pl
from jax.experimental.pallas import tpu as pltpu
from jax.sharding import PartitionSpec as P

EPS = 1e-06
VECS = 16
LOCAL = 4
ROWS = 48
BLOCK = 198
HALF = 99
PACKED = 13
WEIGHTS = (1.0, 0.5, 0.25)
HIGH = lax.Precision.HIGHEST
F32 = jnp.float32
BF16 = jnp.bfloat16


def iota(shape, axis):
    return lax.broadcasted_iota(jnp.int32, shape, axis)


def pick_matrix(dtype):
    col = iota((8, 128), 0)
    lane = iota((8, 128), 1)
    return jnp.where(lane == jnp.where(col < 4, col, col + 120), 1.0, 0.0).astype(dtype)


def nt_dot(left, right, precision=None):
    return lax.dot_general(
        left, right, (((1,), (1,)), ((), ())), precision=precision, preferred_element_type=F32
    )


def full_dot(left, right):
    return lax.dot_general(
        left, right, (((1,), (0,)), ((), ())), precision=HIGH, preferred_element_type=F32
    )


def pack_y_kernel(block_ref, out_ref):
    pick = pick_matrix(BF16)
    for tile in range(PACKED):
        first = tile * 16
        count = min(16, BLOCK - first)
        rows = block_ref[first : first + count].astype(F32).reshape(count * 8, 128).astype(BF16)
        picked = nt_dot(pick, rows)
        if count < 16:
            picked = jnp.concatenate([picked, jnp.zeros((8, 128 - count * 8), F32)], axis=1)
        out_ref[:, tile * 128 : (tile + 1) * 128] = picked.astype(BF16)


def pack_x_kernel(*refs):
    blocks, packed, lo_ref, hi_ref = refs[:4], refs[4:8], refs[8], refs[9]
    top = iota((1, 8, 128), 1) < 4
    for d in range(LOCAL):
        block = blocks[d]

        def body(step, carry, block=block, d=d):
            first = step * 3

            def pair(one, two, at, size):
                one = one.astype(F32)
                two = pltpu.roll(two.astype(F32), 4, 1)
                lo_ref[pl.ds(d * HALF + at, size)] = jnp.where(top, one, two).astype(BF16)
                hi_ref[pl.ds(d * HALF + at, size)] = jnp.where(top, two, one).astype(BF16)

            pair(block[pl.ds(first, 3)], block[pl.ds(first + 96, 3)], first, 3)
            return carry

        lax.fori_loop(0, 32, body, 0)
        one = block[192:195].astype(F32)
        two = pltpu.roll(block[195:198].astype(F32), 4, 1)
        lo_ref[d * HALF + 96 : d * HALF + 99] = jnp.where(top, one, two).astype(BF16)
        hi_ref[d * HALF + 96 : d * HALF + 99] = jnp.where(top, two, one).astype(BF16)
        for tile in range(PACKED):
            piece = packed[d][:, tile * 128 : (tile + 1) * 128]
            lo_ref[4 * HALF + d * PACKED + tile] = piece
            hi_ref[4 * HALF + d * PACKED + tile] = piece


def vector_row(blocks, d, kl, j):
    return blocks[d][kl * ROWS + j].astype(F32)


def inner_all(blocks, field, sums_ref):
    def body(j, accs):
        one, two = field(0, j), field(1, j)
        new = []
        for d in range(LOCAL):
            for kl in range(LOCAL):
                vec = vector_row(blocks, d, kl, j)
                at = 2 * (d * LOCAL + kl)
                new.append(accs[at] + vec * one)
                new.append(accs[at + 1] + vec * two)
        return tuple(new)

    zero = jnp.zeros((8, 128), F32)
    accs = lax.fori_loop(0, ROWS, body, (zero,) * (2 * VECS))
    for k in range(VECS):
        for s in range(2):
            sums_ref[s * VECS + k : s * VECS + k + 1] = jnp.sum(
                accs[2 * k + s], axis=0, keepdims=True
            )


def inner_pairs(pairs, sums_ref, first):
    count = len(pairs)
    for s in range(2):

        def body(j, accs, s=s):
            return tuple(
                acc + one(s, j) * two(s, j) for acc, (one, two) in zip(accs, pairs)
            )

        zero = jnp.zeros((8, 128), F32)
        accs = lax.fori_loop(0, ROWS, body, (zero,) * count)
        for i in range(count):
            at = first + s * count + i
            sums_ref[at : at + 1] = jnp.sum(accs[i], axis=0, keepdims=True)


def row_of_sums(sums_ref):
    return nt_dot(jnp.ones((8, 128), F32), sums_ref[...], HIGH)[0:1]


def entry(row, lane):
    return row[:, lane : lane + 1]


def column_of(row, first):
    part = row[:, first : first + VECS]
    eye = iota((VECS, VECS), 0) == iota((VECS, VECS), 1)
    return jnp.sum(jnp.where(eye, part, 0.0), axis=1, keepdims=True)


def solve(inverse, row, first):
    return jnp.sum(inverse[:, :VECS] * row[:, first : first + VECS], axis=1, keepdims=True)


def spread(value):
    return jnp.broadcast_to(value, (8, 128))


def grid_mask(size_x, size_y):
    row, lane = iota((16, 256), 0), iota((16, 256), 1)
    x_pos = lax.axis_index("gx") * 8 + jnp.where(row < 12, row, row - 16)
    y_pos = lax.axis_index("gy") * 128 + jnp.where(lane < 132, lane, lane - 256)
    inside = (x_pos >= 0) & (x_pos < size_x) & (y_pos >= 0) & (y_pos < size_y)
    inside = inside & ((lane < 132) | (lane >= 252))
    return x_pos, y_pos, inside


def primary_field(cell, z, x_pos, y_pos, size_x, size_y):
    plane = size_x * size_y
    src_z = cell // plane
    rest = cell % plane
    d_z = (z - src_z).astype(F32)
    d_x = (x_pos - rest // size_y).astype(F32)
    d_y = (y_pos - rest % size_y).astype(F32)
    dist = jnp.sqrt(d_z * d_z + d_x * d_x + d_y * d_y)
    return jnp.exp(-dist / ((size_x + size_y) / 8.0))


def combine_ext(coeffs, blocks, packed, ln_ref, hp_ref, interior, halo_x, unpacked_ref):
    top = iota((8, 128), 0) < 4

    def body(j, carry):
        inner = [jnp.zeros((8, 128), F32)] * 2
        straight = [jnp.zeros((8, 128), F32)] * 2
        rolled = [jnp.zeros((8, 128), F32)] * 2
        for d in range(LOCAL):
            for kl in range(LOCAL):
                k = d * LOCAL + kl
                vec = vector_row(blocks, d, kl, j)
                at = d * HALF + (kl % 2) * ROWS + j
                after, before = ln_ref[at].astype(F32), hp_ref[at].astype(F32)
                outer = straight if kl < 2 else rolled
                edge = jnp.where(top, after, before) if kl < 2 else jnp.where(top, before, after)
                for s in range(2):
                    inner[s] = inner[s] + coeffs[s][k] * vec
                    outer[s] = outer[s] + coeffs[s][k] * edge
        for s in range(2):
            interior(s, j, inner[s])
            halo_x(s, j, straight[s] + pltpu.roll(rolled[s], 4, 0))
        return carry

    lax.fori_loop(0, ROWS, body, 0)
    pick = pick_matrix(F32)
    from_next = iota((8, 128), 1) % 8 < 4
    for s in range(2):
        for tile in range(3):
            near = jnp.zeros((8, 128), F32)
            far = jnp.zeros((8, 128), F32)
            for d in range(LOCAL):
                for kl in range(LOCAL):
                    k = d * LOCAL + kl
                    t = kl * 3 + tile
                    at = 4 * HALF + d * PACKED + t
                    near = near + coeffs[s][k] * packed[d][:, t * 128 : (t + 1) * 128].astype(F32)
                    edge = jnp.where(from_next, ln_ref[at].astype(F32), hp_ref[at].astype(F32))
                    far = far + coeffs[s][k] * edge
            place = s * ROWS + tile * 16
            near = full_dot(jnp.transpose(near), pick).reshape(16, 8, 128)
            far = full_dot(jnp.transpose(far), pick).reshape(16, 8, 128)
            unpacked_ref[place : place + 16, 0:8] = near
            unpacked_ref[place : place + 16, 8:16] = far


def apply_operator(e_ref, m_ref, out_ref, mask):
    def ahead(f, axis):
        return pltpu.roll(f, f.shape[axis] - 1, axis)

    def behind(f, axis):
        return pltpu.roll(f, 1, axis)

    def body(index, carry):
        base = index * 24
        other = jnp.where(index % 2 == 0, base + 24, base - 24)
        sign = jnp.where(index % 2 == 0, -1.0, 1.0).astype(F32)
        zero = jnp.zeros((16, 256), F32)
        b_x_old = -e_ref[base + 8]
        b_y_old = e_ref[base]
        for z in range(8):
            e_x, e_y, e_z = e_ref[base + z], e_ref[base + 8 + z], e_ref[base + 16 + z]
            up_x = e_ref[base + z + 1] if z < 7 else zero
            up_y = e_ref[base + 8 + z + 1] if z < 7 else zero
            b_x = (ahead(e_z, 1) - e_z) - (up_y - e_y)
            b_y = (up_x - e_x) - (ahead(e_z, 0) - e_z)
            b_z = (ahead(e_y, 0) - e_y) - (ahead(e_x, 1) - e_x)
            c_x = (b_z - behind(b_z, 1)) - (b_y - b_y_old)
            c_y = (b_x - b_x_old) - (b_z - behind(b_z, 0))
            c_z = (b_y - behind(b_y, 0)) - (b_x - behind(b_x, 1))
            for c, value in enumerate((c_x, c_y, c_z)):
                at = c * 8 + z
                value = value + sign * (m_ref[at] * e_ref[other + at])
                out_ref[base + at] = jnp.where(mask, value, 0.0)
            b_x_old, b_y_old = b_x, b_y
        return carry

    lax.fori_loop(0, 4, body, 0)


def brick(ref):
    return lambda s, j: ref[s * ROWS + j, 0:8, 0:128]


def pick_layer(values, z):
    want = lax.rem(lax.axis_index("tx") - z // 2 + LOCAL, LOCAL)
    result = values[0]
    for d in range(1, LOCAL):
        result = jnp.where(want == d, values[d], result)
    return result


def gram_kernel(size_x, size_y, src_ref, *refs):
    blocks, out_ref, field_ref, sums_ref = refs[:4], refs[4], refs[5], refs[6]
    x_pos = lax.axis_index("gx") * 8 + iota((8, 128), 0)
    y_pos = lax.axis_index("gy") * 128 + iota((8, 128), 1)
    for z in range(8):
        prim = [
            primary_field(src_ref[s], z, x_pos, y_pos, size_x, size_y) for s in range(2)
        ]
        for c in range(3):
            m = pick_layer([b[192 + 2 * c + z % 2].astype(F32) for b in blocks], z)
            for s in range(2):
                real = (m - 1.0) * WEIGHTS[c] * prim[s]
                field_ref[s * ROWS + c * 8 + z] = real
                field_ref[s * ROWS + 24 + c * 8 + z] = 0.5 * real
    sums_ref[...] = jnp.zeros_like(sums_ref)
    inner_all(blocks, lambda s, j: field_ref[s * ROWS + j], sums_ref)

    def body(j, acc):
        rows = jnp.concatenate(
            [vector_row(blocks, d, kl, j) for d in range(LOCAL) for kl in range(LOCAL)], axis=0
        ).astype(BF16)
        return acc + nt_dot(rows, rows)

    gram = lax.fori_loop(0, ROWS, body, jnp.zeros((128, 128), F32))
    row, lane = iota((128, 128), 0), iota((128, 128), 1)
    gram = jnp.where(row % 8 == lane % 8, gram, 0.0).reshape(VECS, 8, 128)
    gram = jnp.sum(gram, axis=1)
    gram = full_dot(gram, jnp.where(row // 8 == lane % 16, 1.0, 0.0).astype(F32))
    gram = jnp.where(iota((VECS, 128), 1) // 16 == iota((VECS, 128), 0) % 8, gram, 0.0)
    gram = jnp.sum(gram.reshape(2, 8, 128), axis=1)
    rows = jnp.concatenate([gram, row_of_sums(sums_ref), jnp.zeros((1, 128), F32)], axis=0)
    out_ref[...] = jnp.broadcast_to(rows[None], out_ref.shape)


def invert(rows):
    lane, row = iota((VECS, 128), 1), iota((VECS, 128), 0)
    wide = jnp.where(row < 8, rows[0:1], rows[1:2])
    wide = jnp.where(lane // 16 == row % 8, wide, 0.0)
    fold = jnp.where(iota((128, 128), 0) % 16 == iota((128, 128), 1), 1.0, 0.0).astype(F32)
    work = full_dot(wide, fold) + jnp.where(lane == row + VECS, 1.0, 0.0)
    for j in range(VECS):
        pivot = work[j : j + 1] / work[j : j + 1, j : j + 1]
        work = jnp.where(row == j, pivot, work - work[:, j : j + 1] * pivot)
    return pltpu.roll(work, 128 - VECS, 1)


def begin_kernel(size_x, size_y, src_ref, got_ref, *refs):
    blocks, packed, ln_ref, hp_ref = refs[:4], refs[4:8], refs[8], refs[9]
    r_ref, q_ref, m_ref, inv_ref, state_ref, out_ref, side_ref, sums_ref = refs[10:]
    total = jnp.sum(got_ref[...], axis=0)
    inverse = invert(total[0:2])
    inv_ref[...] = inverse
    inner = total[2:3]
    x_pos, y_pos, mask = grid_mask(size_x, size_y)
    start = [solve(inverse, inner, s * VECS) for s in range(2)]
    lane = iota((VECS, 128), 1)
    state_ref[...] = jnp.where(lane == 2, start[0], jnp.where(lane == 3, start[1], 0.0))
    coeffs = [[spread(-start[s][k : k + 1]) for k in range(VECS)] for s in range(2)]

    def put(rows, columns):
        def store(s, j, value):
            r_ref[s * ROWS + j, rows, columns] = value

        return store

    combine_ext(
        coeffs, blocks, packed, ln_ref, hp_ref,
        put(slice(0, 8), slice(0, 128)), put(slice(8, 16), slice(0, 128)), side_ref,
    )
    top = iota((8, 128), 0) < 4
    from_next = iota((8, 128), 1) % 8 < 4
    pick = pick_matrix(F32)
    sides = []
    for d in range(LOCAL):
        at = 4 * HALF + d * PACKED + 12
        near = packed[d][:, 12 * 128 : 13 * 128].astype(F32)
        far = jnp.where(from_next, ln_ref[at].astype(F32), hp_ref[at].astype(F32))
        near = full_dot(jnp.transpose(near), pick)[:48].reshape(6, 8, 128)
        far = full_dot(jnp.transpose(far), pick)[:48].reshape(6, 8, 128)
        sides.append((near, far))
    for c in range(3):
        for z in range(8):
            at = 2 * c + z % 2
            quarters = []
            for d in range(LOCAL):
                inner_m = blocks[d][192 + at].astype(F32)
                row = d * HALF + 96 + at % 3
                after, before = ln_ref[row].astype(F32), hp_ref[row].astype(F32)
                if at < 3:
                    edge = jnp.where(top, after, before)
                else:
                    edge = pltpu.roll(jnp.where(top, before, after), 4, 0)
                left = jnp.concatenate([inner_m, edge], axis=0)
                right = jnp.concatenate([sides[d][0][at], sides[d][1][at]], axis=0)
                quarters.append(jnp.concatenate([left, right], axis=1))
            m_ref[c * 8 + z] = pick_layer(quarters, z)

    for s in range(2):

        def body(z, carry, s=s):
            prim = primary_field(src_ref[s], z, x_pos, y_pos, size_x, size_y)
            for c in range(3):
                at = c * 8 + z
                real = jnp.where(mask, (m_ref[at] - 1.0) * WEIGHTS[c] * prim, 0.0)
                for p in range(2):
                    place = s * ROWS + p * 24 + at
                    value = real if p == 0 else 0.5 * real
                    r_ref[place, :, 0:128] = r_ref[place, :, 0:128] + value[:, 0:128]
                    r_ref[place, :, 128:256] = side_ref[place] + value[:, 128:256]
            return carry

        lax.fori_loop(0, 8, body, 0)
    apply_operator(r_ref, m_ref, q_ref, mask)
    finish_first(blocks, r_ref, q_ref, sums_ref, out_ref)


def finish_first(blocks, r_ref, q_ref, sums_ref, out_ref):
    sums_ref[...] = jnp.zeros_like(sums_ref)
    r, q = brick(r_ref), brick(q_ref)
    inner_all(blocks, q, sums_ref)
    inner_pairs([(r, r), (r, q)], sums_ref, 32)
    out_ref[...] = jnp.broadcast_to(row_of_sums(sums_ref), out_ref.shape)


def first_kernel(size_x, size_y, got_ref, *refs):
    blocks, packed, ln_ref, hp_ref = refs[:4], refs[4:8], refs[8], refs[9]
    r_ref, q_ref, m_ref, inv_ref, old_ref = refs[10:15]
    u_ref, a_ref, state_ref, out_ref, side_ref, sums_ref = refs[15:]
    row = jnp.sum(got_ref[...], axis=0, keepdims=True)
    _, _, mask = grid_mask(size_x, size_y)
    lane = iota((VECS, 128), 1)
    state = old_ref[...]
    coeffs, q_scale, r_scale = [], [], []
    for s in range(2):
        rr, rq = entry(row, 32 + 2 * s), entry(row, 33 + 2 * s)
        beta = jnp.sqrt(rr + EPS)
        g_zero = solve(inv_ref[...], row, s * VECS) / beta
        h_00 = rq / (beta * beta)
        coeffs.append([spread(-g_zero[k : k + 1]) for k in range(VECS)])
        q_scale.append(spread(1.0 / beta))
        r_scale.append(spread(-h_00 / beta))
        state = jnp.where(lane == s, g_zero, state)
        state = jnp.where(lane == 8 + s, beta, state)
        state = jnp.where(lane == 10 + s, h_00, state)
        state = jnp.where(lane == 12 + s, rr, state)
    state_ref[...] = state

    def put(rows, columns):
        def store(s, j, value):
            at = s * ROWS + j
            value = value + q_scale[s] * q_ref[at, rows, columns]
            u_ref[at, rows, columns] = value + r_scale[s] * r_ref[at, rows, columns]

        return store

    combine_ext(
        coeffs, blocks, packed, ln_ref, hp_ref,
        put(slice(0, 8), slice(0, 128)), put(slice(8, 16), slice(0, 128)), side_ref,
    )
    for s in range(2):

        def body(j, carry, s=s):
            at = s * ROWS + j
            value = side_ref[at]
            for half in range(2):
                rows = slice(half * 8, half * 8 + 8)
                new = value[rows] + q_scale[s] * q_ref[at, rows, 128:256]
                u_ref[at, rows, 128:256] = new + r_scale[s] * r_ref[at, rows, 128:256]
            return carry

        lax.fori_loop(0, ROWS, body, 0)
    apply_operator(u_ref, m_ref, a_ref, mask)
    sums_ref[...] = jnp.zeros_like(sums_ref)
    r, u, a = brick(r_ref), brick(u_ref), brick(a_ref)
    inner_all(blocks, a, sums_ref)
    inner_pairs([(u, u), (r, u), (r, a), (u, a), (a, a)], sums_ref, 32)
    out_ref[...] = jnp.broadcast_to(row_of_sums(sums_ref), out_ref.shape)


def close_cycle(row, inverse, state, s):
    uu, ru, ra, ua, aa = [entry(row, 32 + 5 * s + i) for i in range(5)]
    g_zero = state[:, s : s + 1]
    beta, h_00, rr = [state[0:1, first + s : first + s + 1] for first in (8, 10, 12)]
    h_10 = jnp.sqrt(uu + EPS)
    inner = column_of(row, s * VECS) / h_10
    g_one = solve(inverse, row, s * VECS) / h_10
    h_01 = ra / (beta * h_10)
    h_11 = ua / (h_10 * h_10)
    left = aa / (h_10 * h_10) - jnp.sum(g_one * inner, axis=0, keepdims=True)
    left = left - 2.0 * (h_01 * h_01 + h_11 * h_11)
    left = left + h_01 * h_01 * (rr / (beta * beta)) + h_11 * h_11 * (uu / (h_10 * h_10))
    left = left + 2.0 * h_01 * h_11 * (ru / (beta * h_10))
    h_21_square = jnp.maximum(left, 0.0) + EPS
    n_00 = h_00 * h_00 + h_10 * h_10
    n_01 = h_00 * h_01 + h_10 * h_11
    n_11 = h_01 * h_01 + h_11 * h_11 + h_21_square
    l_00 = jnp.sqrt(n_00)
    l_10 = n_01 / l_00
    l_11 = jnp.sqrt(n_11 - l_10 * l_10)
    z_0 = beta * h_00 / l_00
    z_1 = (beta * h_01 - l_10 * z_0) / l_11
    y_1 = z_1 / l_11
    y_0 = (z_0 - l_10 * y_1) / l_00
    t_0 = beta - h_00 * y_0 - h_01 * y_1
    t_1 = -h_10 * y_0 - h_11 * y_1
    return {
        "r": (t_0 + y_1 * h_01) / beta,
        "u": (t_1 + y_1 * h_11) / h_10,
        "a": -y_1 / h_10,
        "c": y_1 * g_one,
        "sol_r": y_0 / beta,
        "sol_u": y_1 / h_10,
        "basis": state[:, 2 + s : 3 + s] - g_zero * y_0 - g_one * y_1,
    }


def next_kernel(size_x, size_y, got_ref, *refs):
    blocks, packed, ln_ref, hp_ref = refs[:4], refs[4:8], refs[8], refs[9]
    r_ref, u_ref, a_ref, m_ref, inv_ref, old_ref = refs[10:16]
    new_ref, q_ref, sol_ref, state_ref, out_ref, side_ref, sums_ref = refs[16:]
    row = jnp.sum(got_ref[...], axis=0, keepdims=True)
    _, _, mask = grid_mask(size_x, size_y)
    state = old_ref[...]
    small = [close_cycle(row, inv_ref[...], state, s) for s in range(2)]
    lane = iota((VECS, 128), 1)
    state_ref[...] = jnp.where(
        lane == 2, small[0]["basis"], jnp.where(lane == 3, small[1]["basis"], 0.0)
    )
    coeffs = [[spread(small[s]["c"][k : k + 1]) for k in range(VECS)] for s in range(2)]
    scale = [{name: spread(small[s][name]) for name in ("r", "u", "a", "sol_r", "sol_u")} for s in range(2)]

    def total(s, at, rows, columns, value):
        value = value + scale[s]["r"] * r_ref[at, rows, columns]
        value = value + scale[s]["u"] * u_ref[at, rows, columns]
        return value + scale[s]["a"] * a_ref[at, rows, columns]

    def put(rows, columns):
        def store(s, j, value):
            at = s * ROWS + j
            new_ref[at, rows, columns] = total(s, at, rows, columns, value)

        return store

    combine_ext(
        coeffs, blocks, packed, ln_ref, hp_ref,
        put(slice(0, 8), slice(0, 128)), put(slice(8, 16), slice(0, 128)), side_ref,
    )
    for s in range(2):

        def body(j, carry, s=s):
            at = s * ROWS + j
            value = side_ref[at]
            for half in range(2):
                rows = slice(half * 8, half * 8 + 8)
                new_ref[at, rows, 128:256] = total(s, at, rows, slice(128, 256), value[rows])
            sol_ref[at] = (
                scale[s]["sol_r"] * r_ref[at, 0:8, 0:128]
                + scale[s]["sol_u"] * u_ref[at, 0:8, 0:128]
            )
            return carry

        lax.fori_loop(0, ROWS, body, 0)
    apply_operator(new_ref, m_ref, q_ref, mask)
    finish_first(blocks, new_ref, q_ref, sums_ref, out_ref)


def last_kernel(got_ref, *refs):
    blocks, basis = refs[:4], refs[4:8]
    r_ref, u_ref, a_ref, inv_ref, old_ref, sol_ref = refs[8:14]
    solution_ref, residual_ref = refs[14:]
    row = jnp.sum(got_ref[...], axis=0, keepdims=True)
    state = old_ref[...]
    for s in range(2):
        small = close_cycle(row, inv_ref[...], state, s)
        coeffs = [spread(small["c"][k : k + 1]) for k in range(VECS)]
        base_coeffs = [spread(small["basis"][k : k + 1]) for k in range(VECS)]
        scale = {name: spread(small[name]) for name in ("r", "u", "a", "sol_r", "sol_u")}

        def body(j, carry, s=s, coeffs=coeffs, base_coeffs=base_coeffs, scale=scale):
            at = s * ROWS + j
            r, u, a = brick(r_ref)(s, j), brick(u_ref)(s, j), brick(a_ref)(s, j)
            value = scale["r"] * r + scale["u"] * u + scale["a"] * a
            field = sol_ref[at] + scale["sol_r"] * r + scale["sol_u"] * u
            for d in range(LOCAL):
                for kl in range(LOCAL):
                    k = d * LOCAL + kl
                    value = value + coeffs[k] * vector_row(blocks, d, kl, j)
                    field = field + base_coeffs[k] * vector_row(basis, d, kl, j)
            residual_ref[at] = value
            solution_ref[at] = field
            return carry

        lax.fori_loop(0, ROWS, body, 0)


def call(kernel, outs, args, scratch=(), smem=0):
    vmem = pl.BlockSpec(memory_space=pltpu.VMEM)
    return pl.pallas_call(
        kernel,
        out_shape=outs,
        in_specs=[pl.BlockSpec(memory_space=pltpu.SMEM)] * smem + [vmem] * (len(args) - smem),
        out_specs=jax.tree.map(lambda _: vmem, outs),
        scratch_shapes=list(scratch),
        compiler_params=pltpu.CompilerParams(vmem_limit_bytes=48 * 1024 * 1024),
    )(*args)


def shape(*dims, dtype=F32):
    return jax.ShapeDtypeStruct(dims, dtype)


def exchange(value):
    return lax.all_to_all(value, ("gx", "gy"), 0, 0)


def around(value, axis):
    up = [(i, i + 1) for i in range(lax.axis_size(axis) - 1)]
    return value, up, [(j, i) for i, j in up]


def gather(value):
    return [value] + [
        lax.ppermute(value, "tx", [(i, (i + d) % LOCAL) for i in range(LOCAL)])
        for d in range(1, LOCAL)
    ]


def on_device(src_cell, basis, images, induction):
    size_x, size_y = 8 * lax.axis_size("gx"), 128 * lax.axis_size("gy")
    peers = lax.axis_size("gx") * lax.axis_size("gy")
    block = jnp.concatenate(
        [images.reshape(LOCAL * ROWS, 8, 128), induction.reshape(6, 8, 128)], axis=0
    )
    blocks = gather(block)
    own = call(pack_y_kernel, shape(8, PACKED * 128, dtype=BF16), (block,))
    _, up, down = around(own, "gy")
    after, before = lax.ppermute(own, "gy", down), lax.ppermute(own, "gy", up)
    side = jnp.where(lax.broadcasted_iota(jnp.int32, own.shape, 0) < 4, after, before)
    packed = gather(side)

    half = shape(LOCAL * (HALF + PACKED), 8, 128, dtype=BF16)
    low, high = call(pack_x_kernel, (half, half), (*blocks, *packed))
    _, up, down = around(low, "gx")
    ln, hp = lax.ppermute(low, "gx", down), lax.ppermute(high, "gx", up)

    sums = pltpu.VMEM((128, 128), F32)
    side_scratch = pltpu.VMEM((2 * ROWS, 16, 128), F32)
    sent = call(
        functools.partial(gram_kernel, size_x, size_y),
        shape(peers, 4, 128),
        (src_cell, *blocks),
        (pltpu.VMEM((2 * ROWS, 8, 128), F32), sums),
        smem=1,
    )
    got = exchange(sent)
    wide = shape(2 * ROWS, 16, 256)
    line = shape(peers, 128)
    small = shape(VECS, 128)
    static = (*blocks, *packed, ln, hp)
    r, q, m, inverse, state, sent = call(
        functools.partial(begin_kernel, size_x, size_y),
        (wide, wide, shape(24, 16, 256), small, small, line),
        (src_cell, got, *static),
        (side_scratch, sums),
        smem=1,
    )
    bases = gather(basis.reshape(LOCAL * ROWS, 8, 128))

    def total(value):
        return exchange(value.reshape(peers, 1, 128)).reshape(peers, 128)

    def first(r, q, state, sent):
        return call(
            functools.partial(first_kernel, size_x, size_y),
            (wide, wide, small, line),
            (total(sent), *static, r, q, m, inverse, state),
            (side_scratch, sums),
        )

    u, a, state, sent = first(r, q, state, sent)
    r, q, field, state, sent = call(
        functools.partial(next_kernel, size_x, size_y),
        (wide, wide, shape(2 * ROWS, 8, 128), small, line),
        (total(sent), *static, r, u, a, m, inverse, state),
        (side_scratch, sums),
    )
    u, a, state, sent = first(r, q, state, sent)
    narrow = shape(2 * ROWS, 8, 128)
    field, residual = call(
        last_kernel,
        (narrow, narrow),
        (total(sent), *blocks, *bases, r, u, a, inverse, state, field),
    )
    full = (2, 2, 3, 8, 8, 128)
    return field.reshape(full), residual.reshape(full)


def solution(mesh):
    in_specs = (
        P("tx"),
        P("tx", None, None, None, "gx", "gy"),
        P("tx", None, None, None, "gx", "gy"),
        P(None, "tx", "gx", "gy"),
    )
    out_specs = (P("tx", None, None, None, "gx", "gy"), P("tx", None, None, None, "gx", "gy"))
    return jax.shard_map(
        on_device, mesh=mesh, in_specs=in_specs, out_specs=out_specs, check_vma=False
    )
```

time: 2380 us -> 213 us (0.09)
  blocking collectives: 2080 us -> 48.4 us
  Pallas kernels: 0 us -> 60.6 us
  matrix products: 50.6 us -> 0 us
  other arithmetic: 50.3 us -> 1.14 us
  waiting for transfers between devices: 85.5 us -> 42.9 us
    psum x15 -> x0, blocking collectives: 2070 us -> none  [the longest x4 562 us: on_device(): lax.psum(jnp.stack([per_source(vec, work) for vec in krylov]), ('gx', 'gy'))]
    pallas_call x0 -> x8, Pallas kernels: none -> 60.6 us  [call(): pl.pallas_call(kernel, out_shape=outs, in_specs=[pl.BlockSpec(memory_spac...]
    dot_general x18 -> x0, matrix products: 48.7 us -> none  [the longest x8 24.5 us: combine(): jnp.einsum('ks,kpczxy->spczxy', coeffs, vectors, precision=lax.Precision....]
    all_to_all x0 -> x3, blocking collectives: none -> 48.4 us  [exchange(): return lax.all_to_all(value, ('gx', 'gy'), 0, 0)]
    all_gather x2 -> x0, waiting for transfers between devices: 31.1 us -> none  [the longest x1 31.1 us: on_device(): lax.all_gather(images, 'tx', axis=0, tiled=True)]
    ppermute x16 -> x13, starting transfers between devices: 58.5 us -> 33.8 us  [the longest x9 20.5 us: gather(): lax.ppermute(value, 'tx', [(i, (i + d) % LOCAL) for i in range(LOCAL)])]
    ppermute x16 -> x13, waiting for transfers between devices: 53.7 us -> 34.1 us  [the longest x9 34.1 us: gather(): lax.ppermute(value, 'tx', [(i, (i + d) % LOCAL) for i in range(LOCAL)])]
  transfers between devices with their start and end apart: 18 -> 15, of which waited for: 12 -> 4; matrix products, arithmetic and copies ran while one was open for 2% -> 0% of each run, Pallas kernels for 0% -> 24%
where the time goes in v1:
time: 213 us; the launch traced here: 212 us
  Pallas kernels  60.6 us (28%)
  blocking collectives  48.4 us (23%)
  starting transfers between devices  46.2 us (22%)
  waiting for transfers between devices  42.9 us (20%)
  local copies, waits for them, and re-layouts  12.1 us (6%)
    pallas_call x8, Pallas kernels, call(): pl.pallas_call(kernel, out_shape=outs, in_specs=[pl.BlockSpec(memory_spac...  60.6 us
    all_to_all x3, blocking collectives, exchange(): return lax.all_to_all(value, ('gx', 'gy'), 0, 0)  48.4 us
    ppermute x9, waiting for transfers between devices, gather(): lax.ppermute(value, 'tx', [(i, (i + d) % LOCAL) for i in range(LOCAL)])  34.1 us
    ppermute x9, starting transfers between devices, gather(): lax.ppermute(value, 'tx', [(i, (i + d) % LOCAL) for i in range(LOCAL)])  20.5 us
    all_to_all x2, starting transfers between devices, exchange(): return lax.all_to_all(value, ('gx', 'gy'), 0, 0)  12.4 us
    unnamed x30, local copies, waits for them, and re-layouts  12.1 us
    all_to_all x2, waiting for transfers between devices, exchange(): return lax.all_to_all(value, ('gx', 'gy'), 0, 0)  8.82 us
    ppermute x2, starting transfers between devices, on_device(): ln, hp = (lax.ppermute(low, 'gx', down), lax.ppermute(high, 'gx', up))  7.38 us
  transfers between devices with their start and end apart: 15, of which 4 were waited for; matrix products, arithmetic and copies ran while one was open for 0% of the time, Pallas kernels for 24%

profile of v1, /device:TPU:1, one launch (start us, length us, event | category | flops | bytes accessed | tf_op | source)
XLA Modules:
  0.0 212.2 jit_solution(11184203130190176024)
XLA Ops:
  0.6 1.1 pad_maximum_fusion.refs_0_.block_ref
  1.7 0.3 shard_map.60
  2.0 1.3 collective-permute-start.3
  3.3 4.7 %collective-permute-start.4 = (bf16[8,1664]{1,0:T(8,128)(2,1)S(1)}, bf16[8,1664]{1,0:T(8,128)(2,1)S(1)}, u32[]{:S(2)}, u32[]{:S(2)}) collective-permute-start(bf16[8,1664]{1,0:T(8,128)(2,1)S(1)} %shard_map.60), channel_id=1, source_target_pairs={{0,4},{4,8},{8,12},{1,5},{5,9},{9,13},{2,6},{6,10},{10,14},{3,7},{... | collective-permute-start | bytes 79880 | tf_op jit(solution)/shard_map/ppermute | solution.py:596
  8.0 3.2 %collective-permute-start = (bf16[198,8,128]{2,1,0:T(8,128)(2,1)S(1)}, bf16[198,8,128]{2,1,0:T(8,128)(2,1)S(1)}, u32[]{:S(2)}, u32[]{:S(2)}) collective-permute-start(bf16[198,8,128]{2,1,0:T(8,128)(2,1)S(1)} %pad_maximum_fusion.refs_0_.block_ref), channel_id=1, source_target_pairs={{0,1},{1,2},{2,3},{3,0},{4,5},{5,6},{6,7},{7,4},{8,9},{9,10},{10,1... | collective-permute-start | bytes 1216520 | tf_op jit(solution)/shard_map/ppermute | solution.py:582
  11.2 5.1 %collective-permute-start.1 = (bf16[198,8,128]{2,1,0:T(8,128)(2,1)S(1)}, bf16[198,8,128]{2,1,0:T(8,128)(2,1)S(1)}, u32[]{:S(2)}, u32[]{:S(2)}) collective-permute-start(bf16[198,8,128]{2,1,0:T(8,128)(2,1)S(1)} %pad_maximum_fusion.refs_0_.block_ref), channel_id=1, source_target_pairs={{0,2},{1,3},{2,0},{3,1},{4,6},{5,7},{6,4},{7,5},{8,10},{9,11},{10,... | collective-permute-start | bytes 1216520 | tf_op jit(solution)/shard_map/ppermute | solution.py:582
  16.3 2.4 %collective-permute-start.2 = (bf16[198,8,128]{2,1,0:T(8,128)(2,1)S(1)}, bf16[198,8,128]{2,1,0:T(8,128)(2,1)S(1)}, u32[]{:S(2)}, u32[]{:S(2)}) collective-permute-start(bf16[198,8,128]{2,1,0:T(8,128)(2,1)S(1)} %pad_maximum_fusion.refs_0_.block_ref), channel_id=1, source_target_pairs={{0,3},{1,0},{2,1},{3,2},{4,7},{5,4},{6,5},{7,6},{8,11},{9,8},{10,9... | collective-permute-start | bytes 1216520 | tf_op jit(solution)/shard_map/ppermute | solution.py:582
  18.7 0.1 broadcast_select_fusion.refs_4_
  18.8 0.0 collective-permute-start.5
  18.8 2.1 collective-permute-start.6
  20.9 29.4 %collective-permute-done.5.refs_5_ = bf16[8,1664]{1,0:T(8,128)(2,1)S(1)} collective-permute-done((bf16[8,1664]{1,0:T(8,128)(2,1)S(1)}, bf16[8,1664]{1,0:T(8,128)(2,1)S(1)}, u32[]{:S(2)}, u32[]{:S(2)}) %collective-permute-start.5) | collective-permute-done | bytes 26656 | tf_op jit(solution)/shard_map/ppermute | solution.py:582
  50.3 4.7 %collective-permute-done.7.refs_7_ = bf16[8,1664]{1,0:T(8,128)(2,1)S(1)} collective-permute-done((bf16[8,1664]{1,0:T(8,128)(2,1)S(1)}, bf16[8,1664]{1,0:T(8,128)(2,1)S(1)}, u32[]{:S(2)}, u32[]{:S(2)}) %collective-permute-start.7) | collective-permute-done | bytes 26656 | tf_op jit(solution)/shard_map/ppermute | solution.py:582
  55.0 0.0 collective-permute-done.1.refs_2_
  55.0 2.2 %shard_map.61 = (bf16[448,8,128]{2,1,0:T(8,128)(2,1)}, bf16[448,8,128]{2,1,0:T(8,128)(2,1)}) custom-call(bf16[198,8,128]{2,1,0:T(8,128)(2,1)S(1)} %pad_maximum_fusion.refs_0_.block_ref, bf16[198,8,128]{2,1,0:T(8,128)(2,1)S(1)} %collective-permute-done.refs_1_, bf16[198,8,128]{2,1,0:T(8,128)(2,1)S(1)} %collective-permute-done.1.refs_2_, ...), custom_call_target="tpu_custom_call" | custom-call | tf_op jit(solution)/shard_map/pallas_call | solution.py:557
  57.2 4.4 %collective-permute-start.8 = (bf16[448,8,128]{2,1,0:T(8,128)(2,1)}, bf16[448,8,128]{2,1,0:T(8,128)(2,1)S(1)}, u32[]{:S(2)}, u32[]{:S(2)}) collective-permute-start(bf16[448,8,128]{2,1,0:T(8,128)(2,1)} %get-tuple-element.25), channel_id=1, source_target_pairs={{16,0},{32,16},{48,32},{64,48},{80,64},{96,80},{112,96},{128,112},... | collective-permute-start | bytes 2752520 | tf_op jit(solution)/shard_map/ppermute | solution.py:603
  61.6 3.0 %collective-permute-start.9 = (bf16[448,8,128]{2,1,0:T(8,128)(2,1)}, bf16[448,8,128]{2,1,0:T(8,128)(2,1)S(1)}, u32[]{:S(2)}, u32[]{:S(2)}) collective-permute-start(bf16[448,8,128]{2,1,0:T(8,128)(2,1)} %get-tuple-element.26), channel_id=1, source_target_pairs={{0,16},{16,32},{32,48},{48,64},{64,80},{80,96},{96,112},{112,128},... | collective-permute-start | bytes 2752520 | tf_op jit(solution)/shard_map/ppermute | solution.py:603
  64.6 9.7 %shard_map.59 = f32[64,4,128]{2,1,0:T(4,128)S(1)} custom-call(s32[2]{0:T(128)S(1)} %copy-done.14, bf16[198,8,128]{2,1,0:T(8,128)(2,1)S(1)} %pad_maximum_fusion.refs_0_.block_ref, bf16[198,8,128]{2,1,0:T(8,128)(2,1)S(1)} %collective-permute-done.refs_1_, bf16[198,8,128]{2,1,0:T(8,128)(2,1)S(1)} %collective-permute-done.1.refs_2_, ...), custom_call_target="tpu_custom_call" | custom-call | tf_op jit(solution)/shard_map/pallas_call | solution.py:557
  74.4 0.0 copy-start.7
  74.4 0.6 copy-done.7
  75.0 7.8 %all-to-all-start = ((f32[64,4,128]{2,1,0:T(4,128)}), f32[64,4,128]{2,1,0:T(4,128)}, u32[]{:S(2)}, u32[]{:S(2)}) async-start(f32[64,4,128]{2,1,0:T(4,128)} %copy-done.7), calls=%async_computation | async-start | bytes 262144 | tf_op jit(solution)/shard_map/all_to_all | solution.py:572
  82.8 1.7 collective-permute-start.10
  84.6 3.5 %collective-permute-start.11 = (bf16[192,8,128]{2,1,0:T(8,128)(2,1)}, bf16[192,8,128]{2,1,0:T(8,128)(2,1)}, u32[]{:S(2)}, u32[]{:S(2)}) collective-permute-start(bf16[192,8,128]{2,1,0:T(8,128)(2,1)} %bitcast.22), channel_id=1, source_target_pairs={{0,2},{1,3},{2,0},{3,1},{4,6},{5,7},{6,4},{7,5},{8,10},{9,11},{10,... | collective-permute-start | bytes 1179656 | tf_op jit(solution)/shard_map/ppermute | solution.py:582
  88.1 2.5 %collective-permute-start.12 = (bf16[192,8,128]{2,1,0:T(8,128)(2,1)}, bf16[192,8,128]{2,1,0:T(8,128)(2,1)}, u32[]{:S(2)}, u32[]{:S(2)}) collective-permute-start(bf16[192,8,128]{2,1,0:T(8,128)(2,1)} %bitcast.23), channel_id=1, source_target_pairs={{0,3},{1,0},{2,1},{3,2},{4,7},{5,4},{6,5},{7,6},{8,11},{9,8},{10,9... | collective-permute-start | bytes 1179656 | tf_op jit(solution)/shard_map/ppermute | solution.py:582
  90.5 0.8 all-to-all-done.got_ref
  91.3 0.0 collective-permute-done.8.refs_8_
  91.3 0.0 collective-permute-done.9.refs_9_
  91.3 0.7 copy-done.6
  92.1 10.5 %shard_map.62 = (f32[96,16,256]{2,1,0:T(8,128)S(1)}, f32[96,16,256]{2,1,0:T(8,128)}, f32[24,16,256]{2,1,0:T(8,128)S(1)}, f32[16,128]{1,0:T(8,128)S(1)}, f32[16,128]{1,0:T(8,128)S(1)}, /*index=5*/f32[64,128]{1,0:T(8,128)S(1)}) custom-call(s32[2]{0:T(128)S(1)} %copy-done.14, f32[64,4,128]{2,1,0:T(4,128)} %all-to-all-done.got_ref, ...), custom_call_target="tpu_custom_call" | custom-call | tf_op jit(solution)/shard_map/pallas_call | solution.py:557
  102.5 1.2 copy-done
  103.7 24.2 %all_to_all.25 = f32[64,1,128]{2,1,0:T(1,128)S(1)} all-to-all(f32[64,1,128]{2,1,0:T(1,128)S(1)} %bitcast.31), channel_id=1, replica_groups=mesh['gx'=16,'gy'=4,'tx'=4] {'gx','gy'}, dimensions={0} | all-to-all | bytes 65536 | tf_op jit(solution)/shard_map/all_to_all | solution.py:572
  127.9 9.7 %shard_map.63 = (f32[96,16,256]{2,1,0:T(8,128)S(1)}, f32[96,16,256]{2,1,0:T(8,128)}, f32[16,128]{1,0:T(8,128)S(1)}, f32[64,128]{1,0:T(8,128)S(1)}) custom-call(f32[64,128]{1,0:T(8,128)S(1)} %bitcast.28, bf16[198,8,128]{2,1,0:T(8,128)(2,1)S(1)} %pad_maximum_fusion.refs_0_.block_ref, bf16[198,8,128]{2,1,0:T(8,128)(2,1)S(1)} %collective-permute-done.refs_1_, ...), custom_call_target="tpu_custom_call" | custom-call | tf_op jit(solution)/shard_map/pallas_call | solution.py:557
  137.6 1.2 copy-done.3
  138.8 12.1 %all_to_all.26 = f32[64,1,128]{2,1,0:T(1,128)S(1)} all-to-all(f32[64,1,128]{2,1,0:T(1,128)S(1)} %bitcast.32), channel_id=1, replica_groups=mesh['gx'=16,'gy'=4,'tx'=4] {'gx','gy'}, dimensions={0} | all-to-all | bytes 65536 | tf_op jit(solution)/shard_map/all_to_all | solution.py:572
  151.0 11.0 %shard_map.64 = (f32[96,16,256]{2,1,0:T(8,128)S(1)}, f32[96,16,256]{2,1,0:T(8,128)}, f32[96,8,128]{2,1,0:T(8,128)S(1)}, f32[16,128]{1,0:T(8,128)S(1)}, f32[64,128]{1,0:T(8,128)S(1)}) custom-call(f32[64,128]{1,0:T(8,128)S(1)} %bitcast.27, bf16[198,8,128]{2,1,0:T(8,128)(2,1)S(1)} %pad_maximum_fusion.refs_0_.block_ref, ...), custom_call_target="tpu_custom_call" | custom-call | tf_op jit(solution)/shard_map/pallas_call | solution.py:557
  162.0 1.1 copy-done.1
  163.1 0.7 copy-done.9
  163.9 12.1 %all_to_all.27 = f32[64,1,128]{2,1,0:T(1,128)S(1)} all-to-all(f32[64,1,128]{2,1,0:T(1,128)S(1)} %bitcast.30), channel_id=1, replica_groups=mesh['gx'=16,'gy'=4,'tx'=4] {'gx','gy'}, dimensions={0} | all-to-all | bytes 65536 | tf_op jit(solution)/shard_map/all_to_all | solution.py:572
  176.0 9.8 %shard_map.65 = (f32[96,16,256]{2,1,0:T(8,128)S(1)}, f32[96,16,256]{2,1,0:T(8,128)}, f32[16,128]{1,0:T(8,128)S(1)}, f32[64,128]{1,0:T(8,128)S(1)}) custom-call(f32[64,128]{1,0:T(8,128)S(1)} %bitcast.26, bf16[198,8,128]{2,1,0:T(8,128)(2,1)S(1)} %pad_maximum_fusion.refs_0_.block_ref, bf16[198,8,128]{2,1,0:T(8,128)(2,1)S(1)} %collective-permute-done.refs_1_, ...), custom_call_target="tpu_custom_call" | custom-call | tf_op jit(solution)/shard_map/pallas_call | solution.py:557
  185.8 1.2 copy-done.4
  186.9 0.6 copy-done.11
  187.6 0.6 copy-done.12
  188.1 4.6 %all-to-all-start.4 = ((f32[64,1,128]{2,1,0:T(1,128)}), f32[64,1,128]{2,1,0:T(1,128)S(1)}, u32[]{:S(2)}, u32[]{:S(2)}) async-start(f32[64,1,128]{2,1,0:T(1,128)} %bitcast.29), calls=%async_computation.4 | async-start | bytes 65536 | tf_op jit(solution)/shard_map/all_to_all | solution.py:572
  192.8 8.0 %all-to-all-done.4 = f32[64,1,128]{2,1,0:T(1,128)S(1)} async-done(((f32[64,1,128]{2,1,0:T(1,128)}), f32[64,1,128]{2,1,0:T(1,128)S(1)}, u32[]{:S(2)}, u32[]{:S(2)}) %all-to-all-start.4) | async-done | bytes 32800 | tf_op jit(solution)/shard_map/all_to_all | solution.py:572
  200.8 1.4 copy-done.2
  202.2 1.0 copy-done.8
  203.2 1.0 copy-done.10
  204.2 0.7 copy-done.13
  204.9 7.3 %shard_map.66 = (f32[96,8,128]{2,1,0:T(8,128)}, f32[96,8,128]{2,1,0:T(8,128)}) custom-call(f32[64,128]{1,0:T(8,128)S(1)} %bitcast.25, bf16[198,8,128]{2,1,0:T(8,128)(2,1)S(1)} %pad_maximum_fusion.refs_0_.block_ref, bf16[198,8,128]{2,1,0:T(8,128)(2,1)S(1)} %collective-permute-done.refs_1_, bf16[198,8,128]{2,1,0:T(8,128)(2,1)S(1)} %collective-permute-done.1.refs_2_, ...), custom_call_target="tpu_custom_call" | custom-call | tf_op jit(solution)/shard_map/pallas_call | solution.py:557
  (26 shorter events, 0.1 us)
Async XLA Ops:
  0.6 64.0 %copy-start.14 = (s32[2]{0:T(128)S(1)}, s32[2]{0:T(128)}, u32[]{:S(2)}) copy-start(s32[2]{0:T(128)} %src_ref.3) | copy-start | bytes 28
  2.0 16.7 %collective-permute-start.3 = (bf16[8,1664]{1,0:T(8,128)(2,1)S(1)}, bf16[8,1664]{1,0:T(8,128)(2,1)S(1)}, u32[]{:S(2)}, u32[]{:S(2)}) collective-permute-start(bf16[8,1664]{1,0:T(8,128)(2,1)S(1)} %shard_map.60), channel_id=1, source_target_pairs={{4,0},{8,4},{12,8},{5,1},{9,5},{13,9},{6,2},{10,6},{14,10},{7,3},{... | collective-permute-start | bytes 79880 | tf_op jit(solution)/shard_map/ppermute | solution.py:596
  3.3 15.4 %collective-permute-start.4 = (bf16[8,1664]{1,0:T(8,128)(2,1)S(1)}, bf16[8,1664]{1,0:T(8,128)(2,1)S(1)}, u32[]{:S(2)}, u32[]{:S(2)}) collective-permute-start(bf16[8,1664]{1,0:T(8,128)(2,1)S(1)} %shard_map.60), channel_id=1, source_target_pairs={{0,4},{4,8},{8,12},{1,5},{5,9},{9,13},{2,6},{6,10},{10,14},{3,7},{... | collective-permute-start | bytes 79880 | tf_op jit(solution)/shard_map/ppermute | solution.py:596
  8.0 47.0 %collective-permute-start = (bf16[198,8,128]{2,1,0:T(8,128)(2,1)S(1)}, bf16[198,8,128]{2,1,0:T(8,128)(2,1)S(1)}, u32[]{:S(2)}, u32[]{:S(2)}) collective-permute-start(bf16[198,8,128]{2,1,0:T(8,128)(2,1)S(1)} %pad_maximum_fusion.refs_0_.block_ref), channel_id=1, source_target_pairs={{0,1},{1,2},{2,3},{3,0},{4,5},{5,6},{6,7},{7,4},{8,9},{9,10},{10,1... | collective-permute-start | bytes 1216520 | tf_op jit(solution)/shard_map/ppermute | solution.py:582
  11.2 43.8 %collective-permute-start.1 = (bf16[198,8,128]{2,1,0:T(8,128)(2,1)S(1)}, bf16[198,8,128]{2,1,0:T(8,128)(2,1)S(1)}, u32[]{:S(2)}, u32[]{:S(2)}) collective-permute-start(bf16[198,8,128]{2,1,0:T(8,128)(2,1)S(1)} %pad_maximum_fusion.refs_0_.block_ref), channel_id=1, source_target_pairs={{0,2},{1,3},{2,0},{3,1},{4,6},{5,7},{6,4},{7,5},{8,10},{9,11},{10,... | collective-permute-start | bytes 1216520 | tf_op jit(solution)/shard_map/ppermute | solution.py:582
  16.3 38.7 %collective-permute-start.2 = (bf16[198,8,128]{2,1,0:T(8,128)(2,1)S(1)}, bf16[198,8,128]{2,1,0:T(8,128)(2,1)S(1)}, u32[]{:S(2)}, u32[]{:S(2)}) collective-permute-start(bf16[198,8,128]{2,1,0:T(8,128)(2,1)S(1)} %pad_maximum_fusion.refs_0_.block_ref), channel_id=1, source_target_pairs={{0,3},{1,0},{2,1},{3,2},{4,7},{5,4},{6,5},{7,6},{8,11},{9,8},{10,9... | collective-permute-start | bytes 1216520 | tf_op jit(solution)/shard_map/ppermute | solution.py:582
  18.8 31.5 %collective-permute-start.5 = (bf16[8,1664]{1,0:T(8,128)(2,1)S(1)}, bf16[8,1664]{1,0:T(8,128)(2,1)S(1)}, u32[]{:S(2)}, u32[]{:S(2)}) collective-permute-start(bf16[8,1664]{1,0:T(8,128)(2,1)S(1)} %broadcast_select_fusion.refs_4_), channel_id=1, source_target_pairs={{0,1},{1,2},{2,3},{3,0},{4,5},{5,6},{6,7},{7,4},{8,9},{9,10},{10,1... | collective-permute-start | bytes 79880 | tf_op jit(solution)/shard_map/ppermute | solution.py:582
  18.8 31.5 %collective-permute-start.6 = (bf16[8,1664]{1,0:T(8,128)(2,1)S(1)}, bf16[8,1664]{1,0:T(8,128)(2,1)S(1)}, u32[]{:S(2)}, u32[]{:S(2)}) collective-permute-start(bf16[8,1664]{1,0:T(8,128)(2,1)S(1)} %broadcast_select_fusion.refs_4_), channel_id=1, source_target_pairs={{0,2},{1,3},{2,0},{3,1},{4,6},{5,7},{6,4},{7,5},{8,10},{9,11},{10,... | collective-permute-start | bytes 79880 | tf_op jit(solution)/shard_map/ppermute | solution.py:582
  50.3 4.7 %collective-permute-start.7 = (bf16[8,1664]{1,0:T(8,128)(2,1)S(1)}, bf16[8,1664]{1,0:T(8,128)(2,1)S(1)}, u32[]{:S(2)}, u32[]{:S(2)}) collective-permute-start(bf16[8,1664]{1,0:T(8,128)(2,1)S(1)} %broadcast_select_fusion.refs_4_), channel_id=1, source_target_pairs={{0,3},{1,0},{2,1},{3,2},{4,7},{5,4},{6,5},{7,6},{8,11},{9,8},{10,9... | collective-permute-start | bytes 79880 | tf_op jit(solution)/shard_map/ppermute | solution.py:582
  55.0 6.6 %copy-start.5 = (bf16[8,1664]{1,0:T(8,128)(2,1)}, bf16[8,1664]{1,0:T(8,128)(2,1)S(1)}, u32[]{:S(2)}) copy-start(bf16[8,1664]{1,0:T(8,128)(2,1)S(1)} %collective-permute-done.7.refs_7_) | copy-start | bytes 79876
  57.2 34.1 %collective-permute-start.8 = (bf16[448,8,128]{2,1,0:T(8,128)(2,1)}, bf16[448,8,128]{2,1,0:T(8,128)(2,1)S(1)}, u32[]{:S(2)}, u32[]{:S(2)}) collective-permute-start(bf16[448,8,128]{2,1,0:T(8,128)(2,1)} %get-tuple-element.25), channel_id=1, source_target_pairs={{16,0},{32,16},{48,32},{64,48},{80,64},{96,80},{112,96},{128,112},... | collective-permute-start | bytes 2752520 | tf_op jit(solution)/shard_map/ppermute | solution.py:603
  61.6 29.7 %collective-permute-start.9 = (bf16[448,8,128]{2,1,0:T(8,128)(2,1)}, bf16[448,8,128]{2,1,0:T(8,128)(2,1)S(1)}, u32[]{:S(2)}, u32[]{:S(2)}) collective-permute-start(bf16[448,8,128]{2,1,0:T(8,128)(2,1)} %get-tuple-element.26), channel_id=1, source_target_pairs={{0,16},{16,32},{32,48},{48,64},{64,80},{80,96},{96,112},{112,128},... | collective-permute-start | bytes 2752520 | tf_op jit(solution)/shard_map/ppermute | solution.py:603
  74.4 0.7 copy-start.7
  75.0 16.3 %all-to-all-start = ((f32[64,4,128]{2,1,0:T(4,128)}), f32[64,4,128]{2,1,0:T(4,128)}, u32[]{:S(2)}, u32[]{:S(2)}) async-start(f32[64,4,128]{2,1,0:T(4,128)} %copy-done.7), calls=%async_computation | async-start | bytes 262144 | tf_op jit(solution)/shard_map/all_to_all | solution.py:572
  82.8 109.9 %collective-permute-start.10 = (bf16[192,8,128]{2,1,0:T(8,128)(2,1)}, bf16[192,8,128]{2,1,0:T(8,128)(2,1)}, u32[]{:S(2)}, u32[]{:S(2)}) collective-permute-start(bf16[192,8,128]{2,1,0:T(8,128)(2,1)} %bitcast.21), channel_id=1, source_target_pairs={{0,1},{1,2},{2,3},{3,0},{4,5},{5,6},{6,7},{7,4},{8,9},{9,10},{10,1... | collective-permute-start | bytes 1179656 | tf_op jit(solution)/shard_map/ppermute | solution.py:582
  84.6 108.2 %collective-permute-start.11 = (bf16[192,8,128]{2,1,0:T(8,128)(2,1)}, bf16[192,8,128]{2,1,0:T(8,128)(2,1)}, u32[]{:S(2)}, u32[]{:S(2)}) collective-permute-start(bf16[192,8,128]{2,1,0:T(8,128)(2,1)} %bitcast.22), channel_id=1, source_target_pairs={{0,2},{1,3},{2,0},{3,1},{4,6},{5,7},{6,4},{7,5},{8,10},{9,11},{10,... | collective-permute-start | bytes 1179656 | tf_op jit(solution)/shard_map/ppermute | solution.py:582
  88.1 104.7 %collective-permute-start.12 = (bf16[192,8,128]{2,1,0:T(8,128)(2,1)}, bf16[192,8,128]{2,1,0:T(8,128)(2,1)}, u32[]{:S(2)}, u32[]{:S(2)}) collective-permute-start(bf16[192,8,128]{2,1,0:T(8,128)(2,1)} %bitcast.23), channel_id=1, source_target_pairs={{0,3},{1,0},{2,1},{3,2},{4,7},{5,4},{6,5},{7,6},{8,11},{9,8},{10,9... | collective-permute-start | bytes 1179656 | tf_op jit(solution)/shard_map/ppermute | solution.py:582
  91.3 0.7 copy-start.6
  102.5 1.2 copy-start
  137.6 1.2 copy-start.3
  162.0 1.1 copy-start.1
  163.1 0.7 copy-start.9
  185.8 1.2 copy-start.4
  186.9 0.6 copy-start.11
  187.6 0.6 copy-start.12
  188.1 12.6 %all-to-all-start.4 = ((f32[64,1,128]{2,1,0:T(1,128)}), f32[64,1,128]{2,1,0:T(1,128)S(1)}, u32[]{:S(2)}, u32[]{:S(2)}) async-start(f32[64,1,128]{2,1,0:T(1,128)} %bitcast.29), calls=%async_computation.4 | async-start | bytes 65536 | tf_op jit(solution)/shard_map/all_to_all | solution.py:572
  200.8 1.4 copy-start.2
  202.2 1.0 copy-start.8
  203.2 1.0 copy-start.10
  204.2 0.7 copy-start.13

commit v2 on v1

--- a/solution.py
+++ b/solution.py
@@ -42,6 +42,10 @@
     )
 
 
+def owner(d):
+    return lax.rem(lax.axis_index("tx") - d + LOCAL, LOCAL)
+
+
 def pack_y_kernel(block_ref, out_ref):
     pick = pick_matrix(BF16)
     for tile in range(PACKED):
@@ -55,7 +59,7 @@
 
 
 def pack_x_kernel(*refs):
-    blocks, packed, lo_ref, hi_ref = refs[:4], refs[4:8], refs[8], refs[9]
+    blocks, packed, lo_ref, hi_ref = refs[:4], refs[4], refs[5], refs[6]
     top = iota((1, 8, 128), 1) < 4
     for d in range(LOCAL):
         block = blocks[d]
@@ -78,7 +82,7 @@
         lo_ref[d * HALF + 96 : d * HALF + 99] = jnp.where(top, one, two).astype(BF16)
         hi_ref[d * HALF + 96 : d * HALF + 99] = jnp.where(top, two, one).astype(BF16)
         for tile in range(PACKED):
-            piece = packed[d][:, tile * 128 : (tile + 1) * 128]
+            piece = packed[owner(d), :, tile * 128 : (tile + 1) * 128]
             lo_ref[4 * HALF + d * PACKED + tile] = piece
             hi_ref[4 * HALF + d * PACKED + tile] = piece
 
@@ -201,7 +205,9 @@
                     k = d * LOCAL + kl
                     t = kl * 3 + tile
                     at = 4 * HALF + d * PACKED + t
-                    near = near + coeffs[s][k] * packed[d][:, t * 128 : (t + 1) * 128].astype(F32)
+                    near = near + coeffs[s][k] * packed[
+                        owner(d), :, t * 128 : (t + 1) * 128
+                    ].astype(F32)
                     edge = jnp.where(from_next, ln_ref[at].astype(F32), hp_ref[at].astype(F32))
                     far = far + coeffs[s][k] * edge
             place = s * ROWS + tile * 16
@@ -258,7 +264,7 @@
 
 
 def gram_kernel(size_x, size_y, src_ref, *refs):
-    blocks, out_ref, field_ref, sums_ref = refs[:4], refs[4], refs[5], refs[6]
+    blocks, out_ref, field_ref, rows_ref = refs[:4], refs[4], refs[5], refs[6]
     x_pos = lax.axis_index("gx") * 8 + iota((8, 128), 0)
     y_pos = lax.axis_index("gy") * 128 + iota((8, 128), 1)
     for z in range(8):
@@ -269,25 +275,40 @@
             m = pick_layer([b[192 + 2 * c + z % 2].astype(F32) for b in blocks], z)
             for s in range(2):
                 real = (m - 1.0) * WEIGHTS[c] * prim[s]
-                field_ref[s * ROWS + c * 8 + z] = real
-                field_ref[s * ROWS + 24 + c * 8 + z] = 0.5 * real
-    sums_ref[...] = jnp.zeros_like(sums_ref)
-    inner_all(blocks, lambda s, j: field_ref[s * ROWS + j], sums_ref)
-
-    def body(j, acc):
-        rows = jnp.concatenate(
-            [vector_row(blocks, d, kl, j) for d in range(LOCAL) for kl in range(LOCAL)], axis=0
-        ).astype(BF16)
-        return acc + nt_dot(rows, rows)
-
-    gram = lax.fori_loop(0, ROWS, body, jnp.zeros((128, 128), F32))
+                field_ref[c * 8 + z, s * 8 : s * 8 + 8] = real
+                field_ref[24 + c * 8 + z, s * 8 : s * 8 + 8] = 0.5 * real
+
+    def body(j, carry):
+        columns = pl.ds(pl.multiple_of(j * 128, 128), 128)
+        for pair in range(VECS // 2):
+            d, kl = pair // 2, 2 * (pair % 2)
+            both = [vector_row(blocks, d, kl + i, j) for i in range(2)]
+            rows_ref[16 * pair : 16 * pair + 16, columns] = jnp.concatenate(both).astype(BF16)
+        rest = field_ref[j]
+        for piece in range(3):
+            part = rest.astype(BF16)
+            rest = rest - part.astype(F32)
+            first = 8 * VECS + 16 * piece
+            rows_ref[first : first + 16, columns] = part
+        return carry
+
+    lax.fori_loop(0, ROWS, body, 0)
+    full = nt_dot(rows_ref[0:128], rows_ref[...])
     row, lane = iota((128, 128), 0), iota((128, 128), 1)
-    gram = jnp.where(row % 8 == lane % 8, gram, 0.0).reshape(VECS, 8, 128)
+    gram = jnp.where(row % 8 == lane % 8, full[:, 0:128], 0.0).reshape(VECS, 8, 128)
     gram = jnp.sum(gram, axis=1)
     gram = full_dot(gram, jnp.where(row // 8 == lane % 16, 1.0, 0.0).astype(F32))
     gram = jnp.where(iota((VECS, 128), 1) // 16 == iota((VECS, 128), 0) % 8, gram, 0.0)
     gram = jnp.sum(gram.reshape(2, 8, 128), axis=1)
-    rows = jnp.concatenate([gram, row_of_sums(sums_ref), jnp.zeros((1, 128), F32)], axis=0)
+    inner = full[:, 128:144] + full[:, 144:160] + full[:, 160:176]
+    inner = jnp.where(iota((128, 16), 0) % 8 == iota((128, 16), 1) % 8, inner, 0.0)
+    inner = jnp.sum(inner.reshape(VECS, 8, 16), axis=1)
+    lines = []
+    for s in range(2):
+        chosen = jnp.where(iota((8, 16), 1) // 8 == s, 1.0, 0.0).astype(F32)
+        lines.append(nt_dot(chosen, inner, HIGH)[0:1])
+    line = jnp.concatenate(lines + [jnp.zeros((1, 96), F32)], axis=1)
+    rows = jnp.concatenate([gram, line, jnp.zeros((1, 128), F32)], axis=0)
     out_ref[...] = jnp.broadcast_to(rows[None], out_ref.shape)
 
 
@@ -304,8 +325,8 @@
 
 
 def begin_kernel(size_x, size_y, src_ref, got_ref, *refs):
-    blocks, packed, ln_ref, hp_ref = refs[:4], refs[4:8], refs[8], refs[9]
-    r_ref, q_ref, m_ref, inv_ref, state_ref, out_ref, side_ref, sums_ref = refs[10:]
+    blocks, packed, ln_ref, hp_ref = refs[:4], refs[4], refs[5], refs[6]
+    r_ref, q_ref, m_ref, inv_ref, state_ref, out_ref, side_ref, sums_ref = refs[7:]
     total = jnp.sum(got_ref[...], axis=0)
     inverse = invert(total[0:2])
     inv_ref[...] = inverse
@@ -332,7 +353,7 @@
     sides = []
     for d in range(LOCAL):
         at = 4 * HALF + d * PACKED + 12
-        near = packed[d][:, 12 * 128 : 13 * 128].astype(F32)
+        near = packed[owner(d), :, 12 * 128 : 13 * 128].astype(F32)
         far = jnp.where(from_next, ln_ref[at].astype(F32), hp_ref[at].astype(F32))
         near = full_dot(jnp.transpose(near), pick)[:48].reshape(6, 8, 128)
         far = full_dot(jnp.transpose(far), pick)[:48].reshape(6, 8, 128)
@@ -382,9 +403,9 @@
 
 
 def first_kernel(size_x, size_y, got_ref, *refs):
-    blocks, packed, ln_ref, hp_ref = refs[:4], refs[4:8], refs[8], refs[9]
-    r_ref, q_ref, m_ref, inv_ref, old_ref = refs[10:15]
-    u_ref, a_ref, state_ref, out_ref, side_ref, sums_ref = refs[15:]
+    blocks, packed, ln_ref, hp_ref = refs[:4], refs[4], refs[5], refs[6]
+    r_ref, q_ref, m_ref, inv_ref, old_ref = refs[7:12]
+    u_ref, a_ref, state_ref, out_ref, side_ref, sums_ref = refs[12:]
     row = jnp.sum(got_ref[...], axis=0, keepdims=True)
     _, _, mask = grid_mask(size_x, size_y)
     lane = iota((VECS, 128), 1)
@@ -474,9 +495,9 @@
 
 
 def next_kernel(size_x, size_y, got_ref, *refs):
-    blocks, packed, ln_ref, hp_ref = refs[:4], refs[4:8], refs[8], refs[9]
-    r_ref, u_ref, a_ref, m_ref, inv_ref, old_ref = refs[10:16]
-    new_ref, q_ref, sol_ref, state_ref, out_ref, side_ref, sums_ref = refs[16:]
+    blocks, packed, ln_ref, hp_ref = refs[:4], refs[4], refs[5], refs[6]
+    r_ref, u_ref, a_ref, m_ref, inv_ref, old_ref = refs[7:13]
+    new_ref, q_ref, sol_ref, state_ref, out_ref, side_ref, sums_ref = refs[13:]
     row = jnp.sum(got_ref[...], axis=0, keepdims=True)
     _, _, mask = grid_mask(size_x, size_y)
     state = old_ref[...]
@@ -524,9 +545,9 @@
 
 
 def last_kernel(got_ref, *refs):
-    blocks, basis = refs[:4], refs[4:8]
-    r_ref, u_ref, a_ref, inv_ref, old_ref, sol_ref = refs[8:14]
-    solution_ref, residual_ref = refs[14:]
+    blocks, basis = refs[:4], refs[4]
+    r_ref, u_ref, a_ref, inv_ref, old_ref, sol_ref = refs[5:11]
+    solution_ref, residual_ref = refs[11:]
     row = jnp.sum(got_ref[...], axis=0, keepdims=True)
     state = old_ref[...]
     for s in range(2):
@@ -544,7 +565,9 @@
                 for kl in range(LOCAL):
                     k = d * LOCAL + kl
                     value = value + coeffs[k] * vector_row(blocks, d, kl, j)
-                    field = field + base_coeffs[k] * vector_row(basis, d, kl, j)
+                    field = field + base_coeffs[k] * basis[
+                        (owner(d) * LOCAL + kl) * ROWS + j
+                    ].astype(F32)
             residual_ref[at] = value
             solution_ref[at] = field
             return carry
@@ -560,7 +583,7 @@
         in_specs=[pl.BlockSpec(memory_space=pltpu.SMEM)] * smem + [vmem] * (len(args) - smem),
         out_specs=jax.tree.map(lambda _: vmem, outs),
         scratch_shapes=list(scratch),
-        compiler_params=pltpu.CompilerParams(vmem_limit_bytes=48 * 1024 * 1024),
+        compiler_params=pltpu.CompilerParams(vmem_limit_bytes=20 * 1024 * 1024),
     )(*args)
 
 
@@ -595,10 +618,10 @@
     _, up, down = around(own, "gy")
     after, before = lax.ppermute(own, "gy", down), lax.ppermute(own, "gy", up)
     side = jnp.where(lax.broadcasted_iota(jnp.int32, own.shape, 0) < 4, after, before)
-    packed = gather(side)
+    packed = lax.all_to_all(jnp.broadcast_to(side, (LOCAL, *side.shape)), "tx", 0, 0)
 
     half = shape(LOCAL * (HALF + PACKED), 8, 128, dtype=BF16)
-    low, high = call(pack_x_kernel, (half, half), (*blocks, *packed))
+    low, high = call(pack_x_kernel, (half, half), (*blocks, packed))
     _, up, down = around(low, "gx")
     ln, hp = lax.ppermute(low, "gx", down), lax.ppermute(high, "gx", up)
 
@@ -608,14 +631,14 @@
         functools.partial(gram_kernel, size_x, size_y),
         shape(peers, 4, 128),
         (src_cell, *blocks),
-        (pltpu.VMEM((2 * ROWS, 8, 128), F32), sums),
+        (pltpu.VMEM((ROWS, 16, 128), F32), pltpu.VMEM((8 * VECS + 48, ROWS * 128), BF16)),
         smem=1,
     )
     got = exchange(sent)
     wide = shape(2 * ROWS, 16, 256)
     line = shape(peers, 128)
     small = shape(VECS, 128)
-    static = (*blocks, *packed, ln, hp)
+    static = (*blocks, packed, ln, hp)
     r, q, m, inverse, state, sent = call(
         functools.partial(begin_kernel, size_x, size_y),
         (wide, wide, shape(24, 16, 256), small, small, line),
@@ -623,7 +646,8 @@
         (side_scratch, sums),
         smem=1,
     )
-    bases = gather(basis.reshape(LOCAL * ROWS, 8, 128))
+    own_basis, _ = lax.optimization_barrier((basis.reshape(LOCAL * ROWS, 8, 128), blocks[2]))
+    bases = lax.all_gather(own_basis, "tx", tiled=True)
 
     def total(value):
         return exchange(value.reshape(peers, 1, 128)).reshape(peers, 128)
@@ -648,7 +672,7 @@
     field, residual = call(
         last_kernel,
         (narrow, narrow),
-        (total(sent), *blocks, *bases, r, u, a, inverse, state, field),
+        (total(sent), *blocks, bases, r, u, a, inverse, state, field),
     )
     full = (2, 2, 3, 8, 8, 128)
     return field.reshape(full), residual.reshape(full)

time: 213 us -> 214 us (level)
  blocking collectives: 48.4 us -> 99.4 us
  waiting for transfers between devices: 42.9 us -> 9.62 us
  Pallas kernels: 60.6 us -> 40.4 us
  between operations: 0.8 us -> 14.1 us
  starting transfers between devices: 46.2 us -> 40.8 us
  local copies, waits for them, and re-layouts: 12.1 us -> 7.57 us
    all_to_all x0 -> x1, blocking collectives: none -> 27 us  [on_device(): lax.all_to_all(jnp.broadcast_to(side, (LOCAL, *side.shape)), 'tx', 0, 0)]
    ppermute x9 -> x3, waiting for transfers between devices: 34.1 us -> 9.59 us  [gather(): lax.ppermute(value, 'tx', [(i, (i + d) % LOCAL) for i in range(LOCAL)])]
    all_to_all x3 -> x5, blocking collectives: 48.4 us -> 72.4 us  [exchange(): return lax.all_to_all(value, ('gx', 'gy'), 0, 0)]
    pallas_call x8, Pallas kernels: 60.6 us -> 40.4 us  [call(): pl.pallas_call(kernel, out_shape=outs, in_specs=[pl.BlockSpec(memory_spac...]
    all_to_all x2 -> x0, starting transfers between devices: 12.4 us -> none  [exchange(): return lax.all_to_all(value, ('gx', 'gy'), 0, 0)]
    all_to_all x2 -> x0, waiting for transfers between devices: 8.82 us -> none  [exchange(): return lax.all_to_all(value, ('gx', 'gy'), 0, 0)]
    ppermute x2, starting transfers between devices: 7.38 us -> 15.2 us  [on_device(): ln, hp = (lax.ppermute(low, 'gx', down), lax.ppermute(high, 'gx', up))]
    unnamed x30 -> x16, local copies, waits for them, and re-layouts: 12.1 us -> 7.56 us
  transfers between devices with their start and end apart: 15 -> 8, of which waited for: 4 -> 1; matrix products, arithmetic and copies ran while one was open for 0% -> 0% of each run, Pallas kernels for 24% -> 16%
where the time goes in v2:
time: 214 us; the launch traced here: 213 us
  blocking collectives  99.4 us (46%)
  starting transfers between devices  40.8 us (19%)
  Pallas kernels  40.4 us (19%)
  between operations  14.1 us (7%)
  waiting for transfers between devices  9.62 us (4%)
  local copies, waits for them, and re-layouts  7.57 us (4%)
    all_to_all x5, blocking collectives, exchange(): return lax.all_to_all(value, ('gx', 'gy'), 0, 0)  72.4 us
    pallas_call x8, Pallas kernels, call(): pl.pallas_call(kernel, out_shape=outs, in_specs=[pl.BlockSpec(memory_spac...  40.4 us
    all_to_all x1, blocking collectives, on_device(): lax.all_to_all(jnp.broadcast_to(side, (LOCAL, *side.shape)), 'tx', 0, 0)  27 us
    ppermute x3, starting transfers between devices, gather(): lax.ppermute(value, 'tx', [(i, (i + d) % LOCAL) for i in range(LOCAL)])  19.9 us
    ppermute x2, starting transfers between devices, on_device(): ln, hp = (lax.ppermute(low, 'gx', down), lax.ppermute(high, 'gx', up))  15.2 us
    ppermute x3, waiting for transfers between devices, gather(): lax.ppermute(value, 'tx', [(i, (i + d) % LOCAL) for i in range(LOCAL)])  9.59 us
    unnamed x16, local copies, waits for them, and re-layouts  7.56 us
    ppermute x2, starting transfers between devices, on_device(): after, before = (lax.ppermute(own, 'gy', down), lax.ppermute(own, 'gy', up))  5.67 us
  transfers between devices with their start and end apart: 8, of which 1 were waited for; matrix products, arithmetic and copies ran while one was open for 0% of the time, Pallas kernels for 16%

profile of v2, /device:TPU:1, one launch (start us, length us, event | category | flops | bytes accessed | tf_op | source)
XLA Modules:
  0.0 213.0 jit_solution(11587338889113874170)
XLA Ops:
  7.2 0.0 all-gather.2.cloned.1.call-start
  7.2 1.1 pad_maximum_fusion.refs_0_.block_ref
  8.3 0.0 copy-start.7
  8.3 7.8 %collective-permute-start.1 = (bf16[198,8,128]{2,1,0:T(8,128)(2,1)S(1)}, bf16[198,8,128]{2,1,0:T(8,128)(2,1)S(1)}, u32[]{:S(2)}, u32[]{:S(2)}) collective-permute-start(bf16[198,8,128]{2,1,0:T(8,128)(2,1)S(1)} %pad_maximum_fusion.refs_0_.block_ref), channel_id=1, source_target_pairs={{0,2},{1,3},{2,0},{3,1},{4,6},{5,7},{6,4},{7,5},{8,10},{9,11},{10,... | collective-permute-start | bytes 1216520 | tf_op jit(solution)/shard_map/ppermute | solution.py:605
  16.1 9.6 %collective-permute-done.1.refs_2_ = bf16[198,8,128]{2,1,0:T(8,128)(2,1)S(1)} collective-permute-done((bf16[198,8,128]{2,1,0:T(8,128)(2,1)S(1)}, bf16[198,8,128]{2,1,0:T(8,128)(2,1)S(1)}, u32[]{:S(2)}, u32[]{:S(2)}) %collective-permute-start.1) | collective-permute-done | bytes 405536 | tf_op jit(solution)/shard_map/ppermute | solution.py:605
  25.7 0.0 all-gather.2.cloned.1.call-update
  25.7 0.3 shard_map.60
  26.0 1.3 collective-permute-start.3
  27.3 4.4 %collective-permute-start.4 = (bf16[8,1664]{1,0:T(8,128)(2,1)S(1)}, bf16[8,1664]{1,0:T(8,128)(2,1)S(1)}, u32[]{:S(2)}, u32[]{:S(2)}) collective-permute-start(bf16[8,1664]{1,0:T(8,128)(2,1)S(1)} %shard_map.60), channel_id=1, source_target_pairs={{0,4},{4,8},{8,12},{1,5},{5,9},{9,13},{2,6},{6,10},{10,14},{3,7},{... | collective-permute-start | bytes 79880 | tf_op jit(solution)/shard_map/ppermute | solution.py:619
  31.7 9.4 %collective-permute-start = (bf16[198,8,128]{2,1,0:T(8,128)(2,1)S(1)}, bf16[198,8,128]{2,1,0:T(8,128)(2,1)S(1)}, u32[]{:S(2)}, u32[]{:S(2)}) collective-permute-start(bf16[198,8,128]{2,1,0:T(8,128)(2,1)S(1)} %pad_maximum_fusion.refs_0_.block_ref), channel_id=1, source_target_pairs={{0,1},{1,2},{2,3},{3,0},{4,5},{5,6},{6,7},{7,4},{8,9},{9,10},{10,1... | collective-permute-start | bytes 1216520 | tf_op jit(solution)/shard_map/ppermute | solution.py:605
  41.1 2.7 %collective-permute-start.2 = (bf16[198,8,128]{2,1,0:T(8,128)(2,1)S(1)}, bf16[198,8,128]{2,1,0:T(8,128)(2,1)S(1)}, u32[]{:S(2)}, u32[]{:S(2)}) collective-permute-start(bf16[198,8,128]{2,1,0:T(8,128)(2,1)S(1)} %pad_maximum_fusion.refs_0_.block_ref), channel_id=1, source_target_pairs={{0,3},{1,0},{2,1},{3,2},{4,7},{5,4},{6,5},{7,6},{8,11},{9,8},{10,9... | collective-permute-start | bytes 1216520 | tf_op jit(solution)/shard_map/ppermute | solution.py:605
  43.8 0.0 collective-permute-done.3
  43.8 0.0 collective-permute-done.4
  43.8 0.1 broadcast_select_fusion
  43.9 27.0 %all_to_all.30.refs_4_ = bf16[4,8,1664]{2,1,0:T(8,128)(2,1)S(1)} all-to-all(bf16[4,8,1664]{2,1,0:T(8,128)(2,1)S(1)} %broadcast_in_dim.3), channel_id=1, replica_groups=mesh['gx'=16,'gy'=4,'tx'=4] {'tx'}, dimensions={0} | all-to-all | bytes 212992 | tf_op jit(solution)/shard_map/all_to_all | solution.py:621
  70.9 0.0 collective-permute-done.refs_1_
  70.9 0.0 collective-permute-done.2.refs_3_
  70.9 1.0 shard_map.61
  71.9 12.2 %collective-permute-start.5 = (bf16[448,8,128]{2,1,0:T(8,128)(2,1)S(1)}, bf16[448,8,128]{2,1,0:T(8,128)(2,1)S(1)}, u32[]{:S(2)}, u32[]{:S(2)}) collective-permute-start(bf16[448,8,128]{2,1,0:T(8,128)(2,1)S(1)} %get-tuple-element.26), channel_id=1, source_target_pairs={{16,0},{32,16},{48,32},{64,48},{80,64},{96,80},{112,96},{128,112},... | collective-permute-start | bytes 2752520 | tf_op jit(solution)/shard_map/ppermute | solution.py:626
  84.1 3.0 %collective-permute-start.6 = (bf16[448,8,128]{2,1,0:T(8,128)(2,1)S(1)}, bf16[448,8,128]{2,1,0:T(8,128)(2,1)S(1)}, u32[]{:S(2)}, u32[]{:S(2)}) collective-permute-start(bf16[448,8,128]{2,1,0:T(8,128)(2,1)S(1)} %get-tuple-element.27), channel_id=1, source_target_pairs={{0,16},{16,32},{32,48},{48,64},{64,80},{80,96},{96,112},{112,128},... | collective-permute-start | bytes 2752520 | tf_op jit(solution)/shard_map/ppermute | solution.py:626
  87.1 0.0 copy-done.7
  87.1 2.7 %shard_map.59 = f32[64,4,128]{2,1,0:T(4,128)S(1)} custom-call(s32[2]{0:T(128)S(1)} %copy-done.7, bf16[198,8,128]{2,1,0:T(8,128)(2,1)S(1)} %pad_maximum_fusion.refs_0_.block_ref, bf16[198,8,128]{2,1,0:T(8,128)(2,1)S(1)} %collective-permute-done.refs_1_, bf16[198,8,128]{2,1,0:T(8,128)(2,1)S(1)} %collective-permute-done.1.refs_2_, ...), custom_call_target="tpu_custom_call" | custom-call | tf_op jit(solution)/shard_map/pallas_call | solution.py:580
  89.9 23.7 %all_to_all.31.got_ref = f32[64,4,128]{2,1,0:T(4,128)S(1)} all-to-all(f32[64,4,128]{2,1,0:T(4,128)S(1)} %shard_map.59), channel_id=1, replica_groups=mesh['gx'=16,'gy'=4,'tx'=4] {'gx','gy'}, dimensions={0} | all-to-all | bytes 262144 | tf_op jit(solution)/shard_map/all_to_all | solution.py:595
  113.5 0.0 collective-permute-done.5.refs_5_
  113.6 0.0 collective-permute-done.6.refs_6_
  113.6 9.2 %shard_map.62 = (f32[96,16,256]{2,1,0:T(8,128)S(1)}, f32[96,16,256]{2,1,0:T(8,128)S(1)}, f32[24,16,256]{2,1,0:T(8,128)S(1)}, f32[16,128]{1,0:T(8,128)S(1)}, f32[...) custom-call(s32[2]{0:T(128)S(1)} %copy-done.7, f32[64,4,128]{2,1,0:T(4,128)S(1)} %all_to_all.31.got_ref, ...), custom_call_target="tpu_custom_call" | custom-call | tf_op jit(solution)/shard_map/pallas_call | solution.py:580
  122.7 12.0 %all_to_all.32 = f32[64,1,128]{2,1,0:T(1,128)S(1)} all-to-all(f32[64,1,128]{2,1,0:T(1,128)S(1)} %bitcast.27), channel_id=1, replica_groups=mesh['gx'=16,'gy'=4,'tx'=4] {'gx','gy'}, dimensions={0} | all-to-all | bytes 65536 | tf_op jit(solution)/shard_map/all_to_all | solution.py:595
  134.8 6.8 %shard_map.63 = (f32[96,16,256]{2,1,0:T(8,128)S(1)}, f32[96,16,256]{2,1,0:T(8,128)S(1)}, f32[16,128]{1,0:T(8,128)S(1)}, f32[64,128]{1,0:T(8,128)S(1)}) custom-call(f32[64,128]{1,0:T(8,128)S(1)} %bitcast.24, bf16[198,8,128]{2,1,0:T(8,128)(2,1)S(1)} %pad_maximum_fusion.refs_0_.block_ref, bf16[198,8,128]{2,1,0:T(8,128)(2,1)S(1)} %collective-permute-done.refs_1_, ...), custom_call_target="tpu_custom_call" | custom-call | tf_op jit(solution)/shard_map/pallas_call | solution.py:580
  141.6 12.2 %all_to_all.33 = f32[64,1,128]{2,1,0:T(1,128)S(1)} all-to-all(f32[64,1,128]{2,1,0:T(1,128)S(1)} %bitcast.28), channel_id=1, replica_groups=mesh['gx'=16,'gy'=4,'tx'=4] {'gx','gy'}, dimensions={0} | all-to-all | bytes 65536 | tf_op jit(solution)/shard_map/all_to_all | solution.py:595
  153.8 7.8 %shard_map.64 = (f32[96,16,256]{2,1,0:T(8,128)S(1)}, f32[96,16,256]{2,1,0:T(8,128)S(1)}, f32[96,8,128]{2,1,0:T(8,128)S(1)}, f32[16,128]{1,0:T(8,128)S(1)}, f32[64,128]{1,0:T(8,128)S(1)}) custom-call(f32[64,128]{1,0:T(8,128)S(1)} %bitcast.22, bf16[198,8,128]{2,1,0:T(8,128)(2,1)S(1)} %pad_maximum_fusion.refs_0_.block_ref, ...), custom_call_target="tpu_custom_call" | custom-call | tf_op jit(solution)/shard_map/pallas_call | solution.py:580
  161.6 0.0 copy-start.5
  161.6 12.4 %all_to_all.34 = f32[64,1,128]{2,1,0:T(1,128)S(1)} all-to-all(f32[64,1,128]{2,1,0:T(1,128)S(1)} %bitcast.26), channel_id=1, replica_groups=mesh['gx'=16,'gy'=4,'tx'=4] {'gx','gy'}, dimensions={0} | all-to-all | bytes 65536 | tf_op jit(solution)/shard_map/all_to_all | solution.py:595
  173.9 6.8 %shard_map.65 = (f32[96,16,256]{2,1,0:T(8,128)S(1)}, f32[96,16,256]{2,1,0:T(8,128)S(1)}, f32[16,128]{1,0:T(8,128)S(1)}, f32[64,128]{1,0:T(8,128)S(1)}) custom-call(f32[64,128]{1,0:T(8,128)S(1)} %bitcast.23, bf16[198,8,128]{2,1,0:T(8,128)(2,1)S(1)} %pad_maximum_fusion.refs_0_.block_ref, bf16[198,8,128]{2,1,0:T(8,128)(2,1)S(1)} %collective-permute-done.refs_1_, ...), custom_call_target="tpu_custom_call" | custom-call | tf_op jit(solution)/shard_map/pallas_call | solution.py:580
  180.8 0.0 copy-done.5
  180.8 1.2 copy-done.1
  181.9 0.0 copy-start.3
  181.9 1.2 copy-done.3
  183.1 12.1 %all_to_all.35 = f32[64,1,128]{2,1,0:T(1,128)S(1)} all-to-all(f32[64,1,128]{2,1,0:T(1,128)S(1)} %bitcast.25), channel_id=1, replica_groups=mesh['gx'=16,'gy'=4,'tx'=4] {'gx','gy'}, dimensions={0} | all-to-all | bytes 65536 | tf_op jit(solution)/shard_map/all_to_all | solution.py:595
  195.2 0.0 all-gather.2.cloned.1.call-done.refs_4_
  195.2 0.0 copy-start
  195.2 1.4 copy-done
  196.7 0.0 copy-start.2
  196.7 1.4 copy-done.2
  198.1 0.0 copy-start.4
  198.1 1.4 copy-done.4
  199.5 0.0 copy-start.6
  199.5 1.0 copy-done.6
  200.5 5.7 %shard_map.66 = (f32[96,8,128]{2,1,0:T(8,128)}, f32[96,8,128]{2,1,0:T(8,128)}) custom-call(f32[64,128]{1,0:T(8,128)S(1)} %bitcast.21, bf16[198,8,128]{2,1,0:T(8,128)(2,1)S(1)} %pad_maximum_fusion.refs_0_.block_ref, bf16[198,8,128]{2,1,0:T(8,128)(2,1)S(1)} %collective-permute-done.refs_1_, bf16[198,8,128]{2,1,0:T(8,128)(2,1)S(1)} %collective-permute-done.1.refs_2_, ...), custom_call_target="tpu_custom_call" | custom-call | tf_op jit(solution)/shard_map/pallas_call | solution.py:580
  (3 shorter events, 0.0 us)
Async XLA Ops:
  7.2 188.1 %all-gather.2.cloned.1.call-start = ((), (), s32[]{:S(2)}) async-start(), calls=%async_computation.6 | async-start | bytes 1966080 | tf_op jit(solution)/shard_map/all_gather | solution.py:650
  8.3 78.9 %copy-start.7 = (s32[2]{0:T(128)S(1)}, s32[2]{0:T(128)}, u32[]{:S(2)}) copy-start(s32[2]{0:T(128)} %src_ref.3) | copy-start | bytes 28
  8.3 17.4 %collective-permute-start.1 = (bf16[198,8,128]{2,1,0:T(8,128)(2,1)S(1)}, bf16[198,8,128]{2,1,0:T(8,128)(2,1)S(1)}, u32[]{:S(2)}, u32[]{:S(2)}) collective-permute-start(bf16[198,8,128]{2,1,0:T(8,128)(2,1)S(1)} %pad_maximum_fusion.refs_0_.block_ref), channel_id=1, source_target_pairs={{0,2},{1,3},{2,0},{3,1},{4,6},{5,7},{6,4},{7,5},{8,10},{9,11},{10,... | collective-permute-start | bytes 1216520 | tf_op jit(solution)/shard_map/ppermute | solution.py:605
  26.0 17.8 %collective-permute-start.3 = (bf16[8,1664]{1,0:T(8,128)(2,1)S(1)}, bf16[8,1664]{1,0:T(8,128)(2,1)S(1)}, u32[]{:S(2)}, u32[]{:S(2)}) collective-permute-start(bf16[8,1664]{1,0:T(8,128)(2,1)S(1)} %shard_map.60), channel_id=1, source_target_pairs={{4,0},{8,4},{12,8},{5,1},{9,5},{13,9},{6,2},{10,6},{14,10},{7,3},{... | collective-permute-start | bytes 79880 | tf_op jit(solution)/shard_map/ppermute | solution.py:619
  27.3 16.5 %collective-permute-start.4 = (bf16[8,1664]{1,0:T(8,128)(2,1)S(1)}, bf16[8,1664]{1,0:T(8,128)(2,1)S(1)}, u32[]{:S(2)}, u32[]{:S(2)}) collective-permute-start(bf16[8,1664]{1,0:T(8,128)(2,1)S(1)} %shard_map.60), channel_id=1, source_target_pairs={{0,4},{4,8},{8,12},{1,5},{5,9},{9,13},{2,6},{6,10},{10,14},{3,7},{... | collective-permute-start | bytes 79880 | tf_op jit(solution)/shard_map/ppermute | solution.py:619
  31.7 39.2 %collective-permute-start = (bf16[198,8,128]{2,1,0:T(8,128)(2,1)S(1)}, bf16[198,8,128]{2,1,0:T(8,128)(2,1)S(1)}, u32[]{:S(2)}, u32[]{:S(2)}) collective-permute-start(bf16[198,8,128]{2,1,0:T(8,128)(2,1)S(1)} %pad_maximum_fusion.refs_0_.block_ref), channel_id=1, source_target_pairs={{0,1},{1,2},{2,3},{3,0},{4,5},{5,6},{6,7},{7,4},{8,9},{9,10},{10,1... | collective-permute-start | bytes 1216520 | tf_op jit(solution)/shard_map/ppermute | solution.py:605
  41.1 29.8 %collective-permute-start.2 = (bf16[198,8,128]{2,1,0:T(8,128)(2,1)S(1)}, bf16[198,8,128]{2,1,0:T(8,128)(2,1)S(1)}, u32[]{:S(2)}, u32[]{:S(2)}) collective-permute-start(bf16[198,8,128]{2,1,0:T(8,128)(2,1)S(1)} %pad_maximum_fusion.refs_0_.block_ref), channel_id=1, source_target_pairs={{0,3},{1,0},{2,1},{3,2},{4,7},{5,4},{6,5},{7,6},{8,11},{9,8},{10,9... | collective-permute-start | bytes 1216520 | tf_op jit(solution)/shard_map/ppermute | solution.py:605
  71.9 41.6 %collective-permute-start.5 = (bf16[448,8,128]{2,1,0:T(8,128)(2,1)S(1)}, bf16[448,8,128]{2,1,0:T(8,128)(2,1)S(1)}, u32[]{:S(2)}, u32[]{:S(2)}) collective-permute-start(bf16[448,8,128]{2,1,0:T(8,128)(2,1)S(1)} %get-tuple-element.26), channel_id=1, source_target_pairs={{16,0},{32,16},{48,32},{64,48},{80,64},{96,80},{112,96},{128,112},... | collective-permute-start | bytes 2752520 | tf_op jit(solution)/shard_map/ppermute | solution.py:626
  84.1 29.5 %collective-permute-start.6 = (bf16[448,8,128]{2,1,0:T(8,128)(2,1)S(1)}, bf16[448,8,128]{2,1,0:T(8,128)(2,1)S(1)}, u32[]{:S(2)}, u32[]{:S(2)}) collective-permute-start(bf16[448,8,128]{2,1,0:T(8,128)(2,1)S(1)} %get-tuple-element.27), channel_id=1, source_target_pairs={{0,16},{16,32},{32,48},{48,64},{64,80},{80,96},{96,112},{112,128},... | collective-permute-start | bytes 2752520 | tf_op jit(solution)/shard_map/ppermute | solution.py:626
  161.6 19.2 %copy-start.5 = (f32[96,8,128]{2,1,0:T(8,128)}, f32[96,8,128]{2,1,0:T(8,128)S(1)}, u32[]{:S(2)}) copy-start(f32[96,8,128]{2,1,0:T(8,128)S(1)} %get-tuple-element.47.refs_10_) | copy-start | bytes 1179652
  180.8 1.2 copy-start.1
  181.9 1.2 copy-start.3
  195.2 1.4 copy-start
  196.7 1.4 copy-start.2
  198.1 1.4 copy-start.4
  199.5 1.0 copy-start.6
Sparse Core Ops, SparseCore 0:
  25.8 65.2 all-gather.1

commit v3 on v2

--- a/solution.py
+++ b/solution.py
@@ -622,6 +622,10 @@
 
     half = shape(LOCAL * (HALF + PACKED), 8, 128, dtype=BF16)
     low, high = call(pack_x_kernel, (half, half), (*blocks, packed))
+    low, high, own_basis = lax.optimization_barrier(
+        (low, high, basis.reshape(LOCAL * ROWS, 8, 128))
+    )
+    bases = lax.all_gather(own_basis, "tx", tiled=True)
     _, up, down = around(low, "gx")
     ln, hp = lax.ppermute(low, "gx", down), lax.ppermute(high, "gx", up)
 
@@ -646,8 +650,6 @@
         (side_scratch, sums),
         smem=1,
     )
-    own_basis, _ = lax.optimization_barrier((basis.reshape(LOCAL * ROWS, 8, 128), blocks[2]))
-    bases = lax.all_gather(own_basis, "tx", tiled=True)
 
     def total(value):
         return exchange(value.reshape(peers, 1, 128)).reshape(peers, 128)

time: 214 us -> 212 us (level)
  blocking collectives: 99.4 us -> 124 us
  starting transfers between devices: 40.8 us -> 22.3 us
  waiting for transfers between devices: 9.62 us -> 0.04 us
    all_to_all x5, blocking collectives: 72.4 us -> 87.6 us  [exchange(): return lax.all_to_all(value, ('gx', 'gy'), 0, 0)]
    ppermute x2, starting transfers between devices: 15.2 us -> 5.56 us  [on_device(): ln, hp = (lax.ppermute(low, 'gx', down), lax.ppermute(high, 'gx', up))]
    ppermute x3, waiting for transfers between devices: 9.59 us -> 0.01 us  [gather(): lax.ppermute(value, 'tx', [(i, (i + d) % LOCAL) for i in range(LOCAL)])]
    all_to_all x1, blocking collectives: 27 us -> 36.2 us  [on_device(): lax.all_to_all(jnp.broadcast_to(side, (LOCAL, *side.shape)), 'tx', 0, 0)]
    ppermute x3, starting transfers between devices: 19.9 us -> 10.7 us  [gather(): lax.ppermute(value, 'tx', [(i, (i + d) % LOCAL) for i in range(LOCAL)])]
    unnamed x16 -> x18, local copies, waits for them, and re-layouts: 7.56 us -> 9.3 us
  transfers between devices with their start and end apart: 8 -> 8, of which waited for: 1 -> 0; matrix products, arithmetic and copies ran while one was open for 0% -> 0% of each run, Pallas kernels for 16% -> 16%
where the time goes in v3:
time: 212 us; the launch traced here: 211 us
  blocking collectives  124 us (58%)
  Pallas kernels  40.4 us (19%)
  starting transfers between devices  22.3 us (11%)
  between operations  14.1 us (7%)
  local copies, waits for them, and re-layouts  9.31 us (4%)
    all_to_all x5, blocking collectives, exchange(): return lax.all_to_all(value, ('gx', 'gy'), 0, 0)  87.6 us
    pallas_call x8, Pallas kernels, call(): pl.pallas_call(kernel, out_shape=outs, in_specs=[pl.BlockSpec(memory_spac...  40.4 us
    all_to_all x1, blocking collectives, on_device(): lax.all_to_all(jnp.broadcast_to(side, (LOCAL, *side.shape)), 'tx', 0, 0)  36.2 us
    ppermute x3, starting transfers between devices, gather(): lax.ppermute(value, 'tx', [(i, (i + d) % LOCAL) for i in range(LOCAL)])  10.7 us
    unnamed x18, local copies, waits for them, and re-layouts  9.3 us
    ppermute x2, starting transfers between devices, on_device(): after, before = (lax.ppermute(own, 'gy', down), lax.ppermute(own, 'gy', up))  5.96 us
    ppermute x2, starting transfers between devices, on_device(): ln, hp = (lax.ppermute(low, 'gx', down), lax.ppermute(high, 'gx', up))  5.56 us
  transfers between devices with their start and end apart: 8, of which 0 were waited for; matrix products, arithmetic and copies ran while one was open for 0% of the time, Pallas kernels for 16%

profile of v3, /device:TPU:1, one launch (start us, length us, event | category | flops | bytes accessed | tf_op | source)
XLA Modules:
  0.0 211.1 jit_solution(8183242651756963231)
XLA Ops:
  7.2 0.0 all-gather.2.cloned.1.call-start
  7.2 1.1 pad_maximum_fusion.refs_0_.block_ref
  8.3 0.0 copy-start.7
  8.3 0.3 shard_map.60
  8.6 1.3 collective-permute-start.3
  9.9 4.7 %collective-permute-start.4 = (bf16[8,1664]{1,0:T(8,128)(2,1)S(1)}, bf16[8,1664]{1,0:T(8,128)(2,1)S(1)}, u32[]{:S(2)}, u32[]{:S(2)}) collective-permute-start(bf16[8,1664]{1,0:T(8,128)(2,1)S(1)} %shard_map.60), channel_id=1, source_target_pairs={{0,4},{4,8},{8,12},{1,5},{5,9},{9,13},{2,6},{6,10},{10,14},{3,7},{... | collective-permute-start | bytes 79880 | tf_op jit(solution)/shard_map/ppermute | solution.py:619
  14.6 3.2 %collective-permute-start = (bf16[198,8,128]{2,1,0:T(8,128)(2,1)S(1)}, bf16[198,8,128]{2,1,0:T(8,128)(2,1)S(1)}, u32[]{:S(2)}, u32[]{:S(2)}) collective-permute-start(bf16[198,8,128]{2,1,0:T(8,128)(2,1)S(1)} %pad_maximum_fusion.refs_0_.block_ref), channel_id=1, source_target_pairs={{0,1},{1,2},{2,3},{3,0},{4,5},{5,6},{6,7},{7,4},{8,9},{9,10},{10,1... | collective-permute-start | bytes 1216520 | tf_op jit(solution)/shard_map/ppermute | solution.py:605
  17.8 5.1 %collective-permute-start.1 = (bf16[198,8,128]{2,1,0:T(8,128)(2,1)S(1)}, bf16[198,8,128]{2,1,0:T(8,128)(2,1)S(1)}, u32[]{:S(2)}, u32[]{:S(2)}) collective-permute-start(bf16[198,8,128]{2,1,0:T(8,128)(2,1)S(1)} %pad_maximum_fusion.refs_0_.block_ref), channel_id=1, source_target_pairs={{0,2},{1,3},{2,0},{3,1},{4,6},{5,7},{6,4},{7,5},{8,10},{9,11},{10,... | collective-permute-start | bytes 1216520 | tf_op jit(solution)/shard_map/ppermute | solution.py:605
  22.9 2.4 %collective-permute-start.2 = (bf16[198,8,128]{2,1,0:T(8,128)(2,1)S(1)}, bf16[198,8,128]{2,1,0:T(8,128)(2,1)S(1)}, u32[]{:S(2)}, u32[]{:S(2)}) collective-permute-start(bf16[198,8,128]{2,1,0:T(8,128)(2,1)S(1)} %pad_maximum_fusion.refs_0_.block_ref), channel_id=1, source_target_pairs={{0,3},{1,0},{2,1},{3,2},{4,7},{5,4},{6,5},{7,6},{8,11},{9,8},{10,9... | collective-permute-start | bytes 1216520 | tf_op jit(solution)/shard_map/ppermute | solution.py:605
  25.3 0.0 collective-permute-done.3
  25.3 0.0 collective-permute-done.4
  25.3 0.1 broadcast_select_fusion
  25.4 36.2 %all_to_all.30.refs_4_ = bf16[4,8,1664]{2,1,0:T(8,128)(2,1)S(1)} all-to-all(bf16[4,8,1664]{2,1,0:T(8,128)(2,1)S(1)} %broadcast_in_dim.3), channel_id=1, replica_groups=mesh['gx'=16,'gy'=4,'tx'=4] {'tx'}, dimensions={0} | all-to-all | bytes 212992 | tf_op jit(solution)/shard_map/all_to_all | solution.py:621
  61.6 0.0 collective-permute-done.refs_1_
  61.6 0.0 collective-permute-done.1.refs_2_
  61.6 0.0 collective-permute-done.2.refs_3_
  61.6 1.0 shard_map.61
  62.6 0.0 copy-start.8
  62.7 1.0 copy-done.8
  63.6 0.0 all-gather.2.cloned.1.call-update
  63.6 2.5 %collective-permute-start.5 = (bf16[448,8,128]{2,1,0:T(8,128)(2,1)}, bf16[448,8,128]{2,1,0:T(8,128)(2,1)S(1)}, u32[]{:S(2)}, u32[]{:S(2)}) collective-permute-start(bf16[448,8,128]{2,1,0:T(8,128)(2,1)} %copy-done.8), channel_id=1, source_target_pairs={{16,0},{32,16},{48,32},{64,48},{80,64},{96,80},{112,96},{128,112},... | collective-permute-start | bytes 2752520 | tf_op jit(solution)/shard_map/ppermute | solution.py:630
  66.2 3.0 %collective-permute-start.6 = (bf16[448,8,128]{2,1,0:T(8,128)(2,1)S(1)}, bf16[448,8,128]{2,1,0:T(8,128)(2,1)S(1)}, u32[]{:S(2)}, u32[]{:S(2)}) collective-permute-start(bf16[448,8,128]{2,1,0:T(8,128)(2,1)S(1)} %get-tuple-element.31), channel_id=1, source_target_pairs={{0,16},{16,32},{32,48},{48,64},{64,80},{80,96},{96,112},{112,128},... | collective-permute-start | bytes 2752520 | tf_op jit(solution)/shard_map/ppermute | solution.py:630
  69.2 0.0 copy-done.7
  69.2 2.8 %shard_map.59 = f32[64,4,128]{2,1,0:T(4,128)S(1)} custom-call(s32[2]{0:T(128)S(1)} %copy-done.7, bf16[198,8,128]{2,1,0:T(8,128)(2,1)S(1)} %pad_maximum_fusion.refs_0_.block_ref, bf16[198,8,128]{2,1,0:T(8,128)(2,1)S(1)} %collective-permute-done.refs_1_, bf16[198,8,128]{2,1,0:T(8,128)(2,1)S(1)} %collective-permute-done.1.refs_2_, ...), custom_call_target="tpu_custom_call" | custom-call | tf_op jit(solution)/shard_map/pallas_call | solution.py:580
  72.0 25.9 %all_to_all.31.got_ref = f32[64,4,128]{2,1,0:T(4,128)S(1)} all-to-all(f32[64,4,128]{2,1,0:T(4,128)S(1)} %shard_map.59), channel_id=1, replica_groups=mesh['gx'=16,'gy'=4,'tx'=4] {'gx','gy'}, dimensions={0} | all-to-all | bytes 262144 | tf_op jit(solution)/shard_map/all_to_all | solution.py:595
  97.9 0.0 collective-permute-done.5.refs_5_
  97.9 0.0 collective-permute-done.6.refs_6_
  97.9 9.2 %shard_map.62 = (f32[96,16,256]{2,1,0:T(8,128)S(1)}, f32[96,16,256]{2,1,0:T(8,128)S(1)}, f32[24,16,256]{2,1,0:T(8,128)S(1)}, f32[16,128]{1,0:T(8,128)S(1)}, f32[...) custom-call(s32[2]{0:T(128)S(1)} %copy-done.7, f32[64,4,128]{2,1,0:T(4,128)S(1)} %all_to_all.31.got_ref, ...), custom_call_target="tpu_custom_call" | custom-call | tf_op jit(solution)/shard_map/pallas_call | solution.py:580
  107.1 25.3 %all_to_all.32 = f32[64,1,128]{2,1,0:T(1,128)S(1)} all-to-all(f32[64,1,128]{2,1,0:T(1,128)S(1)} %bitcast.27), channel_id=1, replica_groups=mesh['gx'=16,'gy'=4,'tx'=4] {'gx','gy'}, dimensions={0} | all-to-all | bytes 65536 | tf_op jit(solution)/shard_map/all_to_all | solution.py:595
  132.4 6.8 %shard_map.63 = (f32[96,16,256]{2,1,0:T(8,128)S(1)}, f32[96,16,256]{2,1,0:T(8,128)S(1)}, f32[16,128]{1,0:T(8,128)S(1)}, f32[64,128]{1,0:T(8,128)S(1)}) custom-call(f32[64,128]{1,0:T(8,128)S(1)} %bitcast.24, bf16[198,8,128]{2,1,0:T(8,128)(2,1)S(1)} %pad_maximum_fusion.refs_0_.block_ref, bf16[198,8,128]{2,1,0:T(8,128)(2,1)S(1)} %collective-permute-done.refs_1_, ...), custom_call_target="tpu_custom_call" | custom-call | tf_op jit(solution)/shard_map/pallas_call | solution.py:580
  139.2 12.2 %all_to_all.33 = f32[64,1,128]{2,1,0:T(1,128)S(1)} all-to-all(f32[64,1,128]{2,1,0:T(1,128)S(1)} %bitcast.28), channel_id=1, replica_groups=mesh['gx'=16,'gy'=4,'tx'=4] {'gx','gy'}, dimensions={0} | all-to-all | bytes 65536 | tf_op jit(solution)/shard_map/all_to_all | solution.py:595
  151.4 7.8 %shard_map.64 = (f32[96,16,256]{2,1,0:T(8,128)S(1)}, f32[96,16,256]{2,1,0:T(8,128)S(1)}, f32[96,8,128]{2,1,0:T(8,128)S(1)}, f32[16,128]{1,0:T(8,128)S(1)}, f32[64,128]{1,0:T(8,128)S(1)}) custom-call(f32[64,128]{1,0:T(8,128)S(1)} %bitcast.22, bf16[198,8,128]{2,1,0:T(8,128)(2,1)S(1)} %pad_maximum_fusion.refs_0_.block_ref, ...), custom_call_target="tpu_custom_call" | custom-call | tf_op jit(solution)/shard_map/pallas_call | solution.py:580
  159.1 0.0 copy-start.5
  159.1 0.8 copy-done.5
  159.9 12.1 %all_to_all.34 = f32[64,1,128]{2,1,0:T(1,128)S(1)} all-to-all(f32[64,1,128]{2,1,0:T(1,128)S(1)} %bitcast.26), channel_id=1, replica_groups=mesh['gx'=16,'gy'=4,'tx'=4] {'gx','gy'}, dimensions={0} | all-to-all | bytes 65536 | tf_op jit(solution)/shard_map/all_to_all | solution.py:595
  172.1 6.8 %shard_map.65 = (f32[96,16,256]{2,1,0:T(8,128)S(1)}, f32[96,16,256]{2,1,0:T(8,128)S(1)}, f32[16,128]{1,0:T(8,128)S(1)}, f32[64,128]{1,0:T(8,128)S(1)}) custom-call(f32[64,128]{1,0:T(8,128)S(1)} %bitcast.23, bf16[198,8,128]{2,1,0:T(8,128)(2,1)S(1)} %pad_maximum_fusion.refs_0_.block_ref, bf16[198,8,128]{2,1,0:T(8,128)(2,1)S(1)} %collective-permute-done.refs_1_, ...), custom_call_target="tpu_custom_call" | custom-call | tf_op jit(solution)/shard_map/pallas_call | solution.py:580
  178.9 0.0 copy-start.1
  178.9 1.2 copy-done.1
  180.0 0.0 copy-start.3
  180.0 1.2 copy-done.3
  181.2 12.1 %all_to_all.35 = f32[64,1,128]{2,1,0:T(1,128)S(1)} all-to-all(f32[64,1,128]{2,1,0:T(1,128)S(1)} %bitcast.25), channel_id=1, replica_groups=mesh['gx'=16,'gy'=4,'tx'=4] {'gx','gy'}, dimensions={0} | all-to-all | bytes 65536 | tf_op jit(solution)/shard_map/all_to_all | solution.py:595
  193.3 0.0 all-gather.2.cloned.1.call-done.refs_4_
  193.4 0.0 copy-start
  193.4 1.4 copy-done
  194.8 1.4 copy-done.2
  196.2 1.4 copy-done.4
  197.6 1.0 copy-done.6
  198.6 5.7 %shard_map.66 = (f32[96,8,128]{2,1,0:T(8,128)}, f32[96,8,128]{2,1,0:T(8,128)}) custom-call(f32[64,128]{1,0:T(8,128)S(1)} %bitcast.21, bf16[198,8,128]{2,1,0:T(8,128)(2,1)S(1)} %pad_maximum_fusion.refs_0_.block_ref, bf16[198,8,128]{2,1,0:T(8,128)(2,1)S(1)} %collective-permute-done.refs_1_, bf16[198,8,128]{2,1,0:T(8,128)(2,1)S(1)} %collective-permute-done.1.refs_2_, ...), custom_call_target="tpu_custom_call" | custom-call | tf_op jit(solution)/shard_map/pallas_call | solution.py:580
  (5 shorter events, 0.0 us)
Async XLA Ops:
  7.2 186.2 %all-gather.2.cloned.1.call-start = ((), (), s32[]{:S(2)}) async-start(), calls=%async_computation.6 | async-start | bytes 1966080 | tf_op jit(solution)/shard_map/all_gather | solution.py:628
  8.3 60.9 %copy-start.7 = (s32[2]{0:T(128)S(1)}, s32[2]{0:T(128)}, u32[]{:S(2)}) copy-start(s32[2]{0:T(128)} %src_ref.3) | copy-start | bytes 28
  8.6 16.7 %collective-permute-start.3 = (bf16[8,1664]{1,0:T(8,128)(2,1)S(1)}, bf16[8,1664]{1,0:T(8,128)(2,1)S(1)}, u32[]{:S(2)}, u32[]{:S(2)}) collective-permute-start(bf16[8,1664]{1,0:T(8,128)(2,1)S(1)} %shard_map.60), channel_id=1, source_target_pairs={{4,0},{8,4},{12,8},{5,1},{9,5},{13,9},{6,2},{10,6},{14,10},{7,3},{... | collective-permute-start | bytes 79880 | tf_op jit(solution)/shard_map/ppermute | solution.py:619
  9.9 15.4 %collective-permute-start.4 = (bf16[8,1664]{1,0:T(8,128)(2,1)S(1)}, bf16[8,1664]{1,0:T(8,128)(2,1)S(1)}, u32[]{:S(2)}, u32[]{:S(2)}) collective-permute-start(bf16[8,1664]{1,0:T(8,128)(2,1)S(1)} %shard_map.60), channel_id=1, source_target_pairs={{0,4},{4,8},{8,12},{1,5},{5,9},{9,13},{2,6},{6,10},{10,14},{3,7},{... | collective-permute-start | bytes 79880 | tf_op jit(solution)/shard_map/ppermute | solution.py:619
  14.6 47.1 %collective-permute-start = (bf16[198,8,128]{2,1,0:T(8,128)(2,1)S(1)}, bf16[198,8,128]{2,1,0:T(8,128)(2,1)S(1)}, u32[]{:S(2)}, u32[]{:S(2)}) collective-permute-start(bf16[198,8,128]{2,1,0:T(8,128)(2,1)S(1)} %pad_maximum_fusion.refs_0_.block_ref), channel_id=1, source_target_pairs={{0,1},{1,2},{2,3},{3,0},{4,5},{5,6},{6,7},{7,4},{8,9},{9,10},{10,1... | collective-permute-start | bytes 1216520 | tf_op jit(solution)/shard_map/ppermute | solution.py:605
  17.8 43.9 %collective-permute-start.1 = (bf16[198,8,128]{2,1,0:T(8,128)(2,1)S(1)}, bf16[198,8,128]{2,1,0:T(8,128)(2,1)S(1)}, u32[]{:S(2)}, u32[]{:S(2)}) collective-permute-start(bf16[198,8,128]{2,1,0:T(8,128)(2,1)S(1)} %pad_maximum_fusion.refs_0_.block_ref), channel_id=1, source_target_pairs={{0,2},{1,3},{2,0},{3,1},{4,6},{5,7},{6,4},{7,5},{8,10},{9,11},{10,... | collective-permute-start | bytes 1216520 | tf_op jit(solution)/shard_map/ppermute | solution.py:605
  22.9 38.7 %collective-permute-start.2 = (bf16[198,8,128]{2,1,0:T(8,128)(2,1)S(1)}, bf16[198,8,128]{2,1,0:T(8,128)(2,1)S(1)}, u32[]{:S(2)}, u32[]{:S(2)}) collective-permute-start(bf16[198,8,128]{2,1,0:T(8,128)(2,1)S(1)} %pad_maximum_fusion.refs_0_.block_ref), channel_id=1, source_target_pairs={{0,3},{1,0},{2,1},{3,2},{4,7},{5,4},{6,5},{7,6},{8,11},{9,8},{10,9... | collective-permute-start | bytes 1216520 | tf_op jit(solution)/shard_map/ppermute | solution.py:605
  62.6 1.0 copy-start.8
  63.6 34.2 %collective-permute-start.5 = (bf16[448,8,128]{2,1,0:T(8,128)(2,1)}, bf16[448,8,128]{2,1,0:T(8,128)(2,1)S(1)}, u32[]{:S(2)}, u32[]{:S(2)}) collective-permute-start(bf16[448,8,128]{2,1,0:T(8,128)(2,1)} %copy-done.8), channel_id=1, source_target_pairs={{16,0},{32,16},{48,32},{64,48},{80,64},{96,80},{112,96},{128,112},... | collective-permute-start | bytes 2752520 | tf_op jit(solution)/shard_map/ppermute | solution.py:630
  66.2 31.7 %collective-permute-start.6 = (bf16[448,8,128]{2,1,0:T(8,128)(2,1)S(1)}, bf16[448,8,128]{2,1,0:T(8,128)(2,1)S(1)}, u32[]{:S(2)}, u32[]{:S(2)}) collective-permute-start(bf16[448,8,128]{2,1,0:T(8,128)(2,1)S(1)} %get-tuple-element.31), channel_id=1, source_target_pairs={{0,16},{16,32},{32,48},{48,64},{64,80},{80,96},{96,112},{112,128},... | collective-permute-start | bytes 2752520 | tf_op jit(solution)/shard_map/ppermute | solution.py:630
  159.1 0.8 copy-start.5
  178.9 1.2 copy-start.1
  180.0 1.2 copy-start.3
  193.4 1.4 copy-start
  194.8 1.4 copy-start.2
  196.2 1.4 copy-start.4
  197.6 1.0 copy-start.6
Sparse Core Ops, SparseCore 0:
  63.8 43.5 all-gather.1

commit v4 on v2

--- a/solution.py
+++ b/solution.py
@@ -42,8 +42,26 @@
     )
 
 
-def owner(d):
-    return lax.rem(lax.axis_index("tx") - d + LOCAL, LOCAL)
+BLOCKS = 7
+CUT = 2 * ROWS
+
+
+def vector_row(blocks, d, kl, j):
+    row = kl * ROWS + j
+    if d != 2:
+        return blocks[(0, 1, None, 2)[d]][row].astype(F32)
+    return blocks[3][row].astype(F32) if kl < 2 else blocks[4][row - CUT].astype(F32)
+
+
+def induction_row(blocks, d, at):
+    if d != 2:
+        return blocks[(0, 1, None, 2)[d]][LOCAL * ROWS + at].astype(F32)
+    return blocks[4][LOCAL * ROWS - CUT + at].astype(F32)
+
+
+def side_tile(blocks, d, tile):
+    ref, first = ((5, 0), (3, CUT), (6, 0), (4, BLOCK - CUT))[d]
+    return blocks[ref][first + tile]
 
 
 def pack_y_kernel(block_ref, out_ref):
@@ -55,40 +73,40 @@
         picked = nt_dot(pick, rows)
         if count < 16:
             picked = jnp.concatenate([picked, jnp.zeros((8, 128 - count * 8), F32)], axis=1)
-        out_ref[:, tile * 128 : (tile + 1) * 128] = picked.astype(BF16)
+        out_ref[tile] = picked.astype(BF16)
 
 
 def pack_x_kernel(*refs):
-    blocks, packed, lo_ref, hi_ref = refs[:4], refs[4], refs[5], refs[6]
-    top = iota((1, 8, 128), 1) < 4
+    blocks, lo_ref, hi_ref = refs[:BLOCKS], refs[BLOCKS], refs[BLOCKS + 1]
+    top = iota((8, 128), 0) < 4
+
+    def pair(one, two, at):
+        two = pltpu.roll(two, 4, 0)
+        lo_ref[at] = jnp.where(top, one, two).astype(BF16)
+        hi_ref[at] = jnp.where(top, two, one).astype(BF16)
+
+    def body(j, carry):
+        for d in range(LOCAL):
+            for kl in range(2):
+                pair(
+                    vector_row(blocks, d, kl, j),
+                    vector_row(blocks, d, kl + 2, j),
+                    d * HALF + kl * ROWS + j,
+                )
+        return carry
+
+    lax.fori_loop(0, ROWS, body, 0)
     for d in range(LOCAL):
-        block = blocks[d]
-
-        def body(step, carry, block=block, d=d):
-            first = step * 3
-
-            def pair(one, two, at, size):
-                one = one.astype(F32)
-                two = pltpu.roll(two.astype(F32), 4, 1)
-                lo_ref[pl.ds(d * HALF + at, size)] = jnp.where(top, one, two).astype(BF16)
-                hi_ref[pl.ds(d * HALF + at, size)] = jnp.where(top, two, one).astype(BF16)
-
-            pair(block[pl.ds(first, 3)], block[pl.ds(first + 96, 3)], first, 3)
-            return carry
-
-        lax.fori_loop(0, 32, body, 0)
-        one = block[192:195].astype(F32)
-        two = pltpu.roll(block[195:198].astype(F32), 4, 1)
-        lo_ref[d * HALF + 96 : d * HALF + 99] = jnp.where(top, one, two).astype(BF16)
-        hi_ref[d * HALF + 96 : d * HALF + 99] = jnp.where(top, two, one).astype(BF16)
+        for i in range(3):
+            pair(
+                induction_row(blocks, d, i),
+                induction_row(blocks, d, i + 3),
+                d * HALF + CUT + i,
+            )
         for tile in range(PACKED):
-            piece = packed[owner(d), :, tile * 128 : (tile + 1) * 128]
-            lo_ref[4 * HALF + d * PACKED + tile] = piece
-            hi_ref[4 * HALF + d * PACKED + tile] = piece
-
-
-def vector_row(blocks, d, kl, j):
-    return blocks[d][kl * ROWS + j].astype(F32)
+            piece = side_tile(blocks, d, tile)
+            lo_ref[LOCAL * HALF + d * PACKED + tile] = piece
+            hi_ref[LOCAL * HALF + d * PACKED + tile] = piece
 
 
 def inner_all(blocks, field, sums_ref):
@@ -170,7 +188,7 @@
     return jnp.exp(-dist / ((size_x + size_y) / 8.0))
 
 
-def combine_ext(coeffs, blocks, packed, ln_ref, hp_ref, interior, halo_x, unpacked_ref):
+def combine_ext(coeffs, blocks, ln_ref, hp_ref, interior, halo_x, unpacked_ref):
     top = iota((8, 128), 0) < 4
 
     def body(j, carry):
@@ -205,9 +223,7 @@
                     k = d * LOCAL + kl
                     t = kl * 3 + tile
                     at = 4 * HALF + d * PACKED + t
-                    near = near + coeffs[s][k] * packed[
-                        owner(d), :, t * 128 : (t + 1) * 128
-                    ].astype(F32)
+                    near = near + coeffs[s][k] * side_tile(blocks, d, t).astype(F32)
                     edge = jnp.where(from_next, ln_ref[at].astype(F32), hp_ref[at].astype(F32))
                     far = far + coeffs[s][k] * edge
             place = s * ROWS + tile * 16
@@ -264,7 +280,7 @@
 
 
 def gram_kernel(size_x, size_y, src_ref, *refs):
-    blocks, out_ref, field_ref, rows_ref = refs[:4], refs[4], refs[5], refs[6]
+    blocks, out_ref, field_ref, rows_ref = refs[:BLOCKS], *refs[BLOCKS:]
     x_pos = lax.axis_index("gx") * 8 + iota((8, 128), 0)
     y_pos = lax.axis_index("gy") * 128 + iota((8, 128), 1)
     for z in range(8):
@@ -272,7 +288,7 @@
             primary_field(src_ref[s], z, x_pos, y_pos, size_x, size_y) for s in range(2)
         ]
         for c in range(3):
-            m = pick_layer([b[192 + 2 * c + z % 2].astype(F32) for b in blocks], z)
+            m = pick_layer([induction_row(blocks, d, 2 * c + z % 2) for d in range(LOCAL)], z)
             for s in range(2):
                 real = (m - 1.0) * WEIGHTS[c] * prim[s]
                 field_ref[c * 8 + z, s * 8 : s * 8 + 8] = real
@@ -325,8 +341,9 @@
 
 
 def begin_kernel(size_x, size_y, src_ref, got_ref, *refs):
-    blocks, packed, ln_ref, hp_ref = refs[:4], refs[4], refs[5], refs[6]
-    r_ref, q_ref, m_ref, inv_ref, state_ref, out_ref, side_ref, sums_ref = refs[7:]
+    blocks, ln_ref, hp_ref = refs[:BLOCKS], refs[BLOCKS], refs[BLOCKS + 1]
+    refs = refs[BLOCKS + 2 :]
+    r_ref, q_ref, m_ref, inv_ref, state_ref, out_ref, side_ref, sums_ref = refs
     total = jnp.sum(got_ref[...], axis=0)
     inverse = invert(total[0:2])
     inv_ref[...] = inverse
@@ -344,7 +361,7 @@
         return store
 
     combine_ext(
-        coeffs, blocks, packed, ln_ref, hp_ref,
+        coeffs, blocks, ln_ref, hp_ref,
         put(slice(0, 8), slice(0, 128)), put(slice(8, 16), slice(0, 128)), side_ref,
     )
     top = iota((8, 128), 0) < 4
@@ -353,7 +370,7 @@
     sides = []
     for d in range(LOCAL):
         at = 4 * HALF + d * PACKED + 12
-        near = packed[owner(d), :, 12 * 128 : 13 * 128].astype(F32)
+        near = side_tile(blocks, d, 12).astype(F32)
         far = jnp.where(from_next, ln_ref[at].astype(F32), hp_ref[at].astype(F32))
         near = full_dot(jnp.transpose(near), pick)[:48].reshape(6, 8, 128)
         far = full_dot(jnp.transpose(far), pick)[:48].reshape(6, 8, 128)
@@ -363,7 +380,7 @@
             at = 2 * c + z % 2
             quarters = []
             for d in range(LOCAL):
-                inner_m = blocks[d][192 + at].astype(F32)
+                inner_m = induction_row(blocks, d, at)
                 row = d * HALF + 96 + at % 3
                 after, before = ln_ref[row].astype(F32), hp_ref[row].astype(F32)
                 if at < 3:
@@ -403,9 +420,10 @@
 
 
 def first_kernel(size_x, size_y, got_ref, *refs):
-    blocks, packed, ln_ref, hp_ref = refs[:4], refs[4], refs[5], refs[6]
-    r_ref, q_ref, m_ref, inv_ref, old_ref = refs[7:12]
-    u_ref, a_ref, state_ref, out_ref, side_ref, sums_ref = refs[12:]
+    blocks, ln_ref, hp_ref = refs[:BLOCKS], refs[BLOCKS], refs[BLOCKS + 1]
+    refs = refs[BLOCKS + 2 :]
+    r_ref, q_ref, m_ref, inv_ref, old_ref = refs[:5]
+    u_ref, a_ref, state_ref, out_ref, side_ref, sums_ref = refs[5:]
     row = jnp.sum(got_ref[...], axis=0, keepdims=True)
     _, _, mask = grid_mask(size_x, size_y)
     lane = iota((VECS, 128), 1)
@@ -434,7 +452,7 @@
         return store
 
     combine_ext(
-        coeffs, blocks, packed, ln_ref, hp_ref,
+        coeffs, blocks, ln_ref, hp_ref,
         put(slice(0, 8), slice(0, 128)), put(slice(8, 16), slice(0, 128)), side_ref,
     )
     for s in range(2):
@@ -495,9 +513,10 @@
 
 
 def next_kernel(size_x, size_y, got_ref, *refs):
-    blocks, packed, ln_ref, hp_ref = refs[:4], refs[4], refs[5], refs[6]
-    r_ref, u_ref, a_ref, m_ref, inv_ref, old_ref = refs[7:13]
-    new_ref, q_ref, sol_ref, state_ref, out_ref, side_ref, sums_ref = refs[13:]
+    blocks, ln_ref, hp_ref = refs[:BLOCKS], refs[BLOCKS], refs[BLOCKS + 1]
+    refs = refs[BLOCKS + 2 :]
+    r_ref, u_ref, a_ref, m_ref, inv_ref, old_ref = refs[:6]
+    new_ref, q_ref, sol_ref, state_ref, out_ref, side_ref, sums_ref = refs[6:]
     row = jnp.sum(got_ref[...], axis=0, keepdims=True)
     _, _, mask = grid_mask(size_x, size_y)
     state = old_ref[...]
@@ -522,7 +541,7 @@
         return store
 
     combine_ext(
-        coeffs, blocks, packed, ln_ref, hp_ref,
+        coeffs, blocks, ln_ref, hp_ref,
         put(slice(0, 8), slice(0, 128)), put(slice(8, 16), slice(0, 128)), side_ref,
     )
     for s in range(2):
@@ -544,10 +563,18 @@
     finish_first(blocks, new_ref, q_ref, sums_ref, out_ref)
 
 
+def basis_row(basis, d, kl, j):
+    row = kl * ROWS + j
+    if d == 0:
+        return basis[0][row].astype(F32)
+    first = {1: 1, 3: 3, 2: 5}[d]
+    return basis[first][row].astype(F32) if kl < 2 else basis[first + 1][row - CUT].astype(F32)
+
+
 def last_kernel(got_ref, *refs):
-    blocks, basis = refs[:4], refs[4]
-    r_ref, u_ref, a_ref, inv_ref, old_ref, sol_ref = refs[5:11]
-    solution_ref, residual_ref = refs[11:]
+    blocks, basis, refs = refs[:BLOCKS], refs[BLOCKS : BLOCKS + 7], refs[BLOCKS + 7 :]
+    r_ref, u_ref, a_ref, inv_ref, old_ref, sol_ref = refs[:6]
+    solution_ref, residual_ref = refs[6:]
     row = jnp.sum(got_ref[...], axis=0, keepdims=True)
     state = old_ref[...]
     for s in range(2):
@@ -565,9 +592,7 @@
                 for kl in range(LOCAL):
                     k = d * LOCAL + kl
                     value = value + coeffs[k] * vector_row(blocks, d, kl, j)
-                    field = field + base_coeffs[k] * basis[
-                        (owner(d) * LOCAL + kl) * ROWS + j
-                    ].astype(F32)
+                    field = field + base_coeffs[k] * basis_row(basis, d, kl, j)
             residual_ref[at] = value
             solution_ref[at] = field
             return carry
@@ -595,16 +620,14 @@
     return lax.all_to_all(value, ("gx", "gy"), 0, 0)
 
 
-def around(value, axis):
-    up = [(i, i + 1) for i in range(lax.axis_size(axis) - 1)]
-    return value, up, [(j, i) for i, j in up]
-
-
-def gather(value):
-    return [value] + [
-        lax.ppermute(value, "tx", [(i, (i + d) % LOCAL) for i in range(LOCAL)])
-        for d in range(1, LOCAL)
-    ]
+def steps(axis, wrap=False):
+    size = lax.axis_size(axis)
+    up = [(i, (i + 1) % size) for i in range(size if wrap else size - 1)]
+    return up, [(j, i) for i, j in up]
+
+
+def tied(first, *rest):
+    return lax.optimization_barrier((first, *rest))
 
 
 def on_device(src_cell, basis, images, induction):
@@ -613,16 +636,21 @@
     block = jnp.concatenate(
         [images.reshape(LOCAL * ROWS, 8, 128), induction.reshape(6, 8, 128)], axis=0
     )
-    blocks = gather(block)
-    own = call(pack_y_kernel, shape(8, PACKED * 128, dtype=BF16), (block,))
-    _, up, down = around(own, "gy")
+    right, left = steps("tx", wrap=True)
+    one = lax.ppermute(block, "tx", right)
+    three = lax.ppermute(block, "tx", left)
+    own = call(pack_y_kernel, shape(PACKED, 8, 128, dtype=BF16), (block,))
+    up, down = steps("gy")
     after, before = lax.ppermute(own, "gy", down), lax.ppermute(own, "gy", up)
-    side = jnp.where(lax.broadcasted_iota(jnp.int32, own.shape, 0) < 4, after, before)
-    packed = lax.all_to_all(jnp.broadcast_to(side, (LOCAL, *side.shape)), "tx", 0, 0)
+    side = jnp.where(lax.broadcasted_iota(jnp.int32, own.shape, 1) < 4, after, before)
+    far_low = lax.ppermute(jnp.concatenate([one[:CUT], side]), "tx", right)
+    far_high = lax.ppermute(jnp.concatenate([three[CUT:], side]), "tx", left)
+    far_side = lax.ppermute(side, "tx", [(i, (i + 2) % LOCAL) for i in range(LOCAL)])
+    blocks = (block, one, three, far_low, far_high, side, far_side)
 
     half = shape(LOCAL * (HALF + PACKED), 8, 128, dtype=BF16)
-    low, high = call(pack_x_kernel, (half, half), (*blocks, packed))
-    _, up, down = around(low, "gx")
+    low, high = call(pack_x_kernel, (half, half), blocks)
+    up, down = steps("gx")
     ln, hp = lax.ppermute(low, "gx", down), lax.ppermute(high, "gx", up)
 
     sums = pltpu.VMEM((128, 128), F32)
@@ -638,7 +666,14 @@
     wide = shape(2 * ROWS, 16, 256)
     line = shape(peers, 128)
     small = shape(VECS, 128)
-    static = (*blocks, packed, ln, hp)
+    static = (*blocks, ln, hp)
+    own_basis = basis.reshape(LOCAL * ROWS, 8, 128)
+
+    def total(value):
+        return exchange(value.reshape(peers, 1, 128)).reshape(peers, 128)
+
+    got, piece = tied(got, own_basis[:CUT])
+    one_low, three_low = lax.ppermute(piece, "tx", right), lax.ppermute(piece, "tx", left)
     r, q, m, inverse, state, sent = call(
         functools.partial(begin_kernel, size_x, size_y),
         (wide, wide, shape(24, 16, 256), small, small, line),
@@ -646,33 +681,36 @@
         (side_scratch, sums),
         smem=1,
     )
-    own_basis, _ = lax.optimization_barrier((basis.reshape(LOCAL * ROWS, 8, 128), blocks[2]))
-    bases = lax.all_gather(own_basis, "tx", tiled=True)
-
-    def total(value):
-        return exchange(value.reshape(peers, 1, 128)).reshape(peers, 128)
-
-    def first(r, q, state, sent):
+
+    def first(r, q, state, got):
         return call(
             functools.partial(first_kernel, size_x, size_y),
             (wide, wide, small, line),
-            (total(sent), *static, r, q, m, inverse, state),
+            (got, *static, r, q, m, inverse, state),
             (side_scratch, sums),
         )
 
-    u, a, state, sent = first(r, q, state, sent)
+    sent, one_low, three_low = tied(sent, one_low, three_low)
+    got, piece = tied(total(sent), own_basis[CUT:])
+    one_high, three_high = lax.ppermute(piece, "tx", right), lax.ppermute(piece, "tx", left)
+    u, a, state, sent = first(r, q, state, got)
+    sent, one_high, three_high = tied(sent, one_high, three_high)
+    got, one_low, three_high = tied(total(sent), one_low, three_high)
+    two_low, two_high = lax.ppermute(one_low, "tx", right), lax.ppermute(three_high, "tx", left)
     r, q, field, state, sent = call(
         functools.partial(next_kernel, size_x, size_y),
         (wide, wide, shape(2 * ROWS, 8, 128), small, line),
-        (total(sent), *static, r, u, a, m, inverse, state),
+        (got, *static, r, u, a, m, inverse, state),
         (side_scratch, sums),
     )
-    u, a, state, sent = first(r, q, state, sent)
+    sent, two_low, two_high = tied(sent, two_low, two_high)
+    u, a, state, sent = first(r, q, state, total(sent))
+    bases = (own_basis, one_low, one_high, three_low, three_high, two_low, two_high)
     narrow = shape(2 * ROWS, 8, 128)
     field, residual = call(
         last_kernel,
         (narrow, narrow),
-        (total(sent), *blocks, bases, r, u, a, inverse, state, field),
+        (total(sent), *blocks, *bases, r, u, a, inverse, state, field),
     )
     full = (2, 2, 3, 8, 8, 128)
     return field.reshape(full), residual.reshape(full)

time: 214 us -> 180 us (0.84)
  blocking collectives: 99.4 us -> 49.5 us
  waiting for transfers between devices: 9.62 us -> 32.4 us
  between operations: 14.1 us -> 0.8 us
  starting transfers between devices: 40.8 us -> 50.8 us
  local copies, waits for them, and re-layouts: 7.57 us -> 3.23 us
    all_to_all x1 -> x0, blocking collectives: 27 us -> none  [on_device(): lax.all_to_all(jnp.broadcast_to(side, (LOCAL, *side.shape)), 'tx', 0, 0)]
    all_to_all x5 -> x4, blocking collectives: 72.4 us -> 49.5 us  [exchange(): return lax.all_to_all(value, ('gx', 'gy'), 0, 0)]
    ppermute x3 -> x11, waiting for transfers between devices: 9.59 us -> 22.2 us  [the longest x1 8.99 us: on_device(): lax.ppermute(side, 'tx', [(i, (i + 2) % LOCAL) for i in range(LOCAL)])]
    all_to_all x0 -> x1, starting transfers between devices: none -> 8.24 us  [exchange(): return lax.all_to_all(value, ('gx', 'gy'), 0, 0)]
    all_to_all x0 -> x1, waiting for transfers between devices: none -> 6.68 us  [exchange(): return lax.all_to_all(value, ('gx', 'gy'), 0, 0)]
    unnamed x16 -> x14, local copies, waits for them, and re-layouts: 7.56 us -> 1.41 us
    ppermute x3 -> x11, starting transfers between devices: 19.9 us -> 25.5 us  [the longest x1 6.93 us: on_device(): three = lax.ppermute(block, 'tx', left)]
    ppermute x2, waiting for transfers between devices: 0.01 us -> 3.48 us  [on_device(): after, before = (lax.ppermute(own, 'gy', down), lax.ppermute(own, 'gy', up))]
  transfers between devices with their start and end apart: 8 -> 16, of which waited for: 1 -> 8; matrix products, arithmetic and copies ran while one was open for 0% -> 1% of each run, Pallas kernels for 16% -> 15%
where the time goes in v4:
time: 180 us; the launch traced here: 179 us
  starting transfers between devices  50.8 us (28%)
  blocking collectives  49.5 us (28%)
  Pallas kernels  41.1 us (23%)
  waiting for transfers between devices  32.4 us (18%)
  local copies, waits for them, and re-layouts  3.23 us (2%)
    all_to_all x4, blocking collectives, exchange(): return lax.all_to_all(value, ('gx', 'gy'), 0, 0)  49.5 us
    pallas_call x8, Pallas kernels, call(): pl.pallas_call(kernel, out_shape=outs, in_specs=[pl.BlockSpec(memory_spac...  41.1 us
    ppermute x2, starting transfers between devices, on_device(): ln, hp = (lax.ppermute(low, 'gx', down), lax.ppermute(high, 'gx', up))  12.6 us
    ppermute x1, waiting for transfers between devices, on_device(): lax.ppermute(side, 'tx', [(i, (i + 2) % LOCAL) for i in range(LOCAL)])  8.99 us
    all_to_all x1, starting transfers between devices, exchange(): return lax.all_to_all(value, ('gx', 'gy'), 0, 0)  8.24 us
    ppermute x1, starting transfers between devices, on_device(): three = lax.ppermute(block, 'tx', left)  6.93 us
    ppermute x1, starting transfers between devices, on_device(): far_high = lax.ppermute(jnp.concatenate([three[CUT:], side]), 'tx', left)  6.75 us
    all_to_all x1, waiting for transfers between devices, exchange(): return lax.all_to_all(value, ('gx', 'gy'), 0, 0)  6.68 us
  transfers between devices with their start and end apart: 16, of which 8 were waited for; matrix products, arithmetic and copies ran while one was open for 1% of the time, Pallas kernels for 15%

profile of v4, /device:TPU:1, one launch (start us, length us, event | category | flops | bytes accessed | tf_op | source)
XLA Modules:
  0.0 179.0 jit_solution(17024996844063482478)
XLA Ops:
  0.6 1.1 pad_maximum_fusion.block_ref.refs_0_
  1.7 6.9 %collective-permute-start.1 = (bf16[198,8,128]{2,1,0:T(8,128)(2,1)S(1)}, bf16[198,8,128]{2,1,0:T(8,128)(2,1)S(1)}, u32[]{:S(2)}, u32[]{:S(2)}) collective-permute-start(bf16[198,8,128]{2,1,0:T(8,128)(2,1)S(1)} %pad_maximum_fusion.block_ref.refs_0_), channel_id=1, source_target_pairs={{1,0},{2,1},{3,2},{0,3},{5,4},{6,5},{7,6},{4,7},{9,8},{10,9},{11,1... | collective-permute-start | bytes 1216520 | tf_op jit(solution)/shard_map/ppermute | solution.py:641
  8.6 0.3 shard_map.59
  8.9 3.2 %collective-permute-start.3 = (bf16[13,8,128]{2,1,0:T(8,128)(2,1)S(1)}, bf16[13,8,128]{2,1,0:T(8,128)(2,1)S(1)}, u32[]{:S(2)}, u32[]{:S(2)}) collective-permute-start(bf16[13,8,128]{2,1,0:T(8,128)(2,1)S(1)} %shard_map.59), channel_id=1, source_target_pairs={{0,4},{4,8},{8,12},{1,5},{5,9},{9,13},{2,6},{6,10},{10,14},{3,7},{... | collective-permute-start | bytes 79880 | tf_op jit(solution)/shard_map/ppermute | solution.py:644
  12.1 1.3 collective-permute-start.2
  13.4 0.1 collective-permute-start
  13.5 0.0 collective-permute-done.3
  13.6 3.5 %collective-permute-done.2 = bf16[13,8,128]{2,1,0:T(8,128)(2,1)S(1)} collective-permute-done((bf16[13,8,128]{2,1,0:T(8,128)(2,1)S(1)}, bf16[13,8,128]{2,1,0:T(8,128)(2,1)S(1)}, u32[]{:S(2)}, u32[]{:S(2)}) %collective-permute-start.2) | collective-permute-done | bytes 26656 | tf_op jit(solution)/shard_map/ppermute | solution.py:644
  17.0 0.1 broadcast_select_fusion.refs_5_
  17.1 6.3 %collective-permute-done.1.refs_2_ = bf16[198,8,128]{2,1,0:T(8,128)(2,1)S(1)} collective-permute-done((bf16[198,8,128]{2,1,0:T(8,128)(2,1)S(1)}, bf16[198,8,128]{2,1,0:T(8,128)(2,1)S(1)}, u32[]{:S(2)}, u32[]{:S(2)}) %collective-permute-start.1) | collective-permute-done | bytes 405536 | tf_op jit(solution)/shard_map/ppermute | solution.py:641
  23.4 0.0 copy-start.5
  23.5 6.7 %collective-permute-start.5 = (bf16[115,8,128]{2,1,0:T(8,128)(2,1)S(1)}, bf16[115,8,128]{2,1,0:T(8,128)(2,1)S(1)}, u32[]{:S(2)}, u32[]{:S(2)}) collective-permute-start(bf16[115,8,128]{2,1,0:T(8,128)(2,1)S(1)} %pad_maximum_fusion.1), channel_id=1, source_target_pairs={{1,0},{2,1},{3,2},{0,3},{5,4},{6,5},{7,6},{4,7},{9,8},{10,9},{11,1... | collective-permute-start | bytes 706568 | tf_op jit(solution)/shard_map/ppermute | solution.py:647
  30.2 0.0 collective-permute-done.refs_1_
  30.3 0.1 collective-permute-start.4
  30.3 2.1 %collective-permute-start.6 = (bf16[13,8,128]{2,1,0:T(8,128)(2,1)S(1)}, bf16[13,8,128]{2,1,0:T(8,128)(2,1)S(1)}, u32[]{:S(2)}, u32[]{:S(2)}) collective-permute-start(bf16[13,8,128]{2,1,0:T(8,128)(2,1)S(1)} %broadcast_select_fusion.refs_5_), channel_id=1, source_target_pairs={{0,2},{1,3},{2,0},{3,1},{4,6},{5,7},{6,4},{7,5},{8,10},{9,11},{10,... | collective-permute-start | bytes 79880 | tf_op jit(solution)/shard_map/ppermute | solution.py:648
  32.4 9.0 %collective-permute-done.6.refs_6_ = bf16[13,8,128]{2,1,0:T(8,128)(2,1)S(1)} collective-permute-done((bf16[13,8,128]{2,1,0:T(8,128)(2,1)S(1)}, bf16[13,8,128]{2,1,0:T(8,128)(2,1)S(1)}, u32[]{:S(2)}, u32[]{:S(2)}) %collective-permute-start.6) | collective-permute-done | bytes 26656 | tf_op jit(solution)/shard_map/ppermute | solution.py:648
  41.4 0.0 collective-permute-done.4.refs_3_
  41.4 0.0 collective-permute-done.5.refs_4_
  41.4 2.0 %shard_map.61 = (bf16[448,8,128]{2,1,0:T(8,128)(2,1)}, bf16[448,8,128]{2,1,0:T(8,128)(2,1)}) custom-call(bf16[198,8,128]{2,1,0:T(8,128)(2,1)S(1)} %pad_maximum_fusion.block_ref.refs_0_, bf16[198,8,128]{2,1,0:T(8,128)(2,1)S(1)} %collective-permute-done.refs_1_, bf16[198,8,128]{2,1,0:T(8,128)(2,1)S(1)} %collective-permute-done.1.refs_2_, ...), custom_call_target="tpu_custom_call" | custom-call | tf_op jit(solution)/shard_map/pallas_call | solution.py:605
  43.4 9.5 %collective-permute-start.7 = (bf16[448,8,128]{2,1,0:T(8,128)(2,1)}, bf16[448,8,128]{2,1,0:T(8,128)(2,1)S(1)}, u32[]{:S(2)}, u32[]{:S(2)}) collective-permute-start(bf16[448,8,128]{2,1,0:T(8,128)(2,1)} %get-tuple-element.42), channel_id=1, source_target_pairs={{16,0},{32,16},{48,32},{64,48},{80,64},{96,80},{112,96},{128,112},... | collective-permute-start | bytes 2752520 | tf_op jit(solution)/shard_map/ppermute | solution.py:654
  53.0 3.0 %collective-permute-start.8 = (bf16[448,8,128]{2,1,0:T(8,128)(2,1)}, bf16[448,8,128]{2,1,0:T(8,128)(2,1)S(1)}, u32[]{:S(2)}, u32[]{:S(2)}) collective-permute-start(bf16[448,8,128]{2,1,0:T(8,128)(2,1)} %get-tuple-element.43), channel_id=1, source_target_pairs={{0,16},{16,32},{32,48},{48,64},{64,80},{80,96},{96,112},{112,128},... | collective-permute-start | bytes 2752520 | tf_op jit(solution)/shard_map/ppermute | solution.py:654
  56.0 2.8 %shard_map.60 = f32[64,4,128]{2,1,0:T(4,128)S(1)} custom-call(s32[2]{0:T(128)S(1)} %copy-done.5, bf16[198,8,128]{2,1,0:T(8,128)(2,1)S(1)} %pad_maximum_fusion.block_ref.refs_0_, bf16[198,8,128]{2,1,0:T(8,128)(2,1)S(1)} %collective-permute-done.refs_1_, bf16[198,8,128]{2,1,0:T(8,128)(2,1)S(1)} %collective-permute-done.1.refs_2_, ...), custom_call_target="tpu_custom_call" | custom-call | tf_op jit(solution)/shard_map/pallas_call | solution.py:605
  58.8 0.6 copy-done.4
  59.4 8.2 %all-to-all-start = ((f32[64,4,128]{2,1,0:T(4,128)}), f32[64,4,128]{2,1,0:T(4,128)}, u32[]{:S(2)}, u32[]{:S(2)}) async-start(f32[64,4,128]{2,1,0:T(4,128)} %copy-done.4), calls=%async_computation | async-start | bytes 262144 | tf_op jit(solution)/shard_map/all_to_all | solution.py:620
  67.7 1.8 %fusion = (bf16[2,2,3,8,8,128]{5,4,3,2,1,0:T(8,128)(2,1)}, bf16[2,2,3,8,8,128]{5,4,3,2,1,0:T(8,128)(2,1)}) fusion(bf16[4,2,3,8,8,128]{5,4,3,2,1,0:T(8,128)(2,1)} %param.5), kind=kLoop, calls=%fused_computation.5 | loop fusion | bytes 786432 | tf_op jit(solution)/shard_map/slice | solution.py:694
  69.5 6.7 %all-to-all-done.got_ref = f32[64,4,128]{2,1,0:T(4,128)} async-done(((f32[64,4,128]{2,1,0:T(4,128)}), f32[64,4,128]{2,1,0:T(4,128)}, u32[]{:S(2)}, u32[]{:S(2)}) %all-to-all-start) | async-done | bytes 131104 | tf_op jit(solution)/shard_map/all_to_all | solution.py:620
  76.2 2.4 %collective-permute-start.9 = (bf16[96,8,128]{2,1,0:T(8,128)(2,1)}, bf16[96,8,128]{2,1,0:T(8,128)(2,1)S(1)}, u32[]{:S(2)}, u32[]{:S(2)}) collective-permute-start(bf16[96,8,128]{2,1,0:T(8,128)(2,1)} %bitcast.36), channel_id=1, source_target_pairs={{0,1},{1,2},{2,3},{3,0},{4,5},{5,6},{6,7},{7,4},{8,9},{9,10},{10,1... | collective-permute-start | bytes 589832 | tf_op jit(solution)/shard_map/ppermute | solution.py:676
  78.5 0.0 collective-permute-done.7.refs_7_
  78.5 0.0 collective-permute-done.8.refs_8_
  78.6 0.7 copy-done.2
  79.3 9.6 %shard_map.62 = (f32[96,16,256]{2,1,0:T(8,128)S(1)}, f32[96,16,256]{2,1,0:T(8,128)S(1)}, f32[24,16,256]{2,1,0:T(8,128)S(1)}, f32[16,128]{1,0:T(8,128)S(1)}, f32[...) custom-call(s32[2]{0:T(128)S(1)} %copy-done.5, f32[64,4,128]{2,1,0:T(4,128)} %all-to-all-done.got_ref, ...), custom_call_target="tpu_custom_call" | custom-call | tf_op jit(solution)/shard_map/pallas_call | solution.py:605
  88.9 0.0 collective-permute-done.9.refs_8_
  88.9 12.6 %all_to_all.25 = f32[64,1,128]{2,1,0:T(1,128)S(1)} all-to-all(f32[64,1,128]{2,1,0:T(1,128)S(1)} %bitcast.29), channel_id=1, replica_groups=mesh['gx'=16,'gy'=4,'tx'=4] {'gx','gy'}, dimensions={0} | all-to-all | bytes 65536 | tf_op jit(solution)/shard_map/all_to_all | solution.py:620
  101.5 2.4 %collective-permute-start.12 = (bf16[96,8,128]{2,1,0:T(8,128)(2,1)S(1)}, bf16[96,8,128]{2,1,0:T(8,128)(2,1)S(1)}, u32[]{:S(2)}, u32[]{:S(2)}) collective-permute-start(bf16[96,8,128]{2,1,0:T(8,128)(2,1)S(1)} %bitcast.33), channel_id=1, source_target_pairs={{1,0},{2,1},{3,2},{0,3},{5,4},{6,5},{7,6},{4,7},{9,8},{10,9},{11,1... | collective-permute-start | bytes 589832 | tf_op jit(solution)/shard_map/ppermute | solution.py:695
  103.9 1.2 collective-permute-start.11
  105.1 6.9 %shard_map.63 = (f32[96,16,256]{2,1,0:T(8,128)S(1)}, f32[96,16,256]{2,1,0:T(8,128)S(1)}, f32[16,128]{1,0:T(8,128)S(1)}, f32[64,128]{1,0:T(8,128)S(1)}) custom-call(f32[64,128]{1,0:T(8,128)S(1)} %bitcast.26, bf16[198,8,128]{2,1,0:T(8,128)(2,1)S(1)} %pad_maximum_fusion.block_ref.refs_0_, bf16[198,8,128]{2,1,0:T(8,128)(2,1)S(1)} %collective-permute-done.refs_1_, ...), custom_call_target="tpu_custom_call" | custom-call | tf_op jit(solution)/shard_map/pallas_call | solution.py:605
  111.9 2.5 %collective-permute-done.12.refs_11_ = bf16[96,8,128]{2,1,0:T(8,128)(2,1)S(1)} collective-permute-done((bf16[96,8,128]{2,1,0:T(8,128)(2,1)S(1)}, bf16[96,8,128]{2,1,0:T(8,128)(2,1)S(1)}, u32[]{:S(2)}, u32[]{:S(2)}) %collective-permute-start.12) | collective-permute-done | bytes 196640 | tf_op jit(solution)/shard_map/ppermute | solution.py:695
  114.5 1.7 collective-permute-done.11.refs_9_
  116.2 12.8 %all_to_all.26 = f32[64,1,128]{2,1,0:T(1,128)S(1)} all-to-all(f32[64,1,128]{2,1,0:T(1,128)S(1)} %bitcast.30), channel_id=1, replica_groups=mesh['gx'=16,'gy'=4,'tx'=4] {'gx','gy'}, dimensions={0} | all-to-all | bytes 65536 | tf_op jit(solution)/shard_map/all_to_all | solution.py:620
  129.0 0.9 collective-permute-start.13
  129.9 2.7 %collective-permute-start.14 = (bf16[96,8,128]{2,1,0:T(8,128)(2,1)S(1)}, bf16[96,8,128]{2,1,0:T(8,128)(2,1)S(1)}, u32[]{:S(2)}, u32[]{:S(2)}) collective-permute-start(bf16[96,8,128]{2,1,0:T(8,128)(2,1)S(1)} %collective-permute-done.12.refs_11_), channel_id=1, source_target_pairs={{1,0},{2,1},{3,2},{0,3},{5,4},{6,5},{7,6},{4,7},{9,8},{10,9},{11,1... | collective-permute-start | bytes 589832 | tf_op jit(solution)/shard_map/ppermute | solution.py:699
  132.6 7.6 %shard_map.64 = (f32[96,16,256]{2,1,0:T(8,128)S(1)}, f32[96,16,256]{2,1,0:T(8,128)S(1)}, f32[96,8,128]{2,1,0:T(8,128)S(1)}, f32[16,128]{1,0:T(8,128)S(1)}, f32[64,128]{1,0:T(8,128)S(1)}) custom-call(f32[64,128]{1,0:T(8,128)S(1)} %bitcast.25, bf16[198,8,128]{2,1,0:T(8,128)(2,1)S(1)} %pad_maximum_fusion.block_ref.refs_0_, ...), custom_call_target="tpu_custom_call" | custom-call | tf_op jit(solution)/shard_map/pallas_call | solution.py:605
  140.2 1.5 collective-permute-done.13.refs_12_
  141.7 1.2 collective-permute-done.14.refs_13_
  142.9 11.9 %all_to_all.27 = f32[64,1,128]{2,1,0:T(1,128)S(1)} all-to-all(f32[64,1,128]{2,1,0:T(1,128)S(1)} %bitcast.28), channel_id=1, replica_groups=mesh['gx'=16,'gy'=4,'tx'=4] {'gx','gy'}, dimensions={0} | all-to-all | bytes 65536 | tf_op jit(solution)/shard_map/all_to_all | solution.py:620
  154.8 6.9 %shard_map.65 = (f32[96,16,256]{2,1,0:T(8,128)S(1)}, f32[96,16,256]{2,1,0:T(8,128)S(1)}, f32[16,128]{1,0:T(8,128)S(1)}, f32[64,128]{1,0:T(8,128)S(1)}) custom-call(f32[64,128]{1,0:T(8,128)S(1)} %bitcast.27, bf16[198,8,128]{2,1,0:T(8,128)(2,1)S(1)} %pad_maximum_fusion.block_ref.refs_0_, bf16[198,8,128]{2,1,0:T(8,128)(2,1)S(1)} %collective-permute-done.refs_1_, ...), custom_call_target="tpu_custom_call" | custom-call | tf_op jit(solution)/shard_map/pallas_call | solution.py:605
  161.7 12.2 %all_to_all.28 = f32[64,1,128]{2,1,0:T(1,128)S(1)} all-to-all(f32[64,1,128]{2,1,0:T(1,128)S(1)} %bitcast.31), channel_id=1, replica_groups=mesh['gx'=16,'gy'=4,'tx'=4] {'gx','gy'}, dimensions={0} | all-to-all | bytes 65536 | tf_op jit(solution)/shard_map/all_to_all | solution.py:620
  173.9 5.1 %shard_map.66 = (f32[96,8,128]{2,1,0:T(8,128)}, f32[96,8,128]{2,1,0:T(8,128)}) custom-call(f32[64,128]{1,0:T(8,128)S(1)} %bitcast.24, bf16[198,8,128]{2,1,0:T(8,128)(2,1)S(1)} %pad_maximum_fusion.block_ref.refs_0_, bf16[198,8,128]{2,1,0:T(8,128)(2,1)S(1)} %collective-permute-done.refs_1_, bf16[198,8,128]{2,1,0:T(8,128)(2,1)S(1)} %collective-permute-done.1.refs_2_, ...), custom_call_target="tpu_custom_call" | custom-call | tf_op jit(solution)/shard_map/pallas_call | solution.py:605
  (18 shorter events, 0.1 us)
Async XLA Ops:
  1.7 21.7 %collective-permute-start.1 = (bf16[198,8,128]{2,1,0:T(8,128)(2,1)S(1)}, bf16[198,8,128]{2,1,0:T(8,128)(2,1)S(1)}, u32[]{:S(2)}, u32[]{:S(2)}) collective-permute-start(bf16[198,8,128]{2,1,0:T(8,128)(2,1)S(1)} %pad_maximum_fusion.block_ref.refs_0_), channel_id=1, source_target_pairs={{1,0},{2,1},{3,2},{0,3},{5,4},{6,5},{7,6},{4,7},{9,8},{10,9},{11,1... | collective-permute-start | bytes 1216520 | tf_op jit(solution)/shard_map/ppermute | solution.py:641
  8.9 4.6 %collective-permute-start.3 = (bf16[13,8,128]{2,1,0:T(8,128)(2,1)S(1)}, bf16[13,8,128]{2,1,0:T(8,128)(2,1)S(1)}, u32[]{:S(2)}, u32[]{:S(2)}) collective-permute-start(bf16[13,8,128]{2,1,0:T(8,128)(2,1)S(1)} %shard_map.59), channel_id=1, source_target_pairs={{0,4},{4,8},{8,12},{1,5},{5,9},{9,13},{2,6},{6,10},{10,14},{3,7},{... | collective-permute-start | bytes 79880 | tf_op jit(solution)/shard_map/ppermute | solution.py:644
  12.1 4.9 %collective-permute-start.2 = (bf16[13,8,128]{2,1,0:T(8,128)(2,1)S(1)}, bf16[13,8,128]{2,1,0:T(8,128)(2,1)S(1)}, u32[]{:S(2)}, u32[]{:S(2)}) collective-permute-start(bf16[13,8,128]{2,1,0:T(8,128)(2,1)S(1)} %shard_map.59), channel_id=1, source_target_pairs={{4,0},{8,4},{12,8},{5,1},{9,5},{13,9},{6,2},{10,6},{14,10},{7,3},{... | collective-permute-start | bytes 79880 | tf_op jit(solution)/shard_map/ppermute | solution.py:644
  13.4 16.8 %collective-permute-start = (bf16[198,8,128]{2,1,0:T(8,128)(2,1)S(1)}, bf16[198,8,128]{2,1,0:T(8,128)(2,1)S(1)}, u32[]{:S(2)}, u32[]{:S(2)}) collective-permute-start(bf16[198,8,128]{2,1,0:T(8,128)(2,1)S(1)} %pad_maximum_fusion.block_ref.refs_0_), channel_id=1, source_target_pairs={{0,1},{1,2},{2,3},{3,0},{4,5},{5,6},{6,7},{7,4},{8,9},{9,10},{10,1... | collective-permute-start | bytes 1216520 | tf_op jit(solution)/shard_map/ppermute | solution.py:640
  23.4 32.6 %copy-start.5 = (s32[2]{0:T(128)S(1)}, s32[2]{0:T(128)}, u32[]{:S(2)}) copy-start(s32[2]{0:T(128)} %src_ref.3) | copy-start | bytes 28
  23.5 18.0 %collective-permute-start.5 = (bf16[115,8,128]{2,1,0:T(8,128)(2,1)S(1)}, bf16[115,8,128]{2,1,0:T(8,128)(2,1)S(1)}, u32[]{:S(2)}, u32[]{:S(2)}) collective-permute-start(bf16[115,8,128]{2,1,0:T(8,128)(2,1)S(1)} %pad_maximum_fusion.1), channel_id=1, source_target_pairs={{1,0},{2,1},{3,2},{0,3},{5,4},{6,5},{7,6},{4,7},{9,8},{10,9},{11,1... | collective-permute-start | bytes 706568 | tf_op jit(solution)/shard_map/ppermute | solution.py:647
  30.3 11.2 %collective-permute-start.4 = (bf16[109,8,128]{2,1,0:T(8,128)(2,1)S(1)}, bf16[109,8,128]{2,1,0:T(8,128)(2,1)S(1)}, u32[]{:S(2)}, u32[]{:S(2)}) collective-permute-start(bf16[109,8,128]{2,1,0:T(8,128)(2,1)S(1)} %pad_maximum_fusion.2), channel_id=1, source_target_pairs={{0,1},{1,2},{2,3},{3,0},{4,5},{5,6},{6,7},{7,4},{8,9},{9,10},{10,1... | collective-permute-start | bytes 669704 | tf_op jit(solution)/shard_map/ppermute | solution.py:646
  30.3 11.1 %collective-permute-start.6 = (bf16[13,8,128]{2,1,0:T(8,128)(2,1)S(1)}, bf16[13,8,128]{2,1,0:T(8,128)(2,1)S(1)}, u32[]{:S(2)}, u32[]{:S(2)}) collective-permute-start(bf16[13,8,128]{2,1,0:T(8,128)(2,1)S(1)} %broadcast_select_fusion.refs_5_), channel_id=1, source_target_pairs={{0,2},{1,3},{2,0},{3,1},{4,6},{5,7},{6,4},{7,5},{8,10},{9,11},{10,... | collective-permute-start | bytes 79880 | tf_op jit(solution)/shard_map/ppermute | solution.py:648
  41.4 14.6 %copy-start.1 = (bf16[13,8,128]{2,1,0:T(8,128)(2,1)}, bf16[13,8,128]{2,1,0:T(8,128)(2,1)S(1)}, u32[]{:S(2)}) copy-start(bf16[13,8,128]{2,1,0:T(8,128)(2,1)S(1)} %collective-permute-done.6.refs_6_) | copy-start | bytes 79876
  43.4 35.1 %collective-permute-start.7 = (bf16[448,8,128]{2,1,0:T(8,128)(2,1)}, bf16[448,8,128]{2,1,0:T(8,128)(2,1)S(1)}, u32[]{:S(2)}, u32[]{:S(2)}) collective-permute-start(bf16[448,8,128]{2,1,0:T(8,128)(2,1)} %get-tuple-element.42), channel_id=1, source_target_pairs={{16,0},{32,16},{48,32},{64,48},{80,64},{96,80},{112,96},{128,112},... | collective-permute-start | bytes 2752520 | tf_op jit(solution)/shard_map/ppermute | solution.py:654
  53.0 25.6 %collective-permute-start.8 = (bf16[448,8,128]{2,1,0:T(8,128)(2,1)}, bf16[448,8,128]{2,1,0:T(8,128)(2,1)S(1)}, u32[]{:S(2)}, u32[]{:S(2)}) collective-permute-start(bf16[448,8,128]{2,1,0:T(8,128)(2,1)} %get-tuple-element.43), channel_id=1, source_target_pairs={{0,16},{16,32},{32,48},{48,64},{64,80},{80,96},{96,112},{112,128},... | collective-permute-start | bytes 2752520 | tf_op jit(solution)/shard_map/ppermute | solution.py:654
  58.8 0.7 copy-start.4
  59.4 16.7 %all-to-all-start = ((f32[64,4,128]{2,1,0:T(4,128)}), f32[64,4,128]{2,1,0:T(4,128)}, u32[]{:S(2)}, u32[]{:S(2)}) async-start(f32[64,4,128]{2,1,0:T(4,128)} %copy-done.4), calls=%async_computation | async-start | bytes 262144 | tf_op jit(solution)/shard_map/all_to_all | solution.py:620
  76.2 12.7 %collective-permute-start.10 = (bf16[96,8,128]{2,1,0:T(8,128)(2,1)}, bf16[96,8,128]{2,1,0:T(8,128)(2,1)S(1)}, u32[]{:S(2)}, u32[]{:S(2)}) collective-permute-start(bf16[96,8,128]{2,1,0:T(8,128)(2,1)} %bitcast.35), channel_id=1, source_target_pairs={{1,0},{2,1},{3,2},{0,3},{5,4},{6,5},{7,6},{4,7},{9,8},{10,9},{11,1... | collective-permute-start | bytes 589832 | tf_op jit(solution)/shard_map/ppermute | solution.py:676
  76.2 12.7 %collective-permute-start.9 = (bf16[96,8,128]{2,1,0:T(8,128)(2,1)}, bf16[96,8,128]{2,1,0:T(8,128)(2,1)S(1)}, u32[]{:S(2)}, u32[]{:S(2)}) collective-permute-start(bf16[96,8,128]{2,1,0:T(8,128)(2,1)} %bitcast.36), channel_id=1, source_target_pairs={{0,1},{1,2},{2,3},{3,0},{4,5},{5,6},{6,7},{7,4},{8,9},{9,10},{10,1... | collective-permute-start | bytes 589832 | tf_op jit(solution)/shard_map/ppermute | solution.py:676
  78.6 0.7 copy-start.2
  79.3 22.2 %copy-start.6 = (bf16[2,2,3,8,8,128]{5,4,3,2,1,0:T(8,128)(2,1)S(1)}, bf16[2,2,3,8,8,128]{5,4,3,2,1,0:T(8,128)(2,1)}, u32[]{:S(2)}) copy-start(bf16[2,2,3,8,8,128]{5,4,3,2,1,0:T(8,128)(2,1)} %get-tuple-element.80) | copy-start | bytes 589828
  79.3 25.8 %copy-start.3 = (bf16[13,8,128]{2,1,0:T(8,128)(2,1)S(1)}, bf16[13,8,128]{2,1,0:T(8,128)(2,1)}, u32[]{:S(2)}) copy-start(bf16[13,8,128]{2,1,0:T(8,128)(2,1)} %copy-done.1) | copy-start | bytes 79876
  101.5 13.0 %collective-permute-start.12 = (bf16[96,8,128]{2,1,0:T(8,128)(2,1)S(1)}, bf16[96,8,128]{2,1,0:T(8,128)(2,1)S(1)}, u32[]{:S(2)}, u32[]{:S(2)}) collective-permute-start(bf16[96,8,128]{2,1,0:T(8,128)(2,1)S(1)} %bitcast.33), channel_id=1, source_target_pairs={{1,0},{2,1},{3,2},{0,3},{5,4},{6,5},{7,6},{4,7},{9,8},{10,9},{11,1... | collective-permute-start | bytes 589832 | tf_op jit(solution)/shard_map/ppermute | solution.py:695
  103.9 12.3 %collective-permute-start.11 = (bf16[96,8,128]{2,1,0:T(8,128)(2,1)S(1)}, bf16[96,8,128]{2,1,0:T(8,128)(2,1)S(1)}, u32[]{:S(2)}, u32[]{:S(2)}) collective-permute-start(bf16[96,8,128]{2,1,0:T(8,128)(2,1)S(1)} %bitcast.34), channel_id=1, source_target_pairs={{0,1},{1,2},{2,3},{3,0},{4,5},{5,6},{6,7},{7,4},{8,9},{9,10},{10,1... | collective-permute-start | bytes 589832 | tf_op jit(solution)/shard_map/ppermute | solution.py:695
  129.0 12.7 %collective-permute-start.13 = (bf16[96,8,128]{2,1,0:T(8,128)(2,1)S(1)}, bf16[96,8,128]{2,1,0:T(8,128)(2,1)S(1)}, u32[]{:S(2)}, u32[]{:S(2)}) collective-permute-start(bf16[96,8,128]{2,1,0:T(8,128)(2,1)S(1)} %collective-permute-done.9.refs_8_), channel_id=1, source_target_pairs={{0,1},{1,2},{2,3},{3,0},{4,5},{5,6},{6,7},{7,4},{8,9},{9,10},{10,1... | collective-permute-start | bytes 589832 | tf_op jit(solution)/shard_map/ppermute | solution.py:699
  129.9 12.9 %collective-permute-start.14 = (bf16[96,8,128]{2,1,0:T(8,128)(2,1)S(1)}, bf16[96,8,128]{2,1,0:T(8,128)(2,1)S(1)}, u32[]{:S(2)}, u32[]{:S(2)}) collective-permute-start(bf16[96,8,128]{2,1,0:T(8,128)(2,1)S(1)} %collective-permute-done.12.refs_11_), channel_id=1, source_target_pairs={{1,0},{2,1},{3,2},{0,3},{5,4},{6,5},{7,6},{4,7},{9,8},{10,9},{11,1... | collective-permute-start | bytes 589832 | tf_op jit(solution)/shard_map/ppermute | solution.py:699
  154.8 19.0 %copy-start = (bf16[4,2,3,8,8,128]{5,4,3,2,1,0:T(8,128)(2,1)S(1)}, bf16[4,2,3,8,8,128]{5,4,3,2,1,0:T(8,128)(2,1)}, u32[]{:S(2)}) copy-start(bf16[4,2,3,8,8,128]{5,4,3,2,1,0:T(8,128)(2,1)} %param.5) | copy-start | bytes 1179652

commit v5 on v4

--- a/solution.py
+++ b/solution.py
@@ -109,16 +109,14 @@
             hi_ref[LOCAL * HALF + d * PACKED + tile] = piece
 
 
-def inner_all(blocks, field, sums_ref):
+def inner_all(c_ref, field, sums_ref):
     def body(j, accs):
         one, two = field(0, j), field(1, j)
         new = []
-        for d in range(LOCAL):
-            for kl in range(LOCAL):
-                vec = vector_row(blocks, d, kl, j)
-                at = 2 * (d * LOCAL + kl)
-                new.append(accs[at] + vec * one)
-                new.append(accs[at + 1] + vec * two)
+        for k in range(VECS):
+            vec = c_ref[k * ROWS + j]
+            new.append(accs[2 * k] + vec * one)
+            new.append(accs[2 * k + 1] + vec * two)
         return tuple(new)
 
     zero = jnp.zeros((8, 128), F32)
@@ -188,44 +186,58 @@
     return jnp.exp(-dist / ((size_x + size_y) / 8.0))
 
 
-def combine_ext(coeffs, blocks, ln_ref, hp_ref, interior, halo_x, unpacked_ref):
+def unpack_once(blocks, ln_ref, hp_ref, c_ref, x_ref, near_ref, far_ref):
     top = iota((8, 128), 0) < 4
 
     def body(j, carry):
-        inner = [jnp.zeros((8, 128), F32)] * 2
-        straight = [jnp.zeros((8, 128), F32)] * 2
-        rolled = [jnp.zeros((8, 128), F32)] * 2
         for d in range(LOCAL):
             for kl in range(LOCAL):
                 k = d * LOCAL + kl
-                vec = vector_row(blocks, d, kl, j)
+                c_ref[k * ROWS + j] = vector_row(blocks, d, kl, j)
                 at = d * HALF + (kl % 2) * ROWS + j
                 after, before = ln_ref[at].astype(F32), hp_ref[at].astype(F32)
-                outer = straight if kl < 2 else rolled
-                edge = jnp.where(top, after, before) if kl < 2 else jnp.where(top, before, after)
-                for s in range(2):
-                    inner[s] = inner[s] + coeffs[s][k] * vec
-                    outer[s] = outer[s] + coeffs[s][k] * edge
+                if kl < 2:
+                    x_ref[k * ROWS + j] = jnp.where(top, after, before)
+                else:
+                    x_ref[k * ROWS + j] = pltpu.roll(jnp.where(top, before, after), 4, 0)
+        return carry
+
+    lax.fori_loop(0, ROWS, body, 0)
+    from_next = iota((8, 128), 1) % 8 < 4
+    for d in range(LOCAL):
+        for t in range(PACKED - 1):
+            at = LOCAL * HALF + d * PACKED + t
+            near_ref[d * 12 + t] = side_tile(blocks, d, t).astype(F32)
+            far_ref[d * 12 + t] = jnp.where(
+                from_next, ln_ref[at].astype(F32), hp_ref[at].astype(F32)
+            )
+
+
+def combine_ext(coeffs, fields, interior, halo_x, unpacked_ref):
+    c_ref, x_ref, near_ref, far_ref = fields
+
+    def body(j, carry):
+        inner = [jnp.zeros((8, 128), F32)] * 2
+        outer = [jnp.zeros((8, 128), F32)] * 2
+        for k in range(VECS):
+            vec, edge = c_ref[k * ROWS + j], x_ref[k * ROWS + j]
+            for s in range(2):
+                inner[s] = inner[s] + coeffs[s][k] * vec
+                outer[s] = outer[s] + coeffs[s][k] * edge
         for s in range(2):
             interior(s, j, inner[s])
-            halo_x(s, j, straight[s] + pltpu.roll(rolled[s], 4, 0))
+            halo_x(s, j, outer[s])
         return carry
 
     lax.fori_loop(0, ROWS, body, 0)
     pick = pick_matrix(F32)
-    from_next = iota((8, 128), 1) % 8 < 4
     for s in range(2):
         for tile in range(3):
             near = jnp.zeros((8, 128), F32)
             far = jnp.zeros((8, 128), F32)
-            for d in range(LOCAL):
-                for kl in range(LOCAL):
-                    k = d * LOCAL + kl
-                    t = kl * 3 + tile
-                    at = 4 * HALF + d * PACKED + t
-                    near = near + coeffs[s][k] * side_tile(blocks, d, t).astype(F32)
-                    edge = jnp.where(from_next, ln_ref[at].astype(F32), hp_ref[at].astype(F32))
-                    far = far + coeffs[s][k] * edge
+            for k in range(VECS):
+                near = near + coeffs[s][k] * near_ref[k * 3 + tile]
+                far = far + coeffs[s][k] * far_ref[k * 3 + tile]
             place = s * ROWS + tile * 16
             near = full_dot(jnp.transpose(near), pick).reshape(16, 8, 128)
             far = full_dot(jnp.transpose(far), pick).reshape(16, 8, 128)
@@ -343,7 +355,9 @@
 def begin_kernel(size_x, size_y, src_ref, got_ref, *refs):
     blocks, ln_ref, hp_ref = refs[:BLOCKS], refs[BLOCKS], refs[BLOCKS + 1]
     refs = refs[BLOCKS + 2 :]
-    r_ref, q_ref, m_ref, inv_ref, state_ref, out_ref, side_ref, sums_ref = refs
+    r_ref, q_ref, m_ref, inv_ref, state_ref, out_ref = refs[:6]
+    fields, side_ref, sums_ref = refs[6:10], refs[10], refs[11]
+    unpack_once(blocks, ln_ref, hp_ref, *fields)
     total = jnp.sum(got_ref[...], axis=0)
     inverse = invert(total[0:2])
     inv_ref[...] = inverse
@@ -361,7 +375,7 @@
         return store
 
     combine_ext(
-        coeffs, blocks, ln_ref, hp_ref,
+        coeffs, fields,
         put(slice(0, 8), slice(0, 128)), put(slice(8, 16), slice(0, 128)), side_ref,
     )
     top = iota((8, 128), 0) < 4
@@ -408,20 +422,19 @@
 
         lax.fori_loop(0, 8, body, 0)
     apply_operator(r_ref, m_ref, q_ref, mask)
-    finish_first(blocks, r_ref, q_ref, sums_ref, out_ref)
-
-
-def finish_first(blocks, r_ref, q_ref, sums_ref, out_ref):
+    finish_first(fields[0], r_ref, q_ref, sums_ref, out_ref)
+
+
+def finish_first(c_ref, r_ref, q_ref, sums_ref, out_ref):
     sums_ref[...] = jnp.zeros_like(sums_ref)
     r, q = brick(r_ref), brick(q_ref)
-    inner_all(blocks, q, sums_ref)
+    inner_all(c_ref, q, sums_ref)
     inner_pairs([(r, r), (r, q)], sums_ref, 32)
     out_ref[...] = jnp.broadcast_to(row_of_sums(sums_ref), out_ref.shape)
 
 
 def first_kernel(size_x, size_y, got_ref, *refs):
-    blocks, ln_ref, hp_ref = refs[:BLOCKS], refs[BLOCKS], refs[BLOCKS + 1]
-    refs = refs[BLOCKS + 2 :]
+    fields, refs = refs[:4], refs[4:]
     r_ref, q_ref, m_ref, inv_ref, old_ref = refs[:5]
     u_ref, a_ref, state_ref, out_ref, side_ref, sums_ref = refs[5:]
     row = jnp.sum(got_ref[...], axis=0, keepdims=True)
@@ -452,7 +465,7 @@
         return store
 
     combine_ext(
-        coeffs, blocks, ln_ref, hp_ref,
+        coeffs, fields,
         put(slice(0, 8), slice(0, 128)), put(slice(8, 16), slice(0, 128)), side_ref,
     )
     for s in range(2):
@@ -470,7 +483,7 @@
     apply_operator(u_ref, m_ref, a_ref, mask)
     sums_ref[...] = jnp.zeros_like(sums_ref)
     r, u, a = brick(r_ref), brick(u_ref), brick(a_ref)
-    inner_all(blocks, a, sums_ref)
+    inner_all(fields[0], a, sums_ref)
     inner_pairs([(u, u), (r, u), (r, a), (u, a), (a, a)], sums_ref, 32)
     out_ref[...] = jnp.broadcast_to(row_of_sums(sums_ref), out_ref.shape)
 
@@ -513,8 +526,7 @@
 
 
 def next_kernel(size_x, size_y, got_ref, *refs):
-    blocks, ln_ref, hp_ref = refs[:BLOCKS], refs[BLOCKS], refs[BLOCKS + 1]
-    refs = refs[BLOCKS + 2 :]
+    fields, refs = refs[:4], refs[4:]
     r_ref, u_ref, a_ref, m_ref, inv_ref, old_ref = refs[:6]
     new_ref, q_ref, sol_ref, state_ref, out_ref, side_ref, sums_ref = refs[6:]
     row = jnp.sum(got_ref[...], axis=0, keepdims=True)
@@ -541,7 +553,7 @@
         return store
 
     combine_ext(
-        coeffs, blocks, ln_ref, hp_ref,
+        coeffs, fields,
         put(slice(0, 8), slice(0, 128)), put(slice(8, 16), slice(0, 128)), side_ref,
     )
     for s in range(2):
@@ -560,7 +572,7 @@
 
         lax.fori_loop(0, ROWS, body, 0)
     apply_operator(new_ref, m_ref, q_ref, mask)
-    finish_first(blocks, new_ref, q_ref, sums_ref, out_ref)
+    finish_first(fields[0], new_ref, q_ref, sums_ref, out_ref)
 
 
 def basis_row(basis, d, kl, j):
@@ -571,33 +583,48 @@
     return basis[first][row].astype(F32) if kl < 2 else basis[first + 1][row - CUT].astype(F32)
 
 
-def last_kernel(got_ref, *refs):
-    blocks, basis, refs = refs[:BLOCKS], refs[BLOCKS : BLOCKS + 7], refs[BLOCKS + 7 :]
+def last_kernel(got_ref, c_ref, *refs):
+    basis, refs = refs[:7], refs[7:]
     r_ref, u_ref, a_ref, inv_ref, old_ref, sol_ref = refs[:6]
     solution_ref, residual_ref = refs[6:]
     row = jnp.sum(got_ref[...], axis=0, keepdims=True)
     state = old_ref[...]
-    for s in range(2):
-        small = close_cycle(row, inv_ref[...], state, s)
-        coeffs = [spread(small["c"][k : k + 1]) for k in range(VECS)]
-        base_coeffs = [spread(small["basis"][k : k + 1]) for k in range(VECS)]
-        scale = {name: spread(small[name]) for name in ("r", "u", "a", "sol_r", "sol_u")}
-
-        def body(j, carry, s=s, coeffs=coeffs, base_coeffs=base_coeffs, scale=scale):
-            at = s * ROWS + j
+    small = [close_cycle(row, inv_ref[...], state, s) for s in range(2)]
+    coeffs = [[spread(one["c"][k : k + 1]) for k in range(VECS)] for one in small]
+    basis_coeffs = [[spread(one["basis"][k : k + 1]) for k in range(VECS)] for one in small]
+    names = ("r", "u", "a", "sol_r", "sol_u")
+    scale = [{name: spread(one[name]) for name in names} for one in small]
+
+    def residual_body(j, carry):
+        values = []
+        for s in range(2):
             r, u, a = brick(r_ref)(s, j), brick(u_ref)(s, j), brick(a_ref)(s, j)
-            value = scale["r"] * r + scale["u"] * u + scale["a"] * a
-            field = sol_ref[at] + scale["sol_r"] * r + scale["sol_u"] * u
-            for d in range(LOCAL):
-                for kl in range(LOCAL):
-                    k = d * LOCAL + kl
-                    value = value + coeffs[k] * vector_row(blocks, d, kl, j)
-                    field = field + base_coeffs[k] * basis_row(basis, d, kl, j)
-            residual_ref[at] = value
-            solution_ref[at] = field
-            return carry
-
-        lax.fori_loop(0, ROWS, body, 0)
+            values.append(scale[s]["r"] * r + scale[s]["u"] * u + scale[s]["a"] * a)
+        for k in range(VECS):
+            vec = c_ref[k * ROWS + j]
+            for s in range(2):
+                values[s] = values[s] + coeffs[s][k] * vec
+        for s in range(2):
+            residual_ref[s * ROWS + j] = values[s]
+        return carry
+
+    def solution_body(j, carry):
+        values = []
+        for s in range(2):
+            r, u = brick(r_ref)(s, j), brick(u_ref)(s, j)
+            old = sol_ref[s * ROWS + j]
+            values.append(old + scale[s]["sol_r"] * r + scale[s]["sol_u"] * u)
+        for d in range(LOCAL):
+            for kl in range(LOCAL):
+                vec = basis_row(basis, d, kl, j)
+                for s in range(2):
+                    values[s] = values[s] + basis_coeffs[s][d * LOCAL + kl] * vec
+        for s in range(2):
+            solution_ref[s * ROWS + j] = values[s]
+        return carry
+
+    lax.fori_loop(0, ROWS, residual_body, 0)
+    lax.fori_loop(0, ROWS, solution_body, 0)
 
 
 def call(kernel, outs, args, scratch=(), smem=0):
@@ -643,9 +670,10 @@
     up, down = steps("gy")
     after, before = lax.ppermute(own, "gy", down), lax.ppermute(own, "gy", up)
     side = jnp.where(lax.broadcasted_iota(jnp.int32, own.shape, 1) < 4, after, before)
+    far_side = lax.ppermute(side, "tx", [(i, (i + 2) % LOCAL) for i in range(LOCAL)])
+    far_side, one, three = tied(far_side, one, three)
     far_low = lax.ppermute(jnp.concatenate([one[:CUT], side]), "tx", right)
     far_high = lax.ppermute(jnp.concatenate([three[CUT:], side]), "tx", left)
-    far_side = lax.ppermute(side, "tx", [(i, (i + 2) % LOCAL) for i in range(LOCAL)])
     blocks = (block, one, three, far_low, far_high, side, far_side)
 
     half = shape(LOCAL * (HALF + PACKED), 8, 128, dtype=BF16)
@@ -666,7 +694,6 @@
     wide = shape(2 * ROWS, 16, 256)
     line = shape(peers, 128)
     small = shape(VECS, 128)
-    static = (*blocks, ln, hp)
     own_basis = basis.reshape(LOCAL * ROWS, 8, 128)
 
     def total(value):
@@ -674,10 +701,11 @@
 
     got, piece = tied(got, own_basis[:CUT])
     one_low, three_low = lax.ppermute(piece, "tx", right), lax.ppermute(piece, "tx", left)
-    r, q, m, inverse, state, sent = call(
+    whole, tiles = shape(VECS * ROWS, 8, 128), shape(3 * VECS, 8, 128)
+    r, q, m, inverse, state, sent, *fields = call(
         functools.partial(begin_kernel, size_x, size_y),
-        (wide, wide, shape(24, 16, 256), small, small, line),
-        (src_cell, got, *static),
+        (wide, wide, shape(24, 16, 256), small, small, line, whole, whole, tiles, tiles),
+        (src_cell, got, *blocks, ln, hp),
         (side_scratch, sums),
         smem=1,
     )
@@ -686,7 +714,7 @@
         return call(
             functools.partial(first_kernel, size_x, size_y),
             (wide, wide, small, line),
-            (got, *static, r, q, m, inverse, state),
+            (got, *fields, r, q, m, inverse, state),
             (side_scratch, sums),
         )
 
@@ -700,7 +728,7 @@
     r, q, field, state, sent = call(
         functools.partial(next_kernel, size_x, size_y),
         (wide, wide, shape(2 * ROWS, 8, 128), small, line),
-        (got, *static, r, u, a, m, inverse, state),
+        (got, *fields, r, u, a, m, inverse, state),
         (side_scratch, sums),
     )
     sent, two_low, two_high = tied(sent, two_low, two_high)
@@ -710,7 +738,7 @@
     field, residual = call(
         last_kernel,
         (narrow, narrow),
-        (total(sent), *blocks, *bases, r, u, a, inverse, state, field),
+        (total(sent), fields[0], *bases, r, u, a, inverse, state, field),
     )
     full = (2, 2, 3, 8, 8, 128)
     return field.reshape(full), residual.reshape(full)

time: 180 us -> 173 us (0.961)
  starting transfers between devices: 50.8 us -> 45 us
  local copies, waits for them, and re-layouts: 3.23 us -> 0.75 us
  blocking collectives: 49.5 us -> 51.9 us
    ppermute x1, waiting for transfers between devices: 0.01 us -> 13.2 us  [on_device(): far_low = lax.ppermute(jnp.concatenate([one[:CUT], side]), 'tx', right)]
    ppermute x1, waiting for transfers between devices: 6.3 us -> 0.01 us  [on_device(): three = lax.ppermute(block, 'tx', left)]
    ppermute x2, starting transfers between devices: 12.6 us -> 6.5 us  [on_device(): ln, hp = (lax.ppermute(low, 'gx', down), lax.ppermute(high, 'gx', up))]
    ppermute x1, waiting for transfers between devices: 8.99 us -> 3.71 us  [on_device(): lax.ppermute(side, 'tx', [(i, (i + 2) % LOCAL) for i in range(LOCAL)])]
    all_to_all x4, blocking collectives: 49.5 us -> 51.9 us  [exchange(): return lax.all_to_all(value, ('gx', 'gy'), 0, 0)]
  transfers between devices with their start and end apart: 16 -> 16, of which waited for: 8 -> 6; matrix products, arithmetic and copies ran while one was open for 1% -> 0% of each run, Pallas kernels for 15% -> 16%
where the time goes in v5:
time: 173 us
  blocking collectives  51.9 us (30%)
  starting transfers between devices  45 us (26%)
  Pallas kernels  39.8 us (23%)
  waiting for transfers between devices  33.4 us (19%)
    all_to_all x4, blocking collectives, exchange(): return lax.all_to_all(value, ('gx', 'gy'), 0, 0)  51.9 us
    pallas_call x8, Pallas kernels, call(): pl.pallas_call(kernel, out_shape=outs, in_specs=[pl.BlockSpec(memory_spac...  39.8 us
    ppermute x1, waiting for transfers between devices, on_device(): far_low = lax.ppermute(jnp.concatenate([one[:CUT], side]), 'tx', right)  13.2 us
    all_to_all x1, starting transfers between devices, exchange(): return lax.all_to_all(value, ('gx', 'gy'), 0, 0)  8.65 us
    all_to_all x1, waiting for transfers between devices, exchange(): return lax.all_to_all(value, ('gx', 'gy'), 0, 0)  7.84 us
    ppermute x1, starting transfers between devices, on_device(): three = lax.ppermute(block, 'tx', left)  6.93 us
    ppermute x1, starting transfers between devices, on_device(): far_high = lax.ppermute(jnp.concatenate([three[CUT:], side]), 'tx', left)  6.71 us
    ppermute x2, starting transfers between devices, on_device(): ln, hp = (lax.ppermute(low, 'gx', down), lax.ppermute(high, 'gx', up))  6.5 us
  transfers between devices with their start and end apart: 16, of which 6 were waited for; matrix products, arithmetic and copies ran while one was open for 0% of the time, Pallas kernels for 16%

profile of v5, /device:TPU:1, one launch (start us, length us, event | category | flops | bytes accessed | tf_op | source)
XLA Modules:
  0.0 172.7 jit_solution(15356886769485364967)
XLA Ops:
  0.6 1.1 pad_maximum_fusion.block_ref.refs_0_
  1.7 6.9 %collective-permute-start.4 = (bf16[198,8,128]{2,1,0:T(8,128)(2,1)S(1)}, bf16[198,8,128]{2,1,0:T(8,128)(2,1)S(1)}, u32[]{:S(2)}, u32[]{:S(2)}) collective-permute-start(bf16[198,8,128]{2,1,0:T(8,128)(2,1)S(1)} %pad_maximum_fusion.block_ref.refs_0_), channel_id=1, source_target_pairs={{1,0},{2,1},{3,2},{0,3},{5,4},{6,5},{7,6},{4,7},{9,8},{10,9},{11,1... | collective-permute-start | bytes 1216520 | tf_op jit(solution)/shard_map/ppermute | solution.py:668
  8.6 0.0 collective-permute-start.3
  8.6 0.3 shard_map.59
  8.9 3.2 %collective-permute-start.1 = (bf16[13,8,128]{2,1,0:T(8,128)(2,1)S(1)}, bf16[13,8,128]{2,1,0:T(8,128)(2,1)S(1)}, u32[]{:S(2)}, u32[]{:S(2)}) collective-permute-start(bf16[13,8,128]{2,1,0:T(8,128)(2,1)S(1)} %shard_map.59), channel_id=1, source_target_pairs={{0,4},{4,8},{8,12},{1,5},{5,9},{9,13},{2,6},{6,10},{10,14},{3,7},{... | collective-permute-start | bytes 79880 | tf_op jit(solution)/shard_map/ppermute | solution.py:671
  12.1 1.3 collective-permute-start
  13.5 0.0 collective-permute-done.1
  13.5 3.6 %collective-permute-done = bf16[13,8,128]{2,1,0:T(8,128)(2,1)S(1)} collective-permute-done((bf16[13,8,128]{2,1,0:T(8,128)(2,1)S(1)}, bf16[13,8,128]{2,1,0:T(8,128)(2,1)S(1)}, u32[]{:S(2)}, u32[]{:S(2)}) %collective-permute-start) | collective-permute-done | bytes 26656 | tf_op jit(solution)/shard_map/ppermute | solution.py:671
  17.0 0.1 broadcast_select_fusion.refs_5_
  17.1 3.3 %collective-permute-start.2 = (bf16[13,8,128]{2,1,0:T(8,128)(2,1)S(1)}, bf16[13,8,128]{2,1,0:T(8,128)(2,1)S(1)}, u32[]{:S(2)}, u32[]{:S(2)}) collective-permute-start(bf16[13,8,128]{2,1,0:T(8,128)(2,1)S(1)} %broadcast_select_fusion.refs_5_), channel_id=1, source_target_pairs={{0,2},{1,3},{2,0},{3,1},{4,6},{5,7},{6,4},{7,5},{8,10},{9,11},{10,... | collective-permute-start | bytes 79880 | tf_op jit(solution)/shard_map/ppermute | solution.py:673
  20.4 3.7 %collective-permute-done.2.refs_6_ = bf16[13,8,128]{2,1,0:T(8,128)(2,1)S(1)} collective-permute-done((bf16[13,8,128]{2,1,0:T(8,128)(2,1)S(1)}, bf16[13,8,128]{2,1,0:T(8,128)(2,1)S(1)}, u32[]{:S(2)}, u32[]{:S(2)}) %collective-permute-start.2) | collective-permute-done | bytes 26656 | tf_op jit(solution)/shard_map/ppermute | solution.py:673
  24.1 0.0 collective-permute-done.4.refs_2_
  24.1 0.0 collective-permute-done.3.refs_1_
  24.1 0.0 copy-start.1
  24.2 6.7 %collective-permute-start.6 = (bf16[115,8,128]{2,1,0:T(8,128)(2,1)S(1)}, bf16[115,8,128]{2,1,0:T(8,128)(2,1)S(1)}, u32[]{:S(2)}, u32[]{:S(2)}) collective-permute-start(bf16[115,8,128]{2,1,0:T(8,128)(2,1)S(1)} %pad_maximum_fusion.1), channel_id=1, source_target_pairs={{1,0},{2,1},{3,2},{0,3},{5,4},{6,5},{7,6},{4,7},{9,8},{10,9},{11,1... | collective-permute-start | bytes 706568 | tf_op jit(solution)/shard_map/ppermute | solution.py:676
  30.9 0.0 copy-start
  30.9 0.1 collective-permute-start.5
  31.0 13.2 %collective-permute-done.5.refs_3_ = bf16[109,8,128]{2,1,0:T(8,128)(2,1)S(1)} collective-permute-done((bf16[109,8,128]{2,1,0:T(8,128)(2,1)S(1)}, bf16[109,8,128]{2,1,0:T(8,128)(2,1)S(1)}, u32[]{:S(2)}, u32[]{:S(2)}) %collective-permute-start.5) | collective-permute-done | bytes 223264 | tf_op jit(solution)/shard_map/ppermute | solution.py:675
  44.3 0.0 collective-permute-done.6.refs_4_
  44.3 2.0 %shard_map.61 = (bf16[448,8,128]{2,1,0:T(8,128)(2,1)}, bf16[448,8,128]{2,1,0:T(8,128)(2,1)}) custom-call(bf16[198,8,128]{2,1,0:T(8,128)(2,1)S(1)} %pad_maximum_fusion.block_ref.refs_0_, bf16[198,8,128]{2,1,0:T(8,128)(2,1)S(1)} %collective-permute-done.3.refs_1_, bf16[198,8,128]{2,1,0:T(8,128)(2,1)S(1)} %collective-permute-done.4.refs_2_, ...), custom_call_target="tpu_custom_call" | custom-call | tf_op jit(solution)/shard_map/pallas_call | solution.py:632
  46.2 3.5 %collective-permute-start.7 = (bf16[448,8,128]{2,1,0:T(8,128)(2,1)}, bf16[448,8,128]{2,1,0:T(8,128)(2,1)S(1)}, u32[]{:S(2)}, u32[]{:S(2)}) collective-permute-start(bf16[448,8,128]{2,1,0:T(8,128)(2,1)} %get-tuple-element.52), channel_id=1, source_target_pairs={{16,0},{32,16},{48,32},{64,48},{80,64},{96,80},{112,96},{128,112},... | collective-permute-start | bytes 2752520 | tf_op jit(solution)/shard_map/ppermute | solution.py:682
  49.7 3.0 %collective-permute-start.8 = (bf16[448,8,128]{2,1,0:T(8,128)(2,1)}, bf16[448,8,128]{2,1,0:T(8,128)(2,1)}, u32[]{:S(2)}, u32[]{:S(2)}) collective-permute-start(bf16[448,8,128]{2,1,0:T(8,128)(2,1)} %get-tuple-element.53), channel_id=1, source_target_pairs={{0,16},{16,32},{32,48},{48,64},{64,80},{80,96},{96,112},{112,128},... | collective-permute-start | bytes 2752520 | tf_op jit(solution)/shard_map/ppermute | solution.py:682
  52.8 3.4 %shard_map.60 = f32[64,4,128]{2,1,0:T(4,128)} custom-call(s32[2]{0:T(128)S(1)} %copy-done.1, bf16[198,8,128]{2,1,0:T(8,128)(2,1)S(1)} %pad_maximum_fusion.block_ref.refs_0_, bf16[198,8,128]{2,1,0:T(8,128)(2,1)S(1)} %collective-permute-done.3.refs_1_, bf16[198,8,128]{2,1,0:T(8,128)(2,1)S(1)} %collective-permute-done.4.refs_2_, ...), custom_call_target="tpu_custom_call" | custom-call | tf_op jit(solution)/shard_map/pallas_call | solution.py:632
  56.2 8.6 %all-to-all-start = ((f32[64,4,128]{2,1,0:T(4,128)}), f32[64,4,128]{2,1,0:T(4,128)S(1)}, u32[]{:S(2)}, u32[]{:S(2)}) async-start(f32[64,4,128]{2,1,0:T(4,128)} %shard_map.60), calls=%async_computation | async-start | bytes 262144 | tf_op jit(solution)/shard_map/all_to_all | solution.py:647
  64.9 0.7 fusion
  65.6 7.8 %all-to-all-done.got_ref = f32[64,4,128]{2,1,0:T(4,128)S(1)} async-done(((f32[64,4,128]{2,1,0:T(4,128)}), f32[64,4,128]{2,1,0:T(4,128)S(1)}, u32[]{:S(2)}, u32[]{:S(2)}) %all-to-all-start) | async-done | bytes 131104 | tf_op jit(solution)/shard_map/all_to_all | solution.py:647
  73.4 0.6 collective-permute-start.10
  74.0 1.7 %collective-permute-start.9 = (bf16[96,8,128]{2,1,0:T(8,128)(2,1)}, bf16[96,8,128]{2,1,0:T(8,128)(2,1)S(1)}, u32[]{:S(2)}, u32[]{:S(2)}) collective-permute-start(bf16[96,8,128]{2,1,0:T(8,128)(2,1)} %bitcast.36), channel_id=1, source_target_pairs={{0,1},{1,2},{2,3},{3,0},{4,5},{5,6},{6,7},{7,4},{8,9},{9,10},{10,1... | collective-permute-start | bytes 589832 | tf_op jit(solution)/shard_map/ppermute | solution.py:703
  75.8 0.0 collective-permute-done.7.refs_7_
  75.8 0.0 collective-permute-done.8.refs_8_
  75.8 10.1 %shard_map.62 = (f32[96,16,256]{2,1,0:T(8,128)S(1)}, f32[96,16,256]{2,1,0:T(8,128)S(1)}, f32[24,16,256]{2,1,0:T(8,128)S(1)}, f32[16,128]{1,0:T(8,128)S(1)}, f32[...) custom-call(s32[2]{0:T(128)S(1)} %copy-done.1, ...), custom_call_target="tpu_custom_call" | custom-call | tf_op jit(solution)/shard_map/pallas_call | solution.py:632
  85.9 0.0 collective-permute-done.10.refs_3_
  85.9 0.0 collective-permute-done.9.refs_1_
  85.9 13.3 %all_to_all.25 = f32[64,1,128]{2,1,0:T(1,128)S(1)} all-to-all(f32[64,1,128]{2,1,0:T(1,128)S(1)} %bitcast.28), channel_id=1, replica_groups=mesh['gx'=16,'gy'=4,'tx'=4] {'gx','gy'}, dimensions={0} | all-to-all | bytes 65536 | tf_op jit(solution)/shard_map/all_to_all | solution.py:647
  99.3 1.1 collective-permute-start.12
  100.4 1.3 collective-permute-start.11
  101.6 6.4 %shard_map.63 = (f32[96,16,256]{2,1,0:T(8,128)S(1)}, f32[96,16,256]{2,1,0:T(8,128)S(1)}, f32[16,128]{1,0:T(8,128)S(1)}, f32[64,128]{1,0:T(8,128)S(1)}) custom-call(f32[64,128]{1,0:T(8,128)S(1)} %bitcast.26, f32[768,8,128]{2,1,0:T(8,128)S(1)} %get-tuple-element.58.refs_0_.c_ref, f32[768,8,128]{2,1,0:T(8,128)S(1)} %get-tuple-element.59.refs_1_, ...), custom_call_target="tpu_custom_call" | custom-call | tf_op jit(solution)/shard_map/pallas_call | solution.py:632
  108.0 3.0 %collective-permute-done.12.refs_4_ = bf16[96,8,128]{2,1,0:T(8,128)(2,1)S(1)} collective-permute-done((bf16[96,8,128]{2,1,0:T(8,128)(2,1)S(1)}, bf16[96,8,128]{2,1,0:T(8,128)(2,1)S(1)}, u32[]{:S(2)}, u32[]{:S(2)}) %collective-permute-start.12) | collective-permute-done | bytes 196640 | tf_op jit(solution)/shard_map/ppermute | solution.py:723
  111.0 0.0 collective-permute-done.11.refs_2_
  111.0 14.2 %all_to_all.26 = f32[64,1,128]{2,1,0:T(1,128)S(1)} all-to-all(f32[64,1,128]{2,1,0:T(1,128)S(1)} %bitcast.30), channel_id=1, replica_groups=mesh['gx'=16,'gy'=4,'tx'=4] {'gx','gy'}, dimensions={0} | all-to-all | bytes 65536 | tf_op jit(solution)/shard_map/all_to_all | solution.py:647
  125.2 0.3 collective-permute-start.13
  125.5 3.3 %collective-permute-start.14 = (bf16[96,8,128]{2,1,0:T(8,128)(2,1)S(1)}, bf16[96,8,128]{2,1,0:T(8,128)(2,1)S(1)}, u32[]{:S(2)}, u32[]{:S(2)}) collective-permute-start(bf16[96,8,128]{2,1,0:T(8,128)(2,1)S(1)} %collective-permute-done.12.refs_4_), channel_id=1, source_target_pairs={{1,0},{2,1},{3,2},{0,3},{5,4},{6,5},{7,6},{4,7},{9,8},{10,9},{11,1... | collective-permute-start | bytes 589832 | tf_op jit(solution)/shard_map/ppermute | solution.py:727
  128.8 7.1 %shard_map.64 = (f32[96,16,256]{2,1,0:T(8,128)S(1)}, f32[96,16,256]{2,1,0:T(8,128)S(1)}, f32[96,8,128]{2,1,0:T(8,128)S(1)}, f32[16,128]{1,0:T(8,128)S(1)}, f32[64,128]{1,0:T(8,128)S(1)}) custom-call(f32[64,128]{1,0:T(8,128)S(1)} %bitcast.24, f32[768,8,128]{2,1,0:T(8,128)S(1)} %get-tuple-element.58.refs_0_.c_ref, ...), custom_call_target="tpu_custom_call" | custom-call | tf_op jit(solution)/shard_map/pallas_call | solution.py:632
  135.9 2.0 %collective-permute-done.14.refs_6_ = bf16[96,8,128]{2,1,0:T(8,128)(2,1)S(1)} collective-permute-done((bf16[96,8,128]{2,1,0:T(8,128)(2,1)S(1)}, bf16[96,8,128]{2,1,0:T(8,128)(2,1)S(1)}, u32[]{:S(2)}, u32[]{:S(2)}) %collective-permute-start.14) | collective-permute-done | bytes 196640 | tf_op jit(solution)/shard_map/ppermute | solution.py:727
  137.9 12.2 %all_to_all.27 = f32[64,1,128]{2,1,0:T(1,128)S(1)} all-to-all(f32[64,1,128]{2,1,0:T(1,128)S(1)} %bitcast.29), channel_id=1, replica_groups=mesh['gx'=16,'gy'=4,'tx'=4] {'gx','gy'}, dimensions={0} | all-to-all | bytes 65536 | tf_op jit(solution)/shard_map/all_to_all | solution.py:647
  150.1 6.4 %shard_map.65 = (f32[96,16,256]{2,1,0:T(8,128)S(1)}, f32[96,16,256]{2,1,0:T(8,128)S(1)}, f32[16,128]{1,0:T(8,128)S(1)}, f32[64,128]{1,0:T(8,128)S(1)}) custom-call(f32[64,128]{1,0:T(8,128)S(1)} %bitcast.27, f32[768,8,128]{2,1,0:T(8,128)S(1)} %get-tuple-element.58.refs_0_.c_ref, f32[768,8,128]{2,1,0:T(8,128)S(1)} %get-tuple-element.59.refs_1_, ...), custom_call_target="tpu_custom_call" | custom-call | tf_op jit(solution)/shard_map/pallas_call | solution.py:632
  156.4 12.2 %all_to_all.28 = f32[64,1,128]{2,1,0:T(1,128)S(1)} all-to-all(f32[64,1,128]{2,1,0:T(1,128)S(1)} %bitcast.31), channel_id=1, replica_groups=mesh['gx'=16,'gy'=4,'tx'=4] {'gx','gy'}, dimensions={0} | all-to-all | bytes 65536 | tf_op jit(solution)/shard_map/all_to_all | solution.py:647
  168.6 4.1 %shard_map.66 = (f32[96,8,128]{2,1,0:T(8,128)}, f32[96,8,128]{2,1,0:T(8,128)}) custom-call(f32[64,128]{1,0:T(8,128)S(1)} %bitcast.25, f32[768,8,128]{2,1,0:T(8,128)S(1)} %get-tuple-element.58.refs_0_.c_ref, bf16[192,8,128]{2,1,0:T(8,128)(2,1)S(1)} %bitcast.23, bf16[96,8,128]{2,1,0:T(8,128)(2,1)S(1)} %collective-permute-done.9.refs_1_, ...), custom_call_target="tpu_custom_call" | custom-call | tf_op jit(solution)/shard_map/pallas_call | solution.py:632
  (8 shorter events, 0.1 us)
Async XLA Ops:
  1.7 22.4 %collective-permute-start.4 = (bf16[198,8,128]{2,1,0:T(8,128)(2,1)S(1)}, bf16[198,8,128]{2,1,0:T(8,128)(2,1)S(1)}, u32[]{:S(2)}, u32[]{:S(2)}) collective-permute-start(bf16[198,8,128]{2,1,0:T(8,128)(2,1)S(1)} %pad_maximum_fusion.block_ref.refs_0_), channel_id=1, source_target_pairs={{1,0},{2,1},{3,2},{0,3},{5,4},{6,5},{7,6},{4,7},{9,8},{10,9},{11,1... | collective-permute-start | bytes 1216520 | tf_op jit(solution)/shard_map/ppermute | solution.py:668
  8.6 15.5 %collective-permute-start.3 = (bf16[198,8,128]{2,1,0:T(8,128)(2,1)S(1)}, bf16[198,8,128]{2,1,0:T(8,128)(2,1)S(1)}, u32[]{:S(2)}, u32[]{:S(2)}) collective-permute-start(bf16[198,8,128]{2,1,0:T(8,128)(2,1)S(1)} %pad_maximum_fusion.block_ref.refs_0_), channel_id=1, source_target_pairs={{0,1},{1,2},{2,3},{3,0},{4,5},{5,6},{6,7},{7,4},{8,9},{9,10},{10,1... | collective-permute-start | bytes 1216520 | tf_op jit(solution)/shard_map/ppermute | solution.py:667
  8.9 4.5 %collective-permute-start.1 = (bf16[13,8,128]{2,1,0:T(8,128)(2,1)S(1)}, bf16[13,8,128]{2,1,0:T(8,128)(2,1)S(1)}, u32[]{:S(2)}, u32[]{:S(2)}) collective-permute-start(bf16[13,8,128]{2,1,0:T(8,128)(2,1)S(1)} %shard_map.59), channel_id=1, source_target_pairs={{0,4},{4,8},{8,12},{1,5},{5,9},{9,13},{2,6},{6,10},{10,14},{3,7},{... | collective-permute-start | bytes 79880 | tf_op jit(solution)/shard_map/ppermute | solution.py:671
  12.1 4.9 %collective-permute-start = (bf16[13,8,128]{2,1,0:T(8,128)(2,1)S(1)}, bf16[13,8,128]{2,1,0:T(8,128)(2,1)S(1)}, u32[]{:S(2)}, u32[]{:S(2)}) collective-permute-start(bf16[13,8,128]{2,1,0:T(8,128)(2,1)S(1)} %shard_map.59), channel_id=1, source_target_pairs={{4,0},{8,4},{12,8},{5,1},{9,5},{13,9},{6,2},{10,6},{14,10},{7,3},{... | collective-permute-start | bytes 79880 | tf_op jit(solution)/shard_map/ppermute | solution.py:671
  17.1 7.0 %collective-permute-start.2 = (bf16[13,8,128]{2,1,0:T(8,128)(2,1)S(1)}, bf16[13,8,128]{2,1,0:T(8,128)(2,1)S(1)}, u32[]{:S(2)}, u32[]{:S(2)}) collective-permute-start(bf16[13,8,128]{2,1,0:T(8,128)(2,1)S(1)} %broadcast_select_fusion.refs_5_), channel_id=1, source_target_pairs={{0,2},{1,3},{2,0},{3,1},{4,6},{5,7},{6,4},{7,5},{8,10},{9,11},{10,... | collective-permute-start | bytes 79880 | tf_op jit(solution)/shard_map/ppermute | solution.py:673
  24.1 28.6 %copy-start.1 = (s32[2]{0:T(128)S(1)}, s32[2]{0:T(128)}, u32[]{:S(2)}) copy-start(s32[2]{0:T(128)} %src_ref.3) | copy-start | bytes 28
  24.2 20.1 %collective-permute-start.6 = (bf16[115,8,128]{2,1,0:T(8,128)(2,1)S(1)}, bf16[115,8,128]{2,1,0:T(8,128)(2,1)S(1)}, u32[]{:S(2)}, u32[]{:S(2)}) collective-permute-start(bf16[115,8,128]{2,1,0:T(8,128)(2,1)S(1)} %pad_maximum_fusion.1), channel_id=1, source_target_pairs={{1,0},{2,1},{3,2},{0,3},{5,4},{6,5},{7,6},{4,7},{9,8},{10,9},{11,1... | collective-permute-start | bytes 706568 | tf_op jit(solution)/shard_map/ppermute | solution.py:676
  30.9 33.9 %copy-start = (bf16[4,2,3,8,8,128]{5,4,3,2,1,0:T(8,128)(2,1)S(1)}, bf16[4,2,3,8,8,128]{5,4,3,2,1,0:T(8,128)(2,1)}, u32[]{:S(2)}) copy-start(bf16[4,2,3,8,8,128]{5,4,3,2,1,0:T(8,128)(2,1)} %param.5) | copy-start | bytes 1179652
  30.9 13.3 %collective-permute-start.5 = (bf16[109,8,128]{2,1,0:T(8,128)(2,1)S(1)}, bf16[109,8,128]{2,1,0:T(8,128)(2,1)S(1)}, u32[]{:S(2)}, u32[]{:S(2)}) collective-permute-start(bf16[109,8,128]{2,1,0:T(8,128)(2,1)S(1)} %pad_maximum_fusion.2), channel_id=1, source_target_pairs={{0,1},{1,2},{2,3},{3,0},{4,5},{5,6},{6,7},{7,4},{8,9},{9,10},{10,1... | collective-permute-start | bytes 669704 | tf_op jit(solution)/shard_map/ppermute | solution.py:675
  46.2 29.5 %collective-permute-start.7 = (bf16[448,8,128]{2,1,0:T(8,128)(2,1)}, bf16[448,8,128]{2,1,0:T(8,128)(2,1)S(1)}, u32[]{:S(2)}, u32[]{:S(2)}) collective-permute-start(bf16[448,8,128]{2,1,0:T(8,128)(2,1)} %get-tuple-element.52), channel_id=1, source_target_pairs={{16,0},{32,16},{48,32},{64,48},{80,64},{96,80},{112,96},{128,112},... | collective-permute-start | bytes 2752520 | tf_op jit(solution)/shard_map/ppermute | solution.py:682
  49.7 26.0 %collective-permute-start.8 = (bf16[448,8,128]{2,1,0:T(8,128)(2,1)}, bf16[448,8,128]{2,1,0:T(8,128)(2,1)}, u32[]{:S(2)}, u32[]{:S(2)}) collective-permute-start(bf16[448,8,128]{2,1,0:T(8,128)(2,1)} %get-tuple-element.53), channel_id=1, source_target_pairs={{0,16},{16,32},{32,48},{48,64},{64,80},{80,96},{96,112},{112,128},... | collective-permute-start | bytes 2752520 | tf_op jit(solution)/shard_map/ppermute | solution.py:682
  56.2 17.2 %all-to-all-start = ((f32[64,4,128]{2,1,0:T(4,128)}), f32[64,4,128]{2,1,0:T(4,128)S(1)}, u32[]{:S(2)}, u32[]{:S(2)}) async-start(f32[64,4,128]{2,1,0:T(4,128)} %shard_map.60), calls=%async_computation | async-start | bytes 262144 | tf_op jit(solution)/shard_map/all_to_all | solution.py:647
  73.4 12.5 %collective-permute-start.10 = (bf16[96,8,128]{2,1,0:T(8,128)(2,1)}, bf16[96,8,128]{2,1,0:T(8,128)(2,1)S(1)}, u32[]{:S(2)}, u32[]{:S(2)}) collective-permute-start(bf16[96,8,128]{2,1,0:T(8,128)(2,1)} %bitcast.35), channel_id=1, source_target_pairs={{1,0},{2,1},{3,2},{0,3},{5,4},{6,5},{7,6},{4,7},{9,8},{10,9},{11,1... | collective-permute-start | bytes 589832 | tf_op jit(solution)/shard_map/ppermute | solution.py:703
  74.0 11.9 %collective-permute-start.9 = (bf16[96,8,128]{2,1,0:T(8,128)(2,1)}, bf16[96,8,128]{2,1,0:T(8,128)(2,1)S(1)}, u32[]{:S(2)}, u32[]{:S(2)}) collective-permute-start(bf16[96,8,128]{2,1,0:T(8,128)(2,1)} %bitcast.36), channel_id=1, source_target_pairs={{0,1},{1,2},{2,3},{3,0},{4,5},{5,6},{6,7},{7,4},{8,9},{9,10},{10,1... | collective-permute-start | bytes 589832 | tf_op jit(solution)/shard_map/ppermute | solution.py:703
  99.3 11.7 %collective-permute-start.12 = (bf16[96,8,128]{2,1,0:T(8,128)(2,1)S(1)}, bf16[96,8,128]{2,1,0:T(8,128)(2,1)S(1)}, u32[]{:S(2)}, u32[]{:S(2)}) collective-permute-start(bf16[96,8,128]{2,1,0:T(8,128)(2,1)S(1)} %bitcast.33), channel_id=1, source_target_pairs={{1,0},{2,1},{3,2},{0,3},{5,4},{6,5},{7,6},{4,7},{9,8},{10,9},{11,1... | collective-permute-start | bytes 589832 | tf_op jit(solution)/shard_map/ppermute | solution.py:723
  100.4 10.6 %collective-permute-start.11 = (bf16[96,8,128]{2,1,0:T(8,128)(2,1)S(1)}, bf16[96,8,128]{2,1,0:T(8,128)(2,1)S(1)}, u32[]{:S(2)}, u32[]{:S(2)}) collective-permute-start(bf16[96,8,128]{2,1,0:T(8,128)(2,1)S(1)} %bitcast.34), channel_id=1, source_target_pairs={{0,1},{1,2},{2,3},{3,0},{4,5},{5,6},{6,7},{7,4},{8,9},{9,10},{10,1... | collective-permute-start | bytes 589832 | tf_op jit(solution)/shard_map/ppermute | solution.py:723
  125.2 10.7 %collective-permute-start.13 = (bf16[96,8,128]{2,1,0:T(8,128)(2,1)S(1)}, bf16[96,8,128]{2,1,0:T(8,128)(2,1)S(1)}, u32[]{:S(2)}, u32[]{:S(2)}) collective-permute-start(bf16[96,8,128]{2,1,0:T(8,128)(2,1)S(1)} %collective-permute-done.9.refs_1_), channel_id=1, source_target_pairs={{0,1},{1,2},{2,3},{3,0},{4,5},{5,6},{6,7},{7,4},{8,9},{9,10},{10,1... | collective-permute-start | bytes 589832 | tf_op jit(solution)/shard_map/ppermute | solution.py:727
  125.5 12.4 %collective-permute-start.14 = (bf16[96,8,128]{2,1,0:T(8,128)(2,1)S(1)}, bf16[96,8,128]{2,1,0:T(8,128)(2,1)S(1)}, u32[]{:S(2)}, u32[]{:S(2)}) collective-permute-start(bf16[96,8,128]{2,1,0:T(8,128)(2,1)S(1)} %collective-permute-done.12.refs_4_), channel_id=1, source_target_pairs={{1,0},{2,1},{3,2},{0,3},{5,4},{6,5},{7,6},{4,7},{9,8},{10,9},{11,1... | collective-permute-start | bytes 589832 | tf_op jit(solution)/shard_map/ppermute | solution.py:727

commit v6 on v5

--- a/solution.py
+++ b/solution.py
@@ -76,8 +76,25 @@
         out_ref[tile] = picked.astype(BF16)
 
 
-def pack_x_kernel(*refs):
-    blocks, lo_ref, hi_ref = refs[:BLOCKS], refs[BLOCKS], refs[BLOCKS + 1]
+EARLY, LATE = (0, 1, 3), (2,)
+EARLY_SIDES, LATE_SIDES = (0,), (1, 2, 3)
+
+
+def halo_row(halos, d, row):
+    ref = 2 if d == 2 else 0
+    at = (0 if d == 2 else EARLY.index(d)) * HALF + row
+    return halos[ref][at].astype(F32), halos[ref + 1][at].astype(F32)
+
+
+def halo_side(halos, d, tile):
+    ref = 0 if d == 0 else 2
+    at = (len(EARLY) * HALF if d == 0 else HALF + LATE_SIDES.index(d) * PACKED) + tile
+    after, before = halos[ref][at].astype(F32), halos[ref + 1][at].astype(F32)
+    return jnp.where(iota((8, 128), 1) % 8 < 4, after, before)
+
+
+def pack_x_kernel(group, sides, *refs):
+    blocks, (lo_ref, hi_ref) = refs[:-2], refs[-2:]
     top = iota((8, 128), 0) < 4
 
     def pair(one, two, at):
@@ -86,27 +103,28 @@
         hi_ref[at] = jnp.where(top, two, one).astype(BF16)
 
     def body(j, carry):
-        for d in range(LOCAL):
+        for place, d in enumerate(group):
             for kl in range(2):
                 pair(
                     vector_row(blocks, d, kl, j),
                     vector_row(blocks, d, kl + 2, j),
-                    d * HALF + kl * ROWS + j,
+                    place * HALF + kl * ROWS + j,
                 )
         return carry
 
     lax.fori_loop(0, ROWS, body, 0)
-    for d in range(LOCAL):
+    for place, d in enumerate(group):
         for i in range(3):
             pair(
                 induction_row(blocks, d, i),
                 induction_row(blocks, d, i + 3),
-                d * HALF + CUT + i,
+                place * HALF + CUT + i,
             )
+    for place, d in enumerate(sides):
         for tile in range(PACKED):
             piece = side_tile(blocks, d, tile)
-            lo_ref[LOCAL * HALF + d * PACKED + tile] = piece
-            hi_ref[LOCAL * HALF + d * PACKED + tile] = piece
+            lo_ref[len(group) * HALF + place * PACKED + tile] = piece
+            hi_ref[len(group) * HALF + place * PACKED + tile] = piece
 
 
 def inner_all(c_ref, field, sums_ref):
@@ -186,7 +204,7 @@
     return jnp.exp(-dist / ((size_x + size_y) / 8.0))
 
 
-def unpack_once(blocks, ln_ref, hp_ref, c_ref, x_ref, near_ref, far_ref):
+def unpack_once(blocks, halos, c_ref, x_ref, near_ref, far_ref):
     top = iota((8, 128), 0) < 4
 
     def body(j, carry):
@@ -194,8 +212,7 @@
             for kl in range(LOCAL):
                 k = d * LOCAL + kl
                 c_ref[k * ROWS + j] = vector_row(blocks, d, kl, j)
-                at = d * HALF + (kl % 2) * ROWS + j
-                after, before = ln_ref[at].astype(F32), hp_ref[at].astype(F32)
+                after, before = halo_row(halos, d, (kl % 2) * ROWS + j)
                 if kl < 2:
                     x_ref[k * ROWS + j] = jnp.where(top, after, before)
                 else:
@@ -203,33 +220,39 @@
         return carry
 
     lax.fori_loop(0, ROWS, body, 0)
-    from_next = iota((8, 128), 1) % 8 < 4
     for d in range(LOCAL):
         for t in range(PACKED - 1):
-            at = LOCAL * HALF + d * PACKED + t
             near_ref[d * 12 + t] = side_tile(blocks, d, t).astype(F32)
-            far_ref[d * 12 + t] = jnp.where(
-                from_next, ln_ref[at].astype(F32), hp_ref[at].astype(F32)
-            )
+            far_ref[d * 12 + t] = halo_side(halos, d, t)
+
+
+AT_ONCE = 4
+
+
+def plus(total, term):
+    return term if total is None else total + term
 
 
 def combine_ext(coeffs, fields, interior, halo_x, unpacked_ref):
     c_ref, x_ref, near_ref, far_ref = fields
 
-    def body(j, carry):
-        inner = [jnp.zeros((8, 128), F32)] * 2
-        outer = [jnp.zeros((8, 128), F32)] * 2
+    def body(step, carry):
+        rows = [step * AT_ONCE + i for i in range(AT_ONCE)]
+        inner = [[None] * AT_ONCE, [None] * AT_ONCE]
+        outer = [[None] * AT_ONCE, [None] * AT_ONCE]
         for k in range(VECS):
-            vec, edge = c_ref[k * ROWS + j], x_ref[k * ROWS + j]
+            for i, j in enumerate(rows):
+                vec, edge = c_ref[k * ROWS + j], x_ref[k * ROWS + j]
+                for s in range(2):
+                    inner[s][i] = plus(inner[s][i], coeffs[s][k] * vec)
+                    outer[s][i] = plus(outer[s][i], coeffs[s][k] * edge)
+        for i, j in enumerate(rows):
             for s in range(2):
-                inner[s] = inner[s] + coeffs[s][k] * vec
-                outer[s] = outer[s] + coeffs[s][k] * edge
-        for s in range(2):
-            interior(s, j, inner[s])
-            halo_x(s, j, outer[s])
+                interior(s, j, inner[s][i])
+                halo_x(s, j, outer[s][i])
         return carry
 
-    lax.fori_loop(0, ROWS, body, 0)
+    lax.fori_loop(0, ROWS // AT_ONCE, body, 0)
     pick = pick_matrix(F32)
     for s in range(2):
         for tile in range(3):
@@ -352,40 +375,16 @@
     return pltpu.roll(work, 128 - VECS, 1)
 
 
-def begin_kernel(size_x, size_y, src_ref, got_ref, *refs):
-    blocks, ln_ref, hp_ref = refs[:BLOCKS], refs[BLOCKS], refs[BLOCKS + 1]
-    refs = refs[BLOCKS + 2 :]
-    r_ref, q_ref, m_ref, inv_ref, state_ref, out_ref = refs[:6]
-    fields, side_ref, sums_ref = refs[6:10], refs[10], refs[11]
-    unpack_once(blocks, ln_ref, hp_ref, *fields)
-    total = jnp.sum(got_ref[...], axis=0)
-    inverse = invert(total[0:2])
-    inv_ref[...] = inverse
-    inner = total[2:3]
+def prepare_kernel(size_x, size_y, src_ref, *refs):
+    blocks, halos, refs = refs[:BLOCKS], refs[BLOCKS : BLOCKS + 4], refs[BLOCKS + 4 :]
+    m_ref, rhs_ref, fields = refs[0], refs[1], refs[2:]
+    unpack_once(blocks, halos, *fields)
     x_pos, y_pos, mask = grid_mask(size_x, size_y)
-    start = [solve(inverse, inner, s * VECS) for s in range(2)]
-    lane = iota((VECS, 128), 1)
-    state_ref[...] = jnp.where(lane == 2, start[0], jnp.where(lane == 3, start[1], 0.0))
-    coeffs = [[spread(-start[s][k : k + 1]) for k in range(VECS)] for s in range(2)]
-
-    def put(rows, columns):
-        def store(s, j, value):
-            r_ref[s * ROWS + j, rows, columns] = value
-
-        return store
-
-    combine_ext(
-        coeffs, fields,
-        put(slice(0, 8), slice(0, 128)), put(slice(8, 16), slice(0, 128)), side_ref,
-    )
     top = iota((8, 128), 0) < 4
-    from_next = iota((8, 128), 1) % 8 < 4
     pick = pick_matrix(F32)
     sides = []
     for d in range(LOCAL):
-        at = 4 * HALF + d * PACKED + 12
-        near = side_tile(blocks, d, 12).astype(F32)
-        far = jnp.where(from_next, ln_ref[at].astype(F32), hp_ref[at].astype(F32))
+        near, far = side_tile(blocks, d, 12).astype(F32), halo_side(halos, d, 12)
         near = full_dot(jnp.transpose(near), pick)[:48].reshape(6, 8, 128)
         far = full_dot(jnp.transpose(far), pick)[:48].reshape(6, 8, 128)
         sides.append((near, far))
@@ -395,8 +394,7 @@
             quarters = []
             for d in range(LOCAL):
                 inner_m = induction_row(blocks, d, at)
-                row = d * HALF + 96 + at % 3
-                after, before = ln_ref[row].astype(F32), hp_ref[row].astype(F32)
+                after, before = halo_row(halos, d, CUT + at % 3)
                 if at < 3:
                     edge = jnp.where(top, after, before)
                 else:
@@ -405,22 +403,54 @@
                 right = jnp.concatenate([sides[d][0][at], sides[d][1][at]], axis=0)
                 quarters.append(jnp.concatenate([left, right], axis=1))
             m_ref[c * 8 + z] = pick_layer(quarters, z)
-
     for s in range(2):
 
         def body(z, carry, s=s):
             prim = primary_field(src_ref[s], z, x_pos, y_pos, size_x, size_y)
             for c in range(3):
                 at = c * 8 + z
-                real = jnp.where(mask, (m_ref[at] - 1.0) * WEIGHTS[c] * prim, 0.0)
-                for p in range(2):
-                    place = s * ROWS + p * 24 + at
-                    value = real if p == 0 else 0.5 * real
-                    r_ref[place, :, 0:128] = r_ref[place, :, 0:128] + value[:, 0:128]
-                    r_ref[place, :, 128:256] = side_ref[place] + value[:, 128:256]
+                real = (m_ref[at] - 1.0) * WEIGHTS[c] * prim
+                rhs_ref[s * 24 + at] = jnp.where(mask, real, 0.0)
             return carry
 
         lax.fori_loop(0, 8, body, 0)
+
+
+def begin_kernel(size_x, size_y, got_ref, *refs):
+    fields, m_ref, rhs_ref = refs[:4], refs[4], refs[5]
+    r_ref, q_ref, inv_ref, state_ref, out_ref, side_ref, sums_ref = refs[6:]
+    total = jnp.sum(got_ref[...], axis=0)
+    inverse = invert(total[0:2])
+    inv_ref[...] = inverse
+    inner = total[2:3]
+    _, _, mask = grid_mask(size_x, size_y)
+    start = [solve(inverse, inner, s * VECS) for s in range(2)]
+    lane = iota((VECS, 128), 1)
+    state_ref[...] = jnp.where(lane == 2, start[0], jnp.where(lane == 3, start[1], 0.0))
+    coeffs = [[spread(-start[s][k : k + 1]) for k in range(VECS)] for s in range(2)]
+
+    def rhs(s, j, rows, columns):
+        value = rhs_ref[s * 24 + lax.rem(j, 24), rows, columns]
+        return jnp.where(j < 24, value, 0.5 * value)
+
+    def put(rows, columns):
+        def store(s, j, value):
+            r_ref[s * ROWS + j, rows, columns] = value + rhs(s, j, rows, columns)
+
+        return store
+
+    combine_ext(
+        coeffs, fields,
+        put(slice(0, 8), slice(0, 128)), put(slice(8, 16), slice(0, 128)), side_ref,
+    )
+    for s in range(2):
+
+        def body(j, carry, s=s):
+            at = s * ROWS + j
+            r_ref[at, :, 128:256] = side_ref[at] + rhs(s, j, slice(0, 16), slice(128, 256))
+            return carry
+
+        lax.fori_loop(0, ROWS, body, 0)
     apply_operator(r_ref, m_ref, q_ref, mask)
     finish_first(fields[0], r_ref, q_ref, sums_ref, out_ref)
 
@@ -595,36 +625,44 @@
     names = ("r", "u", "a", "sol_r", "sol_u")
     scale = [{name: spread(one[name]) for name in names} for one in small]
 
-    def residual_body(j, carry):
-        values = []
+    def residual_body(step, carry):
+        rows = [step * AT_ONCE + i for i in range(AT_ONCE)]
+        values = [[], []]
         for s in range(2):
-            r, u, a = brick(r_ref)(s, j), brick(u_ref)(s, j), brick(a_ref)(s, j)
-            values.append(scale[s]["r"] * r + scale[s]["u"] * u + scale[s]["a"] * a)
+            for j in rows:
+                r, u, a = brick(r_ref)(s, j), brick(u_ref)(s, j), brick(a_ref)(s, j)
+                values[s].append(scale[s]["r"] * r + scale[s]["u"] * u + scale[s]["a"] * a)
         for k in range(VECS):
-            vec = c_ref[k * ROWS + j]
-            for s in range(2):
-                values[s] = values[s] + coeffs[s][k] * vec
+            for i, j in enumerate(rows):
+                vec = c_ref[k * ROWS + j]
+                for s in range(2):
+                    values[s][i] = values[s][i] + coeffs[s][k] * vec
         for s in range(2):
-            residual_ref[s * ROWS + j] = values[s]
+            for i, j in enumerate(rows):
+                residual_ref[s * ROWS + j] = values[s][i]
         return carry
 
-    def solution_body(j, carry):
-        values = []
+    def solution_body(step, carry):
+        rows = [step * AT_ONCE + i for i in range(AT_ONCE)]
+        values = [[], []]
         for s in range(2):
-            r, u = brick(r_ref)(s, j), brick(u_ref)(s, j)
-            old = sol_ref[s * ROWS + j]
-            values.append(old + scale[s]["sol_r"] * r + scale[s]["sol_u"] * u)
+            for j in rows:
+                r, u = brick(r_ref)(s, j), brick(u_ref)(s, j)
+                old = sol_ref[s * ROWS + j]
+                values[s].append(old + scale[s]["sol_r"] * r + scale[s]["sol_u"] * u)
         for d in range(LOCAL):
             for kl in range(LOCAL):
-                vec = basis_row(basis, d, kl, j)
-                for s in range(2):
-                    values[s] = values[s] + basis_coeffs[s][d * LOCAL + kl] * vec
+                for i, j in enumerate(rows):
+                    vec = basis_row(basis, d, kl, j)
+                    for s in range(2):
+                        values[s][i] = values[s][i] + basis_coeffs[s][d * LOCAL + kl] * vec
         for s in range(2):
-            solution_ref[s * ROWS + j] = values[s]
+            for i, j in enumerate(rows):
+                solution_ref[s * ROWS + j] = values[s][i]
         return carry
 
-    lax.fori_loop(0, ROWS, residual_body, 0)
-    lax.fori_loop(0, ROWS, solution_body, 0)
+    lax.fori_loop(0, ROWS // AT_ONCE, residual_body, 0)
+    lax.fori_loop(0, ROWS // AT_ONCE, solution_body, 0)
 
 
 def call(kernel, outs, args, scratch=(), smem=0):
@@ -660,13 +698,13 @@
 def on_device(src_cell, basis, images, induction):
     size_x, size_y = 8 * lax.axis_size("gx"), 128 * lax.axis_size("gy")
     peers = lax.axis_size("gx") * lax.axis_size("gy")
+    right, left = steps("tx", wrap=True)
     block = jnp.concatenate(
         [images.reshape(LOCAL * ROWS, 8, 128), induction.reshape(6, 8, 128)], axis=0
     )
-    right, left = steps("tx", wrap=True)
+    own = call(pack_y_kernel, shape(PACKED, 8, 128, dtype=BF16), (block,))
     one = lax.ppermute(block, "tx", right)
     three = lax.ppermute(block, "tx", left)
-    own = call(pack_y_kernel, shape(PACKED, 8, 128, dtype=BF16), (block,))
     up, down = steps("gy")
     after, before = lax.ppermute(own, "gy", down), lax.ppermute(own, "gy", up)
     side = jnp.where(lax.broadcasted_iota(jnp.int32, own.shape, 1) < 4, after, before)
@@ -674,12 +712,18 @@
     far_side, one, three = tied(far_side, one, three)
     far_low = lax.ppermute(jnp.concatenate([one[:CUT], side]), "tx", right)
     far_high = lax.ppermute(jnp.concatenate([three[CUT:], side]), "tx", left)
+    up, down = steps("gx")
+
+    def exchange_x(group, sides, sources):
+        count = len(group) * HALF + len(sides) * PACKED
+        half = shape(count, 8, 128, dtype=BF16)
+        low, high = call(functools.partial(pack_x_kernel, group, sides), (half, half), sources)
+        return lax.ppermute(low, "gx", down), lax.ppermute(high, "gx", up)
+
+    early = exchange_x(EARLY, EARLY_SIDES, (block, one, three, side, side, side))
     blocks = (block, one, three, far_low, far_high, side, far_side)
 
-    half = shape(LOCAL * (HALF + PACKED), 8, 128, dtype=BF16)
-    low, high = call(pack_x_kernel, (half, half), blocks)
-    up, down = steps("gx")
-    ln, hp = lax.ppermute(low, "gx", down), lax.ppermute(high, "gx", up)
+    late = exchange_x(LATE, LATE_SIDES, blocks)
 
     sums = pltpu.VMEM((128, 128), F32)
     side_scratch = pltpu.VMEM((2 * ROWS, 16, 128), F32)
@@ -691,6 +735,13 @@
         smem=1,
     )
     got = exchange(sent)
+    whole, tiles = shape(VECS * ROWS, 8, 128), shape(3 * VECS, 8, 128)
+    m, rhs, *fields = call(
+        functools.partial(prepare_kernel, size_x, size_y),
+        (shape(24, 16, 256), shape(ROWS, 16, 256), whole, whole, tiles, tiles),
+        (src_cell, *blocks, *early, *late),
+        smem=1,
+    )
     wide = shape(2 * ROWS, 16, 256)
     line = shape(peers, 128)
     small = shape(VECS, 128)
@@ -701,13 +752,11 @@
 
     got, piece = tied(got, own_basis[:CUT])
     one_low, three_low = lax.ppermute(piece, "tx", right), lax.ppermute(piece, "tx", left)
-    whole, tiles = shape(VECS * ROWS, 8, 128), shape(3 * VECS, 8, 128)
-    r, q, m, inverse, state, sent, *fields = call(
+    r, q, inverse, state, sent = call(
         functools.partial(begin_kernel, size_x, size_y),
-        (wide, wide, shape(24, 16, 256), small, small, line, whole, whole, tiles, tiles),
-        (src_cell, got, *blocks, ln, hp),
+        (wide, wide, small, small, line),
+        (got, *fields, m, rhs),
         (side_scratch, sums),
-        smem=1,
     )
 
     def first(r, q, state, got):

time: 173 us -> 170 us (0.983)
  waiting for transfers between devices: 33.4 us -> 20 us
  starting transfers between devices: 45 us -> 54.8 us
    ppermute x1, waiting for transfers between devices: 13.2 us -> 2.72 us  [on_device(): far_low = lax.ppermute(jnp.concatenate([one[:CUT], side]), 'tx', right)]
    ppermute x2 -> x4, starting transfers between devices: 6.5 us -> 15.8 us  [exchange_x(): return (lax.ppermute(low, 'gx', down), lax.ppermute(high, 'gx', up))]
    all_to_all x1, waiting for transfers between devices: 7.84 us -> 4.22 us  [exchange(): return lax.all_to_all(value, ('gx', 'gy'), 0, 0)]
    pallas_call x8 -> x10, Pallas kernels: 39.8 us -> 39.3 us  [call(): pl.pallas_call(kernel, out_shape=outs, in_specs=[pl.BlockSpec(memory_spac...]
  transfers between devices with their start and end apart: 16 -> 18, of which waited for: 6 -> 7; matrix products, arithmetic and copies ran while one was open for 0% -> 1% of each run, Pallas kernels for 16% -> 18%
where the time goes in v6:
time: 170 us
  starting transfers between devices  54.8 us (32%)
  blocking collectives  51.6 us (30%)
  Pallas kernels  39.3 us (23%)
  waiting for transfers between devices  20 us (12%)
  local copies, waits for them, and re-layouts  2.18 us (1%)
    all_to_all x4, blocking collectives, exchange(): return lax.all_to_all(value, ('gx', 'gy'), 0, 0)  51.6 us
    pallas_call x10, Pallas kernels, call(): pl.pallas_call(kernel, out_shape=outs, in_specs=[pl.BlockSpec(memory_spac...  39.3 us
    ppermute x4, starting transfers between devices, exchange_x(): return (lax.ppermute(low, 'gx', down), lax.ppermute(high, 'gx', up))  15.8 us
    all_to_all x1, starting transfers between devices, exchange(): return lax.all_to_all(value, ('gx', 'gy'), 0, 0)  9.12 us
    ppermute x1, starting transfers between devices, on_device(): three = lax.ppermute(block, 'tx', left)  6.93 us
    ppermute x1, starting transfers between devices, on_device(): far_high = lax.ppermute(jnp.concatenate([three[CUT:], side]), 'tx', left)  6.71 us
    ppermute x2, starting transfers between devices, on_device(): after, before = (lax.ppermute(own, 'gy', down), lax.ppermute(own, 'gy', up))  4.5 us
    ppermute x2, starting transfers between devices, on_device(): lax.ppermute(piece, 'tx', right)  4.45 us
  transfers between devices with their start and end apart: 18, of which 7 were waited for; matrix products, arithmetic and copies ran while one was open for 1% of the time, Pallas kernels for 18%

profile of v6, /device:TPU:1, one launch (start us, length us, event | category | flops | bytes accessed | tf_op | source)
XLA Modules:
  0.0 169.8 jit_solution(6842162424121049469)
XLA Ops:
  0.6 1.1 pad_maximum_fusion.block_ref.refs_0_
  1.7 6.9 %collective-permute-start.4 = (bf16[198,8,128]{2,1,0:T(8,128)(2,1)S(1)}, bf16[198,8,128]{2,1,0:T(8,128)(2,1)S(1)}, u32[]{:S(2)}, u32[]{:S(2)}) collective-permute-start(bf16[198,8,128]{2,1,0:T(8,128)(2,1)S(1)} %pad_maximum_fusion.block_ref.refs_0_), channel_id=1, source_target_pairs={{1,0},{2,1},{3,2},{0,3},{5,4},{6,5},{7,6},{4,7},{9,8},{10,9},{11,1... | collective-permute-start | bytes 1216520 | tf_op jit(solution)/shard_map/ppermute | solution.py:707
  8.6 0.0 collective-permute-start.3
  8.6 0.3 shard_map.59
  8.9 3.2 %collective-permute-start.1 = (bf16[13,8,128]{2,1,0:T(8,128)(2,1)S(1)}, bf16[13,8,128]{2,1,0:T(8,128)(2,1)S(1)}, u32[]{:S(2)}, u32[]{:S(2)}) collective-permute-start(bf16[13,8,128]{2,1,0:T(8,128)(2,1)S(1)} %shard_map.59), channel_id=1, source_target_pairs={{0,4},{4,8},{8,12},{1,5},{5,9},{9,13},{2,6},{6,10},{10,14},{3,7},{... | collective-permute-start | bytes 79880 | tf_op jit(solution)/shard_map/ppermute | solution.py:709
  12.1 1.3 collective-permute-start
  13.5 0.0 collective-permute-done.1
  13.5 3.6 %collective-permute-done = bf16[13,8,128]{2,1,0:T(8,128)(2,1)S(1)} collective-permute-done((bf16[13,8,128]{2,1,0:T(8,128)(2,1)S(1)}, bf16[13,8,128]{2,1,0:T(8,128)(2,1)S(1)}, u32[]{:S(2)}, u32[]{:S(2)}) %collective-permute-start) | collective-permute-done | bytes 26656 | tf_op jit(solution)/shard_map/ppermute | solution.py:709
  17.0 0.1 broadcast_select_fusion.refs_5_.refs_3_.refs_4_
  17.1 3.3 %collective-permute-start.2 = (bf16[13,8,128]{2,1,0:T(8,128)(2,1)S(1)}, bf16[13,8,128]{2,1,0:T(8,128)(2,1)S(1)}, u32[]{:S(2)}, u32[]{:S(2)}) collective-permute-start(bf16[13,8,128]{2,1,0:T(8,128)(2,1)S(1)} %broadcast_select_fusion.refs_5_.refs_3_.refs_4_), channel_id=1, source_target_pairs={{0,2},{1,3},{2,0},{3,1},{4,6},{5,7},{6,4},{7,5},{8,10},{9,11},{10,... | collective-permute-start | bytes 79880 | tf_op jit(solution)/shard_map/ppermute | solution.py:711
  20.4 3.7 %collective-permute-done.2.refs_6_ = bf16[13,8,128]{2,1,0:T(8,128)(2,1)S(1)} collective-permute-done((bf16[13,8,128]{2,1,0:T(8,128)(2,1)S(1)}, bf16[13,8,128]{2,1,0:T(8,128)(2,1)S(1)}, u32[]{:S(2)}, u32[]{:S(2)}) %collective-permute-start.2) | collective-permute-done | bytes 26656 | tf_op jit(solution)/shard_map/ppermute | solution.py:711
  24.2 6.7 %collective-permute-start.6 = (bf16[115,8,128]{2,1,0:T(8,128)(2,1)S(1)}, bf16[115,8,128]{2,1,0:T(8,128)(2,1)S(1)}, u32[]{:S(2)}, u32[]{:S(2)}) collective-permute-start(bf16[115,8,128]{2,1,0:T(8,128)(2,1)S(1)} %pad_maximum_fusion.1), channel_id=1, source_target_pairs={{1,0},{2,1},{3,2},{0,3},{5,4},{6,5},{7,6},{4,7},{9,8},{10,9},{11,1... | collective-permute-start | bytes 706568 | tf_op jit(solution)/shard_map/ppermute | solution.py:714
  30.9 0.0 copy-start.2
  30.9 0.1 collective-permute-start.5
  31.0 1.7 shard_map.61
  32.7 5.7 %collective-permute-start.7 = (bf16[310,8,128]{2,1,0:T(8,128)(2,1)}, bf16[310,8,128]{2,1,0:T(8,128)(2,1)S(1)}, u32[]{:S(2)}, u32[]{:S(2)}) collective-permute-start(bf16[310,8,128]{2,1,0:T(8,128)(2,1)} %get-tuple-element.55), channel_id=1, source_target_pairs={{16,0},{32,16},{48,32},{64,48},{80,64},{96,80},{112,96},{128,112},... | collective-permute-start | bytes 1904648 | tf_op jit(solution)/shard_map/ppermute | solution.py:721
  38.4 0.0 copy-start
  38.4 3.1 %collective-permute-start.8 = (bf16[310,8,128]{2,1,0:T(8,128)(2,1)}, bf16[310,8,128]{2,1,0:T(8,128)(2,1)S(1)}, u32[]{:S(2)}, u32[]{:S(2)}) collective-permute-start(bf16[310,8,128]{2,1,0:T(8,128)(2,1)} %get-tuple-element.56), channel_id=1, source_target_pairs={{0,16},{16,32},{32,48},{48,64},{64,80},{80,96},{96,112},{112,128},... | collective-permute-start | bytes 1904648 | tf_op jit(solution)/shard_map/ppermute | solution.py:721
  41.5 2.7 %collective-permute-done.5.refs_3_ = bf16[109,8,128]{2,1,0:T(8,128)(2,1)S(1)} collective-permute-done((bf16[109,8,128]{2,1,0:T(8,128)(2,1)S(1)}, bf16[109,8,128]{2,1,0:T(8,128)(2,1)S(1)}, u32[]{:S(2)}, u32[]{:S(2)}) %collective-permute-start.5) | collective-permute-done | bytes 223264 | tf_op jit(solution)/shard_map/ppermute | solution.py:713
  44.3 1.1 shard_map.62
  45.4 0.7 copy-done.3
  46.1 3.5 %collective-permute-start.9 = (bf16[138,8,128]{2,1,0:T(8,128)(2,1)}, bf16[138,8,128]{2,1,0:T(8,128)(2,1)}, u32[]{:S(2)}, u32[]{:S(2)}) collective-permute-start(bf16[138,8,128]{2,1,0:T(8,128)(2,1)} %get-tuple-element.57), channel_id=1, source_target_pairs={{16,0},{32,16},{48,32},{64,48},{80,64},{96,80},{112,96},{128,112},... | collective-permute-start | bytes 847880 | tf_op jit(solution)/shard_map/ppermute | solution.py:721
  49.6 2.8 %shard_map.60 = f32[64,4,128]{2,1,0:T(4,128)S(1)} custom-call(s32[2]{0:T(128)S(1)} %copy-done.2, bf16[198,8,128]{2,1,0:T(8,128)(2,1)S(1)} %pad_maximum_fusion.block_ref.refs_0_, bf16[198,8,128]{2,1,0:T(8,128)(2,1)S(1)} %collective-permute-done.3.refs_1_, bf16[198,8,128]{2,1,0:T(8,128)(2,1)S(1)} %collective-permute-done.4.refs_2_, ...), custom_call_target="tpu_custom_call" | custom-call | tf_op jit(solution)/shard_map/pallas_call | solution.py:670
  52.3 0.6 copy-done.1
  53.0 9.1 %all-to-all-start = ((f32[64,4,128]{2,1,0:T(4,128)}), f32[64,4,128]{2,1,0:T(4,128)S(1)}, u32[]{:S(2)}, u32[]{:S(2)}) async-start(f32[64,4,128]{2,1,0:T(4,128)} %copy-done.1), calls=%async_computation | async-start | bytes 262144 | tf_op jit(solution)/shard_map/all_to_all | solution.py:685
  62.1 3.5 %collective-permute-start.10 = (bf16[138,8,128]{2,1,0:T(8,128)(2,1)}, bf16[138,8,128]{2,1,0:T(8,128)(2,1)}, u32[]{:S(2)}, u32[]{:S(2)}) collective-permute-start(bf16[138,8,128]{2,1,0:T(8,128)(2,1)} %copy-done.3), channel_id=1, source_target_pairs={{0,16},{16,32},{32,48},{48,64},{64,80},{80,96},{96,112},{112,128},... | collective-permute-start | bytes 847880 | tf_op jit(solution)/shard_map/ppermute | solution.py:721
  65.7 0.8 fusion
  66.5 4.2 %all-to-all-done.got_ref = f32[64,4,128]{2,1,0:T(4,128)S(1)} async-done(((f32[64,4,128]{2,1,0:T(4,128)}), f32[64,4,128]{2,1,0:T(4,128)S(1)}, u32[]{:S(2)}, u32[]{:S(2)}) %all-to-all-start) | async-done | bytes 131104 | tf_op jit(solution)/shard_map/all_to_all | solution.py:685
  70.7 0.1 collective-permute-start.12
  70.8 2.2 %collective-permute-start.11 = (bf16[96,8,128]{2,1,0:T(8,128)(2,1)}, bf16[96,8,128]{2,1,0:T(8,128)(2,1)S(1)}, u32[]{:S(2)}, u32[]{:S(2)}) collective-permute-start(bf16[96,8,128]{2,1,0:T(8,128)(2,1)} %bitcast.36), channel_id=1, source_target_pairs={{0,1},{1,2},{2,3},{3,0},{4,5},{5,6},{6,7},{7,4},{8,9},{9,10},{10,1... | collective-permute-start | bytes 589832 | tf_op jit(solution)/shard_map/ppermute | solution.py:754
  73.1 3.0 %shard_map.63 = (f32[24,16,256]{2,1,0:T(8,128)S(1)}, f32[48,16,256]{2,1,0:T(8,128)S(1)}, f32[768,8,128]{2,1,0:T(8,128)S(1)}, f32[768,8,128]{2,1,0:T(8,128)S(1)},...) custom-call(s32[2]{0:T(128)S(1)} %copy-done.2, bf16[198,8,128]{2,1,0:T(8,128)(2,1)S(1)} %pad_maximum_fusion.block_ref.refs_0_, ...), custom_call_target="tpu_custom_call" | custom-call | tf_op jit(solution)/shard_map/pallas_call | solution.py:670
  76.1 8.0 %shard_map.64 = (f32[96,16,256]{2,1,0:T(8,128)S(1)}, f32[96,16,256]{2,1,0:T(8,128)S(1)}, f32[16,128]{1,0:T(8,128)S(1)}, f32[16,128]{1,0:T(8,128)S(1)}, f32[64,128]{1,0:T(8,128)S(1)}) custom-call(f32[64,4,128]{2,1,0:T(4,128)S(1)} %all-to-all-done.got_ref, f32[768,8,128]{2,1,0:T(8,128)S(1)} %get-tuple-element.59.refs_0_.c_ref, ...), custom_call_target="tpu_custom_call" | custom-call | tf_op jit(solution)/shard_map/pallas_call | solution.py:670
  84.2 0.0 collective-permute-done.11.refs_1_
  84.2 14.0 %all_to_all.25 = f32[64,1,128]{2,1,0:T(1,128)S(1)} all-to-all(f32[64,1,128]{2,1,0:T(1,128)S(1)} %bitcast.29), channel_id=1, replica_groups=mesh['gx'=16,'gy'=4,'tx'=4] {'gx','gy'}, dimensions={0} | all-to-all | bytes 65536 | tf_op jit(solution)/shard_map/all_to_all | solution.py:685
  98.2 0.1 collective-permute-start.14
  98.3 2.2 %collective-permute-start.13 = (bf16[96,8,128]{2,1,0:T(8,128)(2,1)S(1)}, bf16[96,8,128]{2,1,0:T(8,128)(2,1)S(1)}, u32[]{:S(2)}, u32[]{:S(2)}) collective-permute-start(bf16[96,8,128]{2,1,0:T(8,128)(2,1)S(1)} %bitcast.34), channel_id=1, source_target_pairs={{0,1},{1,2},{2,3},{3,0},{4,5},{5,6},{6,7},{7,4},{8,9},{9,10},{10,1... | collective-permute-start | bytes 589832 | tf_op jit(solution)/shard_map/ppermute | solution.py:772
  100.6 6.1 %shard_map.65 = (f32[96,16,256]{2,1,0:T(8,128)S(1)}, f32[96,16,256]{2,1,0:T(8,128)S(1)}, f32[16,128]{1,0:T(8,128)S(1)}, f32[64,128]{1,0:T(8,128)S(1)}) custom-call(f32[64,128]{1,0:T(8,128)S(1)} %bitcast.26, f32[768,8,128]{2,1,0:T(8,128)S(1)} %get-tuple-element.59.refs_0_.c_ref, f32[768,8,128]{2,1,0:T(8,128)S(1)} %get-tuple-element.60.refs_1_, ...), custom_call_target="tpu_custom_call" | custom-call | tf_op jit(solution)/shard_map/pallas_call | solution.py:670
  106.6 3.3 %collective-permute-done.14.refs_4_ = bf16[96,8,128]{2,1,0:T(8,128)(2,1)S(1)} collective-permute-done((bf16[96,8,128]{2,1,0:T(8,128)(2,1)S(1)}, bf16[96,8,128]{2,1,0:T(8,128)(2,1)S(1)}, u32[]{:S(2)}, u32[]{:S(2)}) %collective-permute-start.14) | collective-permute-done | bytes 196640 | tf_op jit(solution)/shard_map/ppermute | solution.py:772
  109.9 13.4 %all_to_all.26 = f32[64,1,128]{2,1,0:T(1,128)S(1)} all-to-all(f32[64,1,128]{2,1,0:T(1,128)S(1)} %bitcast.30), channel_id=1, replica_groups=mesh['gx'=16,'gy'=4,'tx'=4] {'gx','gy'}, dimensions={0} | all-to-all | bytes 65536 | tf_op jit(solution)/shard_map/all_to_all | solution.py:685
  123.3 1.1 collective-permute-start.15
  124.4 2.5 %collective-permute-start.16 = (bf16[96,8,128]{2,1,0:T(8,128)(2,1)S(1)}, bf16[96,8,128]{2,1,0:T(8,128)(2,1)S(1)}, u32[]{:S(2)}, u32[]{:S(2)}) collective-permute-start(bf16[96,8,128]{2,1,0:T(8,128)(2,1)S(1)} %collective-permute-done.14.refs_4_), channel_id=1, source_target_pairs={{1,0},{2,1},{3,2},{0,3},{5,4},{6,5},{7,6},{4,7},{9,8},{10,9},{11,1... | collective-permute-start | bytes 589832 | tf_op jit(solution)/shard_map/ppermute | solution.py:776
  126.9 6.9 %shard_map.66 = (f32[96,16,256]{2,1,0:T(8,128)S(1)}, f32[96,16,256]{2,1,0:T(8,128)S(1)}, f32[96,8,128]{2,1,0:T(8,128)S(1)}, f32[16,128]{1,0:T(8,128)S(1)}, f32[64,128]{1,0:T(8,128)S(1)}) custom-call(f32[64,128]{1,0:T(8,128)S(1)} %bitcast.24, f32[768,8,128]{2,1,0:T(8,128)S(1)} %get-tuple-element.59.refs_0_.c_ref, ...), custom_call_target="tpu_custom_call" | custom-call | tf_op jit(solution)/shard_map/pallas_call | solution.py:670
  133.8 0.7 collective-permute-done.15.refs_5_
  134.5 1.7 collective-permute-done.16.refs_6_
  136.2 12.0 %all_to_all.27 = f32[64,1,128]{2,1,0:T(1,128)S(1)} all-to-all(f32[64,1,128]{2,1,0:T(1,128)S(1)} %bitcast.28), channel_id=1, replica_groups=mesh['gx'=16,'gy'=4,'tx'=4] {'gx','gy'}, dimensions={0} | all-to-all | bytes 65536 | tf_op jit(solution)/shard_map/all_to_all | solution.py:685
  148.2 6.1 %shard_map.67 = (f32[96,16,256]{2,1,0:T(8,128)S(1)}, f32[96,16,256]{2,1,0:T(8,128)S(1)}, f32[16,128]{1,0:T(8,128)S(1)}, f32[64,128]{1,0:T(8,128)S(1)}) custom-call(f32[64,128]{1,0:T(8,128)S(1)} %bitcast.27, f32[768,8,128]{2,1,0:T(8,128)S(1)} %get-tuple-element.59.refs_0_.c_ref, f32[768,8,128]{2,1,0:T(8,128)S(1)} %get-tuple-element.60.refs_1_, ...), custom_call_target="tpu_custom_call" | custom-call | tf_op jit(solution)/shard_map/pallas_call | solution.py:670
  154.2 12.2 %all_to_all.28 = f32[64,1,128]{2,1,0:T(1,128)S(1)} all-to-all(f32[64,1,128]{2,1,0:T(1,128)S(1)} %bitcast.31), channel_id=1, replica_groups=mesh['gx'=16,'gy'=4,'tx'=4] {'gx','gy'}, dimensions={0} | all-to-all | bytes 65536 | tf_op jit(solution)/shard_map/all_to_all | solution.py:685
  166.4 3.4 %shard_map.68 = (f32[96,8,128]{2,1,0:T(8,128)}, f32[96,8,128]{2,1,0:T(8,128)}) custom-call(f32[64,128]{1,0:T(8,128)S(1)} %bitcast.25, f32[768,8,128]{2,1,0:T(8,128)S(1)} %get-tuple-element.59.refs_0_.c_ref, bf16[192,8,128]{2,1,0:T(8,128)(2,1)S(1)} %bitcast.23, bf16[96,8,128]{2,1,0:T(8,128)(2,1)S(1)} %collective-permute-done.11.refs_1_, ...), custom_call_target="tpu_custom_call" | custom-call | tf_op jit(solution)/shard_map/pallas_call | solution.py:670
  (20 shorter events, 0.1 us)
Async XLA Ops:
  1.7 22.4 %collective-permute-start.4 = (bf16[198,8,128]{2,1,0:T(8,128)(2,1)S(1)}, bf16[198,8,128]{2,1,0:T(8,128)(2,1)S(1)}, u32[]{:S(2)}, u32[]{:S(2)}) collective-permute-start(bf16[198,8,128]{2,1,0:T(8,128)(2,1)S(1)} %pad_maximum_fusion.block_ref.refs_0_), channel_id=1, source_target_pairs={{1,0},{2,1},{3,2},{0,3},{5,4},{6,5},{7,6},{4,7},{9,8},{10,9},{11,1... | collective-permute-start | bytes 1216520 | tf_op jit(solution)/shard_map/ppermute | solution.py:707
  8.6 15.5 %collective-permute-start.3 = (bf16[198,8,128]{2,1,0:T(8,128)(2,1)S(1)}, bf16[198,8,128]{2,1,0:T(8,128)(2,1)S(1)}, u32[]{:S(2)}, u32[]{:S(2)}) collective-permute-start(bf16[198,8,128]{2,1,0:T(8,128)(2,1)S(1)} %pad_maximum_fusion.block_ref.refs_0_), channel_id=1, source_target_pairs={{0,1},{1,2},{2,3},{3,0},{4,5},{5,6},{6,7},{7,4},{8,9},{9,10},{10,1... | collective-permute-start | bytes 1216520 | tf_op jit(solution)/shard_map/ppermute | solution.py:706
  8.9 4.5 %collective-permute-start.1 = (bf16[13,8,128]{2,1,0:T(8,128)(2,1)S(1)}, bf16[13,8,128]{2,1,0:T(8,128)(2,1)S(1)}, u32[]{:S(2)}, u32[]{:S(2)}) collective-permute-start(bf16[13,8,128]{2,1,0:T(8,128)(2,1)S(1)} %shard_map.59), channel_id=1, source_target_pairs={{0,4},{4,8},{8,12},{1,5},{5,9},{9,13},{2,6},{6,10},{10,14},{3,7},{... | collective-permute-start | bytes 79880 | tf_op jit(solution)/shard_map/ppermute | solution.py:709
  12.1 4.9 %collective-permute-start = (bf16[13,8,128]{2,1,0:T(8,128)(2,1)S(1)}, bf16[13,8,128]{2,1,0:T(8,128)(2,1)S(1)}, u32[]{:S(2)}, u32[]{:S(2)}) collective-permute-start(bf16[13,8,128]{2,1,0:T(8,128)(2,1)S(1)} %shard_map.59), channel_id=1, source_target_pairs={{4,0},{8,4},{12,8},{5,1},{9,5},{13,9},{6,2},{10,6},{14,10},{7,3},{... | collective-permute-start | bytes 79880 | tf_op jit(solution)/shard_map/ppermute | solution.py:709
  17.1 7.0 %collective-permute-start.2 = (bf16[13,8,128]{2,1,0:T(8,128)(2,1)S(1)}, bf16[13,8,128]{2,1,0:T(8,128)(2,1)S(1)}, u32[]{:S(2)}, u32[]{:S(2)}) collective-permute-start(bf16[13,8,128]{2,1,0:T(8,128)(2,1)S(1)} %broadcast_select_fusion.refs_5_.refs_3_.refs_4_), channel_id=1, source_target_pairs={{0,2},{1,3},{2,0},{3,1},{4,6},{5,7},{6,4},{7,5},{8,10},{9,11},{10,... | collective-permute-start | bytes 79880 | tf_op jit(solution)/shard_map/ppermute | solution.py:711
  24.2 20.1 %collective-permute-start.6 = (bf16[115,8,128]{2,1,0:T(8,128)(2,1)S(1)}, bf16[115,8,128]{2,1,0:T(8,128)(2,1)S(1)}, u32[]{:S(2)}, u32[]{:S(2)}) collective-permute-start(bf16[115,8,128]{2,1,0:T(8,128)(2,1)S(1)} %pad_maximum_fusion.1), channel_id=1, source_target_pairs={{1,0},{2,1},{3,2},{0,3},{5,4},{6,5},{7,6},{4,7},{9,8},{10,9},{11,1... | collective-permute-start | bytes 706568 | tf_op jit(solution)/shard_map/ppermute | solution.py:714
  30.9 18.7 %copy-start.2 = (s32[2]{0:T(128)S(1)}, s32[2]{0:T(128)}, u32[]{:S(2)}) copy-start(s32[2]{0:T(128)} %src_ref.3) | copy-start | bytes 28
  30.9 13.3 %collective-permute-start.5 = (bf16[109,8,128]{2,1,0:T(8,128)(2,1)S(1)}, bf16[109,8,128]{2,1,0:T(8,128)(2,1)S(1)}, u32[]{:S(2)}, u32[]{:S(2)}) collective-permute-start(bf16[109,8,128]{2,1,0:T(8,128)(2,1)S(1)} %pad_maximum_fusion.2), channel_id=1, source_target_pairs={{0,1},{1,2},{2,3},{3,0},{4,5},{5,6},{6,7},{7,4},{8,9},{9,10},{10,1... | collective-permute-start | bytes 669704 | tf_op jit(solution)/shard_map/ppermute | solution.py:713
  32.7 40.4 %collective-permute-start.7 = (bf16[310,8,128]{2,1,0:T(8,128)(2,1)}, bf16[310,8,128]{2,1,0:T(8,128)(2,1)S(1)}, u32[]{:S(2)}, u32[]{:S(2)}) collective-permute-start(bf16[310,8,128]{2,1,0:T(8,128)(2,1)} %get-tuple-element.55), channel_id=1, source_target_pairs={{16,0},{32,16},{48,32},{64,48},{80,64},{96,80},{112,96},{128,112},... | collective-permute-start | bytes 1904648 | tf_op jit(solution)/shard_map/ppermute | solution.py:721
  38.4 27.3 %copy-start = (bf16[4,2,3,8,8,128]{5,4,3,2,1,0:T(8,128)(2,1)S(1)}, bf16[4,2,3,8,8,128]{5,4,3,2,1,0:T(8,128)(2,1)}, u32[]{:S(2)}) copy-start(bf16[4,2,3,8,8,128]{5,4,3,2,1,0:T(8,128)(2,1)} %param.5) | copy-start | bytes 1179652
  38.4 34.7 %collective-permute-start.8 = (bf16[310,8,128]{2,1,0:T(8,128)(2,1)}, bf16[310,8,128]{2,1,0:T(8,128)(2,1)S(1)}, u32[]{:S(2)}, u32[]{:S(2)}) collective-permute-start(bf16[310,8,128]{2,1,0:T(8,128)(2,1)} %get-tuple-element.56), channel_id=1, source_target_pairs={{0,16},{16,32},{32,48},{48,64},{64,80},{80,96},{96,112},{112,128},... | collective-permute-start | bytes 1904648 | tf_op jit(solution)/shard_map/ppermute | solution.py:721
  45.4 0.7 copy-start.3
  46.1 24.8 %collective-permute-start.9 = (bf16[138,8,128]{2,1,0:T(8,128)(2,1)}, bf16[138,8,128]{2,1,0:T(8,128)(2,1)}, u32[]{:S(2)}, u32[]{:S(2)}) collective-permute-start(bf16[138,8,128]{2,1,0:T(8,128)(2,1)} %get-tuple-element.57), channel_id=1, source_target_pairs={{16,0},{32,16},{48,32},{64,48},{80,64},{96,80},{112,96},{128,112},... | collective-permute-start | bytes 847880 | tf_op jit(solution)/shard_map/ppermute | solution.py:721
  52.3 0.7 copy-start.1
  53.0 17.7 %all-to-all-start = ((f32[64,4,128]{2,1,0:T(4,128)}), f32[64,4,128]{2,1,0:T(4,128)S(1)}, u32[]{:S(2)}, u32[]{:S(2)}) async-start(f32[64,4,128]{2,1,0:T(4,128)} %copy-done.1), calls=%async_computation | async-start | bytes 262144 | tf_op jit(solution)/shard_map/all_to_all | solution.py:685
  62.1 10.9 %collective-permute-start.10 = (bf16[138,8,128]{2,1,0:T(8,128)(2,1)}, bf16[138,8,128]{2,1,0:T(8,128)(2,1)}, u32[]{:S(2)}, u32[]{:S(2)}) collective-permute-start(bf16[138,8,128]{2,1,0:T(8,128)(2,1)} %copy-done.3), channel_id=1, source_target_pairs={{0,16},{16,32},{32,48},{48,64},{64,80},{80,96},{96,112},{112,128},... | collective-permute-start | bytes 847880 | tf_op jit(solution)/shard_map/ppermute | solution.py:721
  70.7 13.5 %collective-permute-start.12 = (bf16[96,8,128]{2,1,0:T(8,128)(2,1)}, bf16[96,8,128]{2,1,0:T(8,128)(2,1)S(1)}, u32[]{:S(2)}, u32[]{:S(2)}) collective-permute-start(bf16[96,8,128]{2,1,0:T(8,128)(2,1)} %bitcast.35), channel_id=1, source_target_pairs={{1,0},{2,1},{3,2},{0,3},{5,4},{6,5},{7,6},{4,7},{9,8},{10,9},{11,1... | collective-permute-start | bytes 589832 | tf_op jit(solution)/shard_map/ppermute | solution.py:754
  70.8 13.4 %collective-permute-start.11 = (bf16[96,8,128]{2,1,0:T(8,128)(2,1)}, bf16[96,8,128]{2,1,0:T(8,128)(2,1)S(1)}, u32[]{:S(2)}, u32[]{:S(2)}) collective-permute-start(bf16[96,8,128]{2,1,0:T(8,128)(2,1)} %bitcast.36), channel_id=1, source_target_pairs={{0,1},{1,2},{2,3},{3,0},{4,5},{5,6},{6,7},{7,4},{8,9},{9,10},{10,1... | collective-permute-start | bytes 589832 | tf_op jit(solution)/shard_map/ppermute | solution.py:754
  76.1 22.1 %copy-start.4 = (bf16[2,2,3,8,8,128]{5,4,3,2,1,0:T(8,128)(2,1)S(1)}, bf16[2,2,3,8,8,128]{5,4,3,2,1,0:T(8,128)(2,1)}, u32[]{:S(2)}) copy-start(bf16[2,2,3,8,8,128]{5,4,3,2,1,0:T(8,128)(2,1)} %get-tuple-element.100) | copy-start | bytes 589828
  98.2 11.7 %collective-permute-start.14 = (bf16[96,8,128]{2,1,0:T(8,128)(2,1)S(1)}, bf16[96,8,128]{2,1,0:T(8,128)(2,1)S(1)}, u32[]{:S(2)}, u32[]{:S(2)}) collective-permute-start(bf16[96,8,128]{2,1,0:T(8,128)(2,1)S(1)} %bitcast.33), channel_id=1, source_target_pairs={{1,0},{2,1},{3,2},{0,3},{5,4},{6,5},{7,6},{4,7},{9,8},{10,9},{11,1... | collective-permute-start | bytes 589832 | tf_op jit(solution)/shard_map/ppermute | solution.py:772
  98.3 11.6 %collective-permute-start.13 = (bf16[96,8,128]{2,1,0:T(8,128)(2,1)S(1)}, bf16[96,8,128]{2,1,0:T(8,128)(2,1)S(1)}, u32[]{:S(2)}, u32[]{:S(2)}) collective-permute-start(bf16[96,8,128]{2,1,0:T(8,128)(2,1)S(1)} %bitcast.34), channel_id=1, source_target_pairs={{0,1},{1,2},{2,3},{3,0},{4,5},{5,6},{6,7},{7,4},{8,9},{9,10},{10,1... | collective-permute-start | bytes 589832 | tf_op jit(solution)/shard_map/ppermute | solution.py:772
  123.3 11.2 %collective-permute-start.15 = (bf16[96,8,128]{2,1,0:T(8,128)(2,1)S(1)}, bf16[96,8,128]{2,1,0:T(8,128)(2,1)S(1)}, u32[]{:S(2)}, u32[]{:S(2)}) collective-permute-start(bf16[96,8,128]{2,1,0:T(8,128)(2,1)S(1)} %collective-permute-done.11.refs_1_), channel_id=1, source_target_pairs={{0,1},{1,2},{2,3},{3,0},{4,5},{5,6},{6,7},{7,4},{8,9},{9,10},{10,1... | collective-permute-start | bytes 589832 | tf_op jit(solution)/shard_map/ppermute | solution.py:776
  124.4 11.8 %collective-permute-start.16 = (bf16[96,8,128]{2,1,0:T(8,128)(2,1)S(1)}, bf16[96,8,128]{2,1,0:T(8,128)(2,1)S(1)}, u32[]{:S(2)}, u32[]{:S(2)}) collective-permute-start(bf16[96,8,128]{2,1,0:T(8,128)(2,1)S(1)} %collective-permute-done.14.refs_4_), channel_id=1, source_target_pairs={{1,0},{2,1},{3,2},{0,3},{5,4},{6,5},{7,6},{4,7},{9,8},{10,9},{11,1... | collective-permute-start | bytes 589832 | tf_op jit(solution)/shard_map/ppermute | solution.py:776

commit v7 on v6

--- a/solution.py
+++ b/solution.py
@@ -15,6 +15,7 @@
 HALF = 99
 PACKED = 13
 WEIGHTS = (1.0, 0.5, 0.25)
+AT_ONCE = 4
 HIGH = lax.Precision.HIGHEST
 F32 = jnp.float32
 BF16 = jnp.bfloat16
@@ -128,17 +129,18 @@
 
 
 def inner_all(c_ref, field, sums_ref):
-    def body(j, accs):
-        one, two = field(0, j), field(1, j)
-        new = []
-        for k in range(VECS):
-            vec = c_ref[k * ROWS + j]
-            new.append(accs[2 * k] + vec * one)
-            new.append(accs[2 * k + 1] + vec * two)
-        return tuple(new)
+    def body(step, accs):
+        accs = list(accs)
+        for j in (2 * step, 2 * step + 1):
+            one, two = field(0, j), field(1, j)
+            for k in range(VECS):
+                vec = c_ref[k * ROWS + j]
+                accs[2 * k] = accs[2 * k] + vec * one
+                accs[2 * k + 1] = accs[2 * k + 1] + vec * two
+        return tuple(accs)
 
     zero = jnp.zeros((8, 128), F32)
-    accs = lax.fori_loop(0, ROWS, body, (zero,) * (2 * VECS))
+    accs = lax.fori_loop(0, ROWS // 2, body, (zero,) * (2 * VECS))
     for k in range(VECS):
         for s in range(2):
             sums_ref[s * VECS + k : s * VECS + k + 1] = jnp.sum(
@@ -148,18 +150,21 @@
 
 def inner_pairs(pairs, sums_ref, first):
     count = len(pairs)
-    for s in range(2):
-
-        def body(j, accs, s=s):
-            return tuple(
-                acc + one(s, j) * two(s, j) for acc, (one, two) in zip(accs, pairs)
-            )
-
-        zero = jnp.zeros((8, 128), F32)
-        accs = lax.fori_loop(0, ROWS, body, (zero,) * count)
-        for i in range(count):
-            at = first + s * count + i
-            sums_ref[at : at + 1] = jnp.sum(accs[i], axis=0, keepdims=True)
+
+    def body(step, accs):
+        new = []
+        for s in range(2):
+            for i, (one, two) in enumerate(pairs):
+                acc = accs[s * count + i]
+                for row in range(AT_ONCE):
+                    j = step * AT_ONCE + row
+                    acc = acc + one(s, j) * two(s, j)
+                new.append(acc)
+        return tuple(new)
+
+    accs = lax.fori_loop(0, ROWS // AT_ONCE, body, (jnp.zeros((8, 128), F32),) * (2 * count))
+    for i, acc in enumerate(accs):
+        sums_ref[first + i : first + i + 1] = jnp.sum(acc, axis=0, keepdims=True)
 
 
 def row_of_sums(sums_ref):
@@ -219,14 +224,11 @@
                     x_ref[k * ROWS + j] = pltpu.roll(jnp.where(top, before, after), 4, 0)
         return carry
 
-    lax.fori_loop(0, ROWS, body, 0)
+    lax.fori_loop(0, ROWS, body, 0, unroll=2)
     for d in range(LOCAL):
         for t in range(PACKED - 1):
             near_ref[d * 12 + t] = side_tile(blocks, d, t).astype(F32)
             far_ref[d * 12 + t] = halo_side(halos, d, t)
-
-
-AT_ONCE = 4
 
 
 def plus(total, term):
@@ -445,12 +447,14 @@
     )
     for s in range(2):
 
-        def body(j, carry, s=s):
-            at = s * ROWS + j
-            r_ref[at, :, 128:256] = side_ref[at] + rhs(s, j, slice(0, 16), slice(128, 256))
+        def body(step, carry, s=s):
+            for i in range(AT_ONCE):
+                j = step * AT_ONCE + i
+                at = s * ROWS + j
+                r_ref[at, :, 128:256] = side_ref[at] + rhs(s, j, slice(0, 16), slice(128, 256))
             return carry
 
-        lax.fori_loop(0, ROWS, body, 0)
+        lax.fori_loop(0, ROWS // AT_ONCE, body, 0)
     apply_operator(r_ref, m_ref, q_ref, mask)
     finish_first(fields[0], r_ref, q_ref, sums_ref, out_ref)
 
@@ -500,16 +504,16 @@
     )
     for s in range(2):
 
-        def body(j, carry, s=s):
-            at = s * ROWS + j
-            value = side_ref[at]
-            for half in range(2):
-                rows = slice(half * 8, half * 8 + 8)
-                new = value[rows] + q_scale[s] * q_ref[at, rows, 128:256]
-                u_ref[at, rows, 128:256] = new + r_scale[s] * r_ref[at, rows, 128:256]
+        def body(step, carry, s=s):
+            for i in range(AT_ONCE):
+                at = s * ROWS + step * AT_ONCE + i
+                for half in range(2):
+                    rows = slice(half * 8, half * 8 + 8)
+                    new = side_ref[at, rows] + q_scale[s] * q_ref[at, rows, 128:256]
+                    u_ref[at, rows, 128:256] = new + r_scale[s] * r_ref[at, rows, 128:256]
             return carry
 
-        lax.fori_loop(0, ROWS, body, 0)
+        lax.fori_loop(0, ROWS // AT_ONCE, body, 0)
     apply_operator(u_ref, m_ref, a_ref, mask)
     sums_ref[...] = jnp.zeros_like(sums_ref)
     r, u, a = brick(r_ref), brick(u_ref), brick(a_ref)
@@ -588,19 +592,20 @@
     )
     for s in range(2):
 
-        def body(j, carry, s=s):
-            at = s * ROWS + j
-            value = side_ref[at]
-            for half in range(2):
-                rows = slice(half * 8, half * 8 + 8)
-                new_ref[at, rows, 128:256] = total(s, at, rows, slice(128, 256), value[rows])
-            sol_ref[at] = (
-                scale[s]["sol_r"] * r_ref[at, 0:8, 0:128]
-                + scale[s]["sol_u"] * u_ref[at, 0:8, 0:128]
-            )
+        def body(step, carry, s=s):
+            for i in range(AT_ONCE):
+                at = s * ROWS + step * AT_ONCE + i
+                for half in range(2):
+                    rows = slice(half * 8, half * 8 + 8)
+                    value = side_ref[at, rows]
+                    new_ref[at, rows, 128:256] = total(s, at, rows, slice(128, 256), value)
+                sol_ref[at] = (
+                    scale[s]["sol_r"] * r_ref[at, 0:8, 0:128]
+                    + scale[s]["sol_u"] * u_ref[at, 0:8, 0:128]
+                )
             return carry
 
-        lax.fori_loop(0, ROWS, body, 0)
+        lax.fori_loop(0, ROWS // AT_ONCE, body, 0)
     apply_operator(new_ref, m_ref, q_ref, mask)
     finish_first(fields[0], new_ref, q_ref, sums_ref, out_ref)
 

time: 170 us -> 168 us (0.988)
  Pallas kernels: 39.3 us -> 34.3 us
  waiting for transfers between devices: 20 us -> 22.9 us
    pallas_call x10, Pallas kernels: 39.3 us -> 34.3 us  [call(): pl.pallas_call(kernel, out_shape=outs, in_specs=[pl.BlockSpec(memory_spac...]
  transfers between devices with their start and end apart: 18 -> 18, of which waited for: 7 -> 9; matrix products, arithmetic and copies ran while one was open for 1% -> 1% of each run, Pallas kernels for 18% -> 16%
where the time goes in v7:
time: 168 us; the launch traced here: 167 us
  starting transfers between devices  54.8 us (33%)
  blocking collectives  51.1 us (30%)
  Pallas kernels  34.3 us (20%)
  waiting for transfers between devices  22.9 us (14%)
  local copies, waits for them, and re-layouts  2.18 us (1%)
    all_to_all x4, blocking collectives, exchange(): return lax.all_to_all(value, ('gx', 'gy'), 0, 0)  51.1 us
    pallas_call x10, Pallas kernels, call(): pl.pallas_call(kernel, out_shape=outs, in_specs=[pl.BlockSpec(memory_spac...  34.3 us
    ppermute x4, starting transfers between devices, exchange_x(): return (lax.ppermute(low, 'gx', down), lax.ppermute(high, 'gx', up))  15.8 us
    all_to_all x1, starting transfers between devices, exchange(): return lax.all_to_all(value, ('gx', 'gy'), 0, 0)  9.12 us
    ppermute x1, starting transfers between devices, on_device(): three = lax.ppermute(block, 'tx', left)  6.93 us
    ppermute x1, starting transfers between devices, on_device(): far_high = lax.ppermute(jnp.concatenate([three[CUT:], side]), 'tx', left)  6.71 us
    ppermute x2, waiting for transfers between devices, on_device(): lax.ppermute(piece, 'tx', left)  4.53 us
    ppermute x2, starting transfers between devices, on_device(): after, before = (lax.ppermute(own, 'gy', down), lax.ppermute(own, 'gy', up))  4.5 us
  transfers between devices with their start and end apart: 18, of which 9 were waited for; matrix products, arithmetic and copies ran while one was open for 1% of the time, Pallas kernels for 16%

profile of v7, /device:TPU:1, one launch (start us, length us, event | category | flops | bytes accessed | tf_op | source)
XLA Modules:
  0.0 167.3 jit_solution(668586225590795299)
XLA Ops:
  0.6 1.1 pad_maximum_fusion.block_ref.refs_0_
  1.7 6.9 %collective-permute-start.4 = (bf16[198,8,128]{2,1,0:T(8,128)(2,1)S(1)}, bf16[198,8,128]{2,1,0:T(8,128)(2,1)S(1)}, u32[]{:S(2)}, u32[]{:S(2)}) collective-permute-start(bf16[198,8,128]{2,1,0:T(8,128)(2,1)S(1)} %pad_maximum_fusion.block_ref.refs_0_), channel_id=1, source_target_pairs={{1,0},{2,1},{3,2},{0,3},{5,4},{6,5},{7,6},{4,7},{9,8},{10,9},{11,1... | collective-permute-start | bytes 1216520 | tf_op jit(solution)/shard_map/ppermute | solution.py:712
  8.6 0.3 shard_map.59
  8.9 3.2 %collective-permute-start.1 = (bf16[13,8,128]{2,1,0:T(8,128)(2,1)S(1)}, bf16[13,8,128]{2,1,0:T(8,128)(2,1)S(1)}, u32[]{:S(2)}, u32[]{:S(2)}) collective-permute-start(bf16[13,8,128]{2,1,0:T(8,128)(2,1)S(1)} %shard_map.59), channel_id=1, source_target_pairs={{0,4},{4,8},{8,12},{1,5},{5,9},{9,13},{2,6},{6,10},{10,14},{3,7},{... | collective-permute-start | bytes 79880 | tf_op jit(solution)/shard_map/ppermute | solution.py:714
  12.1 1.3 collective-permute-start
  13.5 3.6 %collective-permute-done = bf16[13,8,128]{2,1,0:T(8,128)(2,1)S(1)} collective-permute-done((bf16[13,8,128]{2,1,0:T(8,128)(2,1)S(1)}, bf16[13,8,128]{2,1,0:T(8,128)(2,1)S(1)}, u32[]{:S(2)}, u32[]{:S(2)}) %collective-permute-start) | collective-permute-done | bytes 26656 | tf_op jit(solution)/shard_map/ppermute | solution.py:714
  17.0 0.1 broadcast_select_fusion.refs_5_.refs_3_.refs_4_
  17.1 3.3 %collective-permute-start.2 = (bf16[13,8,128]{2,1,0:T(8,128)(2,1)S(1)}, bf16[13,8,128]{2,1,0:T(8,128)(2,1)S(1)}, u32[]{:S(2)}, u32[]{:S(2)}) collective-permute-start(bf16[13,8,128]{2,1,0:T(8,128)(2,1)S(1)} %broadcast_select_fusion.refs_5_.refs_3_.refs_4_), channel_id=1, source_target_pairs={{0,2},{1,3},{2,0},{3,1},{4,6},{5,7},{6,4},{7,5},{8,10},{9,11},{10,... | collective-permute-start | bytes 79880 | tf_op jit(solution)/shard_map/ppermute | solution.py:716
  20.4 3.7 %collective-permute-done.2.refs_6_ = bf16[13,8,128]{2,1,0:T(8,128)(2,1)S(1)} collective-permute-done((bf16[13,8,128]{2,1,0:T(8,128)(2,1)S(1)}, bf16[13,8,128]{2,1,0:T(8,128)(2,1)S(1)}, u32[]{:S(2)}, u32[]{:S(2)}) %collective-permute-start.2) | collective-permute-done | bytes 26656 | tf_op jit(solution)/shard_map/ppermute | solution.py:716
  24.2 6.7 %collective-permute-start.6 = (bf16[115,8,128]{2,1,0:T(8,128)(2,1)S(1)}, bf16[115,8,128]{2,1,0:T(8,128)(2,1)S(1)}, u32[]{:S(2)}, u32[]{:S(2)}) collective-permute-start(bf16[115,8,128]{2,1,0:T(8,128)(2,1)S(1)} %pad_maximum_fusion.1), channel_id=1, source_target_pairs={{1,0},{2,1},{3,2},{0,3},{5,4},{6,5},{7,6},{4,7},{9,8},{10,9},{11,1... | collective-permute-start | bytes 706568 | tf_op jit(solution)/shard_map/ppermute | solution.py:719
  30.9 0.0 copy-start.2
  30.9 0.1 collective-permute-start.5
  31.0 1.7 %shard_map.61 = (bf16[310,8,128]{2,1,0:T(8,128)(2,1)}, bf16[310,8,128]{2,1,0:T(8,128)(2,1)}) custom-call(bf16[198,8,128]{2,1,0:T(8,128)(2,1)S(1)} %pad_maximum_fusion.block_ref.refs_0_, bf16[198,8,128]{2,1,0:T(8,128)(2,1)S(1)} %collective-permute-done.3.refs_1_, bf16[198,8,128]{2,1,0:T(8,128)(2,1)S(1)} %collective-permute-done.4.refs_2_, ...), custom_call_target="tpu_custom_call" | custom-call | tf_op jit(solution)/shard_map/pallas_call | solution.py:675
  32.7 5.7 %collective-permute-start.7 = (bf16[310,8,128]{2,1,0:T(8,128)(2,1)}, bf16[310,8,128]{2,1,0:T(8,128)(2,1)S(1)}, u32[]{:S(2)}, u32[]{:S(2)}) collective-permute-start(bf16[310,8,128]{2,1,0:T(8,128)(2,1)} %get-tuple-element.55), channel_id=1, source_target_pairs={{16,0},{32,16},{48,32},{64,48},{80,64},{96,80},{112,96},{128,112},... | collective-permute-start | bytes 1904648 | tf_op jit(solution)/shard_map/ppermute | solution.py:726
  38.4 0.0 copy-start
  38.4 3.1 %collective-permute-start.8 = (bf16[310,8,128]{2,1,0:T(8,128)(2,1)}, bf16[310,8,128]{2,1,0:T(8,128)(2,1)S(1)}, u32[]{:S(2)}, u32[]{:S(2)}) collective-permute-start(bf16[310,8,128]{2,1,0:T(8,128)(2,1)} %get-tuple-element.56), channel_id=1, source_target_pairs={{0,16},{16,32},{32,48},{48,64},{64,80},{80,96},{96,112},{112,128},... | collective-permute-start | bytes 1904648 | tf_op jit(solution)/shard_map/ppermute | solution.py:726
  41.5 2.7 %collective-permute-done.5.refs_3_ = bf16[109,8,128]{2,1,0:T(8,128)(2,1)S(1)} collective-permute-done((bf16[109,8,128]{2,1,0:T(8,128)(2,1)S(1)}, bf16[109,8,128]{2,1,0:T(8,128)(2,1)S(1)}, u32[]{:S(2)}, u32[]{:S(2)}) %collective-permute-start.5) | collective-permute-done | bytes 223264 | tf_op jit(solution)/shard_map/ppermute | solution.py:718
  44.3 1.1 shard_map.62
  45.4 0.7 copy-done.3
  46.1 3.5 %collective-permute-start.9 = (bf16[138,8,128]{2,1,0:T(8,128)(2,1)}, bf16[138,8,128]{2,1,0:T(8,128)(2,1)}, u32[]{:S(2)}, u32[]{:S(2)}) collective-permute-start(bf16[138,8,128]{2,1,0:T(8,128)(2,1)} %get-tuple-element.57), channel_id=1, source_target_pairs={{16,0},{32,16},{48,32},{64,48},{80,64},{96,80},{112,96},{128,112},... | collective-permute-start | bytes 847880 | tf_op jit(solution)/shard_map/ppermute | solution.py:726
  49.6 2.8 %shard_map.60 = f32[64,4,128]{2,1,0:T(4,128)S(1)} custom-call(s32[2]{0:T(128)S(1)} %copy-done.2, bf16[198,8,128]{2,1,0:T(8,128)(2,1)S(1)} %pad_maximum_fusion.block_ref.refs_0_, bf16[198,8,128]{2,1,0:T(8,128)(2,1)S(1)} %collective-permute-done.3.refs_1_, bf16[198,8,128]{2,1,0:T(8,128)(2,1)S(1)} %collective-permute-done.4.refs_2_, ...), custom_call_target="tpu_custom_call" | custom-call | tf_op jit(solution)/shard_map/pallas_call | solution.py:675
  52.3 0.6 copy-done.1
  53.0 9.1 %all-to-all-start = ((f32[64,4,128]{2,1,0:T(4,128)}), f32[64,4,128]{2,1,0:T(4,128)S(1)}, u32[]{:S(2)}, u32[]{:S(2)}) async-start(f32[64,4,128]{2,1,0:T(4,128)} %copy-done.1), calls=%async_computation | async-start | bytes 262144 | tf_op jit(solution)/shard_map/all_to_all | solution.py:690
  62.1 3.5 %collective-permute-start.10 = (bf16[138,8,128]{2,1,0:T(8,128)(2,1)}, bf16[138,8,128]{2,1,0:T(8,128)(2,1)}, u32[]{:S(2)}, u32[]{:S(2)}) collective-permute-start(bf16[138,8,128]{2,1,0:T(8,128)(2,1)} %copy-done.3), channel_id=1, source_target_pairs={{0,16},{16,32},{32,48},{48,64},{64,80},{80,96},{96,112},{112,128},... | collective-permute-start | bytes 847880 | tf_op jit(solution)/shard_map/ppermute | solution.py:726
  65.7 0.8 fusion
  66.5 4.2 %all-to-all-done.got_ref = f32[64,4,128]{2,1,0:T(4,128)S(1)} async-done(((f32[64,4,128]{2,1,0:T(4,128)}), f32[64,4,128]{2,1,0:T(4,128)S(1)}, u32[]{:S(2)}, u32[]{:S(2)}) %all-to-all-start) | async-done | bytes 131104 | tf_op jit(solution)/shard_map/all_to_all | solution.py:690
  70.7 0.1 collective-permute-start.12
  70.8 0.0 collective-permute-done.9.refs_9_
  70.8 2.2 %collective-permute-start.11 = (bf16[96,8,128]{2,1,0:T(8,128)(2,1)}, bf16[96,8,128]{2,1,0:T(8,128)(2,1)S(1)}, u32[]{:S(2)}, u32[]{:S(2)}) collective-permute-start(bf16[96,8,128]{2,1,0:T(8,128)(2,1)} %bitcast.36), channel_id=1, source_target_pairs={{0,1},{1,2},{2,3},{3,0},{4,5},{5,6},{6,7},{7,4},{8,9},{9,10},{10,1... | collective-permute-start | bytes 589832 | tf_op jit(solution)/shard_map/ppermute | solution.py:759
  73.1 2.8 %shard_map.63 = (f32[24,16,256]{2,1,0:T(8,128)S(1)}, f32[48,16,256]{2,1,0:T(8,128)S(1)}, f32[768,8,128]{2,1,0:T(8,128)S(1)}, f32[768,8,128]{2,1,0:T(8,128)S(1)},...) custom-call(s32[2]{0:T(128)S(1)} %copy-done.2, bf16[198,8,128]{2,1,0:T(8,128)(2,1)S(1)} %pad_maximum_fusion.block_ref.refs_0_, ...), custom_call_target="tpu_custom_call" | custom-call | tf_op jit(solution)/shard_map/pallas_call | solution.py:675
  75.9 6.7 %shard_map.64 = (f32[96,16,256]{2,1,0:T(8,128)S(1)}, f32[96,16,256]{2,1,0:T(8,128)S(1)}, f32[16,128]{1,0:T(8,128)S(1)}, f32[16,128]{1,0:T(8,128)S(1)}, f32[64,128]{1,0:T(8,128)S(1)}) custom-call(f32[64,4,128]{2,1,0:T(4,128)S(1)} %all-to-all-done.got_ref, f32[768,8,128]{2,1,0:T(8,128)S(1)} %get-tuple-element.59.refs_0_.c_ref, ...), custom_call_target="tpu_custom_call" | custom-call | tf_op jit(solution)/shard_map/pallas_call | solution.py:675
  82.5 0.1 collective-permute-done.12.refs_3_
  82.7 13.9 %all_to_all.25 = f32[64,1,128]{2,1,0:T(1,128)S(1)} all-to-all(f32[64,1,128]{2,1,0:T(1,128)S(1)} %bitcast.29), channel_id=1, replica_groups=mesh['gx'=16,'gy'=4,'tx'=4] {'gx','gy'}, dimensions={0} | all-to-all | bytes 65536 | tf_op jit(solution)/shard_map/all_to_all | solution.py:690
  96.6 0.2 collective-permute-start.14
  96.8 2.2 %collective-permute-start.13 = (bf16[96,8,128]{2,1,0:T(8,128)(2,1)S(1)}, bf16[96,8,128]{2,1,0:T(8,128)(2,1)S(1)}, u32[]{:S(2)}, u32[]{:S(2)}) collective-permute-start(bf16[96,8,128]{2,1,0:T(8,128)(2,1)S(1)} %bitcast.34), channel_id=1, source_target_pairs={{0,1},{1,2},{2,3},{3,0},{4,5},{5,6},{6,7},{7,4},{8,9},{9,10},{10,1... | collective-permute-start | bytes 589832 | tf_op jit(solution)/shard_map/ppermute | solution.py:777
  99.0 5.0 %shard_map.65 = (f32[96,16,256]{2,1,0:T(8,128)S(1)}, f32[96,16,256]{2,1,0:T(8,128)S(1)}, f32[16,128]{1,0:T(8,128)S(1)}, f32[64,128]{1,0:T(8,128)S(1)}) custom-call(f32[64,128]{1,0:T(8,128)S(1)} %bitcast.26, f32[768,8,128]{2,1,0:T(8,128)S(1)} %get-tuple-element.59.refs_0_.c_ref, f32[768,8,128]{2,1,0:T(8,128)S(1)} %get-tuple-element.60.refs_1_, ...), custom_call_target="tpu_custom_call" | custom-call | tf_op jit(solution)/shard_map/pallas_call | solution.py:675
  103.9 4.4 %collective-permute-done.14.refs_4_ = bf16[96,8,128]{2,1,0:T(8,128)(2,1)S(1)} collective-permute-done((bf16[96,8,128]{2,1,0:T(8,128)(2,1)S(1)}, bf16[96,8,128]{2,1,0:T(8,128)(2,1)S(1)}, u32[]{:S(2)}, u32[]{:S(2)}) %collective-permute-start.14) | collective-permute-done | bytes 196640 | tf_op jit(solution)/shard_map/ppermute | solution.py:777
  108.3 0.5 collective-permute-done.13.refs_2_
  108.8 13.0 %all_to_all.26 = f32[64,1,128]{2,1,0:T(1,128)S(1)} all-to-all(f32[64,1,128]{2,1,0:T(1,128)S(1)} %bitcast.30), channel_id=1, replica_groups=mesh['gx'=16,'gy'=4,'tx'=4] {'gx','gy'}, dimensions={0} | all-to-all | bytes 65536 | tf_op jit(solution)/shard_map/all_to_all | solution.py:690
  121.8 1.0 collective-permute-start.15
  122.9 2.5 %collective-permute-start.16 = (bf16[96,8,128]{2,1,0:T(8,128)(2,1)S(1)}, bf16[96,8,128]{2,1,0:T(8,128)(2,1)S(1)}, u32[]{:S(2)}, u32[]{:S(2)}) collective-permute-start(bf16[96,8,128]{2,1,0:T(8,128)(2,1)S(1)} %collective-permute-done.14.refs_4_), channel_id=1, source_target_pairs={{1,0},{2,1},{3,2},{0,3},{5,4},{6,5},{7,6},{4,7},{9,8},{10,9},{11,1... | collective-permute-start | bytes 589832 | tf_op jit(solution)/shard_map/ppermute | solution.py:781
  125.4 5.7 %shard_map.66 = (f32[96,16,256]{2,1,0:T(8,128)S(1)}, f32[96,16,256]{2,1,0:T(8,128)S(1)}, f32[96,8,128]{2,1,0:T(8,128)S(1)}, f32[16,128]{1,0:T(8,128)S(1)}, f32[64,128]{1,0:T(8,128)S(1)}) custom-call(f32[64,128]{1,0:T(8,128)S(1)} %bitcast.24, f32[768,8,128]{2,1,0:T(8,128)S(1)} %get-tuple-element.59.refs_0_.c_ref, ...), custom_call_target="tpu_custom_call" | custom-call | tf_op jit(solution)/shard_map/pallas_call | solution.py:675
  131.1 1.2 collective-permute-done.15.refs_5_
  132.3 2.4 %collective-permute-done.16.refs_6_ = bf16[96,8,128]{2,1,0:T(8,128)(2,1)S(1)} collective-permute-done((bf16[96,8,128]{2,1,0:T(8,128)(2,1)S(1)}, bf16[96,8,128]{2,1,0:T(8,128)(2,1)S(1)}, u32[]{:S(2)}, u32[]{:S(2)}) %collective-permute-start.16) | collective-permute-done | bytes 196640 | tf_op jit(solution)/shard_map/ppermute | solution.py:781
  134.8 12.0 %all_to_all.27 = f32[64,1,128]{2,1,0:T(1,128)S(1)} all-to-all(f32[64,1,128]{2,1,0:T(1,128)S(1)} %bitcast.28), channel_id=1, replica_groups=mesh['gx'=16,'gy'=4,'tx'=4] {'gx','gy'}, dimensions={0} | all-to-all | bytes 65536 | tf_op jit(solution)/shard_map/all_to_all | solution.py:690
  146.7 5.0 %shard_map.67 = (f32[96,16,256]{2,1,0:T(8,128)S(1)}, f32[96,16,256]{2,1,0:T(8,128)S(1)}, f32[16,128]{1,0:T(8,128)S(1)}, f32[64,128]{1,0:T(8,128)S(1)}) custom-call(f32[64,128]{1,0:T(8,128)S(1)} %bitcast.27, f32[768,8,128]{2,1,0:T(8,128)S(1)} %get-tuple-element.59.refs_0_.c_ref, f32[768,8,128]{2,1,0:T(8,128)S(1)} %get-tuple-element.60.refs_1_, ...), custom_call_target="tpu_custom_call" | custom-call | tf_op jit(solution)/shard_map/pallas_call | solution.py:675
  151.7 12.2 %all_to_all.28 = f32[64,1,128]{2,1,0:T(1,128)S(1)} all-to-all(f32[64,1,128]{2,1,0:T(1,128)S(1)} %bitcast.31), channel_id=1, replica_groups=mesh['gx'=16,'gy'=4,'tx'=4] {'gx','gy'}, dimensions={0} | all-to-all | bytes 65536 | tf_op jit(solution)/shard_map/all_to_all | solution.py:690
  163.9 3.4 %shard_map.68 = (f32[96,8,128]{2,1,0:T(8,128)}, f32[96,8,128]{2,1,0:T(8,128)}) custom-call(f32[64,128]{1,0:T(8,128)S(1)} %bitcast.25, f32[768,8,128]{2,1,0:T(8,128)S(1)} %get-tuple-element.59.refs_0_.c_ref, bf16[192,8,128]{2,1,0:T(8,128)(2,1)S(1)} %bitcast.23, bf16[96,8,128]{2,1,0:T(8,128)(2,1)S(1)} %collective-permute-done.11.refs_1_, ...), custom_call_target="tpu_custom_call" | custom-call | tf_op jit(solution)/shard_map/pallas_call | solution.py:675
  (20 shorter events, 0.1 us)
Async XLA Ops:
  1.7 22.4 %collective-permute-start.4 = (bf16[198,8,128]{2,1,0:T(8,128)(2,1)S(1)}, bf16[198,8,128]{2,1,0:T(8,128)(2,1)S(1)}, u32[]{:S(2)}, u32[]{:S(2)}) collective-permute-start(bf16[198,8,128]{2,1,0:T(8,128)(2,1)S(1)} %pad_maximum_fusion.block_ref.refs_0_), channel_id=1, source_target_pairs={{1,0},{2,1},{3,2},{0,3},{5,4},{6,5},{7,6},{4,7},{9,8},{10,9},{11,1... | collective-permute-start | bytes 1216520 | tf_op jit(solution)/shard_map/ppermute | solution.py:712
  8.6 15.5 %collective-permute-start.3 = (bf16[198,8,128]{2,1,0:T(8,128)(2,1)S(1)}, bf16[198,8,128]{2,1,0:T(8,128)(2,1)S(1)}, u32[]{:S(2)}, u32[]{:S(2)}) collective-permute-start(bf16[198,8,128]{2,1,0:T(8,128)(2,1)S(1)} %pad_maximum_fusion.block_ref.refs_0_), channel_id=1, source_target_pairs={{0,1},{1,2},{2,3},{3,0},{4,5},{5,6},{6,7},{7,4},{8,9},{9,10},{10,1... | collective-permute-start | bytes 1216520 | tf_op jit(solution)/shard_map/ppermute | solution.py:711
  8.9 4.5 %collective-permute-start.1 = (bf16[13,8,128]{2,1,0:T(8,128)(2,1)S(1)}, bf16[13,8,128]{2,1,0:T(8,128)(2,1)S(1)}, u32[]{:S(2)}, u32[]{:S(2)}) collective-permute-start(bf16[13,8,128]{2,1,0:T(8,128)(2,1)S(1)} %shard_map.59), channel_id=1, source_target_pairs={{0,4},{4,8},{8,12},{1,5},{5,9},{9,13},{2,6},{6,10},{10,14},{3,7},{... | collective-permute-start | bytes 79880 | tf_op jit(solution)/shard_map/ppermute | solution.py:714
  12.1 4.9 %collective-permute-start = (bf16[13,8,128]{2,1,0:T(8,128)(2,1)S(1)}, bf16[13,8,128]{2,1,0:T(8,128)(2,1)S(1)}, u32[]{:S(2)}, u32[]{:S(2)}) collective-permute-start(bf16[13,8,128]{2,1,0:T(8,128)(2,1)S(1)} %shard_map.59), channel_id=1, source_target_pairs={{4,0},{8,4},{12,8},{5,1},{9,5},{13,9},{6,2},{10,6},{14,10},{7,3},{... | collective-permute-start | bytes 79880 | tf_op jit(solution)/shard_map/ppermute | solution.py:714
  17.1 7.0 %collective-permute-start.2 = (bf16[13,8,128]{2,1,0:T(8,128)(2,1)S(1)}, bf16[13,8,128]{2,1,0:T(8,128)(2,1)S(1)}, u32[]{:S(2)}, u32[]{:S(2)}) collective-permute-start(bf16[13,8,128]{2,1,0:T(8,128)(2,1)S(1)} %broadcast_select_fusion.refs_5_.refs_3_.refs_4_), channel_id=1, source_target_pairs={{0,2},{1,3},{2,0},{3,1},{4,6},{5,7},{6,4},{7,5},{8,10},{9,11},{10,... | collective-permute-start | bytes 79880 | tf_op jit(solution)/shard_map/ppermute | solution.py:716
  24.2 20.1 %collective-permute-start.6 = (bf16[115,8,128]{2,1,0:T(8,128)(2,1)S(1)}, bf16[115,8,128]{2,1,0:T(8,128)(2,1)S(1)}, u32[]{:S(2)}, u32[]{:S(2)}) collective-permute-start(bf16[115,8,128]{2,1,0:T(8,128)(2,1)S(1)} %pad_maximum_fusion.1), channel_id=1, source_target_pairs={{1,0},{2,1},{3,2},{0,3},{5,4},{6,5},{7,6},{4,7},{9,8},{10,9},{11,1... | collective-permute-start | bytes 706568 | tf_op jit(solution)/shard_map/ppermute | solution.py:719
  30.9 18.7 %copy-start.2 = (s32[2]{0:T(128)S(1)}, s32[2]{0:T(128)}, u32[]{:S(2)}) copy-start(s32[2]{0:T(128)} %src_ref.3) | copy-start | bytes 28
  30.9 13.3 %collective-permute-start.5 = (bf16[109,8,128]{2,1,0:T(8,128)(2,1)S(1)}, bf16[109,8,128]{2,1,0:T(8,128)(2,1)S(1)}, u32[]{:S(2)}, u32[]{:S(2)}) collective-permute-start(bf16[109,8,128]{2,1,0:T(8,128)(2,1)S(1)} %pad_maximum_fusion.2), channel_id=1, source_target_pairs={{0,1},{1,2},{2,3},{3,0},{4,5},{5,6},{6,7},{7,4},{8,9},{9,10},{10,1... | collective-permute-start | bytes 669704 | tf_op jit(solution)/shard_map/ppermute | solution.py:718
  32.7 40.4 %collective-permute-start.7 = (bf16[310,8,128]{2,1,0:T(8,128)(2,1)}, bf16[310,8,128]{2,1,0:T(8,128)(2,1)S(1)}, u32[]{:S(2)}, u32[]{:S(2)}) collective-permute-start(bf16[310,8,128]{2,1,0:T(8,128)(2,1)} %get-tuple-element.55), channel_id=1, source_target_pairs={{16,0},{32,16},{48,32},{64,48},{80,64},{96,80},{112,96},{128,112},... | collective-permute-start | bytes 1904648 | tf_op jit(solution)/shard_map/ppermute | solution.py:726
  38.4 27.3 %copy-start = (bf16[4,2,3,8,8,128]{5,4,3,2,1,0:T(8,128)(2,1)S(1)}, bf16[4,2,3,8,8,128]{5,4,3,2,1,0:T(8,128)(2,1)}, u32[]{:S(2)}) copy-start(bf16[4,2,3,8,8,128]{5,4,3,2,1,0:T(8,128)(2,1)} %param.5) | copy-start | bytes 1179652
  38.4 34.7 %collective-permute-start.8 = (bf16[310,8,128]{2,1,0:T(8,128)(2,1)}, bf16[310,8,128]{2,1,0:T(8,128)(2,1)S(1)}, u32[]{:S(2)}, u32[]{:S(2)}) collective-permute-start(bf16[310,8,128]{2,1,0:T(8,128)(2,1)} %get-tuple-element.56), channel_id=1, source_target_pairs={{0,16},{16,32},{32,48},{48,64},{64,80},{80,96},{96,112},{112,128},... | collective-permute-start | bytes 1904648 | tf_op jit(solution)/shard_map/ppermute | solution.py:726
  45.4 0.7 copy-start.3
  46.1 24.8 %collective-permute-start.9 = (bf16[138,8,128]{2,1,0:T(8,128)(2,1)}, bf16[138,8,128]{2,1,0:T(8,128)(2,1)}, u32[]{:S(2)}, u32[]{:S(2)}) collective-permute-start(bf16[138,8,128]{2,1,0:T(8,128)(2,1)} %get-tuple-element.57), channel_id=1, source_target_pairs={{16,0},{32,16},{48,32},{64,48},{80,64},{96,80},{112,96},{128,112},... | collective-permute-start | bytes 847880 | tf_op jit(solution)/shard_map/ppermute | solution.py:726
  52.3 0.7 copy-start.1
  53.0 17.7 %all-to-all-start = ((f32[64,4,128]{2,1,0:T(4,128)}), f32[64,4,128]{2,1,0:T(4,128)S(1)}, u32[]{:S(2)}, u32[]{:S(2)}) async-start(f32[64,4,128]{2,1,0:T(4,128)} %copy-done.1), calls=%async_computation | async-start | bytes 262144 | tf_op jit(solution)/shard_map/all_to_all | solution.py:690
  62.1 10.9 %collective-permute-start.10 = (bf16[138,8,128]{2,1,0:T(8,128)(2,1)}, bf16[138,8,128]{2,1,0:T(8,128)(2,1)}, u32[]{:S(2)}, u32[]{:S(2)}) collective-permute-start(bf16[138,8,128]{2,1,0:T(8,128)(2,1)} %copy-done.3), channel_id=1, source_target_pairs={{0,16},{16,32},{32,48},{48,64},{64,80},{80,96},{96,112},{112,128},... | collective-permute-start | bytes 847880 | tf_op jit(solution)/shard_map/ppermute | solution.py:726
  70.7 12.0 %collective-permute-start.12 = (bf16[96,8,128]{2,1,0:T(8,128)(2,1)}, bf16[96,8,128]{2,1,0:T(8,128)(2,1)S(1)}, u32[]{:S(2)}, u32[]{:S(2)}) collective-permute-start(bf16[96,8,128]{2,1,0:T(8,128)(2,1)} %bitcast.35), channel_id=1, source_target_pairs={{1,0},{2,1},{3,2},{0,3},{5,4},{6,5},{7,6},{4,7},{9,8},{10,9},{11,1... | collective-permute-start | bytes 589832 | tf_op jit(solution)/shard_map/ppermute | solution.py:759
  70.8 11.9 %collective-permute-start.11 = (bf16[96,8,128]{2,1,0:T(8,128)(2,1)}, bf16[96,8,128]{2,1,0:T(8,128)(2,1)S(1)}, u32[]{:S(2)}, u32[]{:S(2)}) collective-permute-start(bf16[96,8,128]{2,1,0:T(8,128)(2,1)} %bitcast.36), channel_id=1, source_target_pairs={{0,1},{1,2},{2,3},{3,0},{4,5},{5,6},{6,7},{7,4},{8,9},{9,10},{10,1... | collective-permute-start | bytes 589832 | tf_op jit(solution)/shard_map/ppermute | solution.py:759
  75.9 20.7 %copy-start.4 = (bf16[2,2,3,8,8,128]{5,4,3,2,1,0:T(8,128)(2,1)S(1)}, bf16[2,2,3,8,8,128]{5,4,3,2,1,0:T(8,128)(2,1)}, u32[]{:S(2)}) copy-start(bf16[2,2,3,8,8,128]{5,4,3,2,1,0:T(8,128)(2,1)} %get-tuple-element.100) | copy-start | bytes 589828
  96.6 11.7 %collective-permute-start.14 = (bf16[96,8,128]{2,1,0:T(8,128)(2,1)S(1)}, bf16[96,8,128]{2,1,0:T(8,128)(2,1)S(1)}, u32[]{:S(2)}, u32[]{:S(2)}) collective-permute-start(bf16[96,8,128]{2,1,0:T(8,128)(2,1)S(1)} %bitcast.33), channel_id=1, source_target_pairs={{1,0},{2,1},{3,2},{0,3},{5,4},{6,5},{7,6},{4,7},{9,8},{10,9},{11,1... | collective-permute-start | bytes 589832 | tf_op jit(solution)/shard_map/ppermute | solution.py:777
  96.8 12.0 %collective-permute-start.13 = (bf16[96,8,128]{2,1,0:T(8,128)(2,1)S(1)}, bf16[96,8,128]{2,1,0:T(8,128)(2,1)S(1)}, u32[]{:S(2)}, u32[]{:S(2)}) collective-permute-start(bf16[96,8,128]{2,1,0:T(8,128)(2,1)S(1)} %bitcast.34), channel_id=1, source_target_pairs={{0,1},{1,2},{2,3},{3,0},{4,5},{5,6},{6,7},{7,4},{8,9},{9,10},{10,1... | collective-permute-start | bytes 589832 | tf_op jit(solution)/shard_map/ppermute | solution.py:777
  121.8 10.5 %collective-permute-start.15 = (bf16[96,8,128]{2,1,0:T(8,128)(2,1)S(1)}, bf16[96,8,128]{2,1,0:T(8,128)(2,1)S(1)}, u32[]{:S(2)}, u32[]{:S(2)}) collective-permute-start(bf16[96,8,128]{2,1,0:T(8,128)(2,1)S(1)} %collective-permute-done.11.refs_1_), channel_id=1, source_target_pairs={{0,1},{1,2},{2,3},{3,0},{4,5},{5,6},{6,7},{7,4},{8,9},{9,10},{10,1... | collective-permute-start | bytes 589832 | tf_op jit(solution)/shard_map/ppermute | solution.py:781
  122.9 11.9 %collective-permute-start.16 = (bf16[96,8,128]{2,1,0:T(8,128)(2,1)S(1)}, bf16[96,8,128]{2,1,0:T(8,128)(2,1)S(1)}, u32[]{:S(2)}, u32[]{:S(2)}) collective-permute-start(bf16[96,8,128]{2,1,0:T(8,128)(2,1)S(1)} %collective-permute-done.14.refs_4_), channel_id=1, source_target_pairs={{1,0},{2,1},{3,2},{0,3},{5,4},{6,5},{7,6},{4,7},{9,8},{10,9},{11,1... | collective-permute-start | bytes 589832 | tf_op jit(solution)/shard_map/ppermute | solution.py:781

commit v8 on v7

--- a/solution.py
+++ b/solution.py
@@ -77,20 +77,17 @@
         out_ref[tile] = picked.astype(BF16)
 
 
-EARLY, LATE = (0, 1, 3), (2,)
-EARLY_SIDES, LATE_SIDES = (0,), (1, 2, 3)
+GROUP = (0, 1, 2, 3)
 
 
 def halo_row(halos, d, row):
-    ref = 2 if d == 2 else 0
-    at = (0 if d == 2 else EARLY.index(d)) * HALF + row
-    return halos[ref][at].astype(F32), halos[ref + 1][at].astype(F32)
+    at = d * HALF + row
+    return halos[0][at].astype(F32), halos[1][at].astype(F32)
 
 
 def halo_side(halos, d, tile):
-    ref = 0 if d == 0 else 2
-    at = (len(EARLY) * HALF if d == 0 else HALF + LATE_SIDES.index(d) * PACKED) + tile
-    after, before = halos[ref][at].astype(F32), halos[ref + 1][at].astype(F32)
+    at = LOCAL * HALF + d * PACKED + tile
+    after, before = halos[0][at].astype(F32), halos[1][at].astype(F32)
     return jnp.where(iota((8, 128), 1) % 8 < 4, after, before)
 
 
@@ -378,7 +375,7 @@
 
 
 def prepare_kernel(size_x, size_y, src_ref, *refs):
-    blocks, halos, refs = refs[:BLOCKS], refs[BLOCKS : BLOCKS + 4], refs[BLOCKS + 4 :]
+    blocks, halos, refs = refs[:BLOCKS], refs[BLOCKS : BLOCKS + 2], refs[BLOCKS + 2 :]
     m_ref, rhs_ref, fields = refs[0], refs[1], refs[2:]
     unpack_once(blocks, halos, *fields)
     x_pos, y_pos, mask = grid_mask(size_x, size_y)
@@ -612,14 +609,12 @@
 
 def basis_row(basis, d, kl, j):
     row = kl * ROWS + j
-    if d == 0:
-        return basis[0][row].astype(F32)
-    first = {1: 1, 3: 3, 2: 5}[d]
+    first = (0, 2, 6, 4)[d]
     return basis[first][row].astype(F32) if kl < 2 else basis[first + 1][row - CUT].astype(F32)
 
 
 def last_kernel(got_ref, c_ref, *refs):
-    basis, refs = refs[:7], refs[7:]
+    basis, refs = refs[:8], refs[8:]
     r_ref, u_ref, a_ref, inv_ref, old_ref, sol_ref = refs[:6]
     solution_ref, residual_ref = refs[6:]
     row = jnp.sum(got_ref[...], axis=0, keepdims=True)
@@ -714,7 +709,10 @@
     after, before = lax.ppermute(own, "gy", down), lax.ppermute(own, "gy", up)
     side = jnp.where(lax.broadcasted_iota(jnp.int32, own.shape, 1) < 4, after, before)
     far_side = lax.ppermute(side, "tx", [(i, (i + 2) % LOCAL) for i in range(LOCAL)])
-    far_side, one, three = tied(far_side, one, three)
+    own_basis = basis.reshape(LOCAL * ROWS, 8, 128)
+    far_side, one, three, basis_low, basis_high = tied(
+        far_side, one, three, own_basis[:CUT], own_basis[CUT:]
+    )
     far_low = lax.ppermute(jnp.concatenate([one[:CUT], side]), "tx", right)
     far_high = lax.ppermute(jnp.concatenate([three[CUT:], side]), "tx", left)
     up, down = steps("gx")
@@ -725,10 +723,9 @@
         low, high = call(functools.partial(pack_x_kernel, group, sides), (half, half), sources)
         return lax.ppermute(low, "gx", down), lax.ppermute(high, "gx", up)
 
-    early = exchange_x(EARLY, EARLY_SIDES, (block, one, three, side, side, side))
     blocks = (block, one, three, far_low, far_high, side, far_side)
 
-    late = exchange_x(LATE, LATE_SIDES, blocks)
+    halos = exchange_x(GROUP, GROUP, blocks)
 
     sums = pltpu.VMEM((128, 128), F32)
     side_scratch = pltpu.VMEM((2 * ROWS, 16, 128), F32)
@@ -744,18 +741,17 @@
     m, rhs, *fields = call(
         functools.partial(prepare_kernel, size_x, size_y),
         (shape(24, 16, 256), shape(ROWS, 16, 256), whole, whole, tiles, tiles),
-        (src_cell, *blocks, *early, *late),
+        (src_cell, *blocks, *halos),
         smem=1,
     )
     wide = shape(2 * ROWS, 16, 256)
     line = shape(peers, 128)
     small = shape(VECS, 128)
-    own_basis = basis.reshape(LOCAL * ROWS, 8, 128)
 
     def total(value):
         return exchange(value.reshape(peers, 1, 128)).reshape(peers, 128)
 
-    got, piece = tied(got, own_basis[:CUT])
+    got, piece = tied(got, basis_low)
     one_low, three_low = lax.ppermute(piece, "tx", right), lax.ppermute(piece, "tx", left)
     r, q, inverse, state, sent = call(
         functools.partial(begin_kernel, size_x, size_y),
@@ -773,7 +769,7 @@
         )
 
     sent, one_low, three_low = tied(sent, one_low, three_low)
-    got, piece = tied(total(sent), own_basis[CUT:])
+    got, piece = tied(total(sent), basis_high)
     one_high, three_high = lax.ppermute(piece, "tx", right), lax.ppermute(piece, "tx", left)
     u, a, state, sent = first(r, q, state, got)
     sent, one_high, three_high = tied(sent, one_high, three_high)
@@ -787,7 +783,7 @@
     )
     sent, two_low, two_high = tied(sent, two_low, two_high)
     u, a, state, sent = first(r, q, state, total(sent))
-    bases = (own_basis, one_low, one_high, three_low, three_high, two_low, two_high)
+    bases = (basis_low, basis_high, one_low, one_high, three_low, three_high, two_low, two_high)
     narrow = shape(2 * ROWS, 8, 128)
     field, residual = call(
         last_kernel,

time: 168 us -> 172 us (1.024)
  blocking collectives: 51.1 us -> 67.6 us
  starting transfers between devices: 54.8 us -> 42.2 us
  waiting for transfers between devices: 22.9 us -> 28 us
  Pallas kernels: 34.3 us -> 32.1 us
  local copies, waits for them, and re-layouts: 2.18 us -> 0.07 us
    all_to_all x4 -> x5, blocking collectives: 51.1 us -> 67.6 us  [exchange(): return lax.all_to_all(value, ('gx', 'gy'), 0, 0)]
    all_to_all x1 -> x0, starting transfers between devices: 9.12 us -> none  [exchange(): return lax.all_to_all(value, ('gx', 'gy'), 0, 0)]
    ppermute x1, waiting for transfers between devices: 3.71 us -> 10.5 us  [on_device(): lax.ppermute(side, 'tx', [(i, (i + 2) % LOCAL) for i in range(LOCAL)])]
    all_to_all x1 -> x0, waiting for transfers between devices: 4.22 us -> none  [exchange(): return lax.all_to_all(value, ('gx', 'gy'), 0, 0)]
    ppermute x1, waiting for transfers between devices: 2.72 us -> 6.79 us  [on_device(): far_low = lax.ppermute(jnp.concatenate([one[:CUT], side]), 'tx', right)]
    ppermute x2, waiting for transfers between devices: 3.57 us -> 0.01 us  [on_device(): after, before = (lax.ppermute(own, 'gy', down), lax.ppermute(own, 'gy', up))]
    ppermute x2, starting transfers between devices: 0.31 us -> 3.33 us  [on_device(): lax.ppermute(piece, 'tx', left)]
    ppermute x4 -> x2, starting transfers between devices: 15.8 us -> 13.3 us  [exchange_x(): return (lax.ppermute(low, 'gx', down), lax.ppermute(high, 'gx', up))]
  transfers between devices with their start and end apart: 18 -> 15, of which waited for: 9 -> 8; matrix products, arithmetic and copies ran while one was open for 1% -> 0% of each run, Pallas kernels for 16% -> 13%
where the time goes in v8:
time: 172 us
  blocking collectives  67.6 us (39%)
  starting transfers between devices  42.2 us (25%)
  Pallas kernels  32.1 us (19%)
  waiting for transfers between devices  28 us (16%)
    all_to_all x5, blocking collectives, exchange(): return lax.all_to_all(value, ('gx', 'gy'), 0, 0)  67.6 us
    pallas_call x9, Pallas kernels, call(): pl.pallas_call(kernel, out_shape=outs, in_specs=[pl.BlockSpec(memory_spac...  32.1 us
    ppermute x2, starting transfers between devices, exchange_x(): return (lax.ppermute(low, 'gx', down), lax.ppermute(high, 'gx', up))  13.3 us
    ppermute x1, waiting for transfers between devices, on_device(): lax.ppermute(side, 'tx', [(i, (i + 2) % LOCAL) for i in range(LOCAL)])  10.5 us
    ppermute x1, waiting for transfers between devices, on_device(): far_low = lax.ppermute(jnp.concatenate([one[:CUT], side]), 'tx', right)  6.79 us
    ppermute x1, starting transfers between devices, on_device(): three = lax.ppermute(block, 'tx', left)  6.1 us
    ppermute x2, starting transfers between devices, on_device(): after, before = (lax.ppermute(own, 'gy', down), lax.ppermute(own, 'gy', up))  5.33 us
    ppermute x1, starting transfers between devices, on_device(): far_high = lax.ppermute(jnp.concatenate([three[CUT:], side]), 'tx', left)  4.39 us
  transfers between devices with their start and end apart: 15, of which 8 were waited for; matrix products, arithmetic and copies ran while one was open for 0% of the time, Pallas kernels for 13%

profile of v8, /device:TPU:1, one launch (start us, length us, event | category | flops | bytes accessed | tf_op | source)
XLA Modules:
  0.0 172.0 jit_solution(14307991083575255005)
XLA Ops:
  0.6 0.0 copy-start.1
  0.6 1.1 pad_maximum_fusion.block_ref.refs_0_
  1.7 0.3 shard_map.59
  2.1 4.0 %collective-permute-start.1 = (bf16[13,8,128]{2,1,0:T(8,128)(2,1)S(1)}, bf16[13,8,128]{2,1,0:T(8,128)(2,1)S(1)}, u32[]{:S(2)}, u32[]{:S(2)}) collective-permute-start(bf16[13,8,128]{2,1,0:T(8,128)(2,1)S(1)} %shard_map.59), channel_id=1, source_target_pairs={{0,4},{4,8},{8,12},{1,5},{5,9},{9,13},{2,6},{6,10},{10,14},{3,7},{... | collective-permute-start | bytes 79880 | tf_op jit(solution)/shard_map/ppermute | solution.py:709
  6.1 1.3 collective-permute-start
  7.4 6.1 %collective-permute-start.4 = (bf16[198,8,128]{2,1,0:T(8,128)(2,1)S(1)}, bf16[198,8,128]{2,1,0:T(8,128)(2,1)S(1)}, u32[]{:S(2)}, u32[]{:S(2)}) collective-permute-start(bf16[198,8,128]{2,1,0:T(8,128)(2,1)S(1)} %pad_maximum_fusion.block_ref.refs_0_), channel_id=1, source_target_pairs={{1,0},{2,1},{3,2},{0,3},{5,4},{6,5},{7,6},{4,7},{9,8},{10,9},{11,1... | collective-permute-start | bytes 1216520 | tf_op jit(solution)/shard_map/ppermute | solution.py:707
  13.5 0.0 collective-permute-start.3
  13.5 0.0 collective-permute-done.1
  13.5 0.0 collective-permute-done
  13.5 0.1 broadcast_select_fusion.refs_5_
  13.6 4.1 %collective-permute-start.2 = (bf16[13,8,128]{2,1,0:T(8,128)(2,1)S(1)}, bf16[13,8,128]{2,1,0:T(8,128)(2,1)S(1)}, u32[]{:S(2)}, u32[]{:S(2)}) collective-permute-start(bf16[13,8,128]{2,1,0:T(8,128)(2,1)S(1)} %broadcast_select_fusion.refs_5_), channel_id=1, source_target_pairs={{0,2},{1,3},{2,0},{3,1},{4,6},{5,7},{6,4},{7,5},{8,10},{9,11},{10,... | collective-permute-start | bytes 79880 | tf_op jit(solution)/shard_map/ppermute | solution.py:711
  17.7 10.5 %collective-permute-done.2.refs_6_ = bf16[13,8,128]{2,1,0:T(8,128)(2,1)S(1)} collective-permute-done((bf16[13,8,128]{2,1,0:T(8,128)(2,1)S(1)}, bf16[13,8,128]{2,1,0:T(8,128)(2,1)S(1)}, u32[]{:S(2)}, u32[]{:S(2)}) %collective-permute-start.2) | collective-permute-done | bytes 26656 | tf_op jit(solution)/shard_map/ppermute | solution.py:711
  28.3 0.6 collective-permute-done.4.refs_2_
  28.9 0.0 collective-permute-done.3.refs_1_
  28.9 0.0 copy-start
  29.0 4.4 %collective-permute-start.6 = (bf16[115,8,128]{2,1,0:T(8,128)(2,1)S(1)}, bf16[115,8,128]{2,1,0:T(8,128)(2,1)S(1)}, u32[]{:S(2)}, u32[]{:S(2)}) collective-permute-start(bf16[115,8,128]{2,1,0:T(8,128)(2,1)S(1)} %pad_maximum_fusion.1), channel_id=1, source_target_pairs={{1,0},{2,1},{3,2},{0,3},{5,4},{6,5},{7,6},{4,7},{9,8},{10,9},{11,1... | collective-permute-start | bytes 706568 | tf_op jit(solution)/shard_map/ppermute | solution.py:717
  33.4 0.2 collective-permute-start.5
  33.6 6.8 %collective-permute-done.5.refs_3_ = bf16[109,8,128]{2,1,0:T(8,128)(2,1)S(1)} collective-permute-done((bf16[109,8,128]{2,1,0:T(8,128)(2,1)S(1)}, bf16[109,8,128]{2,1,0:T(8,128)(2,1)S(1)}, u32[]{:S(2)}, u32[]{:S(2)}) %collective-permute-start.5) | collective-permute-done | bytes 223264 | tf_op jit(solution)/shard_map/ppermute | solution.py:716
  40.4 0.0 collective-permute-done.6.refs_4_
  40.4 0.7 shard_map.61
  41.1 10.3 %collective-permute-start.7 = (bf16[448,8,128]{2,1,0:T(8,128)(2,1)S(1)}, bf16[448,8,128]{2,1,0:T(8,128)(2,1)S(1)}, u32[]{:S(2)}, u32[]{:S(2)}) collective-permute-start(bf16[448,8,128]{2,1,0:T(8,128)(2,1)S(1)} %get-tuple-element.56), channel_id=1, source_target_pairs={{16,0},{32,16},{48,32},{64,48},{80,64},{96,80},{112,96},{128,112},... | collective-permute-start | bytes 2752520 | tf_op jit(solution)/shard_map/ppermute | solution.py:724
  51.4 3.0 %collective-permute-start.8 = (bf16[448,8,128]{2,1,0:T(8,128)(2,1)S(1)}, bf16[448,8,128]{2,1,0:T(8,128)(2,1)S(1)}, u32[]{:S(2)}, u32[]{:S(2)}) collective-permute-start(bf16[448,8,128]{2,1,0:T(8,128)(2,1)S(1)} %get-tuple-element.57), channel_id=1, source_target_pairs={{0,16},{16,32},{32,48},{48,64},{64,80},{80,96},{96,112},{112,128},... | collective-permute-start | bytes 2752520 | tf_op jit(solution)/shard_map/ppermute | solution.py:724
  54.4 2.8 %shard_map.60 = f32[64,4,128]{2,1,0:T(4,128)S(1)} custom-call(s32[2]{0:T(128)S(1)} %copy-done, bf16[198,8,128]{2,1,0:T(8,128)(2,1)S(1)} %pad_maximum_fusion.block_ref.refs_0_, bf16[198,8,128]{2,1,0:T(8,128)(2,1)S(1)} %collective-permute-done.3.refs_1_, bf16[198,8,128]{2,1,0:T(8,128)(2,1)S(1)} %collective-permute-done.4.refs_2_, ...), custom_call_target="tpu_custom_call" | custom-call | tf_op jit(solution)/shard_map/pallas_call | solution.py:670
  57.2 16.4 %all_to_all.25.got_ref = f32[64,4,128]{2,1,0:T(4,128)S(1)} all-to-all(f32[64,4,128]{2,1,0:T(4,128)S(1)} %shard_map.60), channel_id=1, replica_groups=mesh['gx'=16,'gy'=4,'tx'=4] {'gx','gy'}, dimensions={0} | all-to-all | bytes 262144 | tf_op jit(solution)/shard_map/all_to_all | solution.py:685
  73.6 2.9 %collective-permute-start.10 = (bf16[96,8,128]{2,1,0:T(8,128)(2,1)S(1)}, bf16[96,8,128]{2,1,0:T(8,128)(2,1)S(1)}, u32[]{:S(2)}, u32[]{:S(2)}) collective-permute-start(bf16[96,8,128]{2,1,0:T(8,128)(2,1)S(1)} %bitcast.25), channel_id=1, source_target_pairs={{1,0},{2,1},{3,2},{0,3},{5,4},{6,5},{7,6},{4,7},{9,8},{10,9},{11,1... | collective-permute-start | bytes 589832 | tf_op jit(solution)/shard_map/ppermute | solution.py:755
  76.5 0.0 collective-permute-start.9
  76.5 0.0 collective-permute-done.7.refs_7_
  76.5 0.0 collective-permute-done.8.refs_8_
  76.5 2.5 %shard_map.62 = (f32[24,16,256]{2,1,0:T(8,128)S(1)}, f32[48,16,256]{2,1,0:T(8,128)S(1)}, f32[768,8,128]{2,1,0:T(8,128)S(1)}, f32[768,8,128]{2,1,0:T(8,128)S(1)},...) custom-call(s32[2]{0:T(128)S(1)} %copy-done, bf16[198,8,128]{2,1,0:T(8,128)(2,1)S(1)} %pad_maximum_fusion.block_ref.refs_0_, ...), custom_call_target="tpu_custom_call" | custom-call | tf_op jit(solution)/shard_map/pallas_call | solution.py:670
  79.0 6.7 %shard_map.63 = (f32[96,16,256]{2,1,0:T(8,128)S(1)}, f32[96,16,256]{2,1,0:T(8,128)S(1)}, f32[16,128]{1,0:T(8,128)S(1)}, f32[16,128]{1,0:T(8,128)S(1)}, f32[64,128]{1,0:T(8,128)S(1)}) custom-call(f32[64,4,128]{2,1,0:T(4,128)S(1)} %all_to_all.25.got_ref, f32[768,8,128]{2,1,0:T(8,128)S(1)} %get-tuple-element.58.refs_0_.c_ref, ...), custom_call_target="tpu_custom_call" | custom-call | tf_op jit(solution)/shard_map/pallas_call | solution.py:670
  85.7 0.0 collective-permute-done.10.refs_4_
  85.7 1.3 collective-permute-done.9.refs_2_
  87.0 14.5 %all_to_all.26 = f32[64,1,128]{2,1,0:T(1,128)S(1)} all-to-all(f32[64,1,128]{2,1,0:T(1,128)S(1)} %bitcast.33), channel_id=1, replica_groups=mesh['gx'=16,'gy'=4,'tx'=4] {'gx','gy'}, dimensions={0} | all-to-all | bytes 65536 | tf_op jit(solution)/shard_map/all_to_all | solution.py:685
  101.5 0.5 collective-permute-start.12
  101.9 1.9 %collective-permute-start.11 = (bf16[96,8,128]{2,1,0:T(8,128)(2,1)S(1)}, bf16[96,8,128]{2,1,0:T(8,128)(2,1)S(1)}, u32[]{:S(2)}, u32[]{:S(2)}) collective-permute-start(bf16[96,8,128]{2,1,0:T(8,128)(2,1)S(1)} %bitcast.23), channel_id=1, source_target_pairs={{0,1},{1,2},{2,3},{3,0},{4,5},{5,6},{6,7},{7,4},{8,9},{9,10},{10,1... | collective-permute-start | bytes 589832 | tf_op jit(solution)/shard_map/ppermute | solution.py:773
  103.8 5.0 %shard_map.64 = (f32[96,16,256]{2,1,0:T(8,128)S(1)}, f32[96,16,256]{2,1,0:T(8,128)S(1)}, f32[16,128]{1,0:T(8,128)S(1)}, f32[64,128]{1,0:T(8,128)S(1)}) custom-call(f32[64,128]{1,0:T(8,128)S(1)} %bitcast.30, f32[768,8,128]{2,1,0:T(8,128)S(1)} %get-tuple-element.58.refs_0_.c_ref, f32[768,8,128]{2,1,0:T(8,128)S(1)} %get-tuple-element.59.refs_1_, ...), custom_call_target="tpu_custom_call" | custom-call | tf_op jit(solution)/shard_map/pallas_call | solution.py:670
  108.8 4.3 %collective-permute-done.12.refs_5_ = bf16[96,8,128]{2,1,0:T(8,128)(2,1)S(1)} collective-permute-done((bf16[96,8,128]{2,1,0:T(8,128)(2,1)S(1)}, bf16[96,8,128]{2,1,0:T(8,128)(2,1)S(1)}, u32[]{:S(2)}, u32[]{:S(2)}) %collective-permute-start.12) | collective-permute-done | bytes 196640 | tf_op jit(solution)/shard_map/ppermute | solution.py:773
  113.2 0.7 collective-permute-done.11.refs_3_
  113.9 12.6 %all_to_all.27 = f32[64,1,128]{2,1,0:T(1,128)S(1)} all-to-all(f32[64,1,128]{2,1,0:T(1,128)S(1)} %bitcast.34), channel_id=1, replica_groups=mesh['gx'=16,'gy'=4,'tx'=4] {'gx','gy'}, dimensions={0} | all-to-all | bytes 65536 | tf_op jit(solution)/shard_map/all_to_all | solution.py:685
  126.5 1.2 collective-permute-start.13
  127.7 2.4 %collective-permute-start.14 = (bf16[96,8,128]{2,1,0:T(8,128)(2,1)S(1)}, bf16[96,8,128]{2,1,0:T(8,128)(2,1)S(1)}, u32[]{:S(2)}, u32[]{:S(2)}) collective-permute-start(bf16[96,8,128]{2,1,0:T(8,128)(2,1)S(1)} %collective-permute-done.12.refs_5_), channel_id=1, source_target_pairs={{1,0},{2,1},{3,2},{0,3},{5,4},{6,5},{7,6},{4,7},{9,8},{10,9},{11,1... | collective-permute-start | bytes 589832 | tf_op jit(solution)/shard_map/ppermute | solution.py:777
  130.0 5.8 %shard_map.65 = (f32[96,16,256]{2,1,0:T(8,128)S(1)}, f32[96,16,256]{2,1,0:T(8,128)S(1)}, f32[96,8,128]{2,1,0:T(8,128)S(1)}, f32[16,128]{1,0:T(8,128)S(1)}, f32[64,128]{1,0:T(8,128)S(1)}) custom-call(f32[64,128]{1,0:T(8,128)S(1)} %bitcast.29, f32[768,8,128]{2,1,0:T(8,128)S(1)} %get-tuple-element.58.refs_0_.c_ref, ...), custom_call_target="tpu_custom_call" | custom-call | tf_op jit(solution)/shard_map/pallas_call | solution.py:670
  135.8 1.8 %collective-permute-done.13.refs_6_ = bf16[96,8,128]{2,1,0:T(8,128)(2,1)S(1)} collective-permute-done((bf16[96,8,128]{2,1,0:T(8,128)(2,1)S(1)}, bf16[96,8,128]{2,1,0:T(8,128)(2,1)S(1)}, u32[]{:S(2)}, u32[]{:S(2)}) %collective-permute-start.13) | collective-permute-done | bytes 196640 | tf_op jit(solution)/shard_map/ppermute | solution.py:777
  137.6 1.8 %collective-permute-done.14.refs_7_ = bf16[96,8,128]{2,1,0:T(8,128)(2,1)S(1)} collective-permute-done((bf16[96,8,128]{2,1,0:T(8,128)(2,1)S(1)}, bf16[96,8,128]{2,1,0:T(8,128)(2,1)S(1)}, u32[]{:S(2)}, u32[]{:S(2)}) %collective-permute-start.14) | collective-permute-done | bytes 196640 | tf_op jit(solution)/shard_map/ppermute | solution.py:777
  139.5 12.0 %all_to_all.28 = f32[64,1,128]{2,1,0:T(1,128)S(1)} all-to-all(f32[64,1,128]{2,1,0:T(1,128)S(1)} %bitcast.32), channel_id=1, replica_groups=mesh['gx'=16,'gy'=4,'tx'=4] {'gx','gy'}, dimensions={0} | all-to-all | bytes 65536 | tf_op jit(solution)/shard_map/all_to_all | solution.py:685
  151.5 5.0 %shard_map.66 = (f32[96,16,256]{2,1,0:T(8,128)S(1)}, f32[96,16,256]{2,1,0:T(8,128)S(1)}, f32[16,128]{1,0:T(8,128)S(1)}, f32[64,128]{1,0:T(8,128)S(1)}) custom-call(f32[64,128]{1,0:T(8,128)S(1)} %bitcast.31, f32[768,8,128]{2,1,0:T(8,128)S(1)} %get-tuple-element.58.refs_0_.c_ref, f32[768,8,128]{2,1,0:T(8,128)S(1)} %get-tuple-element.59.refs_1_, ...), custom_call_target="tpu_custom_call" | custom-call | tf_op jit(solution)/shard_map/pallas_call | solution.py:670
  156.4 12.2 %all_to_all.29 = f32[64,1,128]{2,1,0:T(1,128)S(1)} all-to-all(f32[64,1,128]{2,1,0:T(1,128)S(1)} %bitcast.35), channel_id=1, replica_groups=mesh['gx'=16,'gy'=4,'tx'=4] {'gx','gy'}, dimensions={0} | all-to-all | bytes 65536 | tf_op jit(solution)/shard_map/all_to_all | solution.py:685
  168.6 3.4 %shard_map.67 = (f32[96,8,128]{2,1,0:T(8,128)}, f32[96,8,128]{2,1,0:T(8,128)}) custom-call(f32[64,128]{1,0:T(8,128)S(1)} %bitcast.28, f32[768,8,128]{2,1,0:T(8,128)S(1)} %get-tuple-element.58.refs_0_.c_ref, bf16[96,8,128]{2,1,0:T(8,128)(2,1)S(1)} %bitcast.27, bf16[96,8,128]{2,1,0:T(8,128)(2,1)S(1)} %bitcast.24, ...), custom_call_target="tpu_custom_call" | custom-call | tf_op jit(solution)/shard_map/pallas_call | solution.py:670
  (8 shorter events, 0.1 us)
Async XLA Ops:
  0.6 17.1 %copy-start.1 = (bf16[4,2,3,8,8,128]{5,4,3,2,1,0:T(8,128)(2,1)S(1)}, bf16[4,2,3,8,8,128]{5,4,3,2,1,0:T(8,128)(2,1)}, u32[]{:S(2)}) copy-start(bf16[4,2,3,8,8,128]{5,4,3,2,1,0:T(8,128)(2,1)} %param.5) | copy-start | bytes 1179652
  2.1 11.5 %collective-permute-start.1 = (bf16[13,8,128]{2,1,0:T(8,128)(2,1)S(1)}, bf16[13,8,128]{2,1,0:T(8,128)(2,1)S(1)}, u32[]{:S(2)}, u32[]{:S(2)}) collective-permute-start(bf16[13,8,128]{2,1,0:T(8,128)(2,1)S(1)} %shard_map.59), channel_id=1, source_target_pairs={{0,4},{4,8},{8,12},{1,5},{5,9},{9,13},{2,6},{6,10},{10,14},{3,7},{... | collective-permute-start | bytes 79880 | tf_op jit(solution)/shard_map/ppermute | solution.py:709
  6.1 7.4 %collective-permute-start = (bf16[13,8,128]{2,1,0:T(8,128)(2,1)S(1)}, bf16[13,8,128]{2,1,0:T(8,128)(2,1)S(1)}, u32[]{:S(2)}, u32[]{:S(2)}) collective-permute-start(bf16[13,8,128]{2,1,0:T(8,128)(2,1)S(1)} %shard_map.59), channel_id=1, source_target_pairs={{4,0},{8,4},{12,8},{5,1},{9,5},{13,9},{6,2},{10,6},{14,10},{7,3},{... | collective-permute-start | bytes 79880 | tf_op jit(solution)/shard_map/ppermute | solution.py:709
  7.4 21.5 %collective-permute-start.4 = (bf16[198,8,128]{2,1,0:T(8,128)(2,1)S(1)}, bf16[198,8,128]{2,1,0:T(8,128)(2,1)S(1)}, u32[]{:S(2)}, u32[]{:S(2)}) collective-permute-start(bf16[198,8,128]{2,1,0:T(8,128)(2,1)S(1)} %pad_maximum_fusion.block_ref.refs_0_), channel_id=1, source_target_pairs={{1,0},{2,1},{3,2},{0,3},{5,4},{6,5},{7,6},{4,7},{9,8},{10,9},{11,1... | collective-permute-start | bytes 1216520 | tf_op jit(solution)/shard_map/ppermute | solution.py:707
  13.5 15.4 %collective-permute-start.3 = (bf16[198,8,128]{2,1,0:T(8,128)(2,1)S(1)}, bf16[198,8,128]{2,1,0:T(8,128)(2,1)S(1)}, u32[]{:S(2)}, u32[]{:S(2)}) collective-permute-start(bf16[198,8,128]{2,1,0:T(8,128)(2,1)S(1)} %pad_maximum_fusion.block_ref.refs_0_), channel_id=1, source_target_pairs={{0,1},{1,2},{2,3},{3,0},{4,5},{5,6},{6,7},{7,4},{8,9},{9,10},{10,1... | collective-permute-start | bytes 1216520 | tf_op jit(solution)/shard_map/ppermute | solution.py:706
  13.6 14.7 %collective-permute-start.2 = (bf16[13,8,128]{2,1,0:T(8,128)(2,1)S(1)}, bf16[13,8,128]{2,1,0:T(8,128)(2,1)S(1)}, u32[]{:S(2)}, u32[]{:S(2)}) collective-permute-start(bf16[13,8,128]{2,1,0:T(8,128)(2,1)S(1)} %broadcast_select_fusion.refs_5_), channel_id=1, source_target_pairs={{0,2},{1,3},{2,0},{3,1},{4,6},{5,7},{6,4},{7,5},{8,10},{9,11},{10,... | collective-permute-start | bytes 79880 | tf_op jit(solution)/shard_map/ppermute | solution.py:711
  28.9 25.5 %copy-start = (s32[2]{0:T(128)S(1)}, s32[2]{0:T(128)}, u32[]{:S(2)}) copy-start(s32[2]{0:T(128)} %src_ref.3) | copy-start | bytes 28
  29.0 11.4 %collective-permute-start.6 = (bf16[115,8,128]{2,1,0:T(8,128)(2,1)S(1)}, bf16[115,8,128]{2,1,0:T(8,128)(2,1)S(1)}, u32[]{:S(2)}, u32[]{:S(2)}) collective-permute-start(bf16[115,8,128]{2,1,0:T(8,128)(2,1)S(1)} %pad_maximum_fusion.1), channel_id=1, source_target_pairs={{1,0},{2,1},{3,2},{0,3},{5,4},{6,5},{7,6},{4,7},{9,8},{10,9},{11,1... | collective-permute-start | bytes 706568 | tf_op jit(solution)/shard_map/ppermute | solution.py:717
  33.4 7.0 %collective-permute-start.5 = (bf16[109,8,128]{2,1,0:T(8,128)(2,1)S(1)}, bf16[109,8,128]{2,1,0:T(8,128)(2,1)S(1)}, u32[]{:S(2)}, u32[]{:S(2)}) collective-permute-start(bf16[109,8,128]{2,1,0:T(8,128)(2,1)S(1)} %pad_maximum_fusion.2), channel_id=1, source_target_pairs={{0,1},{1,2},{2,3},{3,0},{4,5},{5,6},{6,7},{7,4},{8,9},{9,10},{10,1... | collective-permute-start | bytes 669704 | tf_op jit(solution)/shard_map/ppermute | solution.py:716
  41.1 35.4 %collective-permute-start.7 = (bf16[448,8,128]{2,1,0:T(8,128)(2,1)S(1)}, bf16[448,8,128]{2,1,0:T(8,128)(2,1)S(1)}, u32[]{:S(2)}, u32[]{:S(2)}) collective-permute-start(bf16[448,8,128]{2,1,0:T(8,128)(2,1)S(1)} %get-tuple-element.56), channel_id=1, source_target_pairs={{16,0},{32,16},{48,32},{64,48},{80,64},{96,80},{112,96},{128,112},... | collective-permute-start | bytes 2752520 | tf_op jit(solution)/shard_map/ppermute | solution.py:724
  51.4 25.1 %collective-permute-start.8 = (bf16[448,8,128]{2,1,0:T(8,128)(2,1)S(1)}, bf16[448,8,128]{2,1,0:T(8,128)(2,1)S(1)}, u32[]{:S(2)}, u32[]{:S(2)}) collective-permute-start(bf16[448,8,128]{2,1,0:T(8,128)(2,1)S(1)} %get-tuple-element.57), channel_id=1, source_target_pairs={{0,16},{16,32},{32,48},{48,64},{64,80},{80,96},{96,112},{112,128},... | collective-permute-start | bytes 2752520 | tf_op jit(solution)/shard_map/ppermute | solution.py:724
  73.6 12.1 %collective-permute-start.10 = (bf16[96,8,128]{2,1,0:T(8,128)(2,1)S(1)}, bf16[96,8,128]{2,1,0:T(8,128)(2,1)S(1)}, u32[]{:S(2)}, u32[]{:S(2)}) collective-permute-start(bf16[96,8,128]{2,1,0:T(8,128)(2,1)S(1)} %bitcast.25), channel_id=1, source_target_pairs={{1,0},{2,1},{3,2},{0,3},{5,4},{6,5},{7,6},{4,7},{9,8},{10,9},{11,1... | collective-permute-start | bytes 589832 | tf_op jit(solution)/shard_map/ppermute | solution.py:755
  76.5 10.5 %collective-permute-start.9 = (bf16[96,8,128]{2,1,0:T(8,128)(2,1)S(1)}, bf16[96,8,128]{2,1,0:T(8,128)(2,1)S(1)}, u32[]{:S(2)}, u32[]{:S(2)}) collective-permute-start(bf16[96,8,128]{2,1,0:T(8,128)(2,1)S(1)} %bitcast.26), channel_id=1, source_target_pairs={{0,1},{1,2},{2,3},{3,0},{4,5},{5,6},{6,7},{7,4},{8,9},{9,10},{10,1... | collective-permute-start | bytes 589832 | tf_op jit(solution)/shard_map/ppermute | solution.py:755
  101.5 11.7 %collective-permute-start.12 = (bf16[96,8,128]{2,1,0:T(8,128)(2,1)S(1)}, bf16[96,8,128]{2,1,0:T(8,128)(2,1)S(1)}, u32[]{:S(2)}, u32[]{:S(2)}) collective-permute-start(bf16[96,8,128]{2,1,0:T(8,128)(2,1)S(1)} %bitcast.22), channel_id=1, source_target_pairs={{1,0},{2,1},{3,2},{0,3},{5,4},{6,5},{7,6},{4,7},{9,8},{10,9},{11,1... | collective-permute-start | bytes 589832 | tf_op jit(solution)/shard_map/ppermute | solution.py:773
  101.9 12.0 %collective-permute-start.11 = (bf16[96,8,128]{2,1,0:T(8,128)(2,1)S(1)}, bf16[96,8,128]{2,1,0:T(8,128)(2,1)S(1)}, u32[]{:S(2)}, u32[]{:S(2)}) collective-permute-start(bf16[96,8,128]{2,1,0:T(8,128)(2,1)S(1)} %bitcast.23), channel_id=1, source_target_pairs={{0,1},{1,2},{2,3},{3,0},{4,5},{5,6},{6,7},{7,4},{8,9},{9,10},{10,1... | collective-permute-start | bytes 589832 | tf_op jit(solution)/shard_map/ppermute | solution.py:773
  126.5 11.2 %collective-permute-start.13 = (bf16[96,8,128]{2,1,0:T(8,128)(2,1)S(1)}, bf16[96,8,128]{2,1,0:T(8,128)(2,1)S(1)}, u32[]{:S(2)}, u32[]{:S(2)}) collective-permute-start(bf16[96,8,128]{2,1,0:T(8,128)(2,1)S(1)} %collective-permute-done.9.refs_2_), channel_id=1, source_target_pairs={{0,1},{1,2},{2,3},{3,0},{4,5},{5,6},{6,7},{7,4},{8,9},{9,10},{10,1... | collective-permute-start | bytes 589832 | tf_op jit(solution)/shard_map/ppermute | solution.py:777
  127.7 11.8 %collective-permute-start.14 = (bf16[96,8,128]{2,1,0:T(8,128)(2,1)S(1)}, bf16[96,8,128]{2,1,0:T(8,128)(2,1)S(1)}, u32[]{:S(2)}, u32[]{:S(2)}) collective-permute-start(bf16[96,8,128]{2,1,0:T(8,128)(2,1)S(1)} %collective-permute-done.12.refs_5_), channel_id=1, source_target_pairs={{1,0},{2,1},{3,2},{0,3},{5,4},{6,5},{7,6},{4,7},{9,8},{10,9},{11,1... | collective-permute-start | bytes 589832 | tf_op jit(solution)/shard_map/ppermute | solution.py:777

commit v9 on v7

--- a/solution.py
+++ b/solution.py
@@ -15,7 +15,7 @@
 HALF = 99
 PACKED = 13
 WEIGHTS = (1.0, 0.5, 0.25)
-AT_ONCE = 4
+AT_ONCE = 8
 HIGH = lax.Precision.HIGHEST
 F32 = jnp.float32
 BF16 = jnp.bfloat16
@@ -131,7 +131,7 @@
 def inner_all(c_ref, field, sums_ref):
     def body(step, accs):
         accs = list(accs)
-        for j in (2 * step, 2 * step + 1):
+        for j in [AT_ONCE * step + i for i in range(AT_ONCE)]:
             one, two = field(0, j), field(1, j)
             for k in range(VECS):
                 vec = c_ref[k * ROWS + j]
@@ -140,7 +140,7 @@
         return tuple(accs)
 
     zero = jnp.zeros((8, 128), F32)
-    accs = lax.fori_loop(0, ROWS // 2, body, (zero,) * (2 * VECS))
+    accs = lax.fori_loop(0, ROWS // AT_ONCE, body, (zero,) * (2 * VECS))
     for k in range(VECS):
         for s in range(2):
             sums_ref[s * VECS + k : s * VECS + k + 1] = jnp.sum(
@@ -361,7 +361,7 @@
         chosen = jnp.where(iota((8, 16), 1) // 8 == s, 1.0, 0.0).astype(F32)
         lines.append(nt_dot(chosen, inner, HIGH)[0:1])
     line = jnp.concatenate(lines + [jnp.zeros((1, 96), F32)], axis=1)
-    rows = jnp.concatenate([gram, line, jnp.zeros((1, 128), F32)], axis=0)
+    rows = jnp.concatenate([gram, line], axis=0)
     out_ref[...] = jnp.broadcast_to(rows[None], out_ref.shape)
 
 
@@ -734,7 +734,7 @@
     side_scratch = pltpu.VMEM((2 * ROWS, 16, 128), F32)
     sent = call(
         functools.partial(gram_kernel, size_x, size_y),
-        shape(peers, 4, 128),
+        shape(peers, 3, 128),
         (src_cell, *blocks),
         (pltpu.VMEM((ROWS, 16, 128), F32), pltpu.VMEM((8 * VECS + 48, ROWS * 128), BF16)),
         smem=1,

time: 168 us -> 168 us (level)
  waiting for transfers between devices: 22.9 us -> 24.7 us
  Pallas kernels: 34.3 us -> 32.5 us
    pallas_call x10, Pallas kernels: 34.3 us -> 32.5 us  [call(): pl.pallas_call(kernel, out_shape=outs, in_specs=[pl.BlockSpec(memory_spac...]
  transfers between devices with their start and end apart: 18 -> 18, of which waited for: 9 -> 9; matrix products, arithmetic and copies ran while one was open for 1% -> 1% of each run, Pallas kernels for 16% -> 15%
where the time goes in v9:
time: 168 us; the launch traced here: 167 us
  starting transfers between devices  54.8 us (33%)
  blocking collectives  50.9 us (30%)
  Pallas kernels  32.5 us (19%)
  waiting for transfers between devices  24.7 us (15%)
  local copies, waits for them, and re-layouts  2.18 us (1%)
    all_to_all x4, blocking collectives, exchange(): return lax.all_to_all(value, ('gx', 'gy'), 0, 0)  50.9 us
    pallas_call x10, Pallas kernels, call(): pl.pallas_call(kernel, out_shape=outs, in_specs=[pl.BlockSpec(memory_spac...  32.5 us
    ppermute x4, starting transfers between devices, exchange_x(): return (lax.ppermute(low, 'gx', down), lax.ppermute(high, 'gx', up))  15.8 us
    all_to_all x1, starting transfers between devices, exchange(): return lax.all_to_all(value, ('gx', 'gy'), 0, 0)  9.12 us
    ppermute x1, starting transfers between devices, on_device(): three = lax.ppermute(block, 'tx', left)  6.93 us
    ppermute x1, starting transfers between devices, on_device(): far_high = lax.ppermute(jnp.concatenate([three[CUT:], side]), 'tx', left)  6.71 us
    ppermute x2, waiting for transfers between devices, on_device(): lax.ppermute(piece, 'tx', left)  5.35 us
    ppermute x2, starting transfers between devices, on_device(): after, before = (lax.ppermute(own, 'gy', down), lax.ppermute(own, 'gy', up))  4.5 us
  transfers between devices with their start and end apart: 18, of which 9 were waited for; matrix products, arithmetic and copies ran while one was open for 1% of the time, Pallas kernels for 15%

profile of v9, /device:TPU:1, one launch (start us, length us, event | category | flops | bytes accessed | tf_op | source)
XLA Modules:
  0.0 167.1 jit_solution(18135017362486052670)
XLA Ops:
  0.6 1.1 pad_maximum_fusion.block_ref.refs_0_
  1.7 6.9 %collective-permute-start.4 = (bf16[198,8,128]{2,1,0:T(8,128)(2,1)S(1)}, bf16[198,8,128]{2,1,0:T(8,128)(2,1)S(1)}, u32[]{:S(2)}, u32[]{:S(2)}) collective-permute-start(bf16[198,8,128]{2,1,0:T(8,128)(2,1)S(1)} %pad_maximum_fusion.block_ref.refs_0_), channel_id=1, source_target_pairs={{1,0},{2,1},{3,2},{0,3},{5,4},{6,5},{7,6},{4,7},{9,8},{10,9},{11,1... | collective-permute-start | bytes 1216520 | tf_op jit(solution)/shard_map/ppermute | solution.py:712
  8.6 0.3 shard_map.59
  8.9 3.2 %collective-permute-start.1 = (bf16[13,8,128]{2,1,0:T(8,128)(2,1)S(1)}, bf16[13,8,128]{2,1,0:T(8,128)(2,1)S(1)}, u32[]{:S(2)}, u32[]{:S(2)}) collective-permute-start(bf16[13,8,128]{2,1,0:T(8,128)(2,1)S(1)} %shard_map.59), channel_id=1, source_target_pairs={{0,4},{4,8},{8,12},{1,5},{5,9},{9,13},{2,6},{6,10},{10,14},{3,7},{... | collective-permute-start | bytes 79880 | tf_op jit(solution)/shard_map/ppermute | solution.py:714
  12.1 1.3 collective-permute-start
  13.5 0.0 collective-permute-done.1
  13.5 3.6 %collective-permute-done = bf16[13,8,128]{2,1,0:T(8,128)(2,1)S(1)} collective-permute-done((bf16[13,8,128]{2,1,0:T(8,128)(2,1)S(1)}, bf16[13,8,128]{2,1,0:T(8,128)(2,1)S(1)}, u32[]{:S(2)}, u32[]{:S(2)}) %collective-permute-start) | collective-permute-done | bytes 26656 | tf_op jit(solution)/shard_map/ppermute | solution.py:714
  17.0 0.1 broadcast_select_fusion.refs_5_.refs_3_.refs_4_
  17.1 3.3 %collective-permute-start.2 = (bf16[13,8,128]{2,1,0:T(8,128)(2,1)S(1)}, bf16[13,8,128]{2,1,0:T(8,128)(2,1)S(1)}, u32[]{:S(2)}, u32[]{:S(2)}) collective-permute-start(bf16[13,8,128]{2,1,0:T(8,128)(2,1)S(1)} %broadcast_select_fusion.refs_5_.refs_3_.refs_4_), channel_id=1, source_target_pairs={{0,2},{1,3},{2,0},{3,1},{4,6},{5,7},{6,4},{7,5},{8,10},{9,11},{10,... | collective-permute-start | bytes 79880 | tf_op jit(solution)/shard_map/ppermute | solution.py:716
  20.4 3.7 %collective-permute-done.2.refs_6_ = bf16[13,8,128]{2,1,0:T(8,128)(2,1)S(1)} collective-permute-done((bf16[13,8,128]{2,1,0:T(8,128)(2,1)S(1)}, bf16[13,8,128]{2,1,0:T(8,128)(2,1)S(1)}, u32[]{:S(2)}, u32[]{:S(2)}) %collective-permute-start.2) | collective-permute-done | bytes 26656 | tf_op jit(solution)/shard_map/ppermute | solution.py:716
  24.2 6.7 %collective-permute-start.6 = (bf16[115,8,128]{2,1,0:T(8,128)(2,1)S(1)}, bf16[115,8,128]{2,1,0:T(8,128)(2,1)S(1)}, u32[]{:S(2)}, u32[]{:S(2)}) collective-permute-start(bf16[115,8,128]{2,1,0:T(8,128)(2,1)S(1)} %pad_maximum_fusion.1), channel_id=1, source_target_pairs={{1,0},{2,1},{3,2},{0,3},{5,4},{6,5},{7,6},{4,7},{9,8},{10,9},{11,1... | collective-permute-start | bytes 706568 | tf_op jit(solution)/shard_map/ppermute | solution.py:719
  30.9 0.0 copy-start.2
  30.9 0.1 collective-permute-start.5
  31.0 1.7 %shard_map.61 = (bf16[310,8,128]{2,1,0:T(8,128)(2,1)}, bf16[310,8,128]{2,1,0:T(8,128)(2,1)}) custom-call(bf16[198,8,128]{2,1,0:T(8,128)(2,1)S(1)} %pad_maximum_fusion.block_ref.refs_0_, bf16[198,8,128]{2,1,0:T(8,128)(2,1)S(1)} %collective-permute-done.3.refs_1_, bf16[198,8,128]{2,1,0:T(8,128)(2,1)S(1)} %collective-permute-done.4.refs_2_, ...), custom_call_target="tpu_custom_call" | custom-call | tf_op jit(solution)/shard_map/pallas_call | solution.py:675
  32.7 5.7 %collective-permute-start.7 = (bf16[310,8,128]{2,1,0:T(8,128)(2,1)}, bf16[310,8,128]{2,1,0:T(8,128)(2,1)S(1)}, u32[]{:S(2)}, u32[]{:S(2)}) collective-permute-start(bf16[310,8,128]{2,1,0:T(8,128)(2,1)} %get-tuple-element.55), channel_id=1, source_target_pairs={{16,0},{32,16},{48,32},{64,48},{80,64},{96,80},{112,96},{128,112},... | collective-permute-start | bytes 1904648 | tf_op jit(solution)/shard_map/ppermute | solution.py:726
  38.4 0.0 copy-start
  38.4 3.1 %collective-permute-start.8 = (bf16[310,8,128]{2,1,0:T(8,128)(2,1)}, bf16[310,8,128]{2,1,0:T(8,128)(2,1)S(1)}, u32[]{:S(2)}, u32[]{:S(2)}) collective-permute-start(bf16[310,8,128]{2,1,0:T(8,128)(2,1)} %get-tuple-element.56), channel_id=1, source_target_pairs={{0,16},{16,32},{32,48},{48,64},{64,80},{80,96},{96,112},{112,128},... | collective-permute-start | bytes 1904648 | tf_op jit(solution)/shard_map/ppermute | solution.py:726
  41.5 2.7 %collective-permute-done.5.refs_3_ = bf16[109,8,128]{2,1,0:T(8,128)(2,1)S(1)} collective-permute-done((bf16[109,8,128]{2,1,0:T(8,128)(2,1)S(1)}, bf16[109,8,128]{2,1,0:T(8,128)(2,1)S(1)}, u32[]{:S(2)}, u32[]{:S(2)}) %collective-permute-start.5) | collective-permute-done | bytes 223264 | tf_op jit(solution)/shard_map/ppermute | solution.py:718
  44.3 1.1 shard_map.62
  45.4 0.7 copy-done.3
  46.1 3.5 %collective-permute-start.9 = (bf16[138,8,128]{2,1,0:T(8,128)(2,1)}, bf16[138,8,128]{2,1,0:T(8,128)(2,1)}, u32[]{:S(2)}, u32[]{:S(2)}) collective-permute-start(bf16[138,8,128]{2,1,0:T(8,128)(2,1)} %get-tuple-element.57), channel_id=1, source_target_pairs={{16,0},{32,16},{48,32},{64,48},{80,64},{96,80},{112,96},{128,112},... | collective-permute-start | bytes 847880 | tf_op jit(solution)/shard_map/ppermute | solution.py:726
  49.6 2.8 %shard_map.60 = f32[64,3,128]{2,1,0:T(4,128)S(1)} custom-call(s32[2]{0:T(128)S(1)} %copy-done.2, bf16[198,8,128]{2,1,0:T(8,128)(2,1)S(1)} %pad_maximum_fusion.block_ref.refs_0_, bf16[198,8,128]{2,1,0:T(8,128)(2,1)S(1)} %collective-permute-done.3.refs_1_, bf16[198,8,128]{2,1,0:T(8,128)(2,1)S(1)} %collective-permute-done.4.refs_2_, ...), custom_call_target="tpu_custom_call" | custom-call | tf_op jit(solution)/shard_map/pallas_call | solution.py:675
  52.3 0.6 copy-done.1
  53.0 9.1 %all-to-all-start = ((f32[64,3,128]{2,1,0:T(4,128)}), f32[64,3,128]{2,1,0:T(4,128)S(1)}, u32[]{:S(2)}, u32[]{:S(2)}) async-start(f32[64,3,128]{2,1,0:T(4,128)} %copy-done.1), calls=%async_computation | async-start | bytes 262144 | tf_op jit(solution)/shard_map/all_to_all | solution.py:690
  62.1 3.5 %collective-permute-start.10 = (bf16[138,8,128]{2,1,0:T(8,128)(2,1)}, bf16[138,8,128]{2,1,0:T(8,128)(2,1)}, u32[]{:S(2)}, u32[]{:S(2)}) collective-permute-start(bf16[138,8,128]{2,1,0:T(8,128)(2,1)} %copy-done.3), channel_id=1, source_target_pairs={{0,16},{16,32},{32,48},{48,64},{64,80},{80,96},{96,112},{112,128},... | collective-permute-start | bytes 847880 | tf_op jit(solution)/shard_map/ppermute | solution.py:726
  65.7 0.8 fusion
  66.5 4.2 %all-to-all-done.got_ref = f32[64,3,128]{2,1,0:T(4,128)S(1)} async-done(((f32[64,3,128]{2,1,0:T(4,128)}), f32[64,3,128]{2,1,0:T(4,128)S(1)}, u32[]{:S(2)}, u32[]{:S(2)}) %all-to-all-start) | async-done | bytes 98336 | tf_op jit(solution)/shard_map/all_to_all | solution.py:690
  70.7 0.1 collective-permute-start.12
  70.8 2.2 %collective-permute-start.11 = (bf16[96,8,128]{2,1,0:T(8,128)(2,1)}, bf16[96,8,128]{2,1,0:T(8,128)(2,1)S(1)}, u32[]{:S(2)}, u32[]{:S(2)}) collective-permute-start(bf16[96,8,128]{2,1,0:T(8,128)(2,1)} %bitcast.36), channel_id=1, source_target_pairs={{0,1},{1,2},{2,3},{3,0},{4,5},{5,6},{6,7},{7,4},{8,9},{9,10},{10,1... | collective-permute-start | bytes 589832 | tf_op jit(solution)/shard_map/ppermute | solution.py:759
  73.1 2.8 %shard_map.63 = (f32[24,16,256]{2,1,0:T(8,128)S(1)}, f32[48,16,256]{2,1,0:T(8,128)S(1)}, f32[768,8,128]{2,1,0:T(8,128)S(1)}, f32[768,8,128]{2,1,0:T(8,128)S(1)},...) custom-call(s32[2]{0:T(128)S(1)} %copy-done.2, bf16[198,8,128]{2,1,0:T(8,128)(2,1)S(1)} %pad_maximum_fusion.block_ref.refs_0_, ...), custom_call_target="tpu_custom_call" | custom-call | tf_op jit(solution)/shard_map/pallas_call | solution.py:675
  75.9 6.2 %shard_map.64 = (f32[96,16,256]{2,1,0:T(8,128)S(1)}, f32[96,16,256]{2,1,0:T(8,128)S(1)}, f32[16,128]{1,0:T(8,128)S(1)}, f32[16,128]{1,0:T(8,128)S(1)}, f32[64,128]{1,0:T(8,128)S(1)}) custom-call(f32[64,3,128]{2,1,0:T(4,128)S(1)} %all-to-all-done.got_ref, f32[768,8,128]{2,1,0:T(8,128)S(1)} %get-tuple-element.59.refs_0_.c_ref, ...), custom_call_target="tpu_custom_call" | custom-call | tf_op jit(solution)/shard_map/pallas_call | solution.py:675
  82.1 0.6 collective-permute-done.12.refs_3_
  82.7 13.7 %all_to_all.25 = f32[64,1,128]{2,1,0:T(1,128)S(1)} all-to-all(f32[64,1,128]{2,1,0:T(1,128)S(1)} %bitcast.29), channel_id=1, replica_groups=mesh['gx'=16,'gy'=4,'tx'=4] {'gx','gy'}, dimensions={0} | all-to-all | bytes 65536 | tf_op jit(solution)/shard_map/all_to_all | solution.py:690
  96.4 0.4 collective-permute-start.14
  96.8 2.0 %collective-permute-start.13 = (bf16[96,8,128]{2,1,0:T(8,128)(2,1)S(1)}, bf16[96,8,128]{2,1,0:T(8,128)(2,1)S(1)}, u32[]{:S(2)}, u32[]{:S(2)}) collective-permute-start(bf16[96,8,128]{2,1,0:T(8,128)(2,1)S(1)} %bitcast.34), channel_id=1, source_target_pairs={{0,1},{1,2},{2,3},{3,0},{4,5},{5,6},{6,7},{7,4},{8,9},{9,10},{10,1... | collective-permute-start | bytes 589832 | tf_op jit(solution)/shard_map/ppermute | solution.py:777
  98.7 4.6 %shard_map.65 = (f32[96,16,256]{2,1,0:T(8,128)S(1)}, f32[96,16,256]{2,1,0:T(8,128)S(1)}, f32[16,128]{1,0:T(8,128)S(1)}, f32[64,128]{1,0:T(8,128)S(1)}) custom-call(f32[64,128]{1,0:T(8,128)S(1)} %bitcast.26, f32[768,8,128]{2,1,0:T(8,128)S(1)} %get-tuple-element.59.refs_0_.c_ref, f32[768,8,128]{2,1,0:T(8,128)S(1)} %get-tuple-element.60.refs_1_, ...), custom_call_target="tpu_custom_call" | custom-call | tf_op jit(solution)/shard_map/pallas_call | solution.py:675
  103.3 4.8 %collective-permute-done.14.refs_4_ = bf16[96,8,128]{2,1,0:T(8,128)(2,1)S(1)} collective-permute-done((bf16[96,8,128]{2,1,0:T(8,128)(2,1)S(1)}, bf16[96,8,128]{2,1,0:T(8,128)(2,1)S(1)}, u32[]{:S(2)}, u32[]{:S(2)}) %collective-permute-start.14) | collective-permute-done | bytes 196640 | tf_op jit(solution)/shard_map/ppermute | solution.py:777
  108.1 0.6 collective-permute-done.13.refs_2_
  108.7 13.1 %all_to_all.26 = f32[64,1,128]{2,1,0:T(1,128)S(1)} all-to-all(f32[64,1,128]{2,1,0:T(1,128)S(1)} %bitcast.30), channel_id=1, replica_groups=mesh['gx'=16,'gy'=4,'tx'=4] {'gx','gy'}, dimensions={0} | all-to-all | bytes 65536 | tf_op jit(solution)/shard_map/all_to_all | solution.py:690
  121.8 0.8 collective-permute-start.15
  122.7 2.7 %collective-permute-start.16 = (bf16[96,8,128]{2,1,0:T(8,128)(2,1)S(1)}, bf16[96,8,128]{2,1,0:T(8,128)(2,1)S(1)}, u32[]{:S(2)}, u32[]{:S(2)}) collective-permute-start(bf16[96,8,128]{2,1,0:T(8,128)(2,1)S(1)} %collective-permute-done.14.refs_4_), channel_id=1, source_target_pairs={{1,0},{2,1},{3,2},{0,3},{5,4},{6,5},{7,6},{4,7},{9,8},{10,9},{11,1... | collective-permute-start | bytes 589832 | tf_op jit(solution)/shard_map/ppermute | solution.py:781
  125.4 5.3 %shard_map.66 = (f32[96,16,256]{2,1,0:T(8,128)S(1)}, f32[96,16,256]{2,1,0:T(8,128)S(1)}, f32[96,8,128]{2,1,0:T(8,128)S(1)}, f32[16,128]{1,0:T(8,128)S(1)}, f32[64,128]{1,0:T(8,128)S(1)}) custom-call(f32[64,128]{1,0:T(8,128)S(1)} %bitcast.24, f32[768,8,128]{2,1,0:T(8,128)S(1)} %get-tuple-element.59.refs_0_.c_ref, ...), custom_call_target="tpu_custom_call" | custom-call | tf_op jit(solution)/shard_map/pallas_call | solution.py:675
  130.7 2.4 %collective-permute-done.15.refs_5_ = bf16[96,8,128]{2,1,0:T(8,128)(2,1)S(1)} collective-permute-done((bf16[96,8,128]{2,1,0:T(8,128)(2,1)S(1)}, bf16[96,8,128]{2,1,0:T(8,128)(2,1)S(1)}, u32[]{:S(2)}, u32[]{:S(2)}) %collective-permute-start.15) | collective-permute-done | bytes 196640 | tf_op jit(solution)/shard_map/ppermute | solution.py:781
  133.1 2.1 %collective-permute-done.16.refs_6_ = bf16[96,8,128]{2,1,0:T(8,128)(2,1)S(1)} collective-permute-done((bf16[96,8,128]{2,1,0:T(8,128)(2,1)S(1)}, bf16[96,8,128]{2,1,0:T(8,128)(2,1)S(1)}, u32[]{:S(2)}, u32[]{:S(2)}) %collective-permute-start.16) | collective-permute-done | bytes 196640 | tf_op jit(solution)/shard_map/ppermute | solution.py:781
  135.2 11.9 %all_to_all.27 = f32[64,1,128]{2,1,0:T(1,128)S(1)} all-to-all(f32[64,1,128]{2,1,0:T(1,128)S(1)} %bitcast.28), channel_id=1, replica_groups=mesh['gx'=16,'gy'=4,'tx'=4] {'gx','gy'}, dimensions={0} | all-to-all | bytes 65536 | tf_op jit(solution)/shard_map/all_to_all | solution.py:690
  147.1 4.6 %shard_map.67 = (f32[96,16,256]{2,1,0:T(8,128)S(1)}, f32[96,16,256]{2,1,0:T(8,128)S(1)}, f32[16,128]{1,0:T(8,128)S(1)}, f32[64,128]{1,0:T(8,128)S(1)}) custom-call(f32[64,128]{1,0:T(8,128)S(1)} %bitcast.27, f32[768,8,128]{2,1,0:T(8,128)S(1)} %get-tuple-element.59.refs_0_.c_ref, f32[768,8,128]{2,1,0:T(8,128)S(1)} %get-tuple-element.60.refs_1_, ...), custom_call_target="tpu_custom_call" | custom-call | tf_op jit(solution)/shard_map/pallas_call | solution.py:675
  151.7 12.2 %all_to_all.28 = f32[64,1,128]{2,1,0:T(1,128)S(1)} all-to-all(f32[64,1,128]{2,1,0:T(1,128)S(1)} %bitcast.31), channel_id=1, replica_groups=mesh['gx'=16,'gy'=4,'tx'=4] {'gx','gy'}, dimensions={0} | all-to-all | bytes 65536 | tf_op jit(solution)/shard_map/all_to_all | solution.py:690
  163.9 3.2 %shard_map.68 = (f32[96,8,128]{2,1,0:T(8,128)}, f32[96,8,128]{2,1,0:T(8,128)}) custom-call(f32[64,128]{1,0:T(8,128)S(1)} %bitcast.25, f32[768,8,128]{2,1,0:T(8,128)S(1)} %get-tuple-element.59.refs_0_.c_ref, bf16[192,8,128]{2,1,0:T(8,128)(2,1)S(1)} %bitcast.23, bf16[96,8,128]{2,1,0:T(8,128)(2,1)S(1)} %collective-permute-done.11.refs_1_, ...), custom_call_target="tpu_custom_call" | custom-call | tf_op jit(solution)/shard_map/pallas_call | solution.py:675
  (20 shorter events, 0.1 us)
Async XLA Ops:
  1.7 22.4 %collective-permute-start.4 = (bf16[198,8,128]{2,1,0:T(8,128)(2,1)S(1)}, bf16[198,8,128]{2,1,0:T(8,128)(2,1)S(1)}, u32[]{:S(2)}, u32[]{:S(2)}) collective-permute-start(bf16[198,8,128]{2,1,0:T(8,128)(2,1)S(1)} %pad_maximum_fusion.block_ref.refs_0_), channel_id=1, source_target_pairs={{1,0},{2,1},{3,2},{0,3},{5,4},{6,5},{7,6},{4,7},{9,8},{10,9},{11,1... | collective-permute-start | bytes 1216520 | tf_op jit(solution)/shard_map/ppermute | solution.py:712
  8.6 15.5 %collective-permute-start.3 = (bf16[198,8,128]{2,1,0:T(8,128)(2,1)S(1)}, bf16[198,8,128]{2,1,0:T(8,128)(2,1)S(1)}, u32[]{:S(2)}, u32[]{:S(2)}) collective-permute-start(bf16[198,8,128]{2,1,0:T(8,128)(2,1)S(1)} %pad_maximum_fusion.block_ref.refs_0_), channel_id=1, source_target_pairs={{0,1},{1,2},{2,3},{3,0},{4,5},{5,6},{6,7},{7,4},{8,9},{9,10},{10,1... | collective-permute-start | bytes 1216520 | tf_op jit(solution)/shard_map/ppermute | solution.py:711
  8.9 4.5 %collective-permute-start.1 = (bf16[13,8,128]{2,1,0:T(8,128)(2,1)S(1)}, bf16[13,8,128]{2,1,0:T(8,128)(2,1)S(1)}, u32[]{:S(2)}, u32[]{:S(2)}) collective-permute-start(bf16[13,8,128]{2,1,0:T(8,128)(2,1)S(1)} %shard_map.59), channel_id=1, source_target_pairs={{0,4},{4,8},{8,12},{1,5},{5,9},{9,13},{2,6},{6,10},{10,14},{3,7},{... | collective-permute-start | bytes 79880 | tf_op jit(solution)/shard_map/ppermute | solution.py:714
  12.1 4.9 %collective-permute-start = (bf16[13,8,128]{2,1,0:T(8,128)(2,1)S(1)}, bf16[13,8,128]{2,1,0:T(8,128)(2,1)S(1)}, u32[]{:S(2)}, u32[]{:S(2)}) collective-permute-start(bf16[13,8,128]{2,1,0:T(8,128)(2,1)S(1)} %shard_map.59), channel_id=1, source_target_pairs={{4,0},{8,4},{12,8},{5,1},{9,5},{13,9},{6,2},{10,6},{14,10},{7,3},{... | collective-permute-start | bytes 79880 | tf_op jit(solution)/shard_map/ppermute | solution.py:714
  17.1 7.0 %collective-permute-start.2 = (bf16[13,8,128]{2,1,0:T(8,128)(2,1)S(1)}, bf16[13,8,128]{2,1,0:T(8,128)(2,1)S(1)}, u32[]{:S(2)}, u32[]{:S(2)}) collective-permute-start(bf16[13,8,128]{2,1,0:T(8,128)(2,1)S(1)} %broadcast_select_fusion.refs_5_.refs_3_.refs_4_), channel_id=1, source_target_pairs={{0,2},{1,3},{2,0},{3,1},{4,6},{5,7},{6,4},{7,5},{8,10},{9,11},{10,... | collective-permute-start | bytes 79880 | tf_op jit(solution)/shard_map/ppermute | solution.py:716
  24.2 20.1 %collective-permute-start.6 = (bf16[115,8,128]{2,1,0:T(8,128)(2,1)S(1)}, bf16[115,8,128]{2,1,0:T(8,128)(2,1)S(1)}, u32[]{:S(2)}, u32[]{:S(2)}) collective-permute-start(bf16[115,8,128]{2,1,0:T(8,128)(2,1)S(1)} %pad_maximum_fusion.1), channel_id=1, source_target_pairs={{1,0},{2,1},{3,2},{0,3},{5,4},{6,5},{7,6},{4,7},{9,8},{10,9},{11,1... | collective-permute-start | bytes 706568 | tf_op jit(solution)/shard_map/ppermute | solution.py:719
  30.9 18.7 %copy-start.2 = (s32[2]{0:T(128)S(1)}, s32[2]{0:T(128)}, u32[]{:S(2)}) copy-start(s32[2]{0:T(128)} %src_ref.3) | copy-start | bytes 28
  30.9 13.3 %collective-permute-start.5 = (bf16[109,8,128]{2,1,0:T(8,128)(2,1)S(1)}, bf16[109,8,128]{2,1,0:T(8,128)(2,1)S(1)}, u32[]{:S(2)}, u32[]{:S(2)}) collective-permute-start(bf16[109,8,128]{2,1,0:T(8,128)(2,1)S(1)} %pad_maximum_fusion.2), channel_id=1, source_target_pairs={{0,1},{1,2},{2,3},{3,0},{4,5},{5,6},{6,7},{7,4},{8,9},{9,10},{10,1... | collective-permute-start | bytes 669704 | tf_op jit(solution)/shard_map/ppermute | solution.py:718
  32.7 40.4 %collective-permute-start.7 = (bf16[310,8,128]{2,1,0:T(8,128)(2,1)}, bf16[310,8,128]{2,1,0:T(8,128)(2,1)S(1)}, u32[]{:S(2)}, u32[]{:S(2)}) collective-permute-start(bf16[310,8,128]{2,1,0:T(8,128)(2,1)} %get-tuple-element.55), channel_id=1, source_target_pairs={{16,0},{32,16},{48,32},{64,48},{80,64},{96,80},{112,96},{128,112},... | collective-permute-start | bytes 1904648 | tf_op jit(solution)/shard_map/ppermute | solution.py:726
  38.4 27.3 %copy-start = (bf16[4,2,3,8,8,128]{5,4,3,2,1,0:T(8,128)(2,1)S(1)}, bf16[4,2,3,8,8,128]{5,4,3,2,1,0:T(8,128)(2,1)}, u32[]{:S(2)}) copy-start(bf16[4,2,3,8,8,128]{5,4,3,2,1,0:T(8,128)(2,1)} %param.5) | copy-start | bytes 1179652
  38.4 34.7 %collective-permute-start.8 = (bf16[310,8,128]{2,1,0:T(8,128)(2,1)}, bf16[310,8,128]{2,1,0:T(8,128)(2,1)S(1)}, u32[]{:S(2)}, u32[]{:S(2)}) collective-permute-start(bf16[310,8,128]{2,1,0:T(8,128)(2,1)} %get-tuple-element.56), channel_id=1, source_target_pairs={{0,16},{16,32},{32,48},{48,64},{64,80},{80,96},{96,112},{112,128},... | collective-permute-start | bytes 1904648 | tf_op jit(solution)/shard_map/ppermute | solution.py:726
  45.4 0.7 copy-start.3
  46.1 24.8 %collective-permute-start.9 = (bf16[138,8,128]{2,1,0:T(8,128)(2,1)}, bf16[138,8,128]{2,1,0:T(8,128)(2,1)}, u32[]{:S(2)}, u32[]{:S(2)}) collective-permute-start(bf16[138,8,128]{2,1,0:T(8,128)(2,1)} %get-tuple-element.57), channel_id=1, source_target_pairs={{16,0},{32,16},{48,32},{64,48},{80,64},{96,80},{112,96},{128,112},... | collective-permute-start | bytes 847880 | tf_op jit(solution)/shard_map/ppermute | solution.py:726
  52.3 0.7 copy-start.1
  53.0 17.7 %all-to-all-start = ((f32[64,3,128]{2,1,0:T(4,128)}), f32[64,3,128]{2,1,0:T(4,128)S(1)}, u32[]{:S(2)}, u32[]{:S(2)}) async-start(f32[64,3,128]{2,1,0:T(4,128)} %copy-done.1), calls=%async_computation | async-start | bytes 262144 | tf_op jit(solution)/shard_map/all_to_all | solution.py:690
  62.1 10.9 %collective-permute-start.10 = (bf16[138,8,128]{2,1,0:T(8,128)(2,1)}, bf16[138,8,128]{2,1,0:T(8,128)(2,1)}, u32[]{:S(2)}, u32[]{:S(2)}) collective-permute-start(bf16[138,8,128]{2,1,0:T(8,128)(2,1)} %copy-done.3), channel_id=1, source_target_pairs={{0,16},{16,32},{32,48},{48,64},{64,80},{80,96},{96,112},{112,128},... | collective-permute-start | bytes 847880 | tf_op jit(solution)/shard_map/ppermute | solution.py:726
  70.7 12.0 %collective-permute-start.12 = (bf16[96,8,128]{2,1,0:T(8,128)(2,1)}, bf16[96,8,128]{2,1,0:T(8,128)(2,1)S(1)}, u32[]{:S(2)}, u32[]{:S(2)}) collective-permute-start(bf16[96,8,128]{2,1,0:T(8,128)(2,1)} %bitcast.35), channel_id=1, source_target_pairs={{1,0},{2,1},{3,2},{0,3},{5,4},{6,5},{7,6},{4,7},{9,8},{10,9},{11,1... | collective-permute-start | bytes 589832 | tf_op jit(solution)/shard_map/ppermute | solution.py:759
  70.8 11.9 %collective-permute-start.11 = (bf16[96,8,128]{2,1,0:T(8,128)(2,1)}, bf16[96,8,128]{2,1,0:T(8,128)(2,1)S(1)}, u32[]{:S(2)}, u32[]{:S(2)}) collective-permute-start(bf16[96,8,128]{2,1,0:T(8,128)(2,1)} %bitcast.36), channel_id=1, source_target_pairs={{0,1},{1,2},{2,3},{3,0},{4,5},{5,6},{6,7},{7,4},{8,9},{9,10},{10,1... | collective-permute-start | bytes 589832 | tf_op jit(solution)/shard_map/ppermute | solution.py:759
  75.9 20.5 %copy-start.4 = (bf16[2,2,3,8,8,128]{5,4,3,2,1,0:T(8,128)(2,1)S(1)}, bf16[2,2,3,8,8,128]{5,4,3,2,1,0:T(8,128)(2,1)}, u32[]{:S(2)}) copy-start(bf16[2,2,3,8,8,128]{5,4,3,2,1,0:T(8,128)(2,1)} %get-tuple-element.100) | copy-start | bytes 589828
  96.4 11.7 %collective-permute-start.14 = (bf16[96,8,128]{2,1,0:T(8,128)(2,1)S(1)}, bf16[96,8,128]{2,1,0:T(8,128)(2,1)S(1)}, u32[]{:S(2)}, u32[]{:S(2)}) collective-permute-start(bf16[96,8,128]{2,1,0:T(8,128)(2,1)S(1)} %bitcast.33), channel_id=1, source_target_pairs={{1,0},{2,1},{3,2},{0,3},{5,4},{6,5},{7,6},{4,7},{9,8},{10,9},{11,1... | collective-permute-start | bytes 589832 | tf_op jit(solution)/shard_map/ppermute | solution.py:777
  96.8 11.9 %collective-permute-start.13 = (bf16[96,8,128]{2,1,0:T(8,128)(2,1)S(1)}, bf16[96,8,128]{2,1,0:T(8,128)(2,1)S(1)}, u32[]{:S(2)}, u32[]{:S(2)}) collective-permute-start(bf16[96,8,128]{2,1,0:T(8,128)(2,1)S(1)} %bitcast.34), channel_id=1, source_target_pairs={{0,1},{1,2},{2,3},{3,0},{4,5},{5,6},{6,7},{7,4},{8,9},{9,10},{10,1... | collective-permute-start | bytes 589832 | tf_op jit(solution)/shard_map/ppermute | solution.py:777
  121.8 11.3 %collective-permute-start.15 = (bf16[96,8,128]{2,1,0:T(8,128)(2,1)S(1)}, bf16[96,8,128]{2,1,0:T(8,128)(2,1)S(1)}, u32[]{:S(2)}, u32[]{:S(2)}) collective-permute-start(bf16[96,8,128]{2,1,0:T(8,128)(2,1)S(1)} %collective-permute-done.11.refs_1_), channel_id=1, source_target_pairs={{0,1},{1,2},{2,3},{3,0},{4,5},{5,6},{6,7},{7,4},{8,9},{9,10},{10,1... | collective-permute-start | bytes 589832 | tf_op jit(solution)/shard_map/ppermute | solution.py:781
  122.7 12.5 %collective-permute-start.16 = (bf16[96,8,128]{2,1,0:T(8,128)(2,1)S(1)}, bf16[96,8,128]{2,1,0:T(8,128)(2,1)S(1)}, u32[]{:S(2)}, u32[]{:S(2)}) collective-permute-start(bf16[96,8,128]{2,1,0:T(8,128)(2,1)S(1)} %collective-permute-done.14.refs_4_), channel_id=1, source_target_pairs={{1,0},{2,1},{3,2},{0,3},{5,4},{6,5},{7,6},{4,7},{9,8},{10,9},{11,1... | collective-permute-start | bytes 589832 | tf_op jit(solution)/shard_map/ppermute | solution.py:781

commit v10 on v9

--- a/solution.py
+++ b/solution.py
@@ -15,7 +15,7 @@
 HALF = 99
 PACKED = 13
 WEIGHTS = (1.0, 0.5, 0.25)
-AT_ONCE = 8
+AT_ONCE = 12
 HIGH = lax.Precision.HIGHEST
 F32 = jnp.float32
 BF16 = jnp.bfloat16

time: 168 us -> 167 us (level)
  no operation moved by 1% of the time
where the time goes in v10:
time: 167 us
  starting transfers between devices  54.8 us (33%)
  blocking collectives  50.9 us (30%)
  Pallas kernels  32.2 us (19%)
  waiting for transfers between devices  24.9 us (15%)
  local copies, waits for them, and re-layouts  2.18 us (1%)
    all_to_all x4, blocking collectives, exchange(): return lax.all_to_all(value, ('gx', 'gy'), 0, 0)  50.9 us
    pallas_call x10, Pallas kernels, call(): pl.pallas_call(kernel, out_shape=outs, in_specs=[pl.BlockSpec(memory_spac...  32.2 us
    ppermute x4, starting transfers between devices, exchange_x(): return (lax.ppermute(low, 'gx', down), lax.ppermute(high, 'gx', up))  15.8 us
    all_to_all x1, starting transfers between devices, exchange(): return lax.all_to_all(value, ('gx', 'gy'), 0, 0)  9.12 us
    ppermute x1, starting transfers between devices, on_device(): three = lax.ppermute(block, 'tx', left)  6.93 us
    ppermute x1, starting transfers between devices, on_device(): far_high = lax.ppermute(jnp.concatenate([three[CUT:], side]), 'tx', left)  6.71 us
    ppermute x2, waiting for transfers between devices, on_device(): lax.ppermute(piece, 'tx', left)  5.47 us
    ppermute x2, starting transfers between devices, on_device(): after, before = (lax.ppermute(own, 'gy', down), lax.ppermute(own, 'gy', up))  4.5 us
  transfers between devices with their start and end apart: 18, of which 9 were waited for; matrix products, arithmetic and copies ran while one was open for 1% of the time, Pallas kernels for 15%

profile of v10, /device:TPU:1, one launch (start us, length us, event | category | flops | bytes accessed | tf_op | source)
XLA Modules:
  0.0 167.0 jit_solution(13638604785823562178)
XLA Ops:
  0.6 1.1 pad_maximum_fusion.block_ref.refs_0_
  1.7 6.9 %collective-permute-start.4 = (bf16[198,8,128]{2,1,0:T(8,128)(2,1)S(1)}, bf16[198,8,128]{2,1,0:T(8,128)(2,1)S(1)}, u32[]{:S(2)}, u32[]{:S(2)}) collective-permute-start(bf16[198,8,128]{2,1,0:T(8,128)(2,1)S(1)} %pad_maximum_fusion.block_ref.refs_0_), channel_id=1, source_target_pairs={{1,0},{2,1},{3,2},{0,3},{5,4},{6,5},{7,6},{4,7},{9,8},{10,9},{11,1... | collective-permute-start | bytes 1216520 | tf_op jit(solution)/shard_map/ppermute | solution.py:712
  8.6 0.3 shard_map.59
  8.9 3.2 %collective-permute-start.1 = (bf16[13,8,128]{2,1,0:T(8,128)(2,1)S(1)}, bf16[13,8,128]{2,1,0:T(8,128)(2,1)S(1)}, u32[]{:S(2)}, u32[]{:S(2)}) collective-permute-start(bf16[13,8,128]{2,1,0:T(8,128)(2,1)S(1)} %shard_map.59), channel_id=1, source_target_pairs={{0,4},{4,8},{8,12},{1,5},{5,9},{9,13},{2,6},{6,10},{10,14},{3,7},{... | collective-permute-start | bytes 79880 | tf_op jit(solution)/shard_map/ppermute | solution.py:714
  12.1 1.3 collective-permute-start
  13.5 3.6 %collective-permute-done = bf16[13,8,128]{2,1,0:T(8,128)(2,1)S(1)} collective-permute-done((bf16[13,8,128]{2,1,0:T(8,128)(2,1)S(1)}, bf16[13,8,128]{2,1,0:T(8,128)(2,1)S(1)}, u32[]{:S(2)}, u32[]{:S(2)}) %collective-permute-start) | collective-permute-done | bytes 26656 | tf_op jit(solution)/shard_map/ppermute | solution.py:714
  17.0 0.1 broadcast_select_fusion.refs_5_.refs_3_.refs_4_
  17.1 3.3 %collective-permute-start.2 = (bf16[13,8,128]{2,1,0:T(8,128)(2,1)S(1)}, bf16[13,8,128]{2,1,0:T(8,128)(2,1)S(1)}, u32[]{:S(2)}, u32[]{:S(2)}) collective-permute-start(bf16[13,8,128]{2,1,0:T(8,128)(2,1)S(1)} %broadcast_select_fusion.refs_5_.refs_3_.refs_4_), channel_id=1, source_target_pairs={{0,2},{1,3},{2,0},{3,1},{4,6},{5,7},{6,4},{7,5},{8,10},{9,11},{10,... | collective-permute-start | bytes 79880 | tf_op jit(solution)/shard_map/ppermute | solution.py:716
  20.4 3.7 %collective-permute-done.2.refs_6_ = bf16[13,8,128]{2,1,0:T(8,128)(2,1)S(1)} collective-permute-done((bf16[13,8,128]{2,1,0:T(8,128)(2,1)S(1)}, bf16[13,8,128]{2,1,0:T(8,128)(2,1)S(1)}, u32[]{:S(2)}, u32[]{:S(2)}) %collective-permute-start.2) | collective-permute-done | bytes 26656 | tf_op jit(solution)/shard_map/ppermute | solution.py:716
  24.2 6.7 %collective-permute-start.6 = (bf16[115,8,128]{2,1,0:T(8,128)(2,1)S(1)}, bf16[115,8,128]{2,1,0:T(8,128)(2,1)S(1)}, u32[]{:S(2)}, u32[]{:S(2)}) collective-permute-start(bf16[115,8,128]{2,1,0:T(8,128)(2,1)S(1)} %pad_maximum_fusion.1), channel_id=1, source_target_pairs={{1,0},{2,1},{3,2},{0,3},{5,4},{6,5},{7,6},{4,7},{9,8},{10,9},{11,1... | collective-permute-start | bytes 706568 | tf_op jit(solution)/shard_map/ppermute | solution.py:719
  30.9 0.0 copy-start.2
  30.9 0.1 collective-permute-start.5
  31.0 1.7 %shard_map.61 = (bf16[310,8,128]{2,1,0:T(8,128)(2,1)}, bf16[310,8,128]{2,1,0:T(8,128)(2,1)}) custom-call(bf16[198,8,128]{2,1,0:T(8,128)(2,1)S(1)} %pad_maximum_fusion.block_ref.refs_0_, bf16[198,8,128]{2,1,0:T(8,128)(2,1)S(1)} %collective-permute-done.3.refs_1_, bf16[198,8,128]{2,1,0:T(8,128)(2,1)S(1)} %collective-permute-done.4.refs_2_, ...), custom_call_target="tpu_custom_call" | custom-call | tf_op jit(solution)/shard_map/pallas_call | solution.py:675
  32.7 5.7 %collective-permute-start.7 = (bf16[310,8,128]{2,1,0:T(8,128)(2,1)}, bf16[310,8,128]{2,1,0:T(8,128)(2,1)S(1)}, u32[]{:S(2)}, u32[]{:S(2)}) collective-permute-start(bf16[310,8,128]{2,1,0:T(8,128)(2,1)} %get-tuple-element.55), channel_id=1, source_target_pairs={{16,0},{32,16},{48,32},{64,48},{80,64},{96,80},{112,96},{128,112},... | collective-permute-start | bytes 1904648 | tf_op jit(solution)/shard_map/ppermute | solution.py:726
  38.4 0.0 copy-start
  38.4 3.1 %collective-permute-start.8 = (bf16[310,8,128]{2,1,0:T(8,128)(2,1)}, bf16[310,8,128]{2,1,0:T(8,128)(2,1)S(1)}, u32[]{:S(2)}, u32[]{:S(2)}) collective-permute-start(bf16[310,8,128]{2,1,0:T(8,128)(2,1)} %get-tuple-element.56), channel_id=1, source_target_pairs={{0,16},{16,32},{32,48},{48,64},{64,80},{80,96},{96,112},{112,128},... | collective-permute-start | bytes 1904648 | tf_op jit(solution)/shard_map/ppermute | solution.py:726
  41.5 2.7 %collective-permute-done.5.refs_3_ = bf16[109,8,128]{2,1,0:T(8,128)(2,1)S(1)} collective-permute-done((bf16[109,8,128]{2,1,0:T(8,128)(2,1)S(1)}, bf16[109,8,128]{2,1,0:T(8,128)(2,1)S(1)}, u32[]{:S(2)}, u32[]{:S(2)}) %collective-permute-start.5) | collective-permute-done | bytes 223264 | tf_op jit(solution)/shard_map/ppermute | solution.py:718
  44.3 1.1 shard_map.62
  45.4 0.7 copy-done.3
  46.1 3.5 %collective-permute-start.9 = (bf16[138,8,128]{2,1,0:T(8,128)(2,1)}, bf16[138,8,128]{2,1,0:T(8,128)(2,1)}, u32[]{:S(2)}, u32[]{:S(2)}) collective-permute-start(bf16[138,8,128]{2,1,0:T(8,128)(2,1)} %get-tuple-element.57), channel_id=1, source_target_pairs={{16,0},{32,16},{48,32},{64,48},{80,64},{96,80},{112,96},{128,112},... | collective-permute-start | bytes 847880 | tf_op jit(solution)/shard_map/ppermute | solution.py:726
  49.6 2.8 %shard_map.60 = f32[64,3,128]{2,1,0:T(4,128)S(1)} custom-call(s32[2]{0:T(128)S(1)} %copy-done.2, bf16[198,8,128]{2,1,0:T(8,128)(2,1)S(1)} %pad_maximum_fusion.block_ref.refs_0_, bf16[198,8,128]{2,1,0:T(8,128)(2,1)S(1)} %collective-permute-done.3.refs_1_, bf16[198,8,128]{2,1,0:T(8,128)(2,1)S(1)} %collective-permute-done.4.refs_2_, ...), custom_call_target="tpu_custom_call" | custom-call | tf_op jit(solution)/shard_map/pallas_call | solution.py:675
  52.3 0.6 copy-done.1
  53.0 9.1 %all-to-all-start = ((f32[64,3,128]{2,1,0:T(4,128)}), f32[64,3,128]{2,1,0:T(4,128)S(1)}, u32[]{:S(2)}, u32[]{:S(2)}) async-start(f32[64,3,128]{2,1,0:T(4,128)} %copy-done.1), calls=%async_computation | async-start | bytes 262144 | tf_op jit(solution)/shard_map/all_to_all | solution.py:690
  62.1 3.5 %collective-permute-start.10 = (bf16[138,8,128]{2,1,0:T(8,128)(2,1)}, bf16[138,8,128]{2,1,0:T(8,128)(2,1)}, u32[]{:S(2)}, u32[]{:S(2)}) collective-permute-start(bf16[138,8,128]{2,1,0:T(8,128)(2,1)} %copy-done.3), channel_id=1, source_target_pairs={{0,16},{16,32},{32,48},{48,64},{64,80},{80,96},{96,112},{112,128},... | collective-permute-start | bytes 847880 | tf_op jit(solution)/shard_map/ppermute | solution.py:726
  65.7 0.8 fusion
  66.5 4.2 %all-to-all-done.got_ref = f32[64,3,128]{2,1,0:T(4,128)S(1)} async-done(((f32[64,3,128]{2,1,0:T(4,128)}), f32[64,3,128]{2,1,0:T(4,128)S(1)}, u32[]{:S(2)}, u32[]{:S(2)}) %all-to-all-start) | async-done | bytes 98336 | tf_op jit(solution)/shard_map/all_to_all | solution.py:690
  70.7 0.1 collective-permute-start.12
  70.8 0.0 collective-permute-done.9.refs_9_
  70.8 2.2 %collective-permute-start.11 = (bf16[96,8,128]{2,1,0:T(8,128)(2,1)}, bf16[96,8,128]{2,1,0:T(8,128)(2,1)S(1)}, u32[]{:S(2)}, u32[]{:S(2)}) collective-permute-start(bf16[96,8,128]{2,1,0:T(8,128)(2,1)} %bitcast.36), channel_id=1, source_target_pairs={{0,1},{1,2},{2,3},{3,0},{4,5},{5,6},{6,7},{7,4},{8,9},{9,10},{10,1... | collective-permute-start | bytes 589832 | tf_op jit(solution)/shard_map/ppermute | solution.py:759
  73.1 2.8 %shard_map.63 = (f32[24,16,256]{2,1,0:T(8,128)S(1)}, f32[48,16,256]{2,1,0:T(8,128)S(1)}, f32[768,8,128]{2,1,0:T(8,128)S(1)}, f32[768,8,128]{2,1,0:T(8,128)S(1)},...) custom-call(s32[2]{0:T(128)S(1)} %copy-done.2, bf16[198,8,128]{2,1,0:T(8,128)(2,1)S(1)} %pad_maximum_fusion.block_ref.refs_0_, ...), custom_call_target="tpu_custom_call" | custom-call | tf_op jit(solution)/shard_map/pallas_call | solution.py:675
  75.9 6.1 %shard_map.64 = (f32[96,16,256]{2,1,0:T(8,128)S(1)}, f32[96,16,256]{2,1,0:T(8,128)S(1)}, f32[16,128]{1,0:T(8,128)S(1)}, f32[16,128]{1,0:T(8,128)S(1)}, f32[64,128]{1,0:T(8,128)S(1)}) custom-call(f32[64,3,128]{2,1,0:T(4,128)S(1)} %all-to-all-done.got_ref, f32[768,8,128]{2,1,0:T(8,128)S(1)} %get-tuple-element.59.refs_0_.c_ref, ...), custom_call_target="tpu_custom_call" | custom-call | tf_op jit(solution)/shard_map/pallas_call | solution.py:675
  82.0 0.7 collective-permute-done.12.refs_3_
  82.7 13.7 %all_to_all.25 = f32[64,1,128]{2,1,0:T(1,128)S(1)} all-to-all(f32[64,1,128]{2,1,0:T(1,128)S(1)} %bitcast.29), channel_id=1, replica_groups=mesh['gx'=16,'gy'=4,'tx'=4] {'gx','gy'}, dimensions={0} | all-to-all | bytes 65536 | tf_op jit(solution)/shard_map/all_to_all | solution.py:690
  96.4 0.4 collective-permute-start.14
  96.8 2.0 %collective-permute-start.13 = (bf16[96,8,128]{2,1,0:T(8,128)(2,1)S(1)}, bf16[96,8,128]{2,1,0:T(8,128)(2,1)S(1)}, u32[]{:S(2)}, u32[]{:S(2)}) collective-permute-start(bf16[96,8,128]{2,1,0:T(8,128)(2,1)S(1)} %bitcast.34), channel_id=1, source_target_pairs={{0,1},{1,2},{2,3},{3,0},{4,5},{5,6},{6,7},{7,4},{8,9},{9,10},{10,1... | collective-permute-start | bytes 589832 | tf_op jit(solution)/shard_map/ppermute | solution.py:777
  98.7 4.6 %shard_map.65 = (f32[96,16,256]{2,1,0:T(8,128)S(1)}, f32[96,16,256]{2,1,0:T(8,128)S(1)}, f32[16,128]{1,0:T(8,128)S(1)}, f32[64,128]{1,0:T(8,128)S(1)}) custom-call(f32[64,128]{1,0:T(8,128)S(1)} %bitcast.26, f32[768,8,128]{2,1,0:T(8,128)S(1)} %get-tuple-element.59.refs_0_.c_ref, f32[768,8,128]{2,1,0:T(8,128)S(1)} %get-tuple-element.60.refs_1_, ...), custom_call_target="tpu_custom_call" | custom-call | tf_op jit(solution)/shard_map/pallas_call | solution.py:675
  103.3 4.8 %collective-permute-done.14.refs_4_ = bf16[96,8,128]{2,1,0:T(8,128)(2,1)S(1)} collective-permute-done((bf16[96,8,128]{2,1,0:T(8,128)(2,1)S(1)}, bf16[96,8,128]{2,1,0:T(8,128)(2,1)S(1)}, u32[]{:S(2)}, u32[]{:S(2)}) %collective-permute-start.14) | collective-permute-done | bytes 196640 | tf_op jit(solution)/shard_map/ppermute | solution.py:777
  108.1 0.6 collective-permute-done.13.refs_2_
  108.7 13.1 %all_to_all.26 = f32[64,1,128]{2,1,0:T(1,128)S(1)} all-to-all(f32[64,1,128]{2,1,0:T(1,128)S(1)} %bitcast.30), channel_id=1, replica_groups=mesh['gx'=16,'gy'=4,'tx'=4] {'gx','gy'}, dimensions={0} | all-to-all | bytes 65536 | tf_op jit(solution)/shard_map/all_to_all | solution.py:690
  121.8 0.8 collective-permute-start.15
  122.7 2.7 %collective-permute-start.16 = (bf16[96,8,128]{2,1,0:T(8,128)(2,1)S(1)}, bf16[96,8,128]{2,1,0:T(8,128)(2,1)S(1)}, u32[]{:S(2)}, u32[]{:S(2)}) collective-permute-start(bf16[96,8,128]{2,1,0:T(8,128)(2,1)S(1)} %collective-permute-done.14.refs_4_), channel_id=1, source_target_pairs={{1,0},{2,1},{3,2},{0,3},{5,4},{6,5},{7,6},{4,7},{9,8},{10,9},{11,1... | collective-permute-start | bytes 589832 | tf_op jit(solution)/shard_map/ppermute | solution.py:781
  125.4 5.2 %shard_map.66 = (f32[96,16,256]{2,1,0:T(8,128)S(1)}, f32[96,16,256]{2,1,0:T(8,128)S(1)}, f32[96,8,128]{2,1,0:T(8,128)S(1)}, f32[16,128]{1,0:T(8,128)S(1)}, f32[64,128]{1,0:T(8,128)S(1)}) custom-call(f32[64,128]{1,0:T(8,128)S(1)} %bitcast.24, f32[768,8,128]{2,1,0:T(8,128)S(1)} %get-tuple-element.59.refs_0_.c_ref, ...), custom_call_target="tpu_custom_call" | custom-call | tf_op jit(solution)/shard_map/pallas_call | solution.py:675
  130.6 2.5 %collective-permute-done.15.refs_5_ = bf16[96,8,128]{2,1,0:T(8,128)(2,1)S(1)} collective-permute-done((bf16[96,8,128]{2,1,0:T(8,128)(2,1)S(1)}, bf16[96,8,128]{2,1,0:T(8,128)(2,1)S(1)}, u32[]{:S(2)}, u32[]{:S(2)}) %collective-permute-start.15) | collective-permute-done | bytes 196640 | tf_op jit(solution)/shard_map/ppermute | solution.py:781
  133.1 2.1 %collective-permute-done.16.refs_6_ = bf16[96,8,128]{2,1,0:T(8,128)(2,1)S(1)} collective-permute-done((bf16[96,8,128]{2,1,0:T(8,128)(2,1)S(1)}, bf16[96,8,128]{2,1,0:T(8,128)(2,1)S(1)}, u32[]{:S(2)}, u32[]{:S(2)}) %collective-permute-start.16) | collective-permute-done | bytes 196640 | tf_op jit(solution)/shard_map/ppermute | solution.py:781
  135.2 11.9 %all_to_all.27 = f32[64,1,128]{2,1,0:T(1,128)S(1)} all-to-all(f32[64,1,128]{2,1,0:T(1,128)S(1)} %bitcast.28), channel_id=1, replica_groups=mesh['gx'=16,'gy'=4,'tx'=4] {'gx','gy'}, dimensions={0} | all-to-all | bytes 65536 | tf_op jit(solution)/shard_map/all_to_all | solution.py:690
  147.1 4.6 %shard_map.67 = (f32[96,16,256]{2,1,0:T(8,128)S(1)}, f32[96,16,256]{2,1,0:T(8,128)S(1)}, f32[16,128]{1,0:T(8,128)S(1)}, f32[64,128]{1,0:T(8,128)S(1)}) custom-call(f32[64,128]{1,0:T(8,128)S(1)} %bitcast.27, f32[768,8,128]{2,1,0:T(8,128)S(1)} %get-tuple-element.59.refs_0_.c_ref, f32[768,8,128]{2,1,0:T(8,128)S(1)} %get-tuple-element.60.refs_1_, ...), custom_call_target="tpu_custom_call" | custom-call | tf_op jit(solution)/shard_map/pallas_call | solution.py:675
  151.7 12.2 %all_to_all.28 = f32[64,1,128]{2,1,0:T(1,128)S(1)} all-to-all(f32[64,1,128]{2,1,0:T(1,128)S(1)} %bitcast.31), channel_id=1, replica_groups=mesh['gx'=16,'gy'=4,'tx'=4] {'gx','gy'}, dimensions={0} | all-to-all | bytes 65536 | tf_op jit(solution)/shard_map/all_to_all | solution.py:690
  163.9 3.1 %shard_map.68 = (f32[96,8,128]{2,1,0:T(8,128)}, f32[96,8,128]{2,1,0:T(8,128)}) custom-call(f32[64,128]{1,0:T(8,128)S(1)} %bitcast.25, f32[768,8,128]{2,1,0:T(8,128)S(1)} %get-tuple-element.59.refs_0_.c_ref, bf16[192,8,128]{2,1,0:T(8,128)(2,1)S(1)} %bitcast.23, bf16[96,8,128]{2,1,0:T(8,128)(2,1)S(1)} %collective-permute-done.11.refs_1_, ...), custom_call_target="tpu_custom_call" | custom-call | tf_op jit(solution)/shard_map/pallas_call | solution.py:675
  (20 shorter events, 0.1 us)
Async XLA Ops:
  1.7 22.4 %collective-permute-start.4 = (bf16[198,8,128]{2,1,0:T(8,128)(2,1)S(1)}, bf16[198,8,128]{2,1,0:T(8,128)(2,1)S(1)}, u32[]{:S(2)}, u32[]{:S(2)}) collective-permute-start(bf16[198,8,128]{2,1,0:T(8,128)(2,1)S(1)} %pad_maximum_fusion.block_ref.refs_0_), channel_id=1, source_target_pairs={{1,0},{2,1},{3,2},{0,3},{5,4},{6,5},{7,6},{4,7},{9,8},{10,9},{11,1... | collective-permute-start | bytes 1216520 | tf_op jit(solution)/shard_map/ppermute | solution.py:712
  8.6 15.5 %collective-permute-start.3 = (bf16[198,8,128]{2,1,0:T(8,128)(2,1)S(1)}, bf16[198,8,128]{2,1,0:T(8,128)(2,1)S(1)}, u32[]{:S(2)}, u32[]{:S(2)}) collective-permute-start(bf16[198,8,128]{2,1,0:T(8,128)(2,1)S(1)} %pad_maximum_fusion.block_ref.refs_0_), channel_id=1, source_target_pairs={{0,1},{1,2},{2,3},{3,0},{4,5},{5,6},{6,7},{7,4},{8,9},{9,10},{10,1... | collective-permute-start | bytes 1216520 | tf_op jit(solution)/shard_map/ppermute | solution.py:711
  8.9 4.5 %collective-permute-start.1 = (bf16[13,8,128]{2,1,0:T(8,128)(2,1)S(1)}, bf16[13,8,128]{2,1,0:T(8,128)(2,1)S(1)}, u32[]{:S(2)}, u32[]{:S(2)}) collective-permute-start(bf16[13,8,128]{2,1,0:T(8,128)(2,1)S(1)} %shard_map.59), channel_id=1, source_target_pairs={{0,4},{4,8},{8,12},{1,5},{5,9},{9,13},{2,6},{6,10},{10,14},{3,7},{... | collective-permute-start | bytes 79880 | tf_op jit(solution)/shard_map/ppermute | solution.py:714
  12.1 4.9 %collective-permute-start = (bf16[13,8,128]{2,1,0:T(8,128)(2,1)S(1)}, bf16[13,8,128]{2,1,0:T(8,128)(2,1)S(1)}, u32[]{:S(2)}, u32[]{:S(2)}) collective-permute-start(bf16[13,8,128]{2,1,0:T(8,128)(2,1)S(1)} %shard_map.59), channel_id=1, source_target_pairs={{4,0},{8,4},{12,8},{5,1},{9,5},{13,9},{6,2},{10,6},{14,10},{7,3},{... | collective-permute-start | bytes 79880 | tf_op jit(solution)/shard_map/ppermute | solution.py:714
  17.1 7.0 %collective-permute-start.2 = (bf16[13,8,128]{2,1,0:T(8,128)(2,1)S(1)}, bf16[13,8,128]{2,1,0:T(8,128)(2,1)S(1)}, u32[]{:S(2)}, u32[]{:S(2)}) collective-permute-start(bf16[13,8,128]{2,1,0:T(8,128)(2,1)S(1)} %broadcast_select_fusion.refs_5_.refs_3_.refs_4_), channel_id=1, source_target_pairs={{0,2},{1,3},{2,0},{3,1},{4,6},{5,7},{6,4},{7,5},{8,10},{9,11},{10,... | collective-permute-start | bytes 79880 | tf_op jit(solution)/shard_map/ppermute | solution.py:716
  24.2 20.1 %collective-permute-start.6 = (bf16[115,8,128]{2,1,0:T(8,128)(2,1)S(1)}, bf16[115,8,128]{2,1,0:T(8,128)(2,1)S(1)}, u32[]{:S(2)}, u32[]{:S(2)}) collective-permute-start(bf16[115,8,128]{2,1,0:T(8,128)(2,1)S(1)} %pad_maximum_fusion.1), channel_id=1, source_target_pairs={{1,0},{2,1},{3,2},{0,3},{5,4},{6,5},{7,6},{4,7},{9,8},{10,9},{11,1... | collective-permute-start | bytes 706568 | tf_op jit(solution)/shard_map/ppermute | solution.py:719
  30.9 18.7 %copy-start.2 = (s32[2]{0:T(128)S(1)}, s32[2]{0:T(128)}, u32[]{:S(2)}) copy-start(s32[2]{0:T(128)} %src_ref.3) | copy-start | bytes 28
  30.9 13.3 %collective-permute-start.5 = (bf16[109,8,128]{2,1,0:T(8,128)(2,1)S(1)}, bf16[109,8,128]{2,1,0:T(8,128)(2,1)S(1)}, u32[]{:S(2)}, u32[]{:S(2)}) collective-permute-start(bf16[109,8,128]{2,1,0:T(8,128)(2,1)S(1)} %pad_maximum_fusion.2), channel_id=1, source_target_pairs={{0,1},{1,2},{2,3},{3,0},{4,5},{5,6},{6,7},{7,4},{8,9},{9,10},{10,1... | collective-permute-start | bytes 669704 | tf_op jit(solution)/shard_map/ppermute | solution.py:718
  32.7 40.4 %collective-permute-start.7 = (bf16[310,8,128]{2,1,0:T(8,128)(2,1)}, bf16[310,8,128]{2,1,0:T(8,128)(2,1)S(1)}, u32[]{:S(2)}, u32[]{:S(2)}) collective-permute-start(bf16[310,8,128]{2,1,0:T(8,128)(2,1)} %get-tuple-element.55), channel_id=1, source_target_pairs={{16,0},{32,16},{48,32},{64,48},{80,64},{96,80},{112,96},{128,112},... | collective-permute-start | bytes 1904648 | tf_op jit(solution)/shard_map/ppermute | solution.py:726
  38.4 27.3 %copy-start = (bf16[4,2,3,8,8,128]{5,4,3,2,1,0:T(8,128)(2,1)S(1)}, bf16[4,2,3,8,8,128]{5,4,3,2,1,0:T(8,128)(2,1)}, u32[]{:S(2)}) copy-start(bf16[4,2,3,8,8,128]{5,4,3,2,1,0:T(8,128)(2,1)} %param.5) | copy-start | bytes 1179652
  38.4 34.7 %collective-permute-start.8 = (bf16[310,8,128]{2,1,0:T(8,128)(2,1)}, bf16[310,8,128]{2,1,0:T(8,128)(2,1)S(1)}, u32[]{:S(2)}, u32[]{:S(2)}) collective-permute-start(bf16[310,8,128]{2,1,0:T(8,128)(2,1)} %get-tuple-element.56), channel_id=1, source_target_pairs={{0,16},{16,32},{32,48},{48,64},{64,80},{80,96},{96,112},{112,128},... | collective-permute-start | bytes 1904648 | tf_op jit(solution)/shard_map/ppermute | solution.py:726
  45.4 0.7 copy-start.3
  46.1 24.8 %collective-permute-start.9 = (bf16[138,8,128]{2,1,0:T(8,128)(2,1)}, bf16[138,8,128]{2,1,0:T(8,128)(2,1)}, u32[]{:S(2)}, u32[]{:S(2)}) collective-permute-start(bf16[138,8,128]{2,1,0:T(8,128)(2,1)} %get-tuple-element.57), channel_id=1, source_target_pairs={{16,0},{32,16},{48,32},{64,48},{80,64},{96,80},{112,96},{128,112},... | collective-permute-start | bytes 847880 | tf_op jit(solution)/shard_map/ppermute | solution.py:726
  52.3 0.7 copy-start.1
  53.0 17.7 %all-to-all-start = ((f32[64,3,128]{2,1,0:T(4,128)}), f32[64,3,128]{2,1,0:T(4,128)S(1)}, u32[]{:S(2)}, u32[]{:S(2)}) async-start(f32[64,3,128]{2,1,0:T(4,128)} %copy-done.1), calls=%async_computation | async-start | bytes 262144 | tf_op jit(solution)/shard_map/all_to_all | solution.py:690
  62.1 10.9 %collective-permute-start.10 = (bf16[138,8,128]{2,1,0:T(8,128)(2,1)}, bf16[138,8,128]{2,1,0:T(8,128)(2,1)}, u32[]{:S(2)}, u32[]{:S(2)}) collective-permute-start(bf16[138,8,128]{2,1,0:T(8,128)(2,1)} %copy-done.3), channel_id=1, source_target_pairs={{0,16},{16,32},{32,48},{48,64},{64,80},{80,96},{96,112},{112,128},... | collective-permute-start | bytes 847880 | tf_op jit(solution)/shard_map/ppermute | solution.py:726
  70.7 12.0 %collective-permute-start.12 = (bf16[96,8,128]{2,1,0:T(8,128)(2,1)}, bf16[96,8,128]{2,1,0:T(8,128)(2,1)S(1)}, u32[]{:S(2)}, u32[]{:S(2)}) collective-permute-start(bf16[96,8,128]{2,1,0:T(8,128)(2,1)} %bitcast.35), channel_id=1, source_target_pairs={{1,0},{2,1},{3,2},{0,3},{5,4},{6,5},{7,6},{4,7},{9,8},{10,9},{11,1... | collective-permute-start | bytes 589832 | tf_op jit(solution)/shard_map/ppermute | solution.py:759
  70.8 11.9 %collective-permute-start.11 = (bf16[96,8,128]{2,1,0:T(8,128)(2,1)}, bf16[96,8,128]{2,1,0:T(8,128)(2,1)S(1)}, u32[]{:S(2)}, u32[]{:S(2)}) collective-permute-start(bf16[96,8,128]{2,1,0:T(8,128)(2,1)} %bitcast.36), channel_id=1, source_target_pairs={{0,1},{1,2},{2,3},{3,0},{4,5},{5,6},{6,7},{7,4},{8,9},{9,10},{10,1... | collective-permute-start | bytes 589832 | tf_op jit(solution)/shard_map/ppermute | solution.py:759
  75.9 20.5 %copy-start.4 = (bf16[2,2,3,8,8,128]{5,4,3,2,1,0:T(8,128)(2,1)S(1)}, bf16[2,2,3,8,8,128]{5,4,3,2,1,0:T(8,128)(2,1)}, u32[]{:S(2)}) copy-start(bf16[2,2,3,8,8,128]{5,4,3,2,1,0:T(8,128)(2,1)} %get-tuple-element.100) | copy-start | bytes 589828
  96.4 11.7 %collective-permute-start.14 = (bf16[96,8,128]{2,1,0:T(8,128)(2,1)S(1)}, bf16[96,8,128]{2,1,0:T(8,128)(2,1)S(1)}, u32[]{:S(2)}, u32[]{:S(2)}) collective-permute-start(bf16[96,8,128]{2,1,0:T(8,128)(2,1)S(1)} %bitcast.33), channel_id=1, source_target_pairs={{1,0},{2,1},{3,2},{0,3},{5,4},{6,5},{7,6},{4,7},{9,8},{10,9},{11,1... | collective-permute-start | bytes 589832 | tf_op jit(solution)/shard_map/ppermute | solution.py:777
  96.8 11.9 %collective-permute-start.13 = (bf16[96,8,128]{2,1,0:T(8,128)(2,1)S(1)}, bf16[96,8,128]{2,1,0:T(8,128)(2,1)S(1)}, u32[]{:S(2)}, u32[]{:S(2)}) collective-permute-start(bf16[96,8,128]{2,1,0:T(8,128)(2,1)S(1)} %bitcast.34), channel_id=1, source_target_pairs={{0,1},{1,2},{2,3},{3,0},{4,5},{5,6},{6,7},{7,4},{8,9},{9,10},{10,1... | collective-permute-start | bytes 589832 | tf_op jit(solution)/shard_map/ppermute | solution.py:777
  121.8 11.3 %collective-permute-start.15 = (bf16[96,8,128]{2,1,0:T(8,128)(2,1)S(1)}, bf16[96,8,128]{2,1,0:T(8,128)(2,1)S(1)}, u32[]{:S(2)}, u32[]{:S(2)}) collective-permute-start(bf16[96,8,128]{2,1,0:T(8,128)(2,1)S(1)} %collective-permute-done.11.refs_1_), channel_id=1, source_target_pairs={{0,1},{1,2},{2,3},{3,0},{4,5},{5,6},{6,7},{7,4},{8,9},{9,10},{10,1... | collective-permute-start | bytes 589832 | tf_op jit(solution)/shard_map/ppermute | solution.py:781
  122.7 12.5 %collective-permute-start.16 = (bf16[96,8,128]{2,1,0:T(8,128)(2,1)S(1)}, bf16[96,8,128]{2,1,0:T(8,128)(2,1)S(1)}, u32[]{:S(2)}, u32[]{:S(2)}) collective-permute-start(bf16[96,8,128]{2,1,0:T(8,128)(2,1)S(1)} %collective-permute-done.14.refs_4_), channel_id=1, source_target_pairs={{1,0},{2,1},{3,2},{0,3},{5,4},{6,5},{7,6},{4,7},{9,8},{10,9},{11,1... | collective-permute-start | bytes 589832 | tf_op jit(solution)/shard_map/ppermute | solution.py:781
